TPU v7x, 32 devices: a whole 2x2x4 slice. The times are simulated.
32 devices in a mesh: dp: 8 (over y, x, core), tensor: 4 (over z).
Axes of the slice: x: 2, y: 2, z: 4, core: 2. Of those that a mesh axis runs over, the one named last changes fastest.
Arguments:
- tokens: bfloat16 [32768, 1024], P('dp'), may hold values from -126 to 126
- route_offset: int32 [8, 512], P('dp'), may hold values from 0 to 7
- unit_sequence: int32 [8, 512], P('dp'), may hold values from 0 to 511, as said below
- cotangent: bfloat16 [32768, 1024], P('dp'), may hold values from -6 to 6
- router_weight: bfloat16 [1024], replicated, may hold values from -0.09375 to 0.09375
- first_gain: bfloat16 [1024], replicated, may hold values from 0.5 to 1.5
- second_gain: bfloat16 [1024], replicated, may hold values from 0.5 to 1.5
- qkv_weight: bfloat16 [3, 1024, 1024], P(None, None, 'tensor'), may hold values from -0.1875 to 0.1875
- out_weight: bfloat16 [1024, 1024], P('tensor'), may hold values from -0.5 to 0.5
- up_weight: bfloat16 [1024, 4096], P(None, 'tensor'), may hold values from -0.1875 to 0.1875
- down_weight: bfloat16 [4096, 1024], P('tensor'), may hold values from -0.09375 to 0.09375
Outputs:
- output: bfloat16 [32768, 1024], P('dp')
- input_grad: bfloat16 [32768, 1024], P('dp')
- router_grad: float32 [1024], replicated
- first_gain_grad: float32 [1024], replicated
- second_gain_grad: float32 [1024], replicated
- qkv_grad: float32 [3, 1024, 1024], P(None, None, 'tensor')
- out_grad: float32 [1024, 1024], P('tensor')
- up_grad: float32 [1024, 4096], P(None, 'tensor')
- down_grad: float32 [4096, 1024], P('tensor')
- score_stats: float32 [2], replicated
Inputs may be any that keep to these rules, and one draw needn't show every extreme that they name: `unit_sequence`: along each row it starts at 0 and rises by 0 or 1 from one group to the next; some row holds a single sequence of 4096 tokens and some row 512 sequences.
All inputs are finite; a program needn't handle non-finite values.
Results may differ from a plain program's by a relative error of at most 0.015.
Values may be sent and summed in bfloat16 or wider, within the bound.
No kernel may reach another device: no remote copies, remote signals or barrier semaphores. Data moves between devices by JAX's collectives and lax.ppermute only.
A program may use at most 128 MiB of HBM per device.

v0:
```python
import jax
import jax.numpy as jnp
from jax import lax
from jax.sharding import PartitionSpec as P

HEAD_DIM = 64


eps = 1e-06
mask_fill = -1000000000.0


def normalize(row_block, gain_row):
    return (
        row_block
        * lax.rsqrt(jnp.mean(row_block * row_block, axis=-1, keepdims=True) + eps)
        * gain_row
    )


def gelu_tanh(value_in):
    return jax.nn.gelu(value_in, approximate=True)


def per_device(
    tokens,
    route_offset,
    unit_sequence,
    cotangent,
    router_weight,
    first_gain,
    second_gain,
    qkv_weight,
    out_weight,
    up_weight,
    down_weight,
):
    rows_local = tokens.shape[0]
    routed_count = route_offset.shape[1]
    score_scale = HEAD_DIM ** (-0.5)
    row_order = jnp.arange(routed_count, dtype=jnp.int32)
    positions = 8 * row_order + route_offset[0]
    seq_ids = unit_sequence[0]
    allowed = (seq_ids[:, None] == seq_ids[None, :]) & (row_order[:, None] >= row_order[None, :])
    scores = jnp.dot(tokens, router_weight, preferred_element_type=jnp.float32)
    routed_scores = scores[positions]
    stat_terms = jnp.stack([jnp.sum(scores * scores), jnp.sum(routed_scores * routed_scores)])
    gating = jax.nn.sigmoid(routed_scores)
    picked_low = tokens[positions]
    picked = picked_low.astype(jnp.float32)
    router_float = router_weight.astype(jnp.float32)
    first_rows, first_back = jax.vjp(normalize, picked, first_gain.astype(jnp.float32))
    first_low = first_rows.astype(jnp.bfloat16)
    projected = jnp.einsum(
        "cd,kdh->kch", first_low, qkv_weight, preferred_element_type=jnp.float32
    ).astype(jnp.bfloat16)
    heads_local = projected.shape[2] // HEAD_DIM
    query_rows = projected[0].reshape(routed_count, heads_local, HEAD_DIM)
    key_rows = projected[1].reshape(routed_count, heads_local, HEAD_DIM)
    value_rows = projected[2].reshape(routed_count, heads_local, HEAD_DIM)

    def masked_logits():
        raw = (
            jnp.einsum("qhe,khe->hqk", query_rows, key_rows, preferred_element_type=jnp.float32)
            * score_scale
        )
        return jnp.where(allowed[None], raw, mask_fill)

    logits = masked_logits()
    row_max = jnp.max(logits, axis=-1, keepdims=True)
    log_total = row_max + jnp.log(jnp.sum(jnp.exp(logits - row_max), axis=-1, keepdims=True))
    probs_low = jnp.exp(logits - log_total).astype(jnp.bfloat16)
    head_out = jnp.einsum("hqk,khe->qhe", probs_low, value_rows, preferred_element_type=jnp.float32)
    head_out = head_out.astype(jnp.bfloat16).reshape(routed_count, heads_local * HEAD_DIM)
    attn_part = jnp.dot(head_out, out_weight, preferred_element_type=jnp.float32)
    attended = lax.psum(attn_part.astype(jnp.bfloat16), "tensor").astype(jnp.float32)
    hidden_in = picked + attended
    second_rows, second_back = jax.vjp(normalize, hidden_in, second_gain.astype(jnp.float32))
    second_low = second_rows.astype(jnp.bfloat16)
    pre_act = jnp.dot(second_low, up_weight, preferred_element_type=jnp.float32)
    activated, gelu_back = jax.vjp(gelu_tanh, pre_act)
    activated_low = activated.astype(jnp.bfloat16)
    mlp_part = jnp.dot(activated_low, down_weight, preferred_element_type=jnp.float32)
    mixer_out = lax.psum(mlp_part.astype(jnp.bfloat16), "tensor").astype(jnp.float32)
    branch = attended + mixer_out
    new_rows = picked + gating[:, None] * branch
    output = tokens.at[positions].set(new_rows.astype(jnp.bfloat16))
    grad_rows = cotangent[positions].astype(jnp.float32)
    grad_gating = jnp.sum(grad_rows * branch, axis=-1)
    grad_score = grad_gating * gating * (1.0 - gating)
    router_part = jnp.dot(grad_score, picked, precision=lax.Precision.HIGHEST)
    grad_branch = gating[:, None] * grad_rows
    grad_mixer = grad_branch.astype(jnp.bfloat16)
    down_part = jnp.einsum(
        "cf,cd->fd", activated_low, grad_mixer, preferred_element_type=jnp.float32
    )
    grad_act = jnp.einsum("cd,fd->cf", grad_mixer, down_weight, preferred_element_type=jnp.float32)
    grad_pre = gelu_back(grad_act)[0].astype(jnp.bfloat16)
    up_part = jnp.einsum("cd,cf->df", second_low, grad_pre, preferred_element_type=jnp.float32)
    grad_second = lax.psum(
        jnp.einsum("cf,df->cd", grad_pre, up_weight, preferred_element_type=jnp.float32).astype(
            jnp.bfloat16
        ),
        "tensor",
    ).astype(jnp.float32)
    grad_hidden, second_gain_part = second_back(grad_second)
    grad_attended = (grad_branch + grad_hidden).astype(jnp.bfloat16)
    out_part = jnp.einsum("cj,cd->jd", head_out, grad_attended, preferred_element_type=jnp.float32)
    grad_head = jnp.einsum(
        "cd,jd->cj", grad_attended, out_weight, preferred_element_type=jnp.float32
    )
    grad_head = grad_head.astype(jnp.bfloat16).reshape(routed_count, heads_local, HEAD_DIM)
    exact_probs = jnp.exp(masked_logits() - log_total)
    grad_probs = jnp.einsum(
        "qhe,khe->hqk", grad_head, value_rows, preferred_element_type=jnp.float32
    )
    grad_values = jnp.einsum(
        "hqk,qhe->khe", probs_low, grad_head, preferred_element_type=jnp.float32
    )
    grad_logits = exact_probs * (
        grad_probs - jnp.sum(exact_probs * grad_probs, axis=-1, keepdims=True)
    )
    grad_logits = grad_logits.astype(jnp.bfloat16)
    grad_query = (
        jnp.einsum("hqk,khe->qhe", grad_logits, key_rows, preferred_element_type=jnp.float32)
        * score_scale
    )
    grad_keys = (
        jnp.einsum("hqk,qhe->khe", grad_logits, query_rows, preferred_element_type=jnp.float32)
        * score_scale
    )
    grad_projected = jnp.stack([grad_query, grad_keys, grad_values]).reshape(
        3, routed_count, heads_local * HEAD_DIM
    )
    grad_projected = grad_projected.astype(jnp.bfloat16)
    qkv_part = jnp.einsum(
        "cd,kch->kdh", first_low, grad_projected, preferred_element_type=jnp.float32
    )
    grad_first = lax.psum(
        jnp.einsum(
            "kch,kdh->cd", grad_projected, qkv_weight, preferred_element_type=jnp.float32
        ).astype(jnp.bfloat16),
        "tensor",
    ).astype(jnp.float32)
    grad_norm, first_gain_part = first_back(grad_first)
    grad_input_rows = (
        grad_rows + grad_hidden + grad_norm + grad_score[:, None] * router_float[None, :]
    )
    input_grad = cotangent.at[positions].set(grad_input_rows.astype(jnp.bfloat16))
    (
        qkv_grad,
        out_grad,
        up_grad,
        down_grad,
        first_gain_grad,
        second_gain_grad,
        router_grad,
        stat_sums,
    ) = lax.psum(
        (
            qkv_part,
            out_part,
            up_part,
            down_part,
            first_gain_part,
            second_gain_part,
            router_part,
            stat_terms,
        ),
        "dp",
    )
    devices_dp = lax.axis_size("dp")
    score_stats = jnp.stack(
        [stat_sums[0] / (rows_local * devices_dp), stat_sums[1] / (routed_count * devices_dp)]
    )
    return (
        output,
        input_grad,
        router_grad,
        first_gain_grad,
        second_gain_grad,
        qkv_grad,
        out_grad,
        up_grad,
        down_grad,
        score_stats,
    )


def solution(mesh):
    placed = (
        P("dp", None),
        P("dp", None),
        P("dp", None),
        P("dp", None),
        P(),
        P(),
        P(),
        P(None, None, "tensor"),
        P("tensor", None),
        P(None, "tensor"),
        P("tensor", None),
    )
    return jax.shard_map(
        per_device,
        mesh=mesh,
        in_specs=placed,
        out_specs=(
            P("dp", None),
            P("dp", None),
            P(),
            P(),
            P(),
            P(None, None, "tensor"),
            P("tensor", None),
            P(None, "tensor"),
            P("tensor", None),
            P(),
        ),
        check_vma=False,
    )
```

profile of v0, /device:TPU:0, one launch (start us, length us, event | category | flops | bytes accessed | tf_op | source)
XLA Modules:
  0.0 463.4 jit_solution(4609117516671059229)
XLA Ops:
  7.2 7.9 %copy.59 = bf16[4096,1024]{1,0:T(8,128)(2,1)} copy(bf16[4096,1024]{1,0:T(8,128)(2,1)} %param.11) | data formatting | bytes 16777216
  15.1 7.8 %copy.60 = bf16[4096,1024]{1,0:T(8,128)(2,1)} copy(bf16[4096,1024]{1,0:T(8,128)(2,1)} %param.14) | data formatting | bytes 16777216
  23.0 7.2 %gather_fusion = bf16[512,1024]{1,0:T(8,128)(2,1)S(1)} fusion(bf16[4096,1024]{1,0:T(8,128)(2,1)} %copy.59, s32[1024]{0:T(1024)S(1)} %pad_clamp_fusion), kind=kCustom, calls=%fused_computation | custom fusion | bytes 2099200 | tf_op jit(solution)/shard_map/gather | solution.py:49
  30.5 2.5 fusion.27
  33.3 0.9 fusion
  34.3 0.9 exponential_reduce_fusion
  35.2 1.1 copy-done.2
  36.3 1.3 convolution_convert_fusion.6
  38.3 1.4 convolution_convert_fusion.2
  40.3 7.9 %gather_fusion.2 = bf16[512,1024]{1,0:T(8,128)(2,1)} fusion(bf16[4096,1024]{1,0:T(8,128)(2,1)} %copy.60, s32[1024]{0:T(1024)S(1)} %pad_clamp_fusion), kind=kCustom, calls=%fused_computation.2 | custom fusion | bytes 2099200 | tf_op jit(solution)/shard_map/gather | solution.py:88
  48.2 5.7 %fusion.53 = f32[1,4096]{1,0:T(1,128)S(1)} fusion(bf16[4096,1024]{1,0:T(8,128)(2,1)} %copy.59, bf16[1024,1]{0,1:T(2,128)(2,1)S(1)} %reshape.217), kind=kOutput, calls=%fused_computation.102 | convolution fusion | flops 8388608 | bytes 8407040 | tf_op jit(solution)/shard_map/dot_general | solution.py:45
  53.9 3.1 gather_fusion.1
  57.0 37.4 %all-reduce.8.cloned.1.call-done = bf16[512,1024]{1,0:T(8,128)(2,1)} async-done(((bf16[512,1024]{1,0:T(8,128)(2,1)}), bf16[512,1024]{1,0:T(8,128)(2,1)}) %all-reduce.8.cloned.1.call-update) | async-done | bytes 1048592 | tf_op jit(solution)/shard_map/psum | solution.py:76
  94.4 1.7 multiply_reduce_fusion.1
  96.1 2.9 fusion.50
  99.1 2.4 convolution_convert_fusion.1
  101.5 2.4 fusion.19
  103.9 1.0 copy-done.18
  104.9 2.3 convolution_convert_fusion
  107.4 86.4 %all-reduce.14.cloned.1.call-done = (bf16[512,1024]{1,0:T(8,128)(2,1)}, bf16[512,1024]{1,0:T(8,128)(2,1)}) async-done(((bf16[512,1024]{1,0:T(8,128)(2,1)}, bf16[512,1024]{1,0:T(8,128)(2,1)}), (bf16[512,1024]{1,0:T(8,128)(2,1)}, bf16[512,1024]{1,0:T(8,128)(2,1)})) %all-reduce.14.cloned.1.call-update) | async-done | bytes 2097168 | tf_op jit(solution)/shard_map/psum | solution.py:84
  193.8 3.1 fusion.11
  197.0 0.9 fusion.9
  198.5 1.2 copy-done.3
  199.7 2.0 convolution_convert_fusion.4
  201.7 1.5 multiply_reduce_fusion
  203.3 1.3 multiply_convert_fusion
  205.5 1.2 fusion.28
  206.7 1.8 copy.38
  208.5 0.8 copy.37
  209.3 1.1 copy.36
  210.4 3.6 bitcast_convert_fusion
  214.3 4.8 %fusion.49 = f32[1024,1024]{1,0:T(8,128)} fusion(bf16[512,1024]{1,0:T(8,128)(2,1)} %copy-done.18, bf16[512,1024]{1,0:T(8,128)(2,1)S(1)} %copy-done.5, bf16[512,1024]{1,0:T(8,128)(2,1)S(1)} %gather_fusion, f32[1024]{0:T(1024)S(1)} %convert_element_type.95, f32[512]{0:T(512)S(1)} %fusion.44), kind=kOutput, calls=%fused_computation.98 | convolution fusion | flops 1076887552 | bytes 7346176 | tf_op jit(solution)/shard_map/cd,cf->df/dot_general | solution.py:99
  219.1 3.6 fusion.37
  222.7 1.4 fusion.55
  224.2 2.8 convolution_bitcast_fusion
  227.6 12.2 %scatter_custom_fusion = bf16[4096,1024]{1,0:T(8,128)(2,1)} fusion(bf16[4096,1024]{1,0:T(8,128)(2,1)} %copy.59, s32[512]{0:T(512)S(1)} %bitcast.82, bf16[512,1024]{1,0:T(8,128)(2,1)S(1)} %gather_fusion, bf16[512,1024]{1,0:T(8,128)(2,1)} %get-tuple-element.43, bf16[512,1024]{1,0:T(8,128)(2,1)S(1)} %copy-done.5, f32[512]{0:T(512)S(1)} %add_divide_fusion), kind=kCustom, calls=%fused_computation.72 | custom fusion | flops 3670016 | bytes 11536384 | tf_op jit(solution)/shard_map/scatter | solution.py:87
  240.5 1.4 pad_maximum_fusion.3
  242.3 22.6 %all-reduce.10.cloned.1.call-done = bf16[512,1024]{1,0:T(8,128)(2,1)} async-done(((bf16[512,1024]{1,0:T(8,128)(2,1)}), bf16[512,1024]{1,0:T(8,128)(2,1)}) %all-reduce.10.cloned.1.call-update) | async-done | bytes 1048592 | tf_op jit(solution)/shard_map/psum | solution.py:139
  264.9 2.3 fusion.12
  267.3 2.5 fusion.22
  269.8 11.8 %scatter_fusion = bf16[4096,1024]{1,0:T(8,128)(2,1)} fusion(bf16[4096,1024]{1,0:T(8,128)(2,1)} %copy.60, s32[512]{0:T(512)S(1)} %bitcast.83, bf16[512,1024]{1,0:T(8,128)(2,1)} %fusion.22), kind=kCustom, calls=%fused_computation.4 | custom fusion | bytes 3147776 | tf_op jit(solution)/shard_map/scatter | solution.py:149
  281.6 25.6 %all-reduce = (f32[1024]{0:T(1024)}, f32[1024]{0:T(1024)}, f32[1024]{0:T(1024)}, f32[2]{0:T(128)S(1)}) all-reduce(f32[1024]{0:T(1024)S(1)} %bitcast.84, f32[1024]{0:T(1024)S(1)} %get-tuple-element.32, f32[1024]{0:T(1024)S(1)} %get-tuple-element.30, f32[2]{0:T(128)S(1)} %pad_maximum_fusion.3), channel_id=1, replica_groups=mesh['dp'=8,'tensor'=4] {'dp'}, use_global_device_ids=true, to_apply=%region_14.15 | all-reduce | flops 3074 | bytes 24592 | tf_op jit(solution)/shard_map/psum | solution.py:159
  309.7 134.1 %all-reduce.12.cloned.1.call-done = (f32[3,1024,256]{1,2,0:T(8,128)}, f32[256,1024]{1,0:T(8,128)}, f32[1024,1024]{1,0:T(8,128)}, f32[1024,1024]{1,0:T(8,128)}) async-done(((f32[3,1024,256]{1,2,0:T(8,128)}, f32[256,1024]{1,0:T(8,128)}, f32[1024,1024]{1,0:T(8,128)}, f32[1024,1024]{1,0:T(8,128)}), (f32[3,1024,256]{1,2,0:T(8,128)}, f32[256,1024]{1,0:T(8,128)}, f32[1024,1024]{1,0:T(8,128)}, ...) | async-done | bytes 12582928 | tf_op jit(solution)/shard_map/psum | solution.py:159
  443.7 3.6 copy.40
  447.4 1.0 copy.61
  448.3 4.9 %copy.62 = f32[1024,1024]{1,0:T(8,128)} copy(f32[1024,1024]{1,0:T(8,128)} %get-tuple-element.63) | data formatting | bytes 8388608
  453.3 2.1 copy.63
  455.4 1.0 copy-done.1
  (98 shorter events, 7.0 us)
Async XLA Ops:
  7.2 91.9 %copy-start = (bf16[1024,1024]{1,0:T(8,128)(2,1)S(1)}, bf16[1024,1024]{1,0:T(8,128)(2,1)}, u32[]{:S(2)}) copy-start(bf16[1024,1024]{1,0:T(8,128)(2,1)} %param.21) | copy-start | bytes 6291460
  7.2 87.2 %all-reduce.8.cloned.1.call-start = ((), (), s32[]{:S(2)}) async-start(), calls=%async_computation | async-start | bytes 2097152 | tf_op jit(solution)/shard_map/psum | solution.py:76
  15.1 7.8 %copy-start.32 = (s32[1,512]{1,0:T(1,128)S(1)}, s32[1,512]{1,0:T(1,128)}, u32[]{:S(2)}) copy-start(s32[1,512]{1,0:T(1,128)} %param.12) | copy-start | bytes 6148
  15.1 7.8 %copy-start.30 = (bf16[1024]{0:T(1024)(128)(2,1)S(1)}, bf16[1024]{0:T(1024)(128)(2,1)}, u32[]{:S(2)}) copy-start(bf16[1024]{0:T(1024)(128)(2,1)} %param.16) | copy-start | bytes 6148
  30.5 2.6 copy-start.28
  33.1 1.2 copy-start.14
  33.1 1.2 copy-start.16
  33.1 2.1 copy-start.22
  34.3 2.0 copy-start.2
  36.3 2.0 copy-start.24
  37.5 0.7 copy-start.19
  37.6 2.7 copy-start.31
  39.7 154.1 %all-reduce.14.cloned.1.call-start = ((), (), s32[]{:S(2)}) async-start(), calls=%async_computation.3 | async-start | bytes 4194304 | tf_op jit(solution)/shard_map/psum | solution.py:84
  40.2 7.9 %copy-start.29 = (bf16[1024]{0:T(1024)(128)(2,1)S(1)}, bf16[1024]{0:T(1024)(128)(2,1)}, u32[]{:S(2)}) copy-start(bf16[1024]{0:T(1024)(128)(2,1)} %param.15) | copy-start | bytes 6148
  94.4 1.7 copy-start.4
  99.1 2.4 copy-start.34
  99.1 2.4 copy-start.6
  101.5 3.4 copy-start.33
  103.9 1.0 copy-start.18
  107.2 86.6 %copy-start.5 = (bf16[512,1024]{1,0:T(8,128)(2,1)S(1)}, bf16[512,1024]{1,0:T(8,128)(2,1)}, u32[]{:S(2)}) copy-start(bf16[512,1024]{1,0:T(8,128)(2,1)} %all-reduce.8.cloned.1.call-done) | copy-start | bytes 3145732
  107.2 86.6 %copy-start.7 = (bf16[512,1024]{1,0:T(8,128)(2,1)S(1)}, bf16[512,1024]{1,0:T(8,128)(2,1)}, u32[]{:S(2)}) copy-start(bf16[512,1024]{1,0:T(8,128)(2,1)} %gather_fusion.2) | copy-start | bytes 3145732
  107.2 157.7 %all-reduce.10.cloned.1.call-start = ((), (), s32[]{:S(2)}) async-start(), calls=%async_computation.1 | async-start | bytes 2097152 | tf_op jit(solution)/shard_map/psum | solution.py:139
  193.8 3.2 copy-start.8
  197.0 1.0 copy-start.25
  197.0 2.7 copy-start.3
  198.0 3.7 copy-start.11
  199.7 2.0 copy-start.23
  203.2 1.3 copy-start.17
  204.5 1.0 copy-start.15
  214.0 229.7 %all-reduce.12.cloned.1.call-start = ((), (), s32[]{:S(2)}) async-start(), calls=%async_computation.2 | async-start | bytes 25165824 | tf_op jit(solution)/shard_map/psum | solution.py:159
  214.2 4.8 %copy-start.35 = (f32[512,1024]{1,0:T(8,128)S(1)}, f32[512,1024]{1,0:T(8,128)}, u32[]{:S(2)}) copy-start(f32[512,1024]{1,0:T(8,128)} %copy-done.34) | copy-start | bytes 6291460
  219.1 3.6 copy-start.12
  219.1 3.6 copy-start.20
  222.7 1.5 copy-start.26
  222.7 1.5 copy-start.27
  264.9 2.3 copy-start.9
  264.9 2.3 copy-start.10
  443.7 3.6 copy-start.21
  448.3 4.9 %copy-start.13 = (f32[1024,1024]{1,0:T(8,128)S(1)}, f32[1024,1024]{1,0:T(8,128)}, u32[]{:S(2)}) copy-start(f32[1024,1024]{1,0:T(8,128)} %get-tuple-element.64) | copy-start | bytes 12582916
  453.3 3.1 copy-start.1
Sparse Core Ops, SparseCore 0:
  39.8 54.5 all-reduce.7
  107.3 86.4 all-reduce.13
  214.1 50.7 all-reduce.9
  270.5 173.2 all-reduce.11
where the time goes:
time: 471 us; the launch traced here: 463 us
  waiting for transfers between devices  280 us (59%)
  local copies, waits for them, and re-layouts  67.2 us (14%)
  matrix products  44.5 us (9%)
  other arithmetic  28.7 us (6%)
  blocking collectives  25.6 us (5%)
  between operations  15.9 us (3%)
    psum x1, waiting for transfers between devices, per_device(): lax.psum((qkv_part, out_part, up_part, down_part, first_gain_part, second...  134 us
    psum x1, waiting for transfers between devices, per_device(): lax.psum(mlp_part.astype(jnp.bfloat16), 'tensor').astype(jnp.float32)  86.4 us
    psum x1, waiting for transfers between devices, per_device(): lax.psum(attn_part.astype(jnp.bfloat16), 'tensor').astype(jnp.float32)  37.4 us
    unnamed x79, local copies, waits for them, and re-layouts  32.7 us
    psum x1, blocking collectives, per_device(): lax.psum((qkv_part, out_part, up_part, down_part, first_gain_part, second...  25.6 us
    psum x1, waiting for transfers between devices, per_device(): lax.psum(jnp.einsum('kch,kdh->cd', grad_projected, qkv_weight, preferred_...  22.6 us
    scatter x1, other arithmetic, per_device(): output = tokens.at[positions].set(new_rows.astype(jnp.bfloat16))  12.2 us
    scatter x1, local copies, waits for them, and re-layouts, per_device(): cotangent.at[positions].set(grad_input_rows.astype(jnp.bfloat16))  11.8 us
  transfers between devices with their start and end apart: 4, of which 4 were waited for; matrix products, arithmetic and copies ran while one was open for 14% of the time, Pallas kernels for 0%

commit v1 on v0

v1 whole, which is shorter than its diff:
```python
import jax
import jax.numpy as jnp
from jax import lax
from jax.sharding import PartitionSpec as P

HEAD_DIM = 64
eps = 1e-06
mask_fill = -1000000000.0
BF = jnp.bfloat16
F32 = jnp.float32


def swap(values, axis, bits):
    size = lax.axis_size(axis)
    return lax.ppermute(values, axis, [(i, i ^ bits) for i in range(size)])


def dot(left, right, dims):
    return lax.dot_general(left, right, (dims, ((), ())), preferred_element_type=F32)


NN = ((1,), (0,))
NT = ((1,), (1,))
TN = ((0,), (0,))


def inverse_rms(rows):
    return lax.rsqrt(jnp.mean(rows * rows, axis=-1, keepdims=True) + eps)


def norm_back(grad, rows, inverse, gain):
    scaled = grad * gain
    along = jnp.mean(scaled * rows, axis=-1, keepdims=True)
    return inverse * scaled - rows * (inverse * inverse * inverse * along)


def relative_blocks(whole, index, count):
    rows = whole.shape[0] // count
    return [
        lax.dynamic_slice_in_dim(whole, (index ^ k) * rows, rows, 0) for k in range(count)
    ]


def reduce_blocks(blocks, order):
    kept = list(range(len(blocks)))
    held = jnp.stack(blocks)
    for bit in order:
        stay = [n for n, k in enumerate(kept) if not k & bit]
        leave = [kept.index(kept[n] | bit) for n in stay]
        sent = swap(jnp.stack([held[n] for n in leave]), "dp", bit)
        mine = jnp.stack([held[n] for n in stay])
        held = (mine.astype(F32) + sent.astype(F32)).astype(BF)
        kept = [kept[n] for n in stay]
    return held[0]


def gather_blocks(own, order):
    held = own[None]
    keys = [0]
    for bit in order:
        other = swap(held, "dp", bit)
        held = jnp.concatenate([held, other])
        keys = keys + [k ^ bit for k in keys]
    return {k: held[n] for n, k in enumerate(keys)}


def per_device(
    tokens,
    route_offset,
    unit_sequence,
    cotangent,
    router_weight,
    first_gain,
    second_gain,
    qkv_weight,
    out_weight,
    up_weight,
    down_weight,
):
    rows_local, width = tokens.shape
    routed = route_offset.shape[1]
    ways = lax.axis_size("tensor")
    copies = lax.axis_size("dp")
    mine = lax.axis_index("tensor")
    part = lax.axis_index("dp")
    peers = range(1, ways)
    score_scale = HEAD_DIM ** (-0.5)

    quarter = part & 3
    piece_rows = out_weight.shape[0] // 4
    piece = lax.dynamic_slice_in_dim(out_weight, quarter * piece_rows, piece_rows, 0)
    here = jnp.stack([swap(piece, "tensor", k) for k in peers])
    beside = swap(here, "dp", 2)
    across = swap(jnp.stack([here, beside]), "dp", 1)
    pair_even = jnp.where(part & 1 == 0, jnp.stack([here, across[0]]), jnp.stack([across[0], here]))
    pair_odd = jnp.where(part & 1 == 0, jnp.stack([beside, across[1]]), jnp.stack([across[1], beside]))
    quads = jnp.where(
        part & 2 == 0,
        jnp.concatenate([pair_even, pair_odd]),
        jnp.concatenate([pair_odd, pair_even]),
    )
    out_groups = [out_weight] + [
        quads[:, k - 1].reshape(out_weight.shape) for k in peers
    ]

    row_order = jnp.arange(routed, dtype=jnp.int32)
    positions = 8 * row_order + route_offset[0]
    seq_ids = unit_sequence[0]
    allowed = (seq_ids[:, None] == seq_ids[None, :]) & (row_order[:, None] >= row_order[None, :])
    scores = jnp.dot(tokens, router_weight, preferred_element_type=F32)
    picked_low = tokens[positions]
    picked = picked_low.astype(F32)
    routed_scores = scores[positions]
    gating = jax.nn.sigmoid(routed_scores)[:, None]
    router_float = router_weight.astype(F32)
    gain_one = first_gain.astype(F32)
    gain_two = second_gain.astype(F32)

    inverse_one = inverse_rms(picked)
    first_low = (picked * inverse_one * gain_one).astype(BF)
    weight_wide = jnp.concatenate([qkv_weight[0], qkv_weight[1], qkv_weight[2]], axis=1)
    projected = dot(first_low, weight_wide, NN).astype(BF)
    heads_width = qkv_weight.shape[2]
    heads_local = heads_width // HEAD_DIM

    def split(rows):
        return rows.reshape(routed, heads_local, HEAD_DIM)

    query_rows = split(projected[:, :heads_width])
    key_rows = split(projected[:, heads_width : 2 * heads_width])
    value_rows = split(projected[:, 2 * heads_width :])
    raw = jnp.einsum("qhe,khe->hqk", query_rows, key_rows, preferred_element_type=F32) * score_scale
    logits = jnp.where(allowed[None], raw, mask_fill)
    row_max = jnp.max(logits, axis=-1, keepdims=True)
    raised = jnp.exp(logits - row_max)
    probs = raised / jnp.sum(raised, axis=-1, keepdims=True)
    probs_low = probs.astype(BF)
    head_out = jnp.einsum("hqk,khe->qhe", probs_low, value_rows, preferred_element_type=F32)
    head_out = head_out.astype(BF).reshape(routed, heads_width)

    head_groups = [head_out] + [swap(head_out, "tensor", k) for k in peers]
    attended = sum(dot(rows, weight, NN) for rows, weight in zip(head_groups, out_groups))
    hidden_in = picked + attended
    inverse_two = inverse_rms(hidden_in)
    second_low = (hidden_in * inverse_two * gain_two).astype(BF)
    pre_act = dot(second_low, up_weight, NN)
    activated, gelu_back = jax.vjp(lambda v: jax.nn.gelu(v, approximate=True), pre_act)
    activated_low = activated.astype(BF)
    grad_rows = cotangent[positions].astype(F32)
    grad_branch = gating * grad_rows
    grad_mixer = grad_branch.astype(BF)
    grad_act = dot(grad_mixer, down_weight, NT)
    grad_pre = gelu_back(grad_act)[0].astype(BF)
    second_part = dot(grad_pre, up_weight, NT)
    hidden_part = norm_back(second_part, hidden_in, inverse_two, gain_two)
    second_gain_part = jnp.sum(second_part * hidden_in * inverse_two, axis=0)
    attended_part = (hidden_part + grad_branch * (1.0 / ways)).astype(BF)

    head_sent = [dot(attended_part, weight, NT).astype(BF) for weight in out_groups]
    head_terms = [head_sent[0]] + [swap(head_sent[k], "tensor", k) for k in peers]
    grad_head = split(sum(term.astype(F32) for term in head_terms).astype(BF))

    mixer_part = dot(activated_low, down_weight, NN).astype(BF)
    mixer_blocks = relative_blocks(mixer_part, mine, ways)
    mixer_own = sum(
        term.astype(F32)
        for term in [mixer_blocks[0]] + [swap(mixer_blocks[k], "tensor", k) for k in peers]
    )
    own_rows = routed // ways

    def own(rows):
        return lax.dynamic_slice_in_dim(rows, mine * own_rows, own_rows, 0)

    picked_own, gating_own, attended_own, grad_own = own(picked), own(gating), own(attended), own(grad_rows)
    branch_own = attended_own + mixer_own
    new_own = (picked_own + gating_own * branch_own).astype(BF)
    grad_gating = jnp.sum(grad_own * branch_own, axis=-1, keepdims=True)
    grad_score = grad_gating * gating_own * (1.0 - gating_own)
    router_part = jnp.sum(grad_score * picked_own, axis=0)

    down_part = dot(activated_low, grad_mixer, TN).astype(BF)
    up_part = dot(second_low, grad_pre, TN).astype(BF)
    ladder = [1 << b for b in range(1, copies.bit_length() - 1)]
    order_a = [1] + ladder
    order_b = [1] + ladder[::-1]
    down_own = reduce_blocks(relative_blocks(down_part, part, copies), order_a)
    up_own = reduce_blocks(relative_blocks(up_part, part, copies), order_b)

    grad_probs = jnp.einsum("qhe,khe->hqk", grad_head, value_rows, preferred_element_type=F32)
    grad_values = jnp.einsum("hqk,qhe->khe", probs_low, grad_head, preferred_element_type=F32)
    grad_logits = probs * (grad_probs - jnp.sum(probs * grad_probs, axis=-1, keepdims=True))
    grad_logits = grad_logits.astype(BF)
    grad_query = jnp.einsum("hqk,khe->qhe", grad_logits, key_rows, preferred_element_type=F32) * score_scale
    grad_keys = jnp.einsum("hqk,qhe->khe", grad_logits, query_rows, preferred_element_type=F32) * score_scale
    grad_projected = jnp.concatenate(
        [g.reshape(routed, heads_width) for g in (grad_query, grad_keys, grad_values)], axis=1
    ).astype(BF)
    first_part = dot(grad_projected, weight_wide, NT)
    norm_part = norm_back(first_part, picked, inverse_one, gain_one)
    first_gain_part = jnp.sum(first_part * picked * inverse_one, axis=0)
    input_part = (hidden_part + norm_part).astype(BF)
    input_blocks = relative_blocks(input_part, mine, ways)
    input_terms = [input_blocks[0]] + [swap(input_blocks[k], "tensor", k) for k in peers]
    input_own = sum(term.astype(F32) for term in input_terms) + grad_own + grad_score * router_float
    input_own = input_own.astype(BF)

    qkv_part = dot(first_low, grad_projected, TN).astype(BF)
    qkv_own = reduce_blocks(relative_blocks(qkv_part, part, copies), order_b)
    out_parts = [dot(rows, attended_part, TN).astype(BF) for rows in head_groups]
    out_blocks = [relative_blocks(block, part, copies) for block in out_parts]
    out_own = reduce_blocks(
        [jnp.stack([out_blocks[k][j] for k in range(ways)]) for j in range(copies)], order_a
    )
    out_own = sum(
        term.astype(F32) for term in [out_own[0]] + [swap(out_own[k], "tensor", k) for k in peers]
    ).astype(BF)

    score_sum = jnp.sum(scores * scores) * (1.0 / ways)
    routed_sum = jnp.sum(routed_scores * routed_scores) * (1.0 / ways)
    stats = jnp.zeros((width,), F32).at[0].set(score_sum).at[1].set(routed_sum)
    small = jnp.stack([router_part, first_gain_part, second_gain_part, stats])
    for bit in [1] + ladder:
        small = small + swap(small, "dp", bit)
    step = 1
    while step < ways:
        small = small + swap(small, "tensor", step)
        step *= 2

    def place(base, blocks, index, rows):
        for k, block in blocks.items():
            base = lax.dynamic_update_slice_in_dim(base, block, (index ^ k) * rows, 0)
        return base

    new_rows = place(
        jnp.zeros((routed, width), BF),
        {k: (new_own if k == 0 else swap(new_own, "tensor", k)) for k in range(ways)},
        mine,
        own_rows,
    )
    input_rows = place(
        jnp.zeros((routed, width), BF),
        {k: (input_own if k == 0 else swap(input_own, "tensor", k)) for k in range(ways)},
        mine,
        own_rows,
    )
    output = tokens.at[positions].set(new_rows)
    input_grad = cotangent.at[positions].set(input_rows)

    def spread(block, order, rows):
        pieces = gather_blocks(block, order[::-1])
        pieces = {k: v.astype(F32) for k, v in pieces.items()}
        return place(jnp.zeros((rows, block.shape[1]), F32), pieces, part, rows // copies)

    down_grad = spread(down_own, order_a, down_weight.shape[0])
    up_grad = spread(up_own, order_b, up_weight.shape[0])
    qkv_wide = spread(qkv_own, order_b, width)
    out_grad = spread(out_own, order_a, out_weight.shape[0])
    qkv_grad = jnp.stack(jnp.split(qkv_wide, 3, axis=1))
    score_stats = jnp.stack(
        [small[3, 0] / (rows_local * copies), small[3, 1] / (routed * copies)]
    )
    return (
        output,
        input_grad,
        small[0],
        small[1],
        small[2],
        qkv_grad,
        out_grad,
        up_grad,
        down_grad,
        score_stats,
    )


def solution(mesh):
    placed = (
        P("dp", None),
        P("dp", None),
        P("dp", None),
        P("dp", None),
        P(),
        P(),
        P(),
        P(None, None, "tensor"),
        P("tensor", None),
        P(None, "tensor"),
        P("tensor", None),
    )
    return jax.shard_map(
        per_device,
        mesh=mesh,
        in_specs=placed,
        out_specs=(
            P("dp", None),
            P("dp", None),
            P(),
            P(),
            P(),
            P(None, None, "tensor"),
            P("tensor", None),
            P(None, "tensor"),
            P("tensor", None),
            P(),
        ),
        check_vma=False,
    )
```

time: 471 us -> 361 us (0.77)
  waiting for transfers between devices: 280 us -> 94.4 us
  starting transfers between devices: 1.01 us -> 89.8 us
  blocking collectives: 25.6 us -> 0 us
  local copies, waits for them, and re-layouts: 67.2 us -> 88.7 us
  between operations: 15.9 us -> 5.35 us
  other arithmetic: 28.7 us -> 35.6 us
    psum x4 -> x0, waiting for transfers between devices: 280 us -> none  [the longest x1 134 us: per_device(): lax.psum((qkv_part, out_part, up_part, down_part, first_gain_part, second...]
    ppermute x0 -> x55, waiting for transfers between devices: none -> 94.4 us  [swap(): return lax.ppermute(values, axis, [(i, i ^ bits) for i in range(size)])]
    ppermute x0 -> x55, starting transfers between devices: none -> 89.8 us  [swap(): return lax.ppermute(values, axis, [(i, i ^ bits) for i in range(size)])]
    psum x1 -> x0, blocking collectives: 25.6 us -> none  [per_device(): lax.psum((qkv_part, out_part, up_part, down_part, first_gain_part, second...]
    scatter x1 -> x0, other arithmetic: 12.2 us -> none  [per_device(): output = tokens.at[positions].set(new_rows.astype(jnp.bfloat16))]
    scatter x1 -> x4, local copies, waits for them, and re-layouts: 11.8 us -> 23.4 us  [the longest x1 11.7 us: per_device(): output = tokens.at[positions].set(new_rows)]
    unnamed x79 -> x113, local copies, waits for them, and re-layouts: 32.7 us -> 21.6 us
    convert_element_type x6 -> x17, other arithmetic: 4.67 us -> 14.9 us  [the longest x9 6.04 us: reduce_blocks(): held = (mine.astype(F32) + sent.astype(F32)).astype(BF)]
  transfers between devices with their start and end apart: 4 -> 55, of which waited for: 4 -> 18; matrix products, arithmetic and copies ran while one was open for 14% -> 36% of each run, Pallas kernels for 0% -> 0%
where the time goes in v1:
time: 361 us; the launch traced here: 357 us
  waiting for transfers between devices  94.4 us (26%)
  starting transfers between devices  89.8 us (25%)
  local copies, waits for them, and re-layouts  88.7 us (25%)
  matrix products  42.9 us (12%)
  other arithmetic  35.6 us (10%)
  between operations  5.35 us (1%)
    ppermute x55, waiting for transfers between devices, swap(): return lax.ppermute(values, axis, [(i, i ^ bits) for i in range(size)])  94.4 us
    ppermute x55, starting transfers between devices, swap(): return lax.ppermute(values, axis, [(i, i ^ bits) for i in range(size)])  89.8 us
    dot_general x21, matrix products, dot(): lax.dot_general(left, right, (dims, ((), ())), preferred_element_type=F32)  29 us
    unnamed x113, local copies, waits for them, and re-layouts  21.6 us
    scatter x1, local copies, waits for them, and re-layouts, per_device(): output = tokens.at[positions].set(new_rows)  11.7 us
    scatter x1, local copies, waits for them, and re-layouts, per_device(): input_grad = cotangent.at[positions].set(input_rows)  11.2 us
    gather x1, local copies, waits for them, and re-layouts, per_device(): grad_rows = cotangent[positions].astype(F32)  8.06 us
    gather x1, local copies, waits for them, and re-layouts, per_device(): picked_low = tokens[positions]  7.4 us
  transfers between devices with their start and end apart: 55, of which 18 were waited for; matrix products, arithmetic and copies ran while one was open for 36% of the time, Pallas kernels for 0%

profile of v1, /device:TPU:0, one launch (start us, length us, event | category | flops | bytes accessed | tf_op | source)
XLA Modules:
  0.0 356.8 jit_solution(8547933073264520205)
XLA Ops:
  0.7 7.9 %copy.97 = bf16[4096,1024]{1,0:T(8,128)(2,1)} copy(bf16[4096,1024]{1,0:T(8,128)(2,1)} %param.15) | data formatting | bytes 16777216
  8.6 7.8 %copy.98 = bf16[4096,1024]{1,0:T(8,128)(2,1)} copy(bf16[4096,1024]{1,0:T(8,128)(2,1)} %param.18) | data formatting | bytes 16777216
  17.9 5.0 %collective-permute-start.3 = (bf16[64,1024]{1,0:T(8,128)(2,1)}, bf16[64,1024]{1,0:T(8,128)(2,1)S(1)}, u32[]{:S(2)}, u32[]{:S(2)}) collective-permute-start(bf16[64,1024]{1,0:T(8,128)(2,1)} %constant_dynamic-slice_fusion.6), channel_id=1, source_target_pairs={{0,3},{1,2},{2,1},{3,0},{4,7},{5,6},{6,5},{7,4},{8,11},{9,10},{10,... | collective-permute-start | bytes 393224 | tf_op jit(solution)/shard_map/ppermute | solution.py:15
  24.1 2.6 slice_bitcast_fusion.5
  26.6 7.4 %gather_fusion = bf16[512,1024]{1,0:T(8,128)(2,1)S(1)} fusion(bf16[4096,1024]{1,0:T(8,128)(2,1)} %copy.97, s32[1024]{0:T(1024)S(1)} %pad_clamp_fusion), kind=kCustom, calls=%fused_computation | custom fusion | bytes 2099200 | tf_op jit(solution)/shard_map/gather | solution.py:111
  34.4 2.4 convolution_convert_fusion.4
  39.7 1.9 copy.36
  41.6 5.3 %fusion.56 = (f32[4,512]{1,0:T(4,128)}, f32[4,512,512]{1,2,0:T(8,128)}) fusion(pred[512,512]{0,1:T(8,128)(4,1)} %fusion.26, bf16[512,4,64]{0,2,1:T(8,128)(2,1)S(1)} %bitcast.393, bf16[512,4,64]{0,2,1:T(8,128)(2,1)} %bitcast.395), kind=kOutput, calls=%fused_computation.296 | convolution fusion | flops 138412544 | bytes 4988928 | tf_op jit(solution)/shard_map/sub | solution.py:135
  46.9 1.8 copy.34
  50.5 1.8 collective-permute-start.4
  52.3 3.6 convolution_convert_fusion.14
  55.8 2.1 collective-permute-start.6
  58.0 2.0 collective-permute-start
  61.9 2.3 fusion.57
  67.6 8.1 %gather_fusion.2 = bf16[512,1024]{1,0:T(8,128)(2,1)} fusion(bf16[4096,1024]{1,0:T(8,128)(2,1)} %copy.98, s32[1024]{0:T(1024)} %copy-done.37), kind=kCustom, calls=%fused_computation.2 | custom fusion | bytes 2099200 | tf_op jit(solution)/shard_map/gather | solution.py:149
  75.7 2.8 convert_element_type.464
  78.5 4.4 %gather_fusion.1 = f32[512]{0:T(512)} fusion(f32[4096]{0:T(1024)S(1)} %bitcast.381, s32[1024]{0:T(1024)} %copy-done.37), kind=kCustom, calls=%fused_computation.1 | custom fusion | bytes 6144 | tf_op jit(solution)/shard_map/gather | solution.py:113
  86.7 1.6 fusion.58
  93.1 1.8 multiply_reduce_fusion.3
  98.1 2.4 fusion.8
  100.5 1.6 multiply_reduce_fusion.1
  107.2 1.8 convolution_convert_fusion
  109.1 3.6 %collective-permute-start.10 = (bf16[128,1024]{1,0:T(8,128)(2,1)S(1)}, bf16[128,1024]{1,0:T(8,128)(2,1)S(1)}, u32[]{:S(2)}, u32[]{:S(2)}) collective-permute-start(bf16[128,1024]{1,0:T(8,128)(2,1)S(1)} %get-tuple-element.100), channel_id=1, source_target_pairs={{0,3},{1,2},{2,1},{3,0},{4,7},{5,6},{6,5},{7,4},{8,11},{9,10},{10,... | collective-permute-start | bytes 786440 | tf_op jit(solution)/shard_map/ppermute | solution.py:15
  112.7 1.7 collective-permute-start.16
  131.4 22.0 %collective-permute-start.8 = (bf16[128,1024]{1,0:T(8,128)(2,1)S(1)}, bf16[128,1024]{1,0:T(8,128)(2,1)S(1)}, u32[]{:S(2)}, u32[]{:S(2)}) collective-permute-start(bf16[128,1024]{1,0:T(8,128)(2,1)S(1)} %get-tuple-element.99), channel_id=1, source_target_pairs={{0,1},{1,0},{2,3},{3,2},{4,5},{5,4},{6,7},{7,6},{8,9},{9,8},{10,11... | collective-permute-start | bytes 786440 | tf_op jit(solution)/shard_map/ppermute | solution.py:15
  153.4 4.8 %collective-permute-done.15 = bf16[512,256]{0,1:T(8,128)(2,1)S(1)} collective-permute-done((bf16[512,256]{0,1:T(8,128)(2,1)S(1)}, bf16[512,256]{0,1:T(8,128)(2,1)S(1)}, u32[]{:S(2)}, u32[]{:S(2)}) %collective-permute-start.15) | collective-permute-done | bytes 262176 | tf_op jit(solution)/shard_map/ppermute | solution.py:15
  176.3 2.6 collective-permute-start.19
  182.0 8.0 %collective-permute-done.26 = f32[4,1024]{1,0:T(4,128)S(1)} collective-permute-done((f32[4,1024]{1,0:T(4,128)S(1)}, f32[4,1024]{1,0:T(4,128)S(1)}, u32[]{:S(2)}, u32[]{:S(2)}) %collective-permute-start.26) | collective-permute-done | bytes 16416 | tf_op jit(solution)/shard_map/ppermute | solution.py:15
  189.9 2.5 collective-permute-start.27
  193.4 9.3 %collective-permute-done.27 = f32[4,1024]{1,0:T(4,128)S(1)} collective-permute-done((f32[4,1024]{1,0:T(4,128)S(1)}, f32[4,1024]{1,0:T(4,128)S(1)}, u32[]{:S(2)}, u32[]{:S(2)}) %collective-permute-start.27) | collective-permute-done | bytes 16416 | tf_op jit(solution)/shard_map/ppermute | solution.py:15
  205.8 3.0 collective-permute-start.12
  208.8 2.7 collective-permute-done.17
  211.5 2.7 collective-permute-start.13
  216.0 11.3 %collective-permute-done.12 = bf16[128,1024]{1,0:T(8,128)(2,1)S(1)} collective-permute-done((bf16[128,1024]{1,0:T(8,128)(2,1)S(1)}, bf16[128,1024]{1,0:T(8,128)(2,1)S(1)}, u32[]{:S(2)}, u32[]{:S(2)}) %collective-permute-start.12) | collective-permute-done | bytes 262176 | tf_op jit(solution)/shard_map/ppermute | solution.py:15
  228.0 2.3 collective-permute-start.22
  231.0 11.7 %scatter_fusion = bf16[4096,1024]{1,0:T(8,128)(2,1)} fusion(bf16[4096,1024]{1,0:T(8,128)(2,1)} %copy.97, s32[512]{0:T(512)S(1)} %bitcast.418, bf16[512,1024]{1,0:T(8,128)(2,1)} %constant_dynamic-update-slice_fusion.4), kind=kCustom, calls=%fused_computation.3 | custom fusion | bytes 3147776 | tf_op jit(solution)/shard_map/scatter | solution.py:246
  243.7 6.2 %collective-permute-done.21 = bf16[128,1024]{1,0:T(8,128)(2,1)} collective-permute-done((bf16[128,1024]{1,0:T(8,128)(2,1)}, bf16[128,1024]{1,0:T(8,128)(2,1)}, u32[]{:S(2)}, u32[]{:S(2)}) %collective-permute-start.21) | collective-permute-done | bytes 262176 | tf_op jit(solution)/shard_map/ppermute | solution.py:15
  251.8 11.2 %scatter_fusion.1 = bf16[4096,1024]{1,0:T(8,128)(2,1)} fusion(bf16[4096,1024]{1,0:T(8,128)(2,1)} %copy.98, s32[512]{0:T(512)S(1)} %bitcast.419, bf16[512,1024]{1,0:T(8,128)(2,1)S(1)} %constant_dynamic-update-slice_fusion), kind=kCustom, calls=%fused_computation.4 | custom fusion | bytes 3147776 | tf_op jit(solution)/shard_map/scatter | solution.py:247
  263.1 1.9 add_convert_fusion.2
  271.9 1.6 add_convert_fusion
  274.6 15.3 %collective-permute-done.29 = bf16[2,128,768]{2,1,0:T(8,128)(2,1)S(1)} collective-permute-done((bf16[2,128,768]{2,1,0:T(8,128)(2,1)S(1)}, bf16[2,128,768]{2,1,0:T(8,128)(2,1)S(1)}, u32[]{:S(2)}, u32[]{:S(2)}) %collective-permute-start.29) | collective-permute-done | bytes 393248 | tf_op jit(solution)/shard_map/ppermute | solution.py:15
  295.0 2.9 collective-permute-done.30
  300.9 2.4 collective-permute-start.39
  303.2 8.9 %collective-permute-start.38 = (bf16[32,1024]{1,0:T(8,128)(2,1)S(1)}, bf16[32,1024]{1,0:T(8,128)(2,1)S(1)}, u32[]{:S(2)}, u32[]{:S(2)}) collective-permute-start(bf16[32,1024]{1,0:T(8,128)(2,1)S(1)} %get-tuple-element.143), channel_id=1, source_target_pairs={{0,2},{1,3},{2,0},{3,1},{4,6},{5,7},{6,4},{7,5},{8,10},{9,11},{10,... | collective-permute-start | bytes 196616 | tf_op jit(solution)/shard_map/ppermute | solution.py:15
  318.7 11.0 %collective-permute-done.40 = bf16[1,32,1024]{2,1,0:T(8,128)(2,1)S(1)} collective-permute-done((bf16[1,32,1024]{2,1,0:T(8,128)(2,1)S(1)}, bf16[1,32,1024]{2,1,0:T(8,128)(2,1)S(1)}, u32[]{:S(2)}, u32[]{:S(2)}) %collective-permute-start.40) | collective-permute-done | bytes 65568 | tf_op jit(solution)/shard_map/ppermute | solution.py:15
  330.0 4.7 %collective-permute-done.41 = bf16[2,32,1024]{2,1,0:T(8,128)(2,1)S(1)} collective-permute-done((bf16[2,32,1024]{2,1,0:T(8,128)(2,1)S(1)}, bf16[2,32,1024]{2,1,0:T(8,128)(2,1)S(1)}, u32[]{:S(2)}, u32[]{:S(2)}) %collective-permute-start.41) | collective-permute-done | bytes 131104 | tf_op jit(solution)/shard_map/ppermute | solution.py:15
  337.3 11.9 %collective-permute-done.47 = bf16[2,128,1024]{2,1,0:T(8,128)(2,1)S(1)} collective-permute-done((bf16[2,128,1024]{2,1,0:T(8,128)(2,1)S(1)}, bf16[2,128,1024]{2,1,0:T(8,128)(2,1)S(1)}, u32[]{:S(2)}, u32[]{:S(2)}) %collective-permute-start.47) | collective-permute-done | bytes 524320 | tf_op jit(solution)/shard_map/ppermute | solution.py:15
  350.8 1.9 pad_maximum_fusion
  (350 shorter events, 105.1 us)
Async XLA Ops:
  17.9 30.8 %collective-permute-start.3 = (bf16[64,1024]{1,0:T(8,128)(2,1)}, bf16[64,1024]{1,0:T(8,128)(2,1)S(1)}, u32[]{:S(2)}, u32[]{:S(2)}) collective-permute-start(bf16[64,1024]{1,0:T(8,128)(2,1)} %constant_dynamic-slice_fusion.6), channel_id=1, source_target_pairs={{0,3},{1,2},{2,1},{3,0},{4,7},{5,6},{6,5},{7,4},{8,11},{9,10},{10,... | collective-permute-start | bytes 393224 | tf_op jit(solution)/shard_map/ppermute | solution.py:15
  23.0 25.8 %collective-permute-start.2 = (bf16[64,1024]{1,0:T(8,128)(2,1)}, bf16[64,1024]{1,0:T(8,128)(2,1)}, u32[]{:S(2)}, u32[]{:S(2)}) collective-permute-start(bf16[64,1024]{1,0:T(8,128)(2,1)} %constant_dynamic-slice_fusion.6), channel_id=1, source_target_pairs={{0,2},{1,3},{2,0},{3,1},{4,6},{5,7},{6,4},{7,5},{8,10},{9,11},{10,... | collective-permute-start | bytes 393224 | tf_op jit(solution)/shard_map/ppermute | solution.py:15
  23.0 25.8 %collective-permute-start.1 = (bf16[64,1024]{1,0:T(8,128)(2,1)}, bf16[64,1024]{1,0:T(8,128)(2,1)}, u32[]{:S(2)}, u32[]{:S(2)}) collective-permute-start(bf16[64,1024]{1,0:T(8,128)(2,1)} %constant_dynamic-slice_fusion.6), channel_id=1, source_target_pairs={{0,1},{1,0},{2,3},{3,2},{4,5},{5,4},{6,7},{7,6},{8,9},{9,8},{10,11... | collective-permute-start | bytes 393224 | tf_op jit(solution)/shard_map/ppermute | solution.py:15
  50.5 10.4 %collective-permute-start.4 = (bf16[3,64,1024]{2,1,0:T(8,128)(2,1)S(1)}, bf16[3,64,1024]{2,1,0:T(8,128)(2,1)S(1)}, u32[]{:S(2)}, u32[]{:S(2)}) collective-permute-start(bf16[3,64,1024]{2,1,0:T(8,128)(2,1)S(1)} %get-tuple-element.140), channel_id=1, source_target_pairs={{0,8},{4,12},{8,0},{12,4},{16,24},{20,28},{24,16},{28,20},{1,9},{5... | collective-permute-start | bytes 1179656 | tf_op jit(solution)/shard_map/ppermute | solution.py:15
  55.8 34.4 %collective-permute-start.6 = (bf16[512,256]{0,1:T(8,128)(2,1)}, bf16[512,256]{0,1:T(8,128)(2,1)}, u32[]{:S(2)}, u32[]{:S(2)}) collective-permute-start(bf16[512,256]{0,1:T(8,128)(2,1)} %bitcast.11), channel_id=1, source_target_pairs={{0,2},{1,3},{2,0},{3,1},{4,6},{5,7},{6,4},{7,5},{8,10},{9,11},{10,... | collective-permute-start | bytes 786440 | tf_op jit(solution)/shard_map/ppermute | solution.py:15
  58.0 33.7 %collective-permute-start = (bf16[512,256]{0,1:T(8,128)(2,1)}, bf16[512,256]{0,1:T(8,128)(2,1)}, u32[]{:S(2)}, u32[]{:S(2)}) collective-permute-start(bf16[512,256]{0,1:T(8,128)(2,1)} %bitcast.11), channel_id=1, source_target_pairs={{0,1},{1,0},{2,3},{3,2},{4,5},{5,4},{6,7},{7,6},{8,9},{9,8},{10,11... | collective-permute-start | bytes 786440 | tf_op jit(solution)/shard_map/ppermute | solution.py:15
  60.0 33.1 %collective-permute-start.7 = (bf16[512,256]{0,1:T(8,128)(2,1)}, bf16[512,256]{0,1:T(8,128)(2,1)}, u32[]{:S(2)}, u32[]{:S(2)}) collective-permute-start(bf16[512,256]{0,1:T(8,128)(2,1)} %bitcast.11), channel_id=1, source_target_pairs={{0,3},{1,2},{2,1},{3,0},{4,7},{5,6},{6,5},{7,4},{8,11},{9,10},{10,... | collective-permute-start | bytes 786440 | tf_op jit(solution)/shard_map/ppermute | solution.py:15
  61.9 26.5 %collective-permute-start.5 = (bf16[2,3,64,1024]{3,2,1,0:T(8,128)(2,1)}, bf16[2,3,64,1024]{3,2,1,0:T(8,128)(2,1)}, u32[]{:S(2)}, u32[]{:S(2)}) collective-permute-start(bf16[2,3,64,1024]{3,2,1,0:T(8,128)(2,1)} %pad_maximum_fusion.8), channel_id=1, source_target_pairs={{0,4},{4,0},{8,12},{12,8},{16,20},{20,16},{24,28},{28,24},{1,5},{5... | collective-permute-start | bytes 2359304 | tf_op jit(solution)/shard_map/ppermute | solution.py:15
  109.1 56.7 %collective-permute-start.10 = (bf16[128,1024]{1,0:T(8,128)(2,1)S(1)}, bf16[128,1024]{1,0:T(8,128)(2,1)S(1)}, u32[]{:S(2)}, u32[]{:S(2)}) collective-permute-start(bf16[128,1024]{1,0:T(8,128)(2,1)S(1)} %get-tuple-element.100), channel_id=1, source_target_pairs={{0,3},{1,2},{2,1},{3,0},{4,7},{5,6},{6,5},{7,4},{8,11},{9,10},{10,... | collective-permute-start | bytes 786440 | tf_op jit(solution)/shard_map/ppermute | solution.py:15
  112.7 53.1 %collective-permute-start.9 = (bf16[128,1024]{1,0:T(8,128)(2,1)S(1)}, bf16[128,1024]{1,0:T(8,128)(2,1)S(1)}, u32[]{:S(2)}, u32[]{:S(2)}) collective-permute-start(bf16[128,1024]{1,0:T(8,128)(2,1)S(1)} %get-tuple-element.101), channel_id=1, source_target_pairs={{0,2},{1,3},{2,0},{3,1},{4,6},{5,7},{6,4},{7,5},{8,10},{9,11},{10,... | collective-permute-start | bytes 786440 | tf_op jit(solution)/shard_map/ppermute | solution.py:15
  112.7 18.7 %collective-permute-start.16 = (bf16[512,256]{0,1:T(8,128)(2,1)S(1)}, bf16[512,256]{0,1:T(8,128)(2,1)S(1)}, u32[]{:S(2)}, u32[]{:S(2)}) collective-permute-start(bf16[512,256]{0,1:T(8,128)(2,1)S(1)} %convolution_convert_fusion.10), channel_id=1, source_target_pairs={{0,3},{1,2},{2,1},{3,0},{4,7},{5,6},{6,5},{7,4},{8,11},{9,10},{10,... | collective-permute-start | bytes 786440 | tf_op jit(solution)/shard_map/ppermute | solution.py:15
  114.4 43.7 %collective-permute-start.15 = (bf16[512,256]{0,1:T(8,128)(2,1)S(1)}, bf16[512,256]{0,1:T(8,128)(2,1)S(1)}, u32[]{:S(2)}, u32[]{:S(2)}) collective-permute-start(bf16[512,256]{0,1:T(8,128)(2,1)S(1)} %convolution_convert_fusion.11), channel_id=1, source_target_pairs={{0,2},{1,3},{2,0},{3,1},{4,6},{5,7},{6,4},{7,5},{8,10},{9,11},{10,... | collective-permute-start | bytes 786440 | tf_op jit(solution)/shard_map/ppermute | solution.py:15
  115.6 42.6 %collective-permute-start.14 = (bf16[512,256]{0,1:T(8,128)(2,1)S(1)}, bf16[512,256]{0,1:T(8,128)(2,1)S(1)}, u32[]{:S(2)}, u32[]{:S(2)}) collective-permute-start(bf16[512,256]{0,1:T(8,128)(2,1)S(1)} %convolution_convert_fusion.12), channel_id=1, source_target_pairs={{0,1},{1,0},{2,3},{3,2},{4,5},{5,4},{6,7},{7,6},{8,9},{9,8},{10,11... | collective-permute-start | bytes 786440 | tf_op jit(solution)/shard_map/ppermute | solution.py:15
  131.4 34.4 %collective-permute-start.8 = (bf16[128,1024]{1,0:T(8,128)(2,1)S(1)}, bf16[128,1024]{1,0:T(8,128)(2,1)S(1)}, u32[]{:S(2)}, u32[]{:S(2)}) collective-permute-start(bf16[128,1024]{1,0:T(8,128)(2,1)S(1)} %get-tuple-element.99), channel_id=1, source_target_pairs={{0,1},{1,0},{2,3},{3,2},{4,5},{5,4},{6,7},{7,6},{8,9},{9,8},{10,11... | collective-permute-start | bytes 786440 | tf_op jit(solution)/shard_map/ppermute | solution.py:15
  158.2 104.9 %collective-permute-start.34 = (bf16[4,4,32,1024]{3,2,1,0:T(8,128)(2,1)}, bf16[4,4,32,1024]{3,2,1,0:T(8,128)(2,1)}, u32[]{:S(2)}, u32[]{:S(2)}) collective-permute-start(bf16[4,4,32,1024]{3,2,1,0:T(8,128)(2,1)} %pad_maximum_fusion.2), channel_id=1, source_target_pairs={{0,4},{4,0},{8,12},{12,8},{16,20},{20,16},{24,28},{28,24},{1,5},{5... | collective-permute-start | bytes 3145736 | tf_op jit(solution)/shard_map/ppermute | solution.py:15
  169.2 46.0 %collective-permute-start.11 = (bf16[128,1024]{1,0:T(8,128)(2,1)S(1)}, bf16[128,1024]{1,0:T(8,128)(2,1)S(1)}, u32[]{:S(2)}, u32[]{:S(2)}) collective-permute-start(bf16[128,1024]{1,0:T(8,128)(2,1)S(1)} %get-tuple-element.51), channel_id=1, source_target_pairs={{0,1},{1,0},{2,3},{3,2},{4,5},{5,4},{6,7},{7,6},{8,9},{9,8},{10,11... | collective-permute-start | bytes 786440 | tf_op jit(solution)/shard_map/ppermute | solution.py:15
  176.3 29.5 %collective-permute-start.19 = (bf16[128,1024]{1,0:T(8,128)(2,1)S(1)}, bf16[128,1024]{1,0:T(8,128)(2,1)S(1)}, u32[]{:S(2)}, u32[]{:S(2)}) collective-permute-start(bf16[128,1024]{1,0:T(8,128)(2,1)S(1)} %get-tuple-element.97), channel_id=1, source_target_pairs={{0,3},{1,2},{2,1},{3,0},{4,7},{5,6},{6,5},{7,4},{8,11},{9,10},{10,... | collective-permute-start | bytes 786440 | tf_op jit(solution)/shard_map/ppermute | solution.py:15
  178.9 26.9 %collective-permute-start.18 = (bf16[128,1024]{1,0:T(8,128)(2,1)S(1)}, bf16[128,1024]{1,0:T(8,128)(2,1)S(1)}, u32[]{:S(2)}, u32[]{:S(2)}) collective-permute-start(bf16[128,1024]{1,0:T(8,128)(2,1)S(1)} %get-tuple-element.98), channel_id=1, source_target_pairs={{0,2},{1,3},{2,0},{3,1},{4,6},{5,7},{6,4},{7,5},{8,10},{9,11},{10,... | collective-permute-start | bytes 786440 | tf_op jit(solution)/shard_map/ppermute | solution.py:15
  179.9 10.0 %collective-permute-start.26 = (f32[4,1024]{1,0:T(4,128)S(1)}, f32[4,1024]{1,0:T(4,128)S(1)}, u32[]{:S(2)}, u32[]{:S(2)}) collective-permute-start(f32[4,1024]{1,0:T(4,128)S(1)} %add.367), channel_id=1, source_target_pairs={{0,1},{1,0},{2,3},{3,2},{4,5},{5,4},{6,7},{7,6},{8,9},{9,8},{10,11... | collective-permute-start | bytes 49160 | tf_op jit(solution)/shard_map/ppermute | solution.py:15
  189.9 12.8 %collective-permute-start.27 = (f32[4,1024]{1,0:T(4,128)S(1)}, f32[4,1024]{1,0:T(4,128)S(1)}, u32[]{:S(2)}, u32[]{:S(2)}) collective-permute-start(f32[4,1024]{1,0:T(4,128)S(1)} %add.368), channel_id=1, source_target_pairs={{0,2},{1,3},{2,0},{3,1},{4,6},{5,7},{6,4},{7,5},{8,10},{9,11},{10,... | collective-permute-start | bytes 49160 | tf_op jit(solution)/shard_map/ppermute | solution.py:15
  202.7 8.8 %collective-permute-start.17 = (bf16[128,1024]{1,0:T(8,128)(2,1)S(1)}, bf16[128,1024]{1,0:T(8,128)(2,1)S(1)}, u32[]{:S(2)}, u32[]{:S(2)}) collective-permute-start(bf16[128,1024]{1,0:T(8,128)(2,1)S(1)} %get-tuple-element.96), channel_id=1, source_target_pairs={{0,1},{1,0},{2,3},{3,2},{4,5},{5,4},{6,7},{7,6},{8,9},{9,8},{10,11... | collective-permute-start | bytes 786440 | tf_op jit(solution)/shard_map/ppermute | solution.py:15
  205.8 61.0 %collective-permute-start.43 = (bf16[4,128,1024]{2,1,0:T(8,128)(2,1)}, bf16[4,128,1024]{2,1,0:T(8,128)(2,1)S(1)}, u32[]{:S(2)}, u32[]{:S(2)}) collective-permute-start(bf16[4,128,1024]{2,1,0:T(8,128)(2,1)} %pad_maximum_fusion.3), channel_id=1, source_target_pairs={{0,4},{4,0},{8,12},{12,8},{16,20},{20,16},{24,28},{28,24},{1,5},{5... | collective-permute-start | bytes 3145736 | tf_op jit(solution)/shard_map/ppermute | solution.py:15
  205.8 21.5 %collective-permute-start.12 = (bf16[128,1024]{1,0:T(8,128)(2,1)S(1)}, bf16[128,1024]{1,0:T(8,128)(2,1)S(1)}, u32[]{:S(2)}, u32[]{:S(2)}) collective-permute-start(bf16[128,1024]{1,0:T(8,128)(2,1)S(1)} %get-tuple-element.51), channel_id=1, source_target_pairs={{0,2},{1,3},{2,0},{3,1},{4,6},{5,7},{6,4},{7,5},{8,10},{9,11},{10,... | collective-permute-start | bytes 786440 | tf_op jit(solution)/shard_map/ppermute | solution.py:15
  211.5 16.5 %collective-permute-start.13 = (bf16[128,1024]{1,0:T(8,128)(2,1)S(1)}, bf16[128,1024]{1,0:T(8,128)(2,1)S(1)}, u32[]{:S(2)}, u32[]{:S(2)}) collective-permute-start(bf16[128,1024]{1,0:T(8,128)(2,1)S(1)} %get-tuple-element.51), channel_id=1, source_target_pairs={{0,3},{1,2},{2,1},{3,0},{4,7},{5,6},{6,5},{7,4},{8,11},{9,10},{10,... | collective-permute-start | bytes 786440 | tf_op jit(solution)/shard_map/ppermute | solution.py:15
  215.3 27.5 %collective-permute-start.20 = (bf16[128,1024]{1,0:T(8,128)(2,1)}, bf16[128,1024]{1,0:T(8,128)(2,1)}, u32[]{:S(2)}, u32[]{:S(2)}) collective-permute-start(bf16[128,1024]{1,0:T(8,128)(2,1)} %get-tuple-element.47), channel_id=1, source_target_pairs={{0,1},{1,0},{2,3},{3,2},{4,5},{5,4},{6,7},{7,6},{8,9},{9,8},{10,11... | collective-permute-start | bytes 786440 | tf_op jit(solution)/shard_map/ppermute | solution.py:15
  227.3 22.6 %collective-permute-start.21 = (bf16[128,1024]{1,0:T(8,128)(2,1)}, bf16[128,1024]{1,0:T(8,128)(2,1)}, u32[]{:S(2)}, u32[]{:S(2)}) collective-permute-start(bf16[128,1024]{1,0:T(8,128)(2,1)} %get-tuple-element.47), channel_id=1, source_target_pairs={{0,2},{1,3},{2,0},{3,1},{4,6},{5,7},{6,4},{7,5},{8,10},{9,11},{10,... | collective-permute-start | bytes 786440 | tf_op jit(solution)/shard_map/ppermute | solution.py:15
  228.0 22.8 %collective-permute-start.22 = (bf16[128,1024]{1,0:T(8,128)(2,1)}, bf16[128,1024]{1,0:T(8,128)(2,1)}, u32[]{:S(2)}, u32[]{:S(2)}) collective-permute-start(bf16[128,1024]{1,0:T(8,128)(2,1)} %get-tuple-element.47), channel_id=1, source_target_pairs={{0,3},{1,2},{2,1},{3,0},{4,7},{5,6},{6,5},{7,4},{8,11},{9,10},{10,... | collective-permute-start | bytes 786440 | tf_op jit(solution)/shard_map/ppermute | solution.py:15
  242.7 28.2 %collective-permute-start.49 = (bf16[4,128,1024]{2,1,0:T(8,128)(2,1)}, bf16[4,128,1024]{2,1,0:T(8,128)(2,1)S(1)}, u32[]{:S(2)}, u32[]{:S(2)}) collective-permute-start(bf16[4,128,1024]{2,1,0:T(8,128)(2,1)} %pad_maximum_fusion.5), channel_id=1, source_target_pairs={{0,4},{4,0},{8,12},{12,8},{16,20},{20,16},{24,28},{28,24},{1,5},{5... | collective-permute-start | bytes 3145736 | tf_op jit(solution)/shard_map/ppermute | solution.py:15
  249.9 18.0 %collective-permute-start.28 = (bf16[4,128,768]{2,1,0:T(8,128)(2,1)}, bf16[4,128,768]{2,1,0:T(8,128)(2,1)}, u32[]{:S(2)}, u32[]{:S(2)}) collective-permute-start(bf16[4,128,768]{2,1,0:T(8,128)(2,1)} %pad_maximum_fusion.11), channel_id=1, source_target_pairs={{0,4},{4,0},{8,12},{12,8},{16,20},{20,16},{24,28},{28,24},{1,5},{5... | collective-permute-start | bytes 2359304 | tf_op jit(solution)/shard_map/ppermute | solution.py:15
  265.2 26.0 %collective-permute-start.35 = (bf16[2,4,32,1024]{3,2,1,0:T(8,128)(2,1)S(1)}, bf16[2,4,32,1024]{3,2,1,0:T(8,128)(2,1)S(1)}, u32[]{:S(2)}, u32[]{:S(2)}) collective-permute-start(bf16[2,4,32,1024]{3,2,1,0:T(8,128)(2,1)S(1)} %pad_maximum_fusion.15), channel_id=1, source_target_pairs={{0,8},{4,12},{8,0},{12,4},{16,24},{20,28},{24,16},{28,20},{1,9},{5... | collective-permute-start | bytes 1572872 | tf_op jit(solution)/shard_map/ppermute | solution.py:15
  267.3 24.7 %collective-permute-start.44 = (bf16[2,128,1024]{2,1,0:T(8,128)(2,1)S(1)}, bf16[2,128,1024]{2,1,0:T(8,128)(2,1)S(1)}, u32[]{:S(2)}, u32[]{:S(2)}) collective-permute-start(bf16[2,128,1024]{2,1,0:T(8,128)(2,1)S(1)} %stack.454), channel_id=1, source_target_pairs={{0,16},{4,20},{8,24},{12,28},{16,0},{20,4},{24,8},{28,12},{1,17},{... | collective-permute-start | bytes 1572872 | tf_op jit(solution)/shard_map/ppermute | solution.py:15
  269.4 20.5 %collective-permute-start.29 = (bf16[2,128,768]{2,1,0:T(8,128)(2,1)S(1)}, bf16[2,128,768]{2,1,0:T(8,128)(2,1)S(1)}, u32[]{:S(2)}, u32[]{:S(2)}) collective-permute-start(bf16[2,128,768]{2,1,0:T(8,128)(2,1)S(1)} %stack.452), channel_id=1, source_target_pairs={{0,16},{4,20},{8,24},{12,28},{16,0},{20,4},{24,8},{28,12},{1,17},{... | collective-permute-start | bytes 1179656 | tf_op jit(solution)/shard_map/ppermute | solution.py:15
  273.7 19.5 %collective-permute-start.50 = (bf16[2,128,1024]{2,1,0:T(8,128)(2,1)S(1)}, bf16[2,128,1024]{2,1,0:T(8,128)(2,1)S(1)}, u32[]{:S(2)}, u32[]{:S(2)}) collective-permute-start(bf16[2,128,1024]{2,1,0:T(8,128)(2,1)S(1)} %pad_maximum_fusion.17), channel_id=1, source_target_pairs={{0,8},{4,12},{8,0},{12,4},{16,24},{20,28},{24,16},{28,20},{1,9},{5... | collective-permute-start | bytes 1572872 | tf_op jit(solution)/shard_map/ppermute | solution.py:15
  290.0 7.9 %collective-permute-start.30 = (bf16[1,128,768]{2,1,0:T(8,128)(2,1)S(1)}, bf16[1,128,768]{2,1,0:T(8,128)(2,1)S(1)}, u32[]{:S(2)}, u32[]{:S(2)}) collective-permute-start(bf16[1,128,768]{2,1,0:T(8,128)(2,1)S(1)} %slice.295), channel_id=1, source_target_pairs={{0,8},{4,12},{8,0},{12,4},{16,24},{20,28},{24,16},{28,20},{1,9},{5... | collective-permute-start | bytes 589832 | tf_op jit(solution)/shard_map/ppermute | solution.py:15
  291.5 9.3 %collective-permute-start.36 = (bf16[1,4,32,1024]{3,2,1,0:T(8,128)(2,1)S(1)}, bf16[1,4,32,1024]{3,2,1,0:T(8,128)(2,1)S(1)}, u32[]{:S(2)}, u32[]{:S(2)}) collective-permute-start(bf16[1,4,32,1024]{3,2,1,0:T(8,128)(2,1)S(1)} %slice.307), channel_id=1, source_target_pairs={{0,16},{4,20},{8,24},{12,28},{16,0},{20,4},{24,8},{28,12},{1,17},{... | collective-permute-start | bytes 786440 | tf_op jit(solution)/shard_map/ppermute | solution.py:15
  292.3 19.8 %collective-permute-start.45 = (bf16[1,128,1024]{2,1,0:T(8,128)(2,1)S(1)}, bf16[1,128,1024]{2,1,0:T(8,128)(2,1)S(1)}, u32[]{:S(2)}, u32[]{:S(2)}) collective-permute-start(bf16[1,128,1024]{2,1,0:T(8,128)(2,1)S(1)} %slice.319), channel_id=1, source_target_pairs={{0,8},{4,12},{8,0},{12,4},{16,24},{20,28},{24,16},{28,20},{1,9},{5... | collective-permute-start | bytes 786440 | tf_op jit(solution)/shard_map/ppermute | solution.py:15
  293.4 20.3 %collective-permute-start.51 = (bf16[1,128,1024]{2,1,0:T(8,128)(2,1)S(1)}, bf16[1,128,1024]{2,1,0:T(8,128)(2,1)S(1)}, u32[]{:S(2)}, u32[]{:S(2)}) collective-permute-start(bf16[1,128,1024]{2,1,0:T(8,128)(2,1)S(1)} %slice.331), channel_id=1, source_target_pairs={{0,16},{4,20},{8,24},{12,28},{16,0},{20,4},{24,8},{28,12},{1,17},{... | collective-permute-start | bytes 786440 | tf_op jit(solution)/shard_map/ppermute | solution.py:15
  298.2 17.5 %collective-permute-start.31 = (bf16[1,128,768]{2,1,0:T(8,128)(2,1)S(1)}, bf16[1,128,768]{2,1,0:T(8,128)(2,1)S(1)}, u32[]{:S(2)}, u32[]{:S(2)}) collective-permute-start(bf16[1,128,768]{2,1,0:T(8,128)(2,1)S(1)} %get-tuple-element.45), channel_id=1, source_target_pairs={{0,8},{4,12},{8,0},{12,4},{16,24},{20,28},{24,16},{28,20},{1,9},{5... | collective-permute-start | bytes 589832 | tf_op jit(solution)/shard_map/ppermute | solution.py:15
  300.9 15.4 %collective-permute-start.39 = (bf16[32,1024]{1,0:T(8,128)(2,1)S(1)}, bf16[32,1024]{1,0:T(8,128)(2,1)S(1)}, u32[]{:S(2)}, u32[]{:S(2)}) collective-permute-start(bf16[32,1024]{1,0:T(8,128)(2,1)S(1)} %get-tuple-element.142), channel_id=1, source_target_pairs={{0,3},{1,2},{2,1},{3,0},{4,7},{5,6},{6,5},{7,4},{8,11},{9,10},{10,... | collective-permute-start | bytes 196616 | tf_op jit(solution)/shard_map/ppermute | solution.py:15
  303.2 14.7 %collective-permute-start.38 = (bf16[32,1024]{1,0:T(8,128)(2,1)S(1)}, bf16[32,1024]{1,0:T(8,128)(2,1)S(1)}, u32[]{:S(2)}, u32[]{:S(2)}) collective-permute-start(bf16[32,1024]{1,0:T(8,128)(2,1)S(1)} %get-tuple-element.143), channel_id=1, source_target_pairs={{0,2},{1,3},{2,0},{3,1},{4,6},{5,7},{6,4},{7,5},{8,10},{9,11},{10,... | collective-permute-start | bytes 196616 | tf_op jit(solution)/shard_map/ppermute | solution.py:15
  312.1 5.8 %collective-permute-start.37 = (bf16[32,1024]{1,0:T(8,128)(2,1)S(1)}, bf16[32,1024]{1,0:T(8,128)(2,1)S(1)}, u32[]{:S(2)}, u32[]{:S(2)}) collective-permute-start(bf16[32,1024]{1,0:T(8,128)(2,1)S(1)} %get-tuple-element.141), channel_id=1, source_target_pairs={{0,1},{1,0},{2,3},{3,2},{4,5},{5,4},{6,7},{7,6},{8,9},{9,8},{10,11... | collective-permute-start | bytes 196616 | tf_op jit(solution)/shard_map/ppermute | solution.py:15
  313.8 21.0 %collective-permute-start.46 = (bf16[1,128,1024]{2,1,0:T(8,128)(2,1)S(1)}, bf16[1,128,1024]{2,1,0:T(8,128)(2,1)S(1)}, u32[]{:S(2)}, u32[]{:S(2)}) collective-permute-start(bf16[1,128,1024]{2,1,0:T(8,128)(2,1)S(1)} %get-tuple-element.41), channel_id=1, source_target_pairs={{0,8},{4,12},{8,0},{12,4},{16,24},{20,28},{24,16},{28,20},{1,9},{5... | collective-permute-start | bytes 786440 | tf_op jit(solution)/shard_map/ppermute | solution.py:15
  315.7 19.8 %collective-permute-start.52 = (bf16[1,128,1024]{2,1,0:T(8,128)(2,1)S(1)}, bf16[1,128,1024]{2,1,0:T(8,128)(2,1)S(1)}, u32[]{:S(2)}, u32[]{:S(2)}) collective-permute-start(bf16[1,128,1024]{2,1,0:T(8,128)(2,1)S(1)} %get-tuple-element.39), channel_id=1, source_target_pairs={{0,16},{4,20},{8,24},{12,28},{16,0},{20,4},{24,8},{28,12},{1,17},{... | collective-permute-start | bytes 786440 | tf_op jit(solution)/shard_map/ppermute | solution.py:15
  316.3 20.6 %collective-permute-start.32 = (bf16[2,128,768]{2,1,0:T(8,128)(2,1)S(1)}, bf16[2,128,768]{2,1,0:T(8,128)(2,1)S(1)}, u32[]{:S(2)}, u32[]{:S(2)}) collective-permute-start(bf16[2,128,768]{2,1,0:T(8,128)(2,1)S(1)} %pad_maximum_fusion.20), channel_id=1, source_target_pairs={{0,16},{4,20},{8,24},{12,28},{16,0},{20,4},{24,8},{28,12},{1,17},{... | collective-permute-start | bytes 1179656 | tf_op jit(solution)/shard_map/ppermute | solution.py:15
  318.0 11.6 %collective-permute-start.40 = (bf16[1,32,1024]{2,1,0:T(8,128)(2,1)S(1)}, bf16[1,32,1024]{2,1,0:T(8,128)(2,1)S(1)}, u32[]{:S(2)}, u32[]{:S(2)}) collective-permute-start(bf16[1,32,1024]{2,1,0:T(8,128)(2,1)S(1)} %bitcast.397), channel_id=1, source_target_pairs={{0,16},{4,20},{8,24},{12,28},{16,0},{20,4},{24,8},{28,12},{1,17},{... | collective-permute-start | bytes 196616 | tf_op jit(solution)/shard_map/ppermute | solution.py:15
  334.8 14.4 %collective-permute-start.47 = (bf16[2,128,1024]{2,1,0:T(8,128)(2,1)S(1)}, bf16[2,128,1024]{2,1,0:T(8,128)(2,1)S(1)}, u32[]{:S(2)}, u32[]{:S(2)}) collective-permute-start(bf16[2,128,1024]{2,1,0:T(8,128)(2,1)S(1)} %pad_maximum_fusion.16), channel_id=1, source_target_pairs={{0,16},{4,20},{8,24},{12,28},{16,0},{20,4},{24,8},{28,12},{1,17},{... | collective-permute-start | bytes 1572872 | tf_op jit(solution)/shard_map/ppermute | solution.py:15
  335.5 14.1 %collective-permute-start.53 = (bf16[2,128,1024]{2,1,0:T(8,128)(2,1)S(1)}, bf16[2,128,1024]{2,1,0:T(8,128)(2,1)S(1)}, u32[]{:S(2)}, u32[]{:S(2)}) collective-permute-start(bf16[2,128,1024]{2,1,0:T(8,128)(2,1)S(1)} %pad_maximum_fusion.18), channel_id=1, source_target_pairs={{0,8},{4,12},{8,0},{12,4},{16,24},{20,28},{24,16},{28,20},{1,9},{5... | collective-permute-start | bytes 1572872 | tf_op jit(solution)/shard_map/ppermute | solution.py:15
  337.0 13.3 %collective-permute-start.33 = (bf16[4,128,768]{2,1,0:T(8,128)(2,1)S(1)}, bf16[4,128,768]{2,1,0:T(8,128)(2,1)S(1)}, u32[]{:S(2)}, u32[]{:S(2)}) collective-permute-start(bf16[4,128,768]{2,1,0:T(8,128)(2,1)S(1)} %pad_maximum_fusion.12), channel_id=1, source_target_pairs={{0,4},{4,0},{8,12},{12,8},{16,20},{20,16},{24,28},{28,24},{1,5},{5... | collective-permute-start | bytes 2359304 | tf_op jit(solution)/shard_map/ppermute | solution.py:15
  (62 other events, 446.8 us)

commit v2 on v0

v2 whole, which is shorter than its diff:
```python
import jax
import jax.numpy as jnp
from jax import lax
from jax.experimental import pallas as pl
from jax.experimental.pallas import tpu as pltpu
from jax.sharding import PartitionSpec as P

BF = jnp.bfloat16
F32 = jnp.float32

NN = ((1,), (0,))
NT = ((1,), (1,))
TN = ((0,), (0,))


def dot(left, right, dims):
    return lax.dot_general(left, right, (dims, ((), ())), preferred_element_type=F32)


def swap(values, axis, bits):
    size = lax.axis_size(axis)
    return lax.ppermute(values, axis, [(i, i ^ bits) for i in range(size)])


def to_all(blocks):
    return lax.all_to_all(blocks, "tensor", 0, 0, tiled=True)


def inverse_rms(rows):
    return lax.rsqrt(jnp.mean(rows * rows, axis=-1, keepdims=True) + eps)


HEAD_DIM = 64
GROUP = 8
TERMS = 4
GAP = 16
eps = 1e-06
mask_fill = -1000000000.0


def small_cost():
    return pl.CostEstimate(flops=1024, bytes_accessed=1024, transcendentals=0)


def cost_of(microseconds):
    return pl.CostEstimate(flops=1024, bytes_accessed=int(microseconds * 3.0e6), transcendentals=0)


def pick_rows(base, offsets, weight, mine, ways, cost, limit):
    rows, width = base.shape
    chunks = 2 * ways
    block = rows // chunks
    sub = 256
    sub_groups = sub // GROUP

    def kernel(mine_ref, base_ref, offset_ref, weight_ref, picked_ref, square_ref, held, sems):
        def load(n):
            part = pl.ds(n * block, block)
            return pltpu.make_async_copy(base_ref.at[part], held.at[part], sems.at[n])

        for n in range(chunks):
            load(n).start()
        row = lax.broadcasted_iota(jnp.int32, (sub, sub_groups), 0)
        group = lax.broadcasted_iota(jnp.int32, (sub, sub_groups), 1)
        local = row - GROUP * group
        for n in range(chunks):
            load(n).wait()
            for s in range(n * block // sub, (n + 1) * block // sub):
                to = slice(s * sub_groups, (s + 1) * sub_groups)
                chosen = (local == offset_ref[:, to]).astype(F32).astype(BF)
                picked_ref[to, :] = dot(chosen, held[s * sub : (s + 1) * sub, :], TN).astype(BF)
        if square_ref is not None:
            weights = weight_ref[...].astype(F32)
            total = jnp.zeros((1, 1), F32)
            for n in range(2):
                start = pl.multiple_of((2 * mine_ref[0] + n) * block, block)
                mult = held[pl.ds(start, block), :].astype(F32) * weights
                score = jnp.sum(mult, axis=1, keepdims=True)
                total = total + jnp.sum(score * score, axis=0, keepdims=True)
            square_ref[...] = jnp.broadcast_to(total, square_ref.shape)

    with_squares = weight is not None
    if with_squares:
        body = kernel
    else:

        def body(mine_ref, base_ref, offset_ref, picked_ref, held, sems):
            kernel(mine_ref, base_ref, offset_ref, None, picked_ref, None, held, sems)

    whole = pl.BlockSpec(memory_space=pltpu.VMEM)
    out_shape = [jax.ShapeDtypeStruct((rows // GROUP, width), BF)]
    operands = [mine, base, offsets]
    in_specs = [pl.BlockSpec(memory_space=pltpu.SMEM), pl.BlockSpec(memory_space=pltpu.HBM), whole]
    if with_squares:
        out_shape.append(jax.ShapeDtypeStruct((1, 128), F32))
        operands.append(weight)
        in_specs.append(whole)
    return pl.pallas_call(
        body,
        in_specs=in_specs,
        out_specs=[whole] * len(out_shape),
        out_shape=out_shape,
        scratch_shapes=[pltpu.VMEM((rows, width), BF), pltpu.SemaphoreType.DMA((chunks,))],
        cost_estimate=cost,
        compiler_params=pltpu.CompilerParams(vmem_limit_bytes=limit << 20),
        name="pick_rows",
    )(*operands)


def merge_rows(base, offsets, pieces, parts, held_out=None):
    rows, width = base.shape
    ways, depth, _ = pieces.shape
    count = rows // ways
    groups = count // GROUP
    kept = [] if held_out is None else [held_out]
    sub = 256
    sub_groups = sub // GROUP

    def kernel(part_ref, base_ref, offset_ref, piece_ref, *rest):
        out_ref = rest[-1]
        local = lax.broadcasted_iota(jnp.int32, (sub, sub_groups), 0) - GROUP * lax.broadcasted_iota(
            jnp.int32, (sub, sub_groups), 1
        )
        for s in range(count // sub):
            here = slice(s * sub, (s + 1) * sub)
            to = slice(s * sub_groups, (s + 1) * sub_groups)
            chosen = (local == offset_ref[:, to]).astype(F32)
            hit = jnp.sum(chosen, axis=1, keepdims=True) > 0.5
            spread = dot(chosen.astype(BF), piece_ref[0, to, :], NN)
            out_ref[here, :] = jnp.where(hit, spread, base_ref[here, :].astype(F32)).astype(BF)

    grid_spec = pltpu.PrefetchScalarGridSpec(
        num_scalar_prefetch=1,
        grid=(parts.shape[0],),
        in_specs=[
            pl.BlockSpec((count, width), lambda i, p: (p[i], 0)),
            pl.BlockSpec((1, groups), lambda i, p: (0, p[i])),
            pl.BlockSpec((1, depth, width), lambda i, p: (p[i], 0, 0)),
        ]
        + [pl.BlockSpec(memory_space=pl.ANY)] * len(kept),
        out_specs=pl.BlockSpec((count, width), lambda i, p: (p[i], 0)),
    )
    return pl.pallas_call(
        kernel,
        grid_spec=grid_spec,
        out_shape=jax.ShapeDtypeStruct((rows, width), BF),
        input_output_aliases={4: 0} if kept else {},
        cost_estimate=small_cost(),
        name="merge_rows",
    )(parts, base, offsets, pieces, *kept)


def attend(picked, gain, weight, seq_row, seq_column, router, ways):
    rows, width = picked.shape
    heads_width = weight.shape[2]
    heads = heads_width // HEAD_DIM
    block = min(256, rows)

    def kernel(
        picked_ref, gain_ref, weight_ref, row_ref, column_ref, router_ref, low_ref, qkv_ref, probs_ref, out_ref, gating_ref, square_ref
    ):
        values = picked_ref[...].astype(F32)
        score = jnp.sum(values * router_ref[...].astype(F32), axis=-1, keepdims=True)
        gating_ref[...] = jax.nn.sigmoid(score)
        square_ref[...] = jnp.broadcast_to(jnp.sum(score * score, axis=0, keepdims=True), square_ref.shape)
        low_ref[...] = (values * inverse_rms(values) * gain_ref[...].astype(F32)).astype(BF)
        for n in range(3):
            qkv_ref[n] = dot(low_ref[...], weight_ref[n], NN).astype(BF)
        lane_head = lax.broadcasted_iota(jnp.int32, (1, heads_width), 1) // HEAD_DIM
        for start in range(0, rows, block):
            stop = start + block
            query = qkv_ref[0, start:stop, :] * BF(HEAD_DIM ** (-0.5))
            order = lax.broadcasted_iota(jnp.int32, (block, stop), 0) + start
            keys = lax.broadcasted_iota(jnp.int32, (block, stop), 1)
            allowed = (column_ref[start:stop, :] == row_ref[:, :stop]) & (order >= keys)
            total = jnp.zeros((block, heads_width), F32)
            for head in range(heads):
                here = lane_head == head
                key = jnp.where(here, qkv_ref[1, :stop, :], BF(0))
                logits = jnp.where(allowed, dot(query, key, NT), mask_fill)
                raised = jnp.exp(logits - jnp.max(logits, axis=-1, keepdims=True))
                probs = (raised * (1.0 / jnp.sum(raised, axis=-1, keepdims=True))).astype(BF)
                probs_ref[head, start:stop, :stop] = probs
                if stop < rows:
                    probs_ref[head, start:stop, stop:] = jnp.zeros((block, rows - stop), BF)
                value = jnp.where(here, qkv_ref[2, :stop, :], BF(0))
                total = total + dot(probs, value, NN)
            for k in range(ways):
                out_ref[k, start:stop, :] = total.astype(BF)

    whole = pl.BlockSpec(memory_space=pltpu.VMEM)
    return pl.pallas_call(
        kernel,
        in_specs=[whole] * 6,
        out_specs=[whole] * 6,
        out_shape=[
            jax.ShapeDtypeStruct((rows, width), BF),
            jax.ShapeDtypeStruct((3, rows, heads_width), BF),
            jax.ShapeDtypeStruct((heads, rows, rows), BF),
            jax.ShapeDtypeStruct((ways, rows, heads_width), BF),
            jax.ShapeDtypeStruct((rows, 1), F32),
            jax.ShapeDtypeStruct((1, 128), F32),
        ],
        cost_estimate=cost_of(5.0),
        compiler_params=pltpu.CompilerParams(vmem_limit_bytes=40 << 20),
        name="attend",
    )(picked, gain, weight, seq_row, seq_column, router)


def feed_forward(heads, here, beside, across, picked, gain, up, grad_act, grad_mixer, part):
    tile = up.shape[1]
    sub = min(256, tile)
    rows, width = picked.shape
    hidden = up.shape[1]
    steps = hidden // tile
    count, _, heads_width = heads.shape
    piece = heads_width // 4
    slope = 0.7978845608028654
    cubic = 0.044715

    def kernel(
        part_ref,
        heads_ref,
        here_ref,
        beside_ref,
        across_ref,
        picked_ref,
        gain_ref,
        up_ref,
        act_grad_ref,
        mixer_ref,
        attended_ref,
        low_ref,
        act_ref,
        pre_ref,
        hidden_ref,
        part_out_ref,
        gain_part_ref,
        sent_ref,
        total,
        state,
        weights,
    ):
        step = pl.program_id(0)

        @pl.when(step == 0)
        def _():
            quarter = part_ref[0] & 3
            for n, source in enumerate((here_ref, across_ref.at[0], beside_ref, across_ref.at[1])):
                start = pl.multiple_of((quarter ^ n) * piece, piece)
                for k in range(count):
                    weights[k, pl.ds(start, piece), :] = source[k]
            attended = dot(heads_ref[0], weights[0], NN)
            for k in range(1, count):
                attended = attended + dot(heads_ref[k], weights[k], NN)
            attended_ref[...] = attended
            state_in = picked_ref[...].astype(F32) + attended
            state[...] = state_in
            low_ref[...] = (state_in * inverse_rms(state_in) * gain_ref[...].astype(F32)).astype(BF)
            total[...] = jnp.zeros_like(total)

        for s in range(tile // sub):
            lanes = slice(s * sub, (s + 1) * sub)
            value = dot(low_ref[...], up_ref[:, lanes], NN)
            square = value * value
            bent = jnp.tanh(value * (slope + (slope * cubic) * square))
            half = 0.5 * (1.0 + bent)
            act_ref[:, lanes] = (value * half).astype(BF)
            rise = half + (0.5 * value) * (1.0 - bent * bent) * (slope + (3.0 * slope * cubic) * square)
            pre = (act_grad_ref[:, lanes] * rise).astype(BF)
            pre_ref[:, lanes] = pre
            total[...] += dot(pre, up_ref[:, lanes], NT)

        @pl.when(step == steps - 1)
        def _():
            state_in = state[...]
            grad = total[...]
            inverse = inverse_rms(state_in)
            normal = state_in * inverse
            gain_part_ref[...] = jnp.sum(grad * normal, axis=0, keepdims=True)
            scaled = grad * gain_ref[...].astype(F32)
            along = jnp.mean(scaled * normal, axis=-1, keepdims=True)
            back = inverse * (scaled - normal * along)
            hidden_ref[...] = back.astype(BF)
            part_out_ref[...] = (back + mixer_ref[...].astype(F32) * (1.0 / count)).astype(BF)
            for k in range(count):
                sent_ref[k] = dot(part_out_ref[...], weights[k], NT).astype(BF)

    def fixed(shape):
        return pl.BlockSpec(shape, lambda i: (0,) * len(shape))

    return pl.pallas_call(
        kernel,
        grid=(steps,),
        in_specs=[
            pl.BlockSpec(memory_space=pltpu.SMEM),
            fixed(heads.shape),
            fixed(here.shape),
            fixed(beside.shape),
            fixed(across.shape),
            fixed((rows, width)),
            fixed((1, width)),
            pl.BlockSpec((width, tile), lambda i: (0, i)),
            pl.BlockSpec((rows, tile), lambda i: (0, i)),
            fixed((rows, width)),
        ],
        out_specs=[
            fixed((rows, width)),
            fixed((rows, width)),
            pl.BlockSpec((rows, tile), lambda i: (0, i)),
            pl.BlockSpec((rows, tile), lambda i: (0, i)),
            fixed((rows, width)),
            fixed((rows, width)),
            fixed((1, width)),
            fixed(heads.shape),
        ],
        out_shape=[
            jax.ShapeDtypeStruct((rows, width), F32),
            jax.ShapeDtypeStruct((rows, width), BF),
            jax.ShapeDtypeStruct((rows, hidden), BF),
            jax.ShapeDtypeStruct((rows, hidden), BF),
            jax.ShapeDtypeStruct((rows, width), BF),
            jax.ShapeDtypeStruct((rows, width), BF),
            jax.ShapeDtypeStruct((1, width), F32),
            jax.ShapeDtypeStruct(heads.shape, BF),
        ],
        scratch_shapes=[
            pltpu.VMEM((rows, width), F32),
            pltpu.VMEM((rows, width), F32),
            pltpu.VMEM((count, heads_width, width), BF),
        ],
        cost_estimate=small_cost(),
        compiler_params=pltpu.CompilerParams(vmem_limit_bytes=48 << 20),
        name="feed_forward",
    )(part, heads, here, beside, across, picked, gain, up, grad_act, grad_mixer)


def act_grads(grad_rows, gating, down):
    rows, width = grad_rows.shape

    def kernel(rows_ref, gating_ref, down_ref, mixer_ref, grad_ref):
        mixer_ref[...] = (gating_ref[...] * rows_ref[...].astype(F32)).astype(BF)
        grad_ref[...] = dot(mixer_ref[...], down_ref[...], NT)

    whole = pl.BlockSpec(memory_space=pltpu.VMEM)
    return pl.pallas_call(
        kernel,
        in_specs=[whole] * 3,
        out_specs=[whole] * 2,
        out_shape=[jax.ShapeDtypeStruct((rows, width), BF), jax.ShapeDtypeStruct((rows, down.shape[0]), F32)],
        cost_estimate=small_cost(),
        name="act_grads",
    )(grad_rows, gating, down)


def attend_back(grad_head_in, qkv, probs, weight, picked, gain, hidden_part):
    rows, width = picked.shape
    heads_width = weight.shape[2]
    heads = heads_width // HEAD_DIM
    block = min(256, rows)
    scale = HEAD_DIM ** (-0.5)

    def kernel(
        head_ref,
        qkv_ref,
        probs_ref,
        weight_ref,
        picked_ref,
        gain_ref,
        hidden_ref,
        grads_ref,
        gain_part_ref,
        result,
        grad_key,
        grad_value,
    ):
        lane_head = lax.broadcasted_iota(jnp.int32, (1, heads_width), 1) // HEAD_DIM
        for start in reversed(range(0, rows, block)):
            stop = start + block
            here_rows = slice(start, stop)
            grad_head = head_ref[here_rows, :]
            query = qkv_ref[0, here_rows, :] * BF(scale)
            grad_query = jnp.zeros((block, heads_width), F32)
            add_key = jnp.zeros((stop, heads_width), F32)
            add_value = jnp.zeros((stop, heads_width), F32)
            for head in range(heads):
                here = lane_head == head
                value = jnp.where(here, qkv_ref[2, :stop, :], BF(0))
                key = jnp.where(here, qkv_ref[1, :stop, :], BF(0))
                low = probs_ref[head, here_rows, :stop]
                weighted = low.astype(F32) * dot(grad_head, value, NT)
                row_sum = jnp.sum(weighted, axis=-1, keepdims=True)
                slopes = (weighted - low.astype(F32) * row_sum).astype(BF)
                grad_query = grad_query + dot(slopes, key, NN)
                add_key = add_key + dot(slopes, jnp.where(here, query, BF(0)), TN)
                add_value = add_value + dot(low, jnp.where(here, grad_head, BF(0)), TN)
            grads_ref[0, here_rows, :] = (grad_query * scale).astype(BF)
            if stop == rows:
                grad_key[...] = add_key
                grad_value[...] = add_value
            else:
                grad_key[:stop, :] += add_key
                grad_value[:stop, :] += add_value
        grads_ref[1] = grad_key[...].astype(BF)
        grads_ref[2] = grad_value[...].astype(BF)
        first = dot(grads_ref[0], weight_ref[0], NT)
        for n in range(1, 3):
            first = first + dot(grads_ref[n], weight_ref[n], NT)
        values = picked_ref[...].astype(F32)
        inverse = inverse_rms(values)
        normal = values * inverse
        gain_part_ref[...] = jnp.sum(first * normal, axis=0, keepdims=True)
        scaled = first * gain_ref[...].astype(F32)
        along = jnp.mean(scaled * normal, axis=-1, keepdims=True)
        result[...] = (hidden_ref[...].astype(F32) + inverse * (scaled - normal * along)).astype(BF)

    whole = pl.BlockSpec(memory_space=pltpu.VMEM)
    return pl.pallas_call(
        kernel,
        in_specs=[whole] * 7,
        out_specs=[whole] * 3,
        out_shape=[
            jax.ShapeDtypeStruct((3, rows, heads_width), BF),
            jax.ShapeDtypeStruct((1, width), F32),
            jax.ShapeDtypeStruct((rows, width), BF),
        ],
        scratch_shapes=[
            pltpu.VMEM((rows, heads_width), F32),
            pltpu.VMEM((rows, heads_width), F32),
        ],
        cost_estimate=small_cost(),
        compiler_params=pltpu.CompilerParams(vmem_limit_bytes=48 << 20),
        name="attend_back",
    )(grad_head_in, qkv, probs, weight, picked, gain, hidden_part)


def spread_rows(down_near, down_far, up_near, up_far, index_down, index_up):
    half, rows, width = down_near.shape

    def kernel(down_index, up_index, down_ref, far_ref, up_ref, up_far_ref, down_out, up_out):
        near = pl.program_id(0) < half

        @pl.when(near)
        def _():
            down_out[...] = down_ref[0].astype(F32)
            up_out[...] = up_ref[0].astype(F32)

        @pl.when(jnp.logical_not(near))
        def _():
            down_out[...] = far_ref[0].astype(F32)
            up_out[...] = up_far_ref[0].astype(F32)

    first = pl.BlockSpec((1, rows, width), lambda i, d, u: (jnp.minimum(i, half - 1), 0, 0))
    second = pl.BlockSpec((1, rows, width), lambda i, d, u: (jnp.maximum(i - half, 0), 0, 0))
    return pl.pallas_call(
        kernel,
        grid_spec=pltpu.PrefetchScalarGridSpec(
            num_scalar_prefetch=2,
            grid=(2 * half,),
            in_specs=[first, second, first, second],
            out_specs=[
                pl.BlockSpec((rows, width), lambda i, d, u: (d[i], 0)),
                pl.BlockSpec((rows, width), lambda i, d, u: (u[i], 0)),
            ],
        ),
        out_shape=[jax.ShapeDtypeStruct((2 * half * rows, width), F32)] * 2,
        cost_estimate=small_cost(),
        name="spread_rows",
    )(index_down, index_up, down_near, down_far, up_near, up_far)


def qkv_part_of(first_low, grads):
    rows, width = first_low.shape
    part_width = grads.shape[2]

    def kernel(low_ref, grads_ref, out_ref):
        for n in range(3):
            product = dot(grads_ref[n], low_ref[...], TN)
            out_ref[n * part_width : (n + 1) * part_width, :] = product.astype(BF)

    whole = pl.BlockSpec(memory_space=pltpu.VMEM)
    return pl.pallas_call(
        kernel,
        in_specs=[whole] * 2,
        out_specs=whole,
        out_shape=jax.ShapeDtypeStruct((3 * part_width, width), BF),
        cost_estimate=small_cost(),
        name="qkv_part",
    )(first_low, grads)


def spread_qkv(lane_a, got_a, lane_b, got_b, first, part_width):
    width = lane_a.shape[1]
    rows = lane_a.shape[0] - first
    tile = 128

    def kernel(a_ref, a_got, b_ref, b_got, out_ref):
        for n in range(2 * rows // tile):
            start = first + n * tile % rows
            ref, got = (a_ref, a_got) if n * tile < rows else (b_ref, b_got)
            lane, column = divmod(n * tile, part_width)
            piece = ref[start : start + tile, :].astype(F32) + got[start : start + tile, :].astype(F32)
            out_ref[lane, :, column : column + tile] = piece.T

    whole = pl.BlockSpec(memory_space=pltpu.VMEM)
    return pl.pallas_call(
        kernel,
        in_specs=[whole] * 4,
        out_specs=whole,
        out_shape=jax.ShapeDtypeStruct((2 * rows // part_width, width, part_width), F32),
        cost_estimate=small_cost(),
        compiler_params=pltpu.CompilerParams(vmem_limit_bytes=16 << 20),
        name="spread_qkv",
    )(lane_a, got_a, lane_b, got_b)


def core_grads(activated, grad_mixer, second_low, grad_pre, heads, attended_part, part, keys_a, keys_b):
    rows, hidden = activated.shape
    width = grad_mixer.shape[1]
    copies = len(keys_a)
    half = copies // 2
    count, _, heads_width = heads.shape
    block = hidden // copies
    small = heads_width // copies
    many = count // 2
    depth = half * (block + many * small)

    def kernel(part_ref, act_ref, mixer_ref, low_ref, pre_ref, heads_ref, term_ref, keep_ref, a_ref, b_ref, full, narrow):
        def place(source, each, lane, keys, first, stride):
            for n, key in enumerate(keys):
                start = pl.multiple_of((part_ref[0] ^ key) * each, each)
                at = first + (n % half) * stride
                piece = source[pl.ds(start, each), :]
                if n < half:
                    keep_ref[lane, at : at + each, :] = piece
                else:
                    (b_ref if lane else a_ref)[at : at + each, :] = piece

        full[...] = dot(act_ref[...], mixer_ref[...], TN).astype(BF)
        place(full, block, 0, keys_a, 0, block)
        full[...] = dot(low_ref[...], pre_ref[...], TN).astype(BF)
        place(full, block, 1, keys_b, 0, block)
        for k in range(count):
            narrow[...] = dot(heads_ref[k], term_ref[...], TN).astype(BF)
            lane, spot = divmod(k, many)
            place(narrow, small, lane, keys_b if lane else keys_a, half * block + spot * small, many * small)

    whole = pl.BlockSpec(memory_space=pltpu.VMEM)
    lane_shape = jax.ShapeDtypeStruct((depth, width), BF)
    return pl.pallas_call(
        kernel,
        in_specs=[pl.BlockSpec(memory_space=pltpu.SMEM)] + [whole] * 6,
        out_specs=[whole] * 3,
        out_shape=[jax.ShapeDtypeStruct((2, depth, width), BF), lane_shape, lane_shape],
        scratch_shapes=[pltpu.VMEM((hidden, width), BF), pltpu.VMEM((heads_width, width), BF)],
        cost_estimate=small_cost(),
        compiler_params=pltpu.CompilerParams(vmem_limit_bytes=24 << 20),
        name="core_grads",
    )(part, activated, grad_mixer, second_low, grad_pre, heads, attended_part)


def plus(left, right):
    return (left.astype(F32) + right.astype(F32)).astype(BF)


def halving_sums(keep, got_a, got_b, wide, narrow):
    width = keep.shape[2]

    def kernel(keep_ref, a_got, b_got, stay_ref, a_out, b_out):
        for lane, got, out in ((0, a_got, a_out), (1, b_got, b_out)):
            for first, size, at in ((0, wide // 2, 0), (wide, narrow // 2, wide // 2)):
                stays, leaves = slice(first, first + size), slice(first + size, first + 2 * size)
                to = slice(at, at + size)
                stay_ref[lane, to, :] = plus(keep_ref[lane, stays, :], got[stays, :])
                out[to, :] = plus(keep_ref[lane, leaves, :], got[leaves, :])

    whole = pl.BlockSpec(memory_space=pltpu.VMEM)
    depth = (wide + narrow) // 2
    lane_shape = jax.ShapeDtypeStruct((depth, width), BF)
    return pl.pallas_call(
        kernel,
        in_specs=[whole] * 3,
        out_specs=[whole] * 3,
        out_shape=[jax.ShapeDtypeStruct((2, depth, width), BF), lane_shape, lane_shape],
        cost_estimate=small_cost(),
        compiler_params=pltpu.CompilerParams(vmem_limit_bytes=16 << 20),
        name="halving_sums",
    )(keep, got_a, got_b)


def owned_sums(keep, got_a, got_b, qkv, qkv_got, fresh, small, wide, ways):
    width = keep.shape[2]
    narrow = keep.shape[1] - wide
    third = qkv.shape[0] // 2
    own = fresh.shape[0]
    terms = small.shape[0]
    many = ways // 2
    each = narrow // many
    depth = own + GAP + each

    def kernel(keep_ref, a_got, b_got, qkv_ref, qkv_got_ref, fresh_ref, small_ref, a_out, b_out, sent_ref):
        high = small_ref[...].astype(BF)
        low = (small_ref[...] - high.astype(F32)).astype(BF)
        sums = jnp.concatenate([high, low, jnp.zeros((GAP - 2 * terms, width), BF)], axis=0)
        for lane, got, out in ((0, a_got, a_out), (1, b_got, b_out)):
            out[:wide, :] = plus(keep_ref[lane, :wide, :], got[:wide, :])
            here = slice(lane * third, (lane + 1) * third)
            out[wide:, :] = plus(qkv_ref[here, :], qkv_got_ref[here, :])
            done = plus(keep_ref[lane, wide:, :], got[wide:, :])
            for spot in range(many):
                k = lane * many + spot
                sent_ref[k, :own, :] = fresh_ref[...]
                sent_ref[k, own : own + GAP, :] = sums
                sent_ref[k, own + GAP :, :] = done[spot * each : (spot + 1) * each, :]

    whole = pl.BlockSpec(memory_space=pltpu.VMEM)
    lane_shape = jax.ShapeDtypeStruct((wide + third, width), BF)
    return pl.pallas_call(
        kernel,
        in_specs=[whole] * 7,
        out_specs=[whole] * 3,
        out_shape=[lane_shape, lane_shape, jax.ShapeDtypeStruct((ways, depth, width), BF)],
        cost_estimate=small_cost(),
        compiler_params=pltpu.CompilerParams(vmem_limit_bytes=20 << 20),
        name="owned_sums",
    )(keep, got_a, got_b, qkv, qkv_got, fresh, small)


def gather_sums(lane_a, got_a, lane_b, got_b, wide):
    depth, width = lane_a.shape

    def kernel(a_ref, a_got, b_ref, b_got, a_out, b_out):
        for ref, got, out in ((a_ref, a_got, a_out), (b_ref, b_got, b_out)):
            out[:wide, :] = ref[:wide, :]
            out[wide : 2 * wide, :] = got[:wide, :]
            out[2 * wide :, :] = plus(ref[wide:, :], got[wide:, :])

    whole = pl.BlockSpec(memory_space=pltpu.VMEM)
    lane_shape = jax.ShapeDtypeStruct((depth + wide, width), BF)
    return pl.pallas_call(
        kernel,
        in_specs=[whole] * 4,
        out_specs=[whole] * 2,
        out_shape=[lane_shape, lane_shape],
        cost_estimate=small_cost(),
        compiler_params=pltpu.CompilerParams(vmem_limit_bytes=16 << 20),
        name="gather_sums",
    )(lane_a, got_a, lane_b, got_b)


def gather_blocks(lane_a, got_a, lane_b, got_b, wide):
    width = lane_a.shape[1]

    def kernel(a_ref, a_got, b_ref, b_got, a_out, b_out):
        for ref, got, out in ((a_ref, a_got, a_out), (b_ref, b_got, b_out)):
            out[:wide, :] = ref[...]
            out[wide:, :] = got[...]

    def top(array):
        return pl.BlockSpec((wide, width), lambda i: (0, 0))

    shape = jax.ShapeDtypeStruct((2 * wide, width), BF)
    return pl.pallas_call(
        kernel,
        grid=(1,),
        in_specs=[top(a) for a in (lane_a, got_a, lane_b, got_b)],
        out_specs=[pl.BlockSpec((2 * wide, width), lambda i: (0, 0))] * 2,
        out_shape=[shape, shape],
        cost_estimate=small_cost(),
        name="gather_blocks",
    )(lane_a, got_a, lane_b, got_b)


def split_sums(values):
    high = values.astype(BF)
    low = (values - high.astype(F32)).astype(BF)
    return jnp.concatenate([high, low, jnp.zeros((GAP - 2 * TERMS, values.shape[1]), BF)], axis=0)


def joined_sums(rows):
    return rows[:TERMS].astype(F32) + rows[TERMS : 2 * TERMS].astype(F32)


def first_small(received, own):
    ways, depth, width = received.shape
    each = depth - own - GAP

    def kernel(got_ref, out_ref):
        total = got_ref[0, own + GAP :, :].astype(F32)
        sums = joined_sums(got_ref[0, own : own + GAP, :])
        for k in range(1, ways):
            total = total + got_ref[k, own + GAP :, :].astype(F32)
            sums = sums + joined_sums(got_ref[k, own : own + GAP, :])
        out_ref[:each, :] = total.astype(BF)
        out_ref[each:, :] = split_sums(sums)

    whole = pl.BlockSpec(memory_space=pltpu.VMEM)
    return pl.pallas_call(
        kernel,
        in_specs=[whole],
        out_specs=whole,
        out_shape=jax.ShapeDtypeStruct((each + GAP, width), BF),
        cost_estimate=small_cost(),
        name="first_small",
    )(received)


def join_small(mine_rows, other_rows):
    depth, width = mine_rows.shape
    each = depth - GAP

    def kernel(mine_ref, other_ref, out_ref):
        out_ref[:each, :] = mine_ref[:each, :]
        out_ref[each : 2 * each, :] = other_ref[:each, :]
        out_ref[2 * each :, :] = split_sums(joined_sums(mine_ref[each:, :]) + joined_sums(other_ref[each:, :]))

    whole = pl.BlockSpec(memory_space=pltpu.VMEM)
    return pl.pallas_call(
        kernel,
        in_specs=[whole] * 2,
        out_specs=whole,
        out_shape=jax.ShapeDtypeStruct((2 * each + GAP, width), BF),
        cost_estimate=small_cost(),
        name="join_small",
    )(mine_rows, other_rows)


def last_small(mine_rows, other_rows, index):
    depth, width = mine_rows.shape
    blocks = index.shape[0]
    total = 2 * (depth - GAP)
    each = total // blocks

    def kernel(index_ref, mine_ref, other_ref, out_ref, small_ref):
        for n in range(blocks):
            source, at = (mine_ref, n) if n < blocks // 2 else (other_ref, n - blocks // 2)
            start = pl.multiple_of(index_ref[n] * each, each)
            out_ref[pl.ds(start, each), :] = source[at * each : (at + 1) * each, :].astype(F32)
        small_ref[...] = joined_sums(mine_ref[depth - GAP :, :]) + joined_sums(other_ref[depth - GAP :, :])

    whole = pl.BlockSpec(memory_space=pltpu.VMEM)
    return pl.pallas_call(
        kernel,
        in_specs=[pl.BlockSpec(memory_space=pltpu.SMEM), whole, whole],
        out_specs=[whole] * 2,
        out_shape=[jax.ShapeDtypeStruct((total, width), F32), jax.ShapeDtypeStruct((TERMS, width), F32)],
        cost_estimate=small_cost(),
        name="last_small",
    )(index, mine_rows, other_rows)


def sum_heads(terms):
    def kernel(terms_ref, out_ref):
        total = terms_ref[0].astype(F32)
        for k in range(1, terms.shape[0]):
            total = total + terms_ref[k].astype(F32)
        out_ref[...] = total.astype(BF)

    whole = pl.BlockSpec(memory_space=pltpu.VMEM)
    return pl.pallas_call(
        kernel,
        in_specs=[whole],
        out_specs=whole,
        out_shape=jax.ShapeDtypeStruct(terms.shape[1:], BF),
        cost_estimate=small_cost(),
        name="sum_heads",
    )(terms)


def finish_rows(mixer_terms, picked, gating, attended, grad_rows, gain_one, gain_two, square, routed_square, mine, ways):
    rows, width = picked.shape
    own = rows // ways

    def kernel(
        mine_ref,
        terms_ref,
        picked_ref,
        gating_ref,
        attended_ref,
        rows_ref,
        one_ref,
        two_ref,
        square_ref,
        routed_ref,
        new_ref,
        score_ref,
        small_ref,
    ):
        branch = attended_ref[...]
        for k in range(ways):
            branch = branch + terms_ref[k].astype(F32)
        values = picked_ref[...].astype(F32)
        gate = gating_ref[...]
        new_ref[...] = (values + gate * branch).astype(BF)
        along = jnp.sum(rows_ref[...].astype(F32) * branch, axis=-1, keepdims=True)
        score = along * gate * (1.0 - gate)
        score_ref[...] = score
        small_ref[0:1, :] = jnp.sum(score * values, axis=0, keepdims=True)
        small_ref[1:2, :] = one_ref[...]
        small_ref[2:3, :] = two_ref[...]
        lane = lax.broadcasted_iota(jnp.int32, (1, width), 1)
        both = jnp.where(lane == 0, square_ref[:, 0:1], routed_ref[:, 0:1] * (1.0 / ways))
        small_ref[3:4, :] = jnp.where(lane < 2, both, 0.0)

    def block(shape):
        return pl.BlockSpec(shape, lambda i, m: (m[0], 0))

    def fixed(shape):
        return pl.BlockSpec(shape, lambda i, m: (0, 0))

    return pl.pallas_call(
        kernel,
        grid_spec=pltpu.PrefetchScalarGridSpec(
            num_scalar_prefetch=1,
            grid=(1,),
            in_specs=[pl.BlockSpec(mixer_terms.shape, lambda i, m: (0, 0, 0))]
            + [block((own, width)), block((own, 1)), block((own, width)), block((own, width))]
            + [fixed((1, width))] * 2
            + [fixed((1, 128))] * 2,
            out_specs=[fixed((own, width)), fixed((own, 1)), fixed((4, width))],
        ),
        out_shape=[
            jax.ShapeDtypeStruct((own, width), BF),
            jax.ShapeDtypeStruct((own, 1), F32),
            jax.ShapeDtypeStruct((4, width), F32),
        ],
        cost_estimate=cost_of(10),
        name="finish_rows",
    )(mine, mixer_terms, picked, gating, attended, grad_rows, gain_one, gain_two, square, routed_square)


def finish_input(terms, grad_rows, score, router, mine, ways):
    rows, width = grad_rows.shape
    own = rows // ways

    def kernel(mine_ref, terms_ref, rows_ref, score_ref, router_ref, out_ref):
        total = rows_ref[...].astype(F32) + score_ref[...] * router_ref[...].astype(F32)
        for k in range(ways):
            total = total + terms_ref[k].astype(F32)
        for k in range(ways):
            out_ref[k] = total.astype(BF)

    def fixed(shape):
        return pl.BlockSpec(shape, lambda i, m: (0,) * len(shape))

    return pl.pallas_call(
        kernel,
        grid_spec=pltpu.PrefetchScalarGridSpec(
            num_scalar_prefetch=1,
            grid=(1,),
            in_specs=[
                fixed((ways, own, width)),
                pl.BlockSpec((own, width), lambda i, m: (m[0], 0)),
                fixed((own, 1)),
                fixed((1, width)),
            ],
            out_specs=fixed((ways, own, width)),
        ),
        out_shape=jax.ShapeDtypeStruct((ways, own, width), BF),
        cost_estimate=small_cost(),
        name="finish_input",
    )(mine, terms, grad_rows, score, router)


def split_kept(count, order):
    keys = [0]
    for bit in reversed(order):
        keys = keys + [k ^ bit for k in keys]
    return keys


def per_device(
    tokens,
    route_offset,
    unit_sequence,
    cotangent,
    router_weight,
    first_gain,
    second_gain,
    qkv_weight,
    out_weight,
    up_weight,
    down_weight,
):
    rows_local, width = tokens.shape
    routed = route_offset.shape[1]
    ways = lax.axis_size("tensor")
    copies = lax.axis_size("dp")
    mine = lax.axis_index("tensor")
    part = lax.axis_index("dp")
    mine_array = jnp.reshape(mine, (1,)).astype(jnp.int32)
    part_array = jnp.reshape(part, (1,)).astype(jnp.int32)
    ladder = [1 << b for b in range(1, copies.bit_length() - 1)]
    order_a = [1] + ladder
    order_b = [1] + ladder[::-1]
    keys_a = split_kept(copies, order_a)
    keys_b = split_kept(copies, order_b)

    tie = lax.optimization_barrier
    own_rows = routed // ways
    heads_width = out_weight.shape[0]
    hidden = up_weight.shape[1]
    by_swaps = copies == 8
    bit_x, bit_y = 2, 4

    quarter = part & 3
    piece_rows = heads_width // 4
    piece = lax.dynamic_slice_in_dim(out_weight, quarter * piece_rows, piece_rows, 0)
    here = to_all(jnp.broadcast_to(piece[None], (ways,) + piece.shape))

    weight_row = router_weight[None]
    picked, square = pick_rows(tokens, route_offset, weight_row, mine_array, ways, small_cost(), 60)
    seq_column = unit_sequence.reshape(routed, 1)
    here, picked, square, seq_column = tie((here, picked, square, seq_column))
    beside = swap(here, "dp", bit_x)
    first_low, qkv, probs, head_out, gating, routed_square = attend(
        picked, first_gain[None], qkv_weight, unit_sequence, seq_column, weight_row, ways
    )
    beside, here, head_out = tie((beside, here, head_out))

    heads = to_all(head_out)
    across = swap(jnp.stack([here, beside]), "dp", 1)
    cotangent, head_out = tie((cotangent, head_out))
    grad_rows = pick_rows(cotangent, route_offset, None, mine_array, ways, small_cost(), 24)[0]
    grad_mixer, grad_act = act_grads(grad_rows, gating, down_weight)
    heads, across, grad_act, grad_mixer = tie((heads, across, grad_act, grad_mixer))
    attended, second_low, activated, grad_pre, hidden_part, attended_part, second_gain_part, head_sent = feed_forward(
        heads, here, beside, across, picked, second_gain[None], up_weight, grad_act, grad_mixer, part_array
    )

    head_terms = to_all(head_sent)
    if by_swaps:
        kept, leave_a, leave_b = core_grads(
            activated, grad_mixer, second_low, grad_pre, heads, attended_part, part_array, keys_a, keys_b
        )
        got_a, got_b = swap(leave_a, "dp", 1), swap(leave_b, "dp", 1)
        activated, kept = tie((activated, kept))
    else:
        down_part = dot(activated, grad_mixer, TN).astype(BF)
        up_part = dot(second_low, grad_pre, TN).astype(BF)
        out_parts = jnp.stack([dot(heads[k], attended_part, TN).astype(BF) for k in range(ways)])
    mixer_part = dot(activated, down_weight, NN).astype(BF).reshape(ways, own_rows, width)
    head_terms, mixer_part = tie((head_terms, mixer_part))

    mixer_terms = to_all(mixer_part)
    grad_head = sum_heads(head_terms)
    wide = hidden // 2
    narrow = heads_width * ways // 4
    if by_swaps:
        got_a, got_b, grad_head = tie((got_a, got_b, grad_head))
        kept, leave_a, leave_b = halving_sums(kept, got_a, got_b, wide, narrow)
        got_a, got_b = swap(leave_a, "dp", bit_x), swap(leave_b, "dp", bit_y)
        grad_head, kept = tie((grad_head, kept))
    grad_projected, first_gain_part, input_part = attend_back(
        grad_head, qkv, probs, qkv_weight, picked, first_gain[None], hidden_part
    )
    qkv_part = qkv_part_of(first_low, grad_projected)
    input_part = input_part.reshape(ways, own_rows, width)
    if by_swaps:
        qkv_got = swap(qkv_part, "dp", 1)
        got_a, got_b, qkv_part, input_part = tie((got_a, got_b, qkv_part, input_part))
        kept, leave_a, leave_b = halving_sums(kept, got_a, got_b, wide // 2, narrow // 2)
        got_a, got_b = swap(leave_a, "dp", bit_y), swap(leave_b, "dp", bit_x)
        mixer_terms, input_part, kept = tie((mixer_terms, input_part, kept))
    else:
        mixer_terms, input_part = tie((mixer_terms, input_part))

    input_terms = to_all(input_part)
    new_own, grad_score, small = finish_rows(
        mixer_terms,
        picked,
        gating,
        attended,
        grad_rows,
        first_gain_part,
        second_gain_part,
        square,
        routed_square,
        mine_array,
        ways,
    )
    if by_swaps:
        got_a, got_b, qkv_got, new_own, grad_score, small = tie((got_a, got_b, qkv_got, new_own, grad_score, small))
        lane_a, lane_b, sent = owned_sums(
            kept, got_a, got_b, qkv_part, qkv_got, new_own, small, wide // 4, ways
        )
        got_a, got_b = swap(lane_a, "dp", bit_y), swap(lane_b, "dp", bit_x)
    else:
        sent = jnp.concatenate([new_own, split_sums(small)])
        sent = jnp.broadcast_to(sent[None], (ways,) + sent.shape)
    input_terms, sent = tie((input_terms, sent))

    fresh = to_all(sent)
    last = finish_input(input_terms, grad_rows, grad_score, weight_row, mine_array, ways)
    if by_swaps:
        got_a, got_b, last = tie((got_a, got_b, last))
        lane_a, lane_b = gather_sums(lane_a, got_a, lane_b, got_b, wide // 4)
        got_a, got_b = swap(lane_a, "dp", bit_x), swap(lane_b, "dp", bit_y)
        fresh, last, lane_a = tie((fresh, last, lane_a))
    else:
        fresh, last = tie((fresh, last))

    input_rows = to_all(last)
    spots = jnp.stack([mine ^ k for k in range(ways)]).astype(jnp.int32)
    if by_swaps:
        blocks = first_small(fresh, own_rows)
        other = swap(blocks, "dp", bit_x)
        fresh, blocks = tie((fresh, blocks))
    output = merge_rows(tokens, route_offset, fresh, spots)
    if by_swaps:

        def gathered(order):
            keys = [0]
            for bit in order:
                keys = keys + [k ^ bit for k in keys]
            return jnp.stack([part ^ k for k in keys]).astype(jnp.int32)

        got_a, got_b, other, output = tie((got_a, got_b, other, output))
        half_blocks = wide // 2
        down_near, up_near = gather_blocks(lane_a, got_a, lane_b, got_b, half_blocks)
        down_far, up_far = swap(down_near, "dp", 1), swap(up_near, "dp", 1)
        blocks = join_small(blocks, other)
        other = swap(blocks, "dp", bit_y)
        lane_a, down_near, up_near, blocks = tie((lane_a, down_near, up_near, blocks))
        qkv_grad = spread_qkv(lane_a, got_a, lane_b, got_b, 2 * (wide // 4), qkv_weight.shape[2])
        other, qkv_grad = tie((other, qkv_grad))
        blocks = join_small(blocks, other)
        other = swap(blocks, "dp", 1)
        cotangent, blocks = tie((cotangent, blocks))
    early = merge_rows(cotangent, route_offset, last, spots[:1])
    if by_swaps:
        other, down_far, up_far, early = tie((other, down_far, up_far, early))
        out_grad, small = last_small(blocks, other, gathered([bit_x, bit_y, 1]))
        each = hidden // copies

        def by_block(array):
            return array.reshape(-1, each, width)

        down_grad, up_grad = spread_rows(
            by_block(down_near),
            by_block(down_far),
            by_block(up_near),
            by_block(up_far),
            gathered([bit_y, bit_x, 1]),
            gathered([bit_x, bit_y, 1]),
        )
        input_rows, early, down_grad, up_grad, out_grad = tie((input_rows, early, down_grad, up_grad, out_grad))
    input_grad = merge_rows(cotangent, route_offset, input_rows, spots[1:], early)
    if not by_swaps:
        small = sum(joined_sums(fresh[k, own_rows:]) for k in range(ways))
        small = lax.psum(small, "dp")
        down_grad, up_grad, qkv_sum, out_sum = (
            lax.psum(v, "dp").astype(F32) for v in (down_part, up_part, qkv_part, out_parts)
        )
        out_grad = jnp.sum(to_all(out_sum.astype(BF)).astype(F32), axis=0)
        qkv_grad = qkv_sum.reshape(3, -1, width).transpose(0, 2, 1)
    score_stats = jnp.stack([small[3, 0] / (rows_local * copies), small[3, 1] / (routed * copies)])
    return (
        output,
        input_grad,
        small[0],
        small[1],
        small[2],
        qkv_grad,
        out_grad,
        up_grad,
        down_grad,
        score_stats,
    )


def solution(mesh):
    placed = (
        P("dp", None),
        P("dp", None),
        P("dp", None),
        P("dp", None),
        P(),
        P(),
        P(),
        P(None, None, "tensor"),
        P("tensor", None),
        P(None, "tensor"),
        P("tensor", None),
    )
    return jax.shard_map(
        per_device,
        mesh=mesh,
        in_specs=placed,
        out_specs=(
            P("dp", None),
            P("dp", None),
            P(),
            P(),
            P(),
            P(None, None, "tensor"),
            P("tensor", None),
            P(None, "tensor"),
            P("tensor", None),
            P(),
        ),
        check_vma=False,
    )
```

time: 471 us -> 276 us (0.59); the launches traced: 463 us -> 274 us
  waiting for transfers between devices: 280 us -> 71.3 us
  Pallas kernels: 0 us -> 108 us
  starting transfers between devices: 1.01 us -> 45.1 us
  matrix products: 44.5 us -> 2.25 us
  other arithmetic: 28.7 us -> 2.85 us
  blocking collectives: 25.6 us -> 0 us
  local copies, waits for them, and re-layouts: 67.2 us -> 42.2 us
  between operations: 15.9 us -> 2.29 us
    psum x4 -> x0, waiting for transfers between devices: 280 us -> none  [the longest x1 134 us: per_device(): lax.psum((qkv_part, out_part, up_part, down_part, first_gain_part, second...]
    pallas_call x0 -> x25, Pallas kernels: none -> 108 us  [the longest x3 20.8 us: merge_rows(): pl.pallas_call(kernel, grid_spec=grid_spec, out_shape=jax.ShapeDtypeStruc...]
    all_to_all x0 -> x7, waiting for transfers between devices: none -> 52 us  [to_all(): return lax.all_to_all(blocks, 'tensor', 0, 0, tiled=True)]
    dot_general x20 -> x1, matrix products: 44.5 us -> 2.25 us  [dot(): lax.dot_general(left, right, (dims, ((), ())), preferred_element_type=F32)]
    all_to_all x0 -> x7, starting transfers between devices: none -> 32.3 us  [to_all(): return lax.all_to_all(blocks, 'tensor', 0, 0, tiled=True)]
    psum x1 -> x0, blocking collectives: 25.6 us -> none  [per_device(): lax.psum((qkv_part, out_part, up_part, down_part, first_gain_part, second...]
    ppermute x0 -> x18, waiting for transfers between devices: none -> 19.4 us  [swap(): return lax.ppermute(values, axis, [(i, i ^ bits) for i in range(size)])]
    gather x3 -> x0, local copies, waits for them, and re-layouts: 18.3 us -> none  [the longest x1 7.93 us: per_device(): grad_rows = cotangent[positions].astype(jnp.float32)]
  transfers between devices with their start and end apart: 4 -> 25, of which waited for: 4 -> 12; matrix products, arithmetic and copies ran while one was open for 14% -> 3% of each run, Pallas kernels for 0% -> 32%
where the time goes in v2:
time: 276 us; the launch traced here: 274 us
  Pallas kernels  108 us (39%)
  waiting for transfers between devices  71.3 us (26%)
  starting transfers between devices  45.1 us (16%)
  local copies, waits for them, and re-layouts  42.2 us (15%)
  other arithmetic  2.85 us (1%)
    all_to_all x7, waiting for transfers between devices, to_all(): return lax.all_to_all(blocks, 'tensor', 0, 0, tiled=True)  52 us
    unnamed x112, local copies, waits for them, and re-layouts  37.5 us
    all_to_all x7, starting transfers between devices, to_all(): return lax.all_to_all(blocks, 'tensor', 0, 0, tiled=True)  32.3 us
    pallas_call x3, Pallas kernels, merge_rows(): pl.pallas_call(kernel, grid_spec=grid_spec, out_shape=jax.ShapeDtypeStruc...  20.8 us
    ppermute x18, waiting for transfers between devices, swap(): return lax.ppermute(values, axis, [(i, i ^ bits) for i in range(size)])  19.4 us
    ppermute x18, starting transfers between devices, swap(): return lax.ppermute(values, axis, [(i, i ^ bits) for i in range(size)])  12.8 us
    pallas_call x1, Pallas kernels, feed_forward(): pl.pallas_call(kernel, grid=(steps,), in_specs=[pl.BlockSpec(memory_space...  11.3 us
    pallas_call x2, Pallas kernels, pick_rows(): pl.pallas_call(body, in_specs=in_specs, out_specs=[whole] * len(out_shape...  9.79 us
  transfers between devices with their start and end apart: 25, of which 12 were waited for; matrix products, arithmetic and copies ran while one was open for 3% of the time, Pallas kernels for 32%

profile of v2, /device:TPU:0, one launch (start us, length us, event | category | flops | bytes accessed | tf_op | source)
XLA Modules:
  0.0 273.7 jit_solution(5699952904293354342)
XLA Ops:
  2.6 6.3 %all-to-all-start = ((bf16[4,64,1024]{2,1,0:T(8,128)(2,1)}), bf16[4,64,1024]{2,1,0:T(8,128)(2,1)S(1)}, u32[]{:S(2)}, u32[]{:S(2)}) async-start(bf16[4,64,1024]{2,1,0:T(8,128)(2,1)} %broadcast_in_dim.16), calls=%async_computation | async-start | bytes 1048576 | tf_op jit(solution)/shard_map/all_to_all | solution.py:26
  10.2 6.2 %pick_rows.2 = (bf16[512,1024]{1,0:T(8,128)(2,1)}, f32[1,128]{1,0:T(1,128)}) custom-call(s32[1]{0:T(128)} %bitcast.1.mine_ref.part_ref, bf16[4096,1024]{1,0:T(8,128)(2,1)} %base_ref.4, s32[1,512]{1,0:T(1,128)} %offset_ref.9, bf16[1,1024]{1,0:T(2,128)(2,1)} %broadcast_in_dim.17.weight_ref.router_ref), custom_call_target="tpu_custom_call" | custom-call | flops 1024 | bytes 1024 | tf_op jit(solution)/shard_map/pick_rows/pallas_call | solution.py:98
  16.4 7.0 %all-to-all-done.here_ref = bf16[4,64,1024]{2,1,0:T(8,128)(2,1)S(1)} async-done(((bf16[4,64,1024]{2,1,0:T(8,128)(2,1)}), bf16[4,64,1024]{2,1,0:T(8,128)(2,1)S(1)}, u32[]{:S(2)}, u32[]{:S(2)}) %all-to-all-start) | async-done | bytes 524320 | tf_op jit(solution)/shard_map/all_to_all | solution.py:26
  26.3 3.7 %attend.1 = (bf16[512,1024]{1,0:T(8,128)(2,1)S(1)}, bf16[3,512,256]{2,1,0:T(8,128)(2,1)S(1)}, bf16[4,512,512]{2,1,0:T(8,128)(2,1)S(1)}, bf16[4,512,256]{2,1,0:T(...) custom-call(bf16[512,1024]{1,0:T(8,128)(2,1)S(1)} %copy-done.3, ...), custom_call_target="tpu_custom_call" | custom-call | flops 1024 | bytes 15000000 | tf_op jit(solution)/shard_map/attend/pallas_call | solution.py:192
  36.3 3.8 %all-to-all-start.1 = ((bf16[4,512,256]{2,1,0:T(8,128)(2,1)}), bf16[4,512,256]{2,1,0:T(8,128)(2,1)S(1)}, u32[]{:S(2)}, u32[]{:S(2)}) async-start(bf16[4,512,256]{2,1,0:T(8,128)(2,1)} %copy-done.29), calls=%async_computation.1 | async-start | bytes 2097152 | tf_op jit(solution)/shard_map/all_to_all | solution.py:26
  41.2 3.4 %copy-done.2 = bf16[4096,1024]{1,0:T(8,128)(2,1)S(1)} copy-done((bf16[4096,1024]{1,0:T(8,128)(2,1)S(1)}, bf16[4096,1024]{1,0:T(8,128)(2,1)}, u32[]{:S(2)}) %copy-start.2) | copy-done | bytes 8388632
  44.6 3.6 %pick_rows.3.rows_ref = bf16[512,1024]{1,0:T(8,128)(2,1)S(1)} custom-call(s32[1]{0:T(128)} %bitcast.1.mine_ref.part_ref, bf16[4096,1024]{1,0:T(8,128)(2,1)S(1)} %copy-done.2, s32[1,512]{1,0:T(1,128)S(1)} %copy-done.42), custom_call_target="tpu_custom_call" | custom-call | flops 1024 | bytes 1024 | tf_op jit(solution)/shard_map/pick_rows/pallas_call | solution.py:98
  49.2 4.7 %act_grads.1 = (bf16[512,1024]{1,0:T(8,128)(2,1)}, f32[512,1024]{1,0:T(8,128)}) custom-call(bf16[512,1024]{1,0:T(8,128)(2,1)} %copy-done.5, f32[512,1]{1,0:T(8,128)} %copy-done.34, bf16[1024,1024]{1,0:T(8,128)(2,1)} %down_ref.1), custom_call_target="tpu_custom_call" | custom-call | flops 1024 | bytes 1024 | tf_op jit(solution)/shard_map/act_grads/pallas_call | solution.py:346
  53.9 10.3 %all-to-all-done.1.heads_ref = bf16[4,512,256]{2,1,0:T(8,128)(2,1)S(1)} async-done(((bf16[4,512,256]{2,1,0:T(8,128)(2,1)}), bf16[4,512,256]{2,1,0:T(8,128)(2,1)S(1)}, u32[]{:S(2)}, u32[]{:S(2)}) %all-to-all-start.1) | async-done | bytes 1048608 | tf_op jit(solution)/shard_map/all_to_all | solution.py:26
  65.2 11.3 %feed_forward.1 = (f32[512,1024]{1,0:T(8,128)}, bf16[512,1024]{1,0:T(8,128)(2,1)S(1)}, bf16[512,1024]{1,0:T(8,128)(2,1)S(1)}, bf16[512,1024]{1,0:T(8,128)(2,1)S(...) custom-call(s32[1]{0:T(128)} %bitcast.part_ref, ...), custom_call_target="tpu_custom_call" | custom-call | flops 1024 | bytes 1024 | tf_op jit(solution)/shard_map/feed_forward/pallas_call | solution.py:292
  80.9 4.6 %all-to-all-start.2 = ((bf16[4,512,256]{2,1,0:T(8,128)(2,1)}), bf16[4,512,256]{2,1,0:T(8,128)(2,1)}, u32[]{:S(2)}, u32[]{:S(2)}) async-start(bf16[4,512,256]{2,1,0:T(8,128)(2,1)} %get-tuple-element.136), calls=%async_computation.2 | async-start | bytes 2097152 | tf_op jit(solution)/shard_map/all_to_all | solution.py:26
  90.5 4.8 %core_grads.1 = (bf16[2,768,1024]{2,1,0:T(8,128)(2,1)S(1)}, bf16[768,1024]{1,0:T(8,128)(2,1)}, bf16[768,1024]{1,0:T(8,128)(2,1)}) custom-call(s32[1]{0:T(128)} %bitcast.part_ref, bf16[512,1024]{1,0:T(8,128)(2,1)S(1)} %copy-done.21, bf16[512,1024]{1,0:T(8,128)(2,1)S(1)} %copy-done.14, bf16[512,1024]{1,0:T(8,128)(2,1)S(1)} %copy-done.23, ...), custom_call_target="tpu_custom_call" | custom-call | flops 1024 | bytes 1024 | tf_op jit(solution)/shard_map/core_grads/pallas_call | solution.py:550
  95.3 1.7 copy-done.15
  97.5 2.2 convolution_convert_fusion
  99.7 10.9 %all-to-all-done.2.terms_ref = bf16[4,512,256]{2,1,0:T(8,128)(2,1)} async-done(((bf16[4,512,256]{2,1,0:T(8,128)(2,1)}), bf16[4,512,256]{2,1,0:T(8,128)(2,1)}, u32[]{:S(2)}, u32[]{:S(2)}) %all-to-all-start.2) | async-done | bytes 1048608 | tf_op jit(solution)/shard_map/all_to_all | solution.py:26
  110.6 4.3 %all-to-all-start.3 = ((bf16[4,128,1024]{2,1,0:T(8,128)(2,1)}), bf16[4,128,1024]{2,1,0:T(8,128)(2,1)}, u32[]{:S(2)}, u32[]{:S(2)}) async-start(bf16[4,128,1024]{2,1,0:T(8,128)(2,1)} %bitcast.5), calls=%async_computation.3 | async-start | bytes 2097152 | tf_op jit(solution)/shard_map/all_to_all | solution.py:26
  114.9 2.2 sum_heads.1.head_ref
  118.2 1.9 copy-done.16
  121.5 3.0 %halving_sums.2 = (bf16[2,384,1024]{2,1,0:T(8,128)(2,1)S(1)}, bf16[384,1024]{1,0:T(8,128)(2,1)}, bf16[384,1024]{1,0:T(8,128)(2,1)}) custom-call(bf16[2,768,1024]{2,1,0:T(8,128)(2,1)S(1)} %copy-done.16, bf16[768,1024]{1,0:T(8,128)(2,1)S(1)} %copy-done.19, bf16[768,1024]{1,0:T(8,128)(2,1)} %collective-permute-done.3.b_got), custom_call_target="tpu_custom_call" | custom-call | flops 1024 | bytes 1024 | tf_op jit(solution)/shard_map/halving_sums/pallas_call | solution.py:580
  124.5 1.5 collective-permute-start.4
  126.0 1.5 collective-permute-start.5
  127.5 7.4 %attend_back.1 = (bf16[3,512,256]{2,1,0:T(8,128)(2,1)S(1)}, f32[1,1024]{1,0:T(1,128)S(1)}, bf16[512,1024]{1,0:T(8,128)(2,1)}) custom-call(bf16[512,256]{1,0:T(8,128)(2,1)S(1)} %copy-done.27, bf16[3,512,256]{2,1,0:T(8,128)(2,1)S(1)} %copy-done.38, bf16[4,512,512]{2,1,0:T(8,128)(2,1)} %copy-done.17, bf16[3,1024,256]{2,1,0:T(8,128)(2,1)} %weight_ref.3, ...), custom_call_target="tpu_custom_call" | custom-call | flops 1024 | bytes 1024 | tf_op jit(solution)/shard_map/attend_back/pallas_call | solution.py:418
  135.8 3.6 %qkv_part.1.qkv_ref = bf16[768,1024]{1,0:T(8,128)(2,1)} custom-call(bf16[512,1024]{1,0:T(8,128)(2,1)} %copy-done.28, bf16[3,512,256]{2,1,0:T(8,128)(2,1)} %copy-done.39), custom_call_target="tpu_custom_call" | custom-call | flops 1024 | bytes 1024 | tf_op jit(solution)/shard_map/qkv_part/pallas_call | solution.py:482
  139.4 3.9 %collective-permute-done.4.a_got = bf16[384,1024]{1,0:T(8,128)(2,1)} collective-permute-done((bf16[384,1024]{1,0:T(8,128)(2,1)}, bf16[384,1024]{1,0:T(8,128)(2,1)}, u32[]{:S(2)}, u32[]{:S(2)}) %collective-permute-start.4) | collective-permute-done | bytes 786464 | tf_op jit(solution)/shard_map/ppermute | solution.py:22
  144.5 1.7 halving_sums.3
  147.1 4.8 %all-to-all-start.4 = ((bf16[4,128,1024]{2,1,0:T(8,128)(2,1)}), bf16[4,128,1024]{2,1,0:T(8,128)(2,1)}, u32[]{:S(2)}, u32[]{:S(2)}) async-start(bf16[4,128,1024]{2,1,0:T(8,128)(2,1)} %bitcast.6), calls=%async_computation.4 | async-start | bytes 2097152 | tf_op jit(solution)/shard_map/all_to_all | solution.py:26
  151.9 1.5 collective-permute-start.6
  153.9 2.8 %finish_rows.1 = (bf16[128,1024]{1,0:T(8,128)(2,1)}, f32[128,1]{1,0:T(8,128)}, f32[4,1024]{1,0:T(4,128)}) custom-call(s32[1]{0:T(128)} %bitcast.1.mine_ref.part_ref, bf16[4,128,1024]{2,1,0:T(8,128)(2,1)} %all-to-all-done.3.terms_ref, bf16[512,1024]{1,0:T(8,128)(2,1)} %get-tuple-element.122.picked_ref, f32[512,1]{1,0:T(8,128)} %copy-done.34, ...), custom_call_target="tpu_custom_call" | custom-call | flops 1024 | bytes 30000000 | tf_op jit(solution)/shard_map/finish_rows/pallas_call | solution.py:811
  156.7 3.9 %collective-permute-done.6.a_got = bf16[192,1024]{1,0:T(8,128)(2,1)S(1)} collective-permute-done((bf16[192,1024]{1,0:T(8,128)(2,1)S(1)}, bf16[192,1024]{1,0:T(8,128)(2,1)S(1)}, u32[]{:S(2)}, u32[]{:S(2)}) %collective-permute-start.6) | collective-permute-done | bytes 393248 | tf_op jit(solution)/shard_map/ppermute | solution.py:22
  164.6 3.2 %owned_sums.1 = (bf16[512,1024]{1,0:T(8,128)(2,1)S(1)}, bf16[512,1024]{1,0:T(8,128)(2,1)}, bf16[4,176,1024]{2,1,0:T(8,128)(2,1)}) custom-call(bf16[2,192,1024]{2,1,0:T(8,128)(2,1)S(1)} %copy-done.36, bf16[192,1024]{1,0:T(8,128)(2,1)S(1)} %collective-permute-done.6.a_got, bf16[192,1024]{1,0:T(8,128)(2,1)S(1)} %collective-permute-done.7.b_got, ...), custom_call_target="tpu_custom_call" | custom-call | flops 1024 | bytes 1024 | tf_op jit(solution)/shard_map/owned_sums/pallas_call | solution.py:618
  169.0 6.5 %all-to-all-done.4.terms_ref = bf16[4,128,1024]{2,1,0:T(8,128)(2,1)} async-done(((bf16[4,128,1024]{2,1,0:T(8,128)(2,1)}), bf16[4,128,1024]{2,1,0:T(8,128)(2,1)}, u32[]{:S(2)}, u32[]{:S(2)}) %all-to-all-start.4) | async-done | bytes 1048608 | tf_op jit(solution)/shard_map/all_to_all | solution.py:26
  175.5 4.3 %all-to-all-start.5 = ((bf16[4,176,1024]{2,1,0:T(8,128)(2,1)}), bf16[4,176,1024]{2,1,0:T(8,128)(2,1)}, u32[]{:S(2)}, u32[]{:S(2)}) async-start(bf16[4,176,1024]{2,1,0:T(8,128)(2,1)} %get-tuple-element.194), calls=%async_computation.5 | async-start | bytes 2883584 | tf_op jit(solution)/shard_map/all_to_all | solution.py:26
  179.8 2.6 finish_input.1.piece_ref
  182.4 7.2 %collective-permute-done.9.a_got = bf16[512,1024]{1,0:T(8,128)(2,1)S(1)} collective-permute-done((bf16[512,1024]{1,0:T(8,128)(2,1)S(1)}, bf16[512,1024]{1,0:T(8,128)(2,1)S(1)}, u32[]{:S(2)}, u32[]{:S(2)}) %collective-permute-start.9) | collective-permute-done | bytes 1048608 | tf_op jit(solution)/shard_map/ppermute | solution.py:22
  191.4 2.8 %gather_sums.1 = (bf16[640,1024]{1,0:T(8,128)(2,1)S(1)}, bf16[640,1024]{1,0:T(8,128)(2,1)}) custom-call(bf16[512,1024]{1,0:T(8,128)(2,1)S(1)} %copy-done.33, bf16[512,1024]{1,0:T(8,128)(2,1)S(1)} %collective-permute-done.9.a_got, bf16[512,1024]{1,0:T(8,128)(2,1)} %get-tuple-element.185.b_ref, bf16[512,1024]{1,0:T(8,128)(2,1)} %collective-permute-done.10.b_got), custom_call_target="tpu_custom_call" | custom-call | flops 1024 | bytes 1024 | tf_op jit(solution)/shard_map/gather_sums/pallas_call | solution.py:640
  196.2 17.3 %all-to-all-done.5.got_ref.piece_ref = bf16[4,176,1024]{2,1,0:T(8,128)(2,1)} async-done(((bf16[4,176,1024]{2,1,0:T(8,128)(2,1)}), bf16[4,176,1024]{2,1,0:T(8,128)(2,1)}, u32[]{:S(2)}, u32[]{:S(2)}) %all-to-all-start.5) | async-done | bytes 1441824 | tf_op jit(solution)/shard_map/all_to_all | solution.py:26
  213.5 4.2 %all-to-all-start.6 = ((bf16[4,128,1024]{2,1,0:T(8,128)(2,1)}), bf16[4,128,1024]{2,1,0:T(8,128)(2,1)}, u32[]{:S(2)}, u32[]{:S(2)}) async-start(bf16[4,128,1024]{2,1,0:T(8,128)(2,1)} %finish_input.1.piece_ref), calls=%async_computation.6 | async-start | bytes 2097152 | tf_op jit(solution)/shard_map/all_to_all | solution.py:26
  217.8 2.1 first_small.1.mine_ref
  221.0 8.9 %merge_rows.3 = bf16[4096,1024]{1,0:T(8,128)(2,1)} custom-call(s32[4]{0:T(128)} %pad_add_fusion.part_ref, bf16[4096,1024]{1,0:T(8,128)(2,1)} %base_ref.4, s32[1,512]{1,0:T(1,128)} %offset_ref.9, bf16[4,176,1024]{2,1,0:T(8,128)(2,1)} %all-to-all-done.5.got_ref.piece_ref), custom_call_target="tpu_custom_call" | custom-call | flops 1024 | bytes 1024 | tf_op jit(solution)/shard_map/merge_rows/pallas_call | solution.py:143
  231.0 2.9 %gather_blocks.1 = (bf16[512,1024]{1,0:T(8,128)(2,1)}, bf16[512,1024]{1,0:T(8,128)(2,1)}) custom-call(bf16[640,1024]{1,0:T(8,128)(2,1)} %copy-done.10, bf16[640,1024]{1,0:T(8,128)(2,1)} %copy-done.12, bf16[640,1024]{1,0:T(8,128)(2,1)} %get-tuple-element.193.b_ref, bf16[640,1024]{1,0:T(8,128)(2,1)} %collective-permute-done.12.b_got), custom_call_target="tpu_custom_call" | custom-call | flops 1024 | bytes 1024 | tf_op jit(solution)/shard_map/gather_blocks/pallas_call | solution.py:663
  234.4 1.6 join_small.2.mine_ref
  236.1 1.5 collective-permute-start.14
  238.9 4.3 %spread_qkv.1 = f32[3,1024,256]{2,1,0:T(8,128)} custom-call(bf16[640,1024]{1,0:T(8,128)(2,1)S(1)} %copy-done.11, bf16[640,1024]{1,0:T(8,128)(2,1)S(1)} %copy-done.13, bf16[640,1024]{1,0:T(8,128)(2,1)} %get-tuple-element.193.b_ref, bf16[640,1024]{1,0:T(8,128)(2,1)} %collective-permute-done.12.b_got), custom_call_target="tpu_custom_call" | custom-call | flops 1024 | bytes 1024 | tf_op jit(solution)/shard_map/spread_qkv/pallas_call | solution.py:506
  243.8 1.7 join_small.3.mine_ref
  247.5 3.6 %merge_rows.4.rest_0_ = bf16[4096,1024]{1,0:T(8,128)(2,1)} custom-call(s32[1]{0:T(128)} %bitcast.1.mine_ref.part_ref, bf16[4096,1024]{1,0:T(8,128)(2,1)} %base_ref.6, s32[1,512]{1,0:T(1,128)} %offset_ref.9, bf16[4,128,1024]{2,1,0:T(8,128)(2,1)} %finish_input.1.piece_ref), custom_call_target="tpu_custom_call" | custom-call | flops 1024 | bytes 1024 | tf_op jit(solution)/shard_map/merge_rows/pallas_call | solution.py:143
  251.8 2.1 last_small.1
  253.9 8.4 %spread_rows.1 = (f32[1024,1024]{1,0:T(8,128)}, f32[1024,1024]{1,0:T(8,128)}) custom-call(s32[8]{0:T(128)} %stack.93.down_index, s32[8]{0:T(128)} %stack.94.up_index.index_ref, bf16[4,128,1024]{2,1,0:T(8,128)(2,1)} %bitcast.31, bf16[4,128,1024]{2,1,0:T(8,128)(2,1)} %bitcast.33, bf16[4,128,1024]{2,1,0:T(8,128)(2,1)} %bitcast.32, ...), custom_call_target="tpu_custom_call" | custom-call | flops 1024 | bytes 1024 | tf_op jit(solution)/shard_map/spread_rows/pallas_call | solution.py:455
  265.4 8.3 %merge_rows.5 = bf16[4096,1024]{1,0:T(8,128)(2,1)} custom-call(s32[3]{0:T(128)} %pad_add_fusion.1.part_ref, bf16[4096,1024]{1,0:T(8,128)(2,1)} %base_ref.6, s32[1,512]{1,0:T(1,128)} %offset_ref.9, bf16[4,128,1024]{2,1,0:T(8,128)(2,1)} %all-to-all-done.6.piece_ref, bf16[4096,1024]{1,0:T(8,128)(2,1)} %merge_rows.4.rest_0_), custom_call_target="tpu_custom_call", output_to_operand_aliasing={{}: (4, {})} | custom-call | flops 1024 | bytes 1024 | tf_op jit(solution)/shard_map/merge_rows/pallas_call | solution.py:143
  (154 shorter events, 49.3 us)
Async XLA Ops:
  2.6 20.8 %all-to-all-start = ((bf16[4,64,1024]{2,1,0:T(8,128)(2,1)}), bf16[4,64,1024]{2,1,0:T(8,128)(2,1)S(1)}, u32[]{:S(2)}, u32[]{:S(2)}) async-start(bf16[4,64,1024]{2,1,0:T(8,128)(2,1)} %broadcast_in_dim.16), calls=%async_computation | async-start | bytes 1048576 | tf_op jit(solution)/shard_map/all_to_all | solution.py:26
  10.2 14.7 %copy-start.54 = (bf16[1024]{0:T(1024)(128)(2,1)S(1)}, bf16[1024]{0:T(1024)(128)(2,1)}, u32[]{:S(2)}) copy-start(bf16[1024]{0:T(1024)(128)(2,1)} %param.16) | copy-start | bytes 6148
  10.2 14.7 %copy-start.44 = (s32[1,512]{1,0:T(1,128)S(1)}, s32[1,512]{1,0:T(1,128)}, u32[]{:S(2)}) copy-start(s32[1,512]{1,0:T(1,128)} %row_ref.1) | copy-start | bytes 6148
  10.2 14.9 %copy-start.9 = (bf16[3,1024,256]{2,1,0:T(8,128)(2,1)S(1)}, bf16[3,1024,256]{2,1,0:T(8,128)(2,1)}, u32[]{:S(2)}) copy-start(bf16[3,1024,256]{2,1,0:T(8,128)(2,1)} %weight_ref.3) | copy-start | bytes 4718596
  10.2 14.9 %copy-start.41 = (bf16[1,1024]{1,0:T(2,128)(2,1)S(1)}, bf16[1,1024]{1,0:T(2,128)(2,1)}, u32[]{:S(2)}) copy-start(bf16[1,1024]{1,0:T(2,128)(2,1)} %broadcast_in_dim.17.weight_ref.router_ref) | copy-start | bytes 6148
  23.4 12.9 %collective-permute-start = (bf16[4,64,1024]{2,1,0:T(8,128)(2,1)S(1)}, bf16[4,64,1024]{2,1,0:T(8,128)(2,1)S(1)}, u32[]{:S(2)}, u32[]{:S(2)}) collective-permute-start(bf16[4,64,1024]{2,1,0:T(8,128)(2,1)S(1)} %all-to-all-done.here_ref), channel_id=1, source_target_pairs={{0,8},{4,12},{8,0},{12,4},{16,24},{20,28},{24,16},{28,20},{1,9},{5... | collective-permute-start | bytes 1572872 | tf_op jit(solution)/shard_map/ppermute | solution.py:22
  34.9 6.3 %copy-start.47 = (f32[1,128]{1,0:T(1,128)}, f32[1,128]{1,0:T(1,128)S(1)}, u32[]{:S(2)}) copy-start(f32[1,128]{1,0:T(1,128)S(1)} %get-tuple-element.174.routed_ref) | copy-start | bytes 1540
  36.3 4.9 %copy-start.55 = (bf16[1024]{0:T(1024)(128)(2,1)S(1)}, bf16[1024]{0:T(1024)(128)(2,1)}, u32[]{:S(2)}) copy-start(bf16[1024]{0:T(1024)(128)(2,1)} %param.17) | copy-start | bytes 6148
  36.3 4.9 %copy-start.42 = (s32[1,512]{1,0:T(1,128)S(1)}, s32[1,512]{1,0:T(1,128)}, u32[]{:S(2)}) copy-start(s32[1,512]{1,0:T(1,128)} %offset_ref.9) | copy-start | bytes 6148
  36.3 27.9 %all-to-all-start.1 = ((bf16[4,512,256]{2,1,0:T(8,128)(2,1)}), bf16[4,512,256]{2,1,0:T(8,128)(2,1)S(1)}, u32[]{:S(2)}, u32[]{:S(2)}) async-start(bf16[4,512,256]{2,1,0:T(8,128)(2,1)} %copy-done.29), calls=%async_computation.1 | async-start | bytes 2097152 | tf_op jit(solution)/shard_map/all_to_all | solution.py:26
  41.2 12.7 %collective-permute-start.1 = (bf16[2,4,64,1024]{3,2,1,0:T(8,128)(2,1)}, bf16[2,4,64,1024]{3,2,1,0:T(8,128)(2,1)}, u32[]{:S(2)}, u32[]{:S(2)}) collective-permute-start(bf16[2,4,64,1024]{3,2,1,0:T(8,128)(2,1)} %pad_maximum_fusion), channel_id=1, source_target_pairs={{0,4},{4,0},{8,12},{12,8},{16,20},{20,16},{24,28},{28,24},{1,5},{5... | collective-permute-start | bytes 3145736 | tf_op jit(solution)/shard_map/ppermute | solution.py:22
  41.2 3.4 %copy-start.2 = (bf16[4096,1024]{1,0:T(8,128)(2,1)S(1)}, bf16[4096,1024]{1,0:T(8,128)(2,1)}, u32[]{:S(2)}) copy-start(bf16[4096,1024]{1,0:T(8,128)(2,1)} %base_ref.6) | copy-start | bytes 25165828
  80.9 4.6 %copy-start.7 = (bf16[4,512,256]{2,1,0:T(8,128)(2,1)S(1)}, bf16[4,512,256]{2,1,0:T(8,128)(2,1)}, u32[]{:S(2)}) copy-start(bf16[4,512,256]{2,1,0:T(8,128)(2,1)} %copy-done.6) | copy-start | bytes 3145732
  80.9 4.6 %copy-start.14 = (bf16[512,1024]{1,0:T(8,128)(2,1)S(1)}, bf16[512,1024]{1,0:T(8,128)(2,1)}, u32[]{:S(2)}) copy-start(bf16[512,1024]{1,0:T(8,128)(2,1)} %get-tuple-element.135.mixer_ref) | copy-start | bytes 3145732
  80.9 29.7 %all-to-all-start.2 = ((bf16[4,512,256]{2,1,0:T(8,128)(2,1)}), bf16[4,512,256]{2,1,0:T(8,128)(2,1)}, u32[]{:S(2)}, u32[]{:S(2)}) async-start(bf16[4,512,256]{2,1,0:T(8,128)(2,1)} %get-tuple-element.136), calls=%async_computation.2 | async-start | bytes 2097152 | tf_op jit(solution)/shard_map/all_to_all | solution.py:26
  90.5 7.0 %copy-start.48 = (bf16[1024,1024]{1,0:T(8,128)(2,1)S(1)}, bf16[1024,1024]{1,0:T(8,128)(2,1)}, u32[]{:S(2)}) copy-start(bf16[1024,1024]{1,0:T(8,128)(2,1)} %down_ref.1) | copy-start | bytes 6291460
  97.0 20.0 %collective-permute-start.2 = (bf16[768,1024]{1,0:T(8,128)(2,1)}, bf16[768,1024]{1,0:T(8,128)(2,1)S(1)}, u32[]{:S(2)}, u32[]{:S(2)}) collective-permute-start(bf16[768,1024]{1,0:T(8,128)(2,1)} %get-tuple-element.145), channel_id=1, source_target_pairs={{0,4},{4,0},{8,12},{12,8},{16,20},{20,16},{24,28},{28,24},{1,5},{5... | collective-permute-start | bytes 4718600 | tf_op jit(solution)/shard_map/ppermute | solution.py:22
  97.0 21.2 %collective-permute-start.3 = (bf16[768,1024]{1,0:T(8,128)(2,1)}, bf16[768,1024]{1,0:T(8,128)(2,1)}, u32[]{:S(2)}, u32[]{:S(2)}) collective-permute-start(bf16[768,1024]{1,0:T(8,128)(2,1)} %get-tuple-element.146), channel_id=1, source_target_pairs={{0,4},{4,0},{8,12},{12,8},{16,20},{20,16},{24,28},{28,24},{1,5},{5... | collective-permute-start | bytes 4718600 | tf_op jit(solution)/shard_map/ppermute | solution.py:22
  110.6 36.5 %all-to-all-start.3 = ((bf16[4,128,1024]{2,1,0:T(8,128)(2,1)}), bf16[4,128,1024]{2,1,0:T(8,128)(2,1)}, u32[]{:S(2)}, u32[]{:S(2)}) async-start(bf16[4,128,1024]{2,1,0:T(8,128)(2,1)} %bitcast.5), calls=%async_computation.3 | async-start | bytes 2097152 | tf_op jit(solution)/shard_map/all_to_all | solution.py:26
  114.9 12.6 %copy-start.31 = (bf16[512,1024]{1,0:T(8,128)(2,1)S(1)}, bf16[512,1024]{1,0:T(8,128)(2,1)}, u32[]{:S(2)}) copy-start(bf16[512,1024]{1,0:T(8,128)(2,1)} %copy-done.30) | copy-start | bytes 3145732
  117.0 10.5 %copy-start.4 = (bf16[512,1024]{1,0:T(8,128)(2,1)S(1)}, bf16[512,1024]{1,0:T(8,128)(2,1)}, u32[]{:S(2)}) copy-start(bf16[512,1024]{1,0:T(8,128)(2,1)} %get-tuple-element.122.picked_ref) | copy-start | bytes 3145732
  121.5 6.0 %copy-start.27 = (bf16[512,256]{1,0:T(8,128)(2,1)S(1)}, bf16[512,256]{1,0:T(8,128)(2,1)}, u32[]{:S(2)}) copy-start(bf16[512,256]{1,0:T(8,128)(2,1)} %sum_heads.1.head_ref) | copy-start | bytes 786436
  121.5 6.0 %copy-start.38 = (bf16[3,512,256]{2,1,0:T(8,128)(2,1)S(1)}, bf16[3,512,256]{2,1,0:T(8,128)(2,1)}, u32[]{:S(2)}) copy-start(bf16[3,512,256]{2,1,0:T(8,128)(2,1)} %copy-done.37) | copy-start | bytes 2359300
  124.5 18.8 %collective-permute-start.4 = (bf16[384,1024]{1,0:T(8,128)(2,1)}, bf16[384,1024]{1,0:T(8,128)(2,1)}, u32[]{:S(2)}, u32[]{:S(2)}) collective-permute-start(bf16[384,1024]{1,0:T(8,128)(2,1)} %get-tuple-element.150), channel_id=1, source_target_pairs={{0,8},{4,12},{8,0},{12,4},{16,24},{20,28},{24,16},{28,20},{1,9},{5... | collective-permute-start | bytes 2359304 | tf_op jit(solution)/shard_map/ppermute | solution.py:22
  126.0 18.5 %collective-permute-start.5 = (bf16[384,1024]{1,0:T(8,128)(2,1)}, bf16[384,1024]{1,0:T(8,128)(2,1)}, u32[]{:S(2)}, u32[]{:S(2)}) collective-permute-start(bf16[384,1024]{1,0:T(8,128)(2,1)} %get-tuple-element.151), channel_id=1, source_target_pairs={{0,16},{4,20},{8,24},{12,28},{16,0},{20,4},{24,8},{28,12},{1,17},{... | collective-permute-start | bytes 2359304 | tf_op jit(solution)/shard_map/ppermute | solution.py:22
  135.8 8.7 %copy-start.46 = (f32[1,1024]{1,0:T(1,128)}, f32[1,1024]{1,0:T(1,128)S(1)}, u32[]{:S(2)}) copy-start(f32[1,1024]{1,0:T(1,128)S(1)} %get-tuple-element.171.one_ref) | copy-start | bytes 12292
  139.4 22.4 %collective-permute-start.8 = (bf16[768,1024]{1,0:T(8,128)(2,1)}, bf16[768,1024]{1,0:T(8,128)(2,1)}, u32[]{:S(2)}, u32[]{:S(2)}) collective-permute-start(bf16[768,1024]{1,0:T(8,128)(2,1)} %qkv_part.1.qkv_ref), channel_id=1, source_target_pairs={{0,4},{4,0},{8,12},{12,8},{16,20},{20,16},{24,28},{28,24},{1,5},{5... | collective-permute-start | bytes 4718600 | tf_op jit(solution)/shard_map/ppermute | solution.py:22
  147.1 28.3 %all-to-all-start.4 = ((bf16[4,128,1024]{2,1,0:T(8,128)(2,1)}), bf16[4,128,1024]{2,1,0:T(8,128)(2,1)}, u32[]{:S(2)}, u32[]{:S(2)}) async-start(bf16[4,128,1024]{2,1,0:T(8,128)(2,1)} %bitcast.6), calls=%async_computation.4 | async-start | bytes 2097152 | tf_op jit(solution)/shard_map/all_to_all | solution.py:26
  151.9 8.7 %collective-permute-start.6 = (bf16[192,1024]{1,0:T(8,128)(2,1)S(1)}, bf16[192,1024]{1,0:T(8,128)(2,1)S(1)}, u32[]{:S(2)}, u32[]{:S(2)}) collective-permute-start(bf16[192,1024]{1,0:T(8,128)(2,1)S(1)} %get-tuple-element.167), channel_id=1, source_target_pairs={{0,16},{4,20},{8,24},{12,28},{16,0},{20,4},{24,8},{28,12},{1,17},{... | collective-permute-start | bytes 1179656 | tf_op jit(solution)/shard_map/ppermute | solution.py:22
  153.4 8.4 %collective-permute-start.7 = (bf16[192,1024]{1,0:T(8,128)(2,1)S(1)}, bf16[192,1024]{1,0:T(8,128)(2,1)S(1)}, u32[]{:S(2)}, u32[]{:S(2)}) collective-permute-start(bf16[192,1024]{1,0:T(8,128)(2,1)S(1)} %get-tuple-element.168), channel_id=1, source_target_pairs={{0,8},{4,12},{8,0},{12,4},{16,24},{20,28},{24,16},{28,20},{1,9},{5... | collective-permute-start | bytes 1179656 | tf_op jit(solution)/shard_map/ppermute | solution.py:22
  153.9 7.9 %copy-start.8 = (bf16[768,1024]{1,0:T(8,128)(2,1)S(1)}, bf16[768,1024]{1,0:T(8,128)(2,1)}, u32[]{:S(2)}) copy-start(bf16[768,1024]{1,0:T(8,128)(2,1)} %qkv_part.1.qkv_ref) | copy-start | bytes 4718596
  167.9 14.5 %copy-start.32 = (bf16[512,1024]{1,0:T(8,128)(2,1)}, bf16[512,1024]{1,0:T(8,128)(2,1)S(1)}, u32[]{:S(2)}) copy-start(bf16[512,1024]{1,0:T(8,128)(2,1)S(1)} %get-tuple-element.184.a_ref) | copy-start | bytes 3145732
  167.9 21.6 %collective-permute-start.9 = (bf16[512,1024]{1,0:T(8,128)(2,1)S(1)}, bf16[512,1024]{1,0:T(8,128)(2,1)S(1)}, u32[]{:S(2)}, u32[]{:S(2)}) collective-permute-start(bf16[512,1024]{1,0:T(8,128)(2,1)S(1)} %get-tuple-element.184.a_ref), channel_id=1, source_target_pairs={{0,16},{4,20},{8,24},{12,28},{16,0},{20,4},{24,8},{28,12},{1,17},{... | collective-permute-start | bytes 3145736 | tf_op jit(solution)/shard_map/ppermute | solution.py:22
  168.4 21.7 %collective-permute-start.10 = (bf16[512,1024]{1,0:T(8,128)(2,1)}, bf16[512,1024]{1,0:T(8,128)(2,1)}, u32[]{:S(2)}, u32[]{:S(2)}) collective-permute-start(bf16[512,1024]{1,0:T(8,128)(2,1)} %get-tuple-element.185.b_ref), channel_id=1, source_target_pairs={{0,8},{4,12},{8,0},{12,4},{16,24},{20,28},{24,16},{28,20},{1,9},{5... | collective-permute-start | bytes 3145736 | tf_op jit(solution)/shard_map/ppermute | solution.py:22
  175.5 38.0 %all-to-all-start.5 = ((bf16[4,176,1024]{2,1,0:T(8,128)(2,1)}), bf16[4,176,1024]{2,1,0:T(8,128)(2,1)}, u32[]{:S(2)}, u32[]{:S(2)}) async-start(bf16[4,176,1024]{2,1,0:T(8,128)(2,1)} %get-tuple-element.194), calls=%async_computation.5 | async-start | bytes 2883584 | tf_op jit(solution)/shard_map/all_to_all | solution.py:26
  194.2 35.7 %copy-start.10 = (bf16[640,1024]{1,0:T(8,128)(2,1)}, bf16[640,1024]{1,0:T(8,128)(2,1)S(1)}, u32[]{:S(2)}) copy-start(bf16[640,1024]{1,0:T(8,128)(2,1)S(1)} %get-tuple-element.207.a_ref) | copy-start | bytes 3932164
  194.2 35.7 %collective-permute-start.11 = (bf16[640,1024]{1,0:T(8,128)(2,1)S(1)}, bf16[640,1024]{1,0:T(8,128)(2,1)S(1)}, u32[]{:S(2)}, u32[]{:S(2)}) collective-permute-start(bf16[640,1024]{1,0:T(8,128)(2,1)S(1)} %get-tuple-element.207.a_ref), channel_id=1, source_target_pairs={{0,8},{4,12},{8,0},{12,4},{16,24},{20,28},{24,16},{28,20},{1,9},{5... | collective-permute-start | bytes 3932168 | tf_op jit(solution)/shard_map/ppermute | solution.py:22
  194.8 35.2 %collective-permute-start.12 = (bf16[640,1024]{1,0:T(8,128)(2,1)}, bf16[640,1024]{1,0:T(8,128)(2,1)}, u32[]{:S(2)}, u32[]{:S(2)}) collective-permute-start(bf16[640,1024]{1,0:T(8,128)(2,1)} %get-tuple-element.193.b_ref), channel_id=1, source_target_pairs={{0,16},{4,20},{8,24},{12,28},{16,0},{20,4},{24,8},{28,12},{1,17},{... | collective-permute-start | bytes 3932168 | tf_op jit(solution)/shard_map/ppermute | solution.py:22
  213.5 51.9 %all-to-all-start.6 = ((bf16[4,128,1024]{2,1,0:T(8,128)(2,1)}), bf16[4,128,1024]{2,1,0:T(8,128)(2,1)}, u32[]{:S(2)}, u32[]{:S(2)}) async-start(bf16[4,128,1024]{2,1,0:T(8,128)(2,1)} %finish_input.1.piece_ref), calls=%async_computation.6 | async-start | bytes 2097152 | tf_op jit(solution)/shard_map/all_to_all | solution.py:26
  219.8 10.1 %collective-permute-start.13 = (bf16[48,1024]{1,0:T(8,128)(2,1)}, bf16[48,1024]{1,0:T(8,128)(2,1)S(1)}, u32[]{:S(2)}, u32[]{:S(2)}) collective-permute-start(bf16[48,1024]{1,0:T(8,128)(2,1)} %first_small.1.mine_ref), channel_id=1, source_target_pairs={{0,8},{4,12},{8,0},{12,4},{16,24},{20,28},{24,16},{28,20},{1,9},{5... | collective-permute-start | bytes 294920 | tf_op jit(solution)/shard_map/ppermute | solution.py:22
  229.9 7.7 %copy-start.11 = (bf16[640,1024]{1,0:T(8,128)(2,1)S(1)}, bf16[640,1024]{1,0:T(8,128)(2,1)}, u32[]{:S(2)}) copy-start(bf16[640,1024]{1,0:T(8,128)(2,1)} %copy-done.10) | copy-start | bytes 3932164
  231.0 2.9 %copy-start.52 = (bf16[48,1024]{1,0:T(8,128)(2,1)}, bf16[48,1024]{1,0:T(8,128)(2,1)S(1)}, u32[]{:S(2)}) copy-start(bf16[48,1024]{1,0:T(8,128)(2,1)S(1)} %collective-permute-done.13.other_ref) | copy-start | bytes 294916
  233.9 17.2 %collective-permute-start.16 = (bf16[512,1024]{1,0:T(8,128)(2,1)}, bf16[512,1024]{1,0:T(8,128)(2,1)S(1)}, u32[]{:S(2)}, u32[]{:S(2)}) collective-permute-start(bf16[512,1024]{1,0:T(8,128)(2,1)} %get-tuple-element.212), channel_id=1, source_target_pairs={{0,4},{4,0},{8,12},{12,8},{16,20},{20,16},{24,28},{28,24},{1,5},{5... | collective-permute-start | bytes 3145736 | tf_op jit(solution)/shard_map/ppermute | solution.py:22
  233.9 17.2 %collective-permute-start.17 = (bf16[512,1024]{1,0:T(8,128)(2,1)}, bf16[512,1024]{1,0:T(8,128)(2,1)}, u32[]{:S(2)}, u32[]{:S(2)}) collective-permute-start(bf16[512,1024]{1,0:T(8,128)(2,1)} %get-tuple-element.214), channel_id=1, source_target_pairs={{0,4},{4,0},{8,12},{12,8},{16,20},{20,16},{24,28},{28,24},{1,5},{5... | collective-permute-start | bytes 3145736 | tf_op jit(solution)/shard_map/ppermute | solution.py:22
  236.1 7.1 %collective-permute-start.14 = (bf16[80,1024]{1,0:T(8,128)(2,1)}, bf16[80,1024]{1,0:T(8,128)(2,1)S(1)}, u32[]{:S(2)}, u32[]{:S(2)}) collective-permute-start(bf16[80,1024]{1,0:T(8,128)(2,1)} %join_small.2.mine_ref), channel_id=1, source_target_pairs={{0,16},{4,20},{8,24},{12,28},{16,0},{20,4},{24,8},{28,12},{1,17},{... | collective-permute-start | bytes 491528 | tf_op jit(solution)/shard_map/ppermute | solution.py:22
  245.6 5.5 %collective-permute-start.15 = (bf16[144,1024]{1,0:T(8,128)(2,1)}, bf16[144,1024]{1,0:T(8,128)(2,1)S(1)}, u32[]{:S(2)}, u32[]{:S(2)}) collective-permute-start(bf16[144,1024]{1,0:T(8,128)(2,1)} %join_small.3.mine_ref), channel_id=1, source_target_pairs={{0,4},{4,0},{8,12},{12,8},{16,20},{20,16},{24,28},{28,24},{1,5},{5... | collective-permute-start | bytes 884744 | tf_op jit(solution)/shard_map/ppermute | solution.py:22
  253.9 8.4 %copy-start.53 = (f32[4,1024]{1,0:T(4,128)S(1)}, f32[4,1024]{1,0:T(4,128)}, u32[]{:S(2)}) copy-start(f32[4,1024]{1,0:T(4,128)} %get-tuple-element.223) | copy-start | bytes 49156
  265.4 8.3 %copy-start.1 = (bf16[256,1024]{1,0:T(8,128)(2,1)S(1)}, bf16[256,1024]{1,0:T(8,128)(2,1)}, u32[]{:S(2)}) copy-start(bf16[256,1024]{1,0:T(8,128)(2,1)} %param.19) | copy-start | bytes 1572868
  (33 other events, 36.9 us)

commit v3 on v2

v3 whole, which is shorter than its diff:
```python
import jax
import jax.numpy as jnp
from jax import lax
from jax.experimental import pallas as pl
from jax.experimental.pallas import tpu as pltpu
from jax.sharding import PartitionSpec as P

BF = jnp.bfloat16
F32 = jnp.float32

NN = ((1,), (0,))
NT = ((1,), (1,))
TN = ((0,), (0,))


def dot(left, right, dims):
    return lax.dot_general(left, right, (dims, ((), ())), preferred_element_type=F32)


def swap(values, axis, bits):
    size = lax.axis_size(axis)
    return lax.ppermute(values, axis, [(i, i ^ bits) for i in range(size)])


def to_all(blocks):
    return lax.all_to_all(blocks, "tensor", 0, 0, tiled=True)


def inverse_rms(rows):
    return lax.rsqrt(jnp.mean(rows * rows, axis=-1, keepdims=True) + eps)


HEAD_DIM = 64
GROUP = 8
TERMS = 4
GAP = 2 * TERMS
eps = 1e-06
mask_fill = -1000000000.0


def small_cost():
    return pl.CostEstimate(flops=1024, bytes_accessed=1024, transcendentals=0)


def cost_of(microseconds):
    return pl.CostEstimate(flops=1024, bytes_accessed=int(microseconds * 3.0e6), transcendentals=0)


def staged(name, body, scalars, arrays, out_shapes, scratch, limit, cost):
    count, outs, extra = len(arrays), len(out_shapes), len(scalars)

    def kernel(*refs):
        scalar_refs, refs = refs[:extra], refs[extra:]
        in_refs, refs = refs[:count], refs[count:]
        out_refs, refs = refs[:outs], refs[outs:]
        held, refs = refs[:count], refs[count:]
        made, refs = refs[:outs], refs[outs:]
        load_sems, store_sems = refs[:2]
        loads = [pltpu.make_async_copy(s, h, load_sems.at[n]) for n, (s, h) in enumerate(zip(in_refs, held))]
        stores = [pltpu.make_async_copy(m, o, store_sems.at[n]) for n, (m, o) in enumerate(zip(made, out_refs))]
        for copy in loads:
            copy.start()
        here, gone = set(), set()

        def load(n):
            if n not in here:
                here.add(n)
                loads[n].wait()
            return held[n]

        def store(*which):
            for n in which:
                gone.add(n)
                stores[n].start()

        body(load, store, made, scalar_refs, refs[2:])
        for n in range(count):
            load(n)
        for n in range(outs):
            if n not in gone:
                store(n)
        for copy in stores:
            copy.wait()

    anywhere = pl.BlockSpec(memory_space=pl.ANY)
    return pl.pallas_call(
        kernel,
        in_specs=[pl.BlockSpec(memory_space=pltpu.SMEM)] * extra + [anywhere] * count,
        out_specs=[anywhere] * outs,
        out_shape=[jax.ShapeDtypeStruct(shape, kind) for shape, kind in out_shapes],
        scratch_shapes=[pltpu.VMEM(a.shape, a.dtype) for a in arrays]
        + [pltpu.VMEM(shape, kind) for shape, kind in out_shapes]
        + [pltpu.SemaphoreType.DMA((count,)), pltpu.SemaphoreType.DMA((outs,))]
        + scratch,
        cost_estimate=cost,
        compiler_params=pltpu.CompilerParams(vmem_limit_bytes=limit << 20),
        name=name,
    )(*scalars, *arrays)


def pick_rows(base, offsets, ways):
    rows, width = base.shape
    chunks = 2 * ways
    block = rows // chunks
    sub = 256
    sub_groups = sub // GROUP

    def kernel(base_ref, offset_ref, picked_ref, held, sems):
        def load(n):
            part = pl.ds(n * block, block)
            return pltpu.make_async_copy(base_ref.at[part], held.at[part], sems.at[n])

        for n in range(chunks):
            load(n).start()
        local = lax.broadcasted_iota(jnp.int32, (sub, sub_groups), 0) - GROUP * lax.broadcasted_iota(
            jnp.int32, (sub, sub_groups), 1
        )
        for n in range(chunks):
            load(n).wait()
            for s in range(n * block // sub, (n + 1) * block // sub):
                to = slice(s * sub_groups, (s + 1) * sub_groups)
                chosen = (local == offset_ref[:, to]).astype(F32).astype(BF)
                picked_ref[to, :] = dot(chosen, held[s * sub : (s + 1) * sub, :], TN).astype(BF)

    whole = pl.BlockSpec(memory_space=pltpu.VMEM)
    return pl.pallas_call(
        kernel,
        in_specs=[pl.BlockSpec(memory_space=pl.ANY), whole],
        out_specs=whole,
        out_shape=jax.ShapeDtypeStruct((rows // GROUP, width), BF),
        scratch_shapes=[pltpu.VMEM((rows, width), BF), pltpu.SemaphoreType.DMA((chunks,))],
        cost_estimate=small_cost(),
        compiler_params=pltpu.CompilerParams(vmem_limit_bytes=60 << 20),
        name="pick_rows",
    )(base, offsets)


def score_sums(base, router, mine, ways):
    rows, width = base.shape
    block = rows // ways

    def kernel(mine_ref, base_ref, router_ref, square_ref):
        score = jnp.sum(base_ref[...].astype(F32) * router_ref[...].astype(F32), axis=1, keepdims=True)
        square_ref[...] = jnp.broadcast_to(jnp.sum(score * score, axis=0, keepdims=True), square_ref.shape)

    return pl.pallas_call(
        kernel,
        grid_spec=pltpu.PrefetchScalarGridSpec(
            num_scalar_prefetch=1,
            grid=(1,),
            in_specs=[
                pl.BlockSpec((block, width), lambda i, m: (m[0], 0)),
                pl.BlockSpec((1, width), lambda i, m: (0, 0)),
            ],
            out_specs=pl.BlockSpec((1, 128), lambda i, m: (0, 0)),
        ),
        out_shape=jax.ShapeDtypeStruct((1, 128), F32),
        cost_estimate=small_cost(),
        name="score_sums",
    )(mine, base, router)


def pick_only(base, offsets, ways):
    rows, width = base.shape
    block = rows // ways
    groups = block // GROUP
    sub = 256
    sub_groups = sub // GROUP

    def kernel(base_ref, offset_ref, picked_ref):
        local = lax.broadcasted_iota(jnp.int32, (sub, sub_groups), 0) - GROUP * lax.broadcasted_iota(
            jnp.int32, (sub, sub_groups), 1
        )
        for s in range(block // sub):
            to = slice(s * sub_groups, (s + 1) * sub_groups)
            chosen = (local == offset_ref[:, to]).astype(F32).astype(BF)
            picked_ref[to, :] = dot(chosen, base_ref[s * sub : (s + 1) * sub, :], TN).astype(BF)

    return pl.pallas_call(
        kernel,
        grid=(ways,),
        in_specs=[pl.BlockSpec((block, width), lambda i: (i, 0)), pl.BlockSpec((1, groups), lambda i: (0, i))],
        out_specs=pl.BlockSpec((groups, width), lambda i: (i, 0)),
        out_shape=jax.ShapeDtypeStruct((rows // GROUP, width), BF),
        cost_estimate=small_cost(),
        name="pick_only",
    )(base, offsets)


def merge_rows(base, offsets, pieces, parts, held_out=None):
    rows, width = base.shape
    ways, depth, _ = pieces.shape
    count = rows // ways
    groups = count // GROUP
    kept = [] if held_out is None else [held_out]
    sub = 256
    sub_groups = sub // GROUP

    def kernel(part_ref, base_ref, offset_ref, piece_ref, *rest):
        out_ref = rest[-1]
        local = lax.broadcasted_iota(jnp.int32, (sub, sub_groups), 0) - GROUP * lax.broadcasted_iota(
            jnp.int32, (sub, sub_groups), 1
        )
        for s in range(count // sub):
            here = slice(s * sub, (s + 1) * sub)
            to = slice(s * sub_groups, (s + 1) * sub_groups)
            chosen = (local == offset_ref[:, to]).astype(F32)
            hit = jnp.sum(chosen, axis=1, keepdims=True) > 0.5
            spread = dot(chosen.astype(BF), piece_ref[0, to, :], NN)
            out_ref[here, :] = jnp.where(hit, spread, base_ref[here, :].astype(F32)).astype(BF)

    grid_spec = pltpu.PrefetchScalarGridSpec(
        num_scalar_prefetch=1,
        grid=(parts.shape[0],),
        in_specs=[
            pl.BlockSpec((count, width), lambda i, p: (p[i], 0)),
            pl.BlockSpec((1, groups), lambda i, p: (0, p[i])),
            pl.BlockSpec((1, depth, width), lambda i, p: (p[i], 0, 0)),
        ]
        + [pl.BlockSpec(memory_space=pl.ANY)] * len(kept),
        out_specs=pl.BlockSpec((count, width), lambda i, p: (p[i], 0)),
    )
    return pl.pallas_call(
        kernel,
        grid_spec=grid_spec,
        out_shape=jax.ShapeDtypeStruct((rows, width), BF),
        input_output_aliases={4: 0} if kept else {},
        cost_estimate=small_cost(),
        name="merge_rows",
    )(parts, base, offsets, pieces, *kept)


def attend(picked, gain, weight, seq_row, ways):
    rows, width = picked.shape
    heads_width = weight.shape[2]
    heads = heads_width // HEAD_DIM
    block = min(256, rows)

    def body(load, store, outs, scalars, scratch):
        low_ref, qkv_ref, probs_ref, out_ref = outs
        values = load(0)[...].astype(F32)
        low_ref[...] = (values * inverse_rms(values) * load(1)[...].astype(F32)).astype(BF)
        store(0)
        weight_ref = load(2)
        for n in range(3):
            qkv_ref[n] = dot(low_ref[...], weight_ref[n], NN).astype(BF)
        store(1)
        sequence = load(3)[...].astype(F32)
        column = jnp.broadcast_to(sequence, (128, rows)).T[:, :1]
        lane_head = lax.broadcasted_iota(jnp.int32, (1, heads_width), 1) // HEAD_DIM
        for start in range(0, rows, block):
            stop = start + block
            query = qkv_ref[0, start:stop, :] * BF(HEAD_DIM ** (-0.5))
            order = lax.broadcasted_iota(jnp.int32, (block, stop), 0) + start
            keys = lax.broadcasted_iota(jnp.int32, (block, stop), 1)
            allowed = (column[start:stop, :] == sequence[:, :stop]) & (order >= keys)
            total = jnp.zeros((block, heads_width), F32)
            for head in range(heads):
                here = lane_head == head
                key = jnp.where(here, qkv_ref[1, :stop, :], BF(0))
                logits = jnp.where(allowed, dot(query, key, NT), mask_fill)
                raised = jnp.exp(logits - jnp.max(logits, axis=-1, keepdims=True))
                probs = (raised * (1.0 / jnp.sum(raised, axis=-1, keepdims=True))).astype(BF)
                probs_ref[head, start:stop, :stop] = probs
                if stop < rows:
                    probs_ref[head, start:stop, stop:] = jnp.zeros((block, rows - stop), BF)
                value = jnp.where(here, qkv_ref[2, :stop, :], BF(0))
                total = total + dot(probs, value, NN)
            for k in range(ways):
                out_ref[k, start:stop, :] = total.astype(BF)

    return staged(
        "attend",
        body,
        [],
        [picked, gain, weight, seq_row],
        [
            ((rows, width), BF),
            ((3, rows, heads_width), BF),
            ((heads, rows, rows), BF),
            ((ways, rows, heads_width), BF),
        ],
        [],
        60,
        small_cost(),
    )


def feed_forward(heads, here, beside, across, picked, gain, up, grad_act, grad_mixer, part, mine, ways):
    rows, width = picked.shape
    hidden = up.shape[1]
    sub = min(256, hidden)
    count, _, heads_width = heads.shape
    piece = heads_width // 4
    own = rows // ways
    slope = 0.7978845608028654
    cubic = 0.044715

    def body(load, store, outs, scalars, scratch):
        part_ref, mine_ref = scalars
        attended_ref, low_ref, act_ref, pre_ref, hidden_ref, part_out_ref, gain_part_ref, sent_ref = outs
        total, state, weights = scratch
        quarter = part_ref[0] & 3
        heads_ref = load(0)
        here_ref, beside_ref, across_ref = load(1), load(2), load(3)
        for n, source in enumerate((here_ref, across_ref.at[0], beside_ref, across_ref.at[1])):
            start = pl.multiple_of((quarter ^ n) * piece, piece)
            for k in range(count):
                weights[k, pl.ds(start, piece), :] = source[k]
        attended = dot(heads_ref[0], weights[0], NN)
        for k in range(1, count):
            attended = attended + dot(heads_ref[k], weights[k], NN)
        total[...] = attended
        attended_ref[...] = total[pl.ds(pl.multiple_of(mine_ref[0] * own, own), own), :]
        state_in = load(4)[...].astype(F32) + attended
        state[...] = state_in
        gain_row = load(5)[...].astype(F32)
        low_ref[...] = (state_in * inverse_rms(state_in) * gain_row).astype(BF)
        store(0, 1)
        up_ref, act_grad_ref = load(6), load(7)
        for s in range(hidden // sub):
            lanes = slice(s * sub, (s + 1) * sub)
            value = dot(low_ref[...], up_ref[:, lanes], NN)
            square = value * value
            bent = jnp.tanh(value * (slope + (slope * cubic) * square))
            half = 0.5 * (1.0 + bent)
            act_ref[:, lanes] = (value * half).astype(BF)
            rise = half + (0.5 * value) * (1.0 - bent * bent) * (slope + (3.0 * slope * cubic) * square)
            pre = (act_grad_ref[:, lanes] * rise).astype(BF)
            pre_ref[:, lanes] = pre
            term = dot(pre, up_ref[:, lanes], NT)
            if s == 0:
                total[...] = term
            else:
                total[...] += term
        store(2, 3)
        state_in = state[...]
        grad = total[...]
        inverse = inverse_rms(state_in)
        normal = state_in * inverse
        gain_part_ref[...] = jnp.sum(grad * normal, axis=0, keepdims=True)
        scaled = grad * gain_row
        along = jnp.mean(scaled * normal, axis=-1, keepdims=True)
        back = inverse * (scaled - normal * along)
        hidden_ref[...] = back.astype(BF)
        part_out_ref[...] = (back + load(8)[...].astype(F32) * (1.0 / count)).astype(BF)
        store(4, 5, 6)
        for k in range(count):
            sent_ref[k] = dot(part_out_ref[...], weights[k], NT).astype(BF)

    return staged(
        "feed_forward",
        body,
        [part, mine],
        [heads, here, beside, across, picked, gain, up, grad_act, grad_mixer],
        [
            ((own, width), F32),
            ((rows, width), BF),
            ((rows, hidden), BF),
            ((rows, hidden), BF),
            ((rows, width), BF),
            ((rows, width), BF),
            ((1, width), F32),
            (heads.shape, BF),
        ],
        [
            pltpu.VMEM((rows, width), F32),
            pltpu.VMEM((rows, width), F32),
            pltpu.VMEM((count, heads_width, width), BF),
        ],
        60,
        small_cost(),
    )


def act_grads(picked, router, grad_rows, down):
    rows, width = grad_rows.shape

    def kernel(picked_ref, router_ref, rows_ref, down_ref, gating_ref, square_ref, mixer_ref, grad_ref):
        score = jnp.sum(picked_ref[...].astype(F32) * router_ref[...].astype(F32), axis=-1, keepdims=True)
        gating = jax.nn.sigmoid(score)
        gating_ref[...] = gating
        square_ref[...] = jnp.broadcast_to(jnp.sum(score * score, axis=0, keepdims=True), square_ref.shape)
        mixer_ref[...] = (gating * rows_ref[...].astype(F32)).astype(BF)
        grad_ref[...] = dot(mixer_ref[...], down_ref[...], NT)

    whole = pl.BlockSpec(memory_space=pltpu.VMEM)
    return pl.pallas_call(
        kernel,
        in_specs=[whole] * 4,
        out_specs=[whole] * 4,
        out_shape=[
            jax.ShapeDtypeStruct((rows, 1), F32),
            jax.ShapeDtypeStruct((1, 128), F32),
            jax.ShapeDtypeStruct((rows, width), BF),
            jax.ShapeDtypeStruct((rows, down.shape[0]), F32),
        ],
        cost_estimate=small_cost(),
        name="act_grads",
    )(picked, router, grad_rows, down)


def attend_back(head_terms, qkv, probs, weight, picked, gain, hidden_part):
    rows, width = picked.shape
    heads_width = weight.shape[2]
    heads = heads_width // HEAD_DIM
    block = min(256, rows)
    scale = HEAD_DIM ** (-0.5)

    def kernel(
        head_ref,
        qkv_ref,
        probs_ref,
        weight_ref,
        picked_ref,
        gain_ref,
        hidden_ref,
        grads_ref,
        gain_part_ref,
        result,
        grad_key,
        grad_value,
    ):
        lane_head = lax.broadcasted_iota(jnp.int32, (1, heads_width), 1) // HEAD_DIM
        for start in reversed(range(0, rows, block)):
            stop = start + block
            here_rows = slice(start, stop)
            grad_head = head_ref[0, here_rows, :].astype(F32)
            for k in range(1, head_ref.shape[0]):
                grad_head = grad_head + head_ref[k, here_rows, :].astype(F32)
            grad_head = grad_head.astype(BF)
            query = qkv_ref[0, here_rows, :] * BF(scale)
            grad_query = jnp.zeros((block, heads_width), F32)
            add_key = jnp.zeros((stop, heads_width), F32)
            add_value = jnp.zeros((stop, heads_width), F32)
            for head in range(heads):
                here = lane_head == head
                value = jnp.where(here, qkv_ref[2, :stop, :], BF(0))
                key = jnp.where(here, qkv_ref[1, :stop, :], BF(0))
                low = probs_ref[head, here_rows, :stop]
                weighted = low.astype(F32) * dot(grad_head, value, NT)
                row_sum = jnp.sum(weighted, axis=-1, keepdims=True)
                slopes = (weighted - low.astype(F32) * row_sum).astype(BF)
                grad_query = grad_query + dot(slopes, key, NN)
                add_key = add_key + dot(slopes, jnp.where(here, query, BF(0)), TN)
                add_value = add_value + dot(low, jnp.where(here, grad_head, BF(0)), TN)
            grads_ref[0, here_rows, :] = (grad_query * scale).astype(BF)
            if stop == rows:
                grad_key[...] = add_key
                grad_value[...] = add_value
            else:
                grad_key[:stop, :] += add_key
                grad_value[:stop, :] += add_value
        grads_ref[1] = grad_key[...].astype(BF)
        grads_ref[2] = grad_value[...].astype(BF)
        first = dot(grads_ref[0], weight_ref[0], NT)
        for n in range(1, 3):
            first = first + dot(grads_ref[n], weight_ref[n], NT)
        values = picked_ref[...].astype(F32)
        inverse = inverse_rms(values)
        normal = values * inverse
        gain_part_ref[...] = jnp.sum(first * normal, axis=0, keepdims=True)
        scaled = first * gain_ref[...].astype(F32)
        along = jnp.mean(scaled * normal, axis=-1, keepdims=True)
        result[...] = (hidden_ref[...].astype(F32) + inverse * (scaled - normal * along)).astype(BF)

    whole = pl.BlockSpec(memory_space=pltpu.VMEM)
    return pl.pallas_call(
        kernel,
        in_specs=[whole] * 7,
        out_specs=[whole] * 3,
        out_shape=[
            jax.ShapeDtypeStruct((3, rows, heads_width), BF),
            jax.ShapeDtypeStruct((1, width), F32),
            jax.ShapeDtypeStruct((rows, width), BF),
        ],
        scratch_shapes=[
            pltpu.VMEM((rows, heads_width), F32),
            pltpu.VMEM((rows, heads_width), F32),
        ],
        cost_estimate=small_cost(),
        compiler_params=pltpu.CompilerParams(vmem_limit_bytes=20 << 20),
        name="attend_back",
    )(head_terms, qkv, probs, weight, picked, gain, hidden_part)


def spread_rows(down_near, down_far, up_near, up_far, index_down, index_up):
    half, rows, width = down_near.shape

    def kernel(down_index, up_index, down_ref, far_ref, up_ref, up_far_ref, down_out, up_out):
        near = pl.program_id(0) < half

        @pl.when(near)
        def _():
            down_out[...] = down_ref[0].astype(F32)
            up_out[...] = up_ref[0].astype(F32)

        @pl.when(jnp.logical_not(near))
        def _():
            down_out[...] = far_ref[0].astype(F32)
            up_out[...] = up_far_ref[0].astype(F32)

    first = pl.BlockSpec((1, rows, width), lambda i, d, u: (jnp.minimum(i, half - 1), 0, 0))
    second = pl.BlockSpec((1, rows, width), lambda i, d, u: (jnp.maximum(i - half, 0), 0, 0))
    return pl.pallas_call(
        kernel,
        grid_spec=pltpu.PrefetchScalarGridSpec(
            num_scalar_prefetch=2,
            grid=(2 * half,),
            in_specs=[first, second, first, second],
            out_specs=[
                pl.BlockSpec((rows, width), lambda i, d, u: (d[i], 0)),
                pl.BlockSpec((rows, width), lambda i, d, u: (u[i], 0)),
            ],
        ),
        out_shape=[jax.ShapeDtypeStruct((2 * half * rows, width), F32)] * 2,
        cost_estimate=small_cost(),
        name="spread_rows",
    )(index_down, index_up, down_near, down_far, up_near, up_far)


def qkv_part_of(first_low, grads):
    rows, width = first_low.shape
    part_width = grads.shape[2]

    def kernel(low_ref, grads_ref, out_ref):
        for n in range(3):
            product = dot(grads_ref[n], low_ref[...], TN)
            out_ref[n * part_width : (n + 1) * part_width, :] = product.astype(BF)

    whole = pl.BlockSpec(memory_space=pltpu.VMEM)
    return pl.pallas_call(
        kernel,
        in_specs=[whole] * 2,
        out_specs=whole,
        out_shape=jax.ShapeDtypeStruct((3 * part_width, width), BF),
        cost_estimate=small_cost(),
        name="qkv_part",
    )(first_low, grads)


def spread_qkv(lane_a, got_a, lane_b, got_b, part_width):
    rows, width = lane_a.shape
    tile = 128

    def kernel(a_ref, a_got, b_ref, b_got, out_ref):
        for n in range(2 * rows // tile):
            start = n * tile % rows
            ref, got = (a_ref, a_got) if n * tile < rows else (b_ref, b_got)
            lane, column = divmod(n * tile, part_width)
            piece = ref[start : start + tile, :].astype(F32) + got[start : start + tile, :].astype(F32)
            out_ref[lane, :, column : column + tile] = piece.T

    whole = pl.BlockSpec(memory_space=pltpu.VMEM)
    return pl.pallas_call(
        kernel,
        in_specs=[whole] * 4,
        out_specs=whole,
        out_shape=jax.ShapeDtypeStruct((2 * rows // part_width, width, part_width), F32),
        cost_estimate=small_cost(),
        compiler_params=pltpu.CompilerParams(vmem_limit_bytes=16 << 20),
        name="spread_qkv",
    )(lane_a, got_a, lane_b, got_b)


def core_grads(activated, grad_mixer, second_low, grad_pre, heads, attended_part, part, keys_a, keys_b):
    rows, hidden = activated.shape
    width = grad_mixer.shape[1]
    copies = len(keys_a)
    half = copies // 2
    count, _, heads_width = heads.shape
    block = hidden // copies
    small = heads_width // copies
    many = count // 2
    depth = half * (block + many * small)

    def kernel(part_ref, act_ref, mixer_ref, low_ref, pre_ref, heads_ref, term_ref, keep_ref, *rest):
        wide_refs, narrow_refs, (full, narrow) = rest[0:2], rest[2:4], rest[4:]

        def place(source, each, lane, keys, first, stride):
            for n, key in enumerate(keys):
                start = pl.multiple_of((part_ref[0] ^ key) * each, each)
                at = first + (n % half) * stride
                piece = source[pl.ds(start, each), :]
                if n < half:
                    keep_ref[lane, at : at + each, :] = piece
                elif first == 0:
                    wide_refs[lane][at : at + each, :] = piece
                else:
                    narrow_refs[lane][at - half * block : at - half * block + each, :] = piece

        full[...] = dot(act_ref[...], mixer_ref[...], TN).astype(BF)
        place(full, block, 0, keys_a, 0, block)
        full[...] = dot(low_ref[...], pre_ref[...], TN).astype(BF)
        place(full, block, 1, keys_b, 0, block)
        for k in range(count):
            narrow[...] = dot(heads_ref[k], term_ref[...], TN).astype(BF)
            lane, spot = divmod(k, many)
            place(narrow, small, lane, keys_b if lane else keys_a, half * block + spot * small, many * small)

    whole = pl.BlockSpec(memory_space=pltpu.VMEM)
    wide_shape = jax.ShapeDtypeStruct((half * block, width), BF)
    narrow_shape = jax.ShapeDtypeStruct((half * many * small, width), BF)
    return pl.pallas_call(
        kernel,
        in_specs=[pl.BlockSpec(memory_space=pltpu.SMEM)] + [whole] * 6,
        out_specs=[whole] * 5,
        out_shape=[jax.ShapeDtypeStruct((2, depth, width), BF)] + [wide_shape] * 2 + [narrow_shape] * 2,
        scratch_shapes=[pltpu.VMEM((hidden, width), BF), pltpu.VMEM((heads_width, width), BF)],
        cost_estimate=small_cost(),
        compiler_params=pltpu.CompilerParams(vmem_limit_bytes=14 << 20),
        name="core_grads",
    )(part, activated, grad_mixer, second_low, grad_pre, heads, attended_part)


def plus(left, right):
    return (left.astype(F32) + right.astype(F32)).astype(BF)


def halving_sums(keep, got_a, got_b, wide, narrow):
    width = keep.shape[2]
    count = len(got_a)

    def kernel(keep_ref, *refs):
        a_got, b_got, (stay_ref, a_out, b_out) = refs[:count], refs[count : 2 * count], refs[2 * count :]
        for lane, got, out in ((0, a_got, a_out), (1, b_got, b_out)):
            for first, size, at in ((0, wide // 2, 0), (wide, narrow // 2, wide // 2)):
                source, shift = (got[1], wide) if count == 2 and first else (got[0], 0)
                to = slice(at, at + size)
                for start, target in ((first, stay_ref.at[lane]), (first + size, out)):
                    here = slice(start - shift, start - shift + size)
                    target[to, :] = plus(keep_ref[lane, start : start + size, :], source[here, :])

    whole = pl.BlockSpec(memory_space=pltpu.VMEM)
    depth = (wide + narrow) // 2
    lane_shape = jax.ShapeDtypeStruct((depth, width), BF)
    return pl.pallas_call(
        kernel,
        in_specs=[whole] * (1 + 2 * count),
        out_specs=[whole] * 3,
        out_shape=[jax.ShapeDtypeStruct((2, depth, width), BF), lane_shape, lane_shape],
        cost_estimate=small_cost(),
        compiler_params=pltpu.CompilerParams(vmem_limit_bytes=14 << 20),
        name="halving_sums",
    )(keep, *got_a, *got_b)


def owned_sums(keep, got_a, got_b, fresh, small, wide, ways):
    width = keep.shape[2]
    narrow = keep.shape[1] - wide
    own = fresh.shape[0]
    many = ways // 2
    each = narrow // many
    depth = own + GAP + each

    def kernel(keep_ref, a_got, b_got, fresh_ref, small_ref, a_out, b_out, sent_ref):
        sums = split_sums(small_ref[...])
        for lane, got, out in ((0, a_got, a_out), (1, b_got, b_out)):
            out[...] = plus(keep_ref[lane, :wide, :], got[:wide, :])
            done = plus(keep_ref[lane, wide:, :], got[wide:, :])
            for spot in range(many):
                k = lane * many + spot
                sent_ref[k, :own, :] = fresh_ref[...]
                sent_ref[k, own : own + GAP, :] = sums
                sent_ref[k, own + GAP :, :] = done[spot * each : (spot + 1) * each, :]

    whole = pl.BlockSpec(memory_space=pltpu.VMEM)
    lane_shape = jax.ShapeDtypeStruct((wide, width), BF)
    return pl.pallas_call(
        kernel,
        in_specs=[whole] * 5,
        out_specs=[whole] * 3,
        out_shape=[lane_shape, lane_shape, jax.ShapeDtypeStruct((ways, depth, width), BF)],
        cost_estimate=small_cost(),
        name="owned_sums",
    )(keep, got_a, got_b, fresh, small)


def core_sums(rows, other):
    depth, width = rows.shape
    third = depth // 2

    def kernel(rows_ref, other_ref, a_out, b_out):
        a_out[...] = plus(rows_ref[:third, :], other_ref[:third, :])
        b_out[...] = plus(rows_ref[third:, :], other_ref[third:, :])

    whole = pl.BlockSpec(memory_space=pltpu.VMEM)
    return pl.pallas_call(
        kernel,
        in_specs=[whole] * 2,
        out_specs=[whole] * 2,
        out_shape=[jax.ShapeDtypeStruct((third, width), BF)] * 2,
        cost_estimate=small_cost(),
        name="core_sums",
    )(rows, other)


def lane_sums(lane_a, got_a, lane_b, got_b):
    def kernel(a_ref, a_got, b_ref, b_got, a_out, b_out):
        a_out[...] = plus(a_ref[...], a_got[...])
        b_out[...] = plus(b_ref[...], b_got[...])

    whole = pl.BlockSpec(memory_space=pltpu.VMEM)
    return pl.pallas_call(
        kernel,
        in_specs=[whole] * 4,
        out_specs=[whole] * 2,
        out_shape=[jax.ShapeDtypeStruct(lane_a.shape, BF)] * 2,
        cost_estimate=small_cost(),
        name="lane_sums",
    )(lane_a, got_a, lane_b, got_b)


def gather_blocks(blocks_a, blocks_b):
    wide, width = blocks_a[0].shape
    count = len(blocks_a)

    def kernel(*refs):
        for lane in range(2):
            for n in range(count):
                refs[2 * count + lane][n * wide : (n + 1) * wide, :] = refs[lane * count + n][...]

    whole = pl.BlockSpec(memory_space=pltpu.VMEM)
    return pl.pallas_call(
        kernel,
        in_specs=[whole] * (2 * count),
        out_specs=[whole] * 2,
        out_shape=[jax.ShapeDtypeStruct((count * wide, width), BF)] * 2,
        cost_estimate=small_cost(),
        name="gather_blocks",
    )(*blocks_a, *blocks_b)


def split_sums(values):
    high = values.astype(BF)
    low = (values - high.astype(F32)).astype(BF)
    return jnp.concatenate([high, low], axis=0)


def joined_sums(rows):
    return rows[:TERMS].astype(F32) + rows[TERMS : 2 * TERMS].astype(F32)


def first_small(received, own):
    ways, depth, width = received.shape
    each = depth - own - GAP

    def kernel(got_ref, out_ref):
        total = got_ref[0, own + GAP :, :].astype(F32)
        sums = joined_sums(got_ref[0, own : own + GAP, :])
        for k in range(1, ways):
            total = total + got_ref[k, own + GAP :, :].astype(F32)
            sums = sums + joined_sums(got_ref[k, own : own + GAP, :])
        out_ref[:each, :] = total.astype(BF)
        out_ref[each:, :] = split_sums(sums)

    whole = pl.BlockSpec(memory_space=pltpu.VMEM)
    return pl.pallas_call(
        kernel,
        in_specs=[whole],
        out_specs=whole,
        out_shape=jax.ShapeDtypeStruct((each + GAP, width), BF),
        cost_estimate=small_cost(),
        name="first_small",
    )(received)


def last_small(blocks, index, shares):
    depth, width = blocks[0].shape
    each = depth - GAP
    count = len(blocks)

    def kernel(index_ref, *refs):
        out_ref, small_refs = refs[count], refs[count + 1 :]
        total = joined_sums(refs[0][each:, :])
        for n in range(1, count):
            total = total + joined_sums(refs[n][each:, :])
        for n in range(TERMS - 1):
            small_refs[n][...] = total[n : n + 1, :]
        lane = lax.broadcasted_iota(jnp.int32, (1, 128), 1)
        small_refs[TERMS - 1][...] = total[TERMS - 1 :, :128] * jnp.where(lane == 0, shares[0], shares[1])
        for n in range(count):
            start = pl.multiple_of(index_ref[n] * each, each)
            out_ref[pl.ds(start, each), :] = refs[n][:each, :].astype(F32)

    whole = pl.BlockSpec(memory_space=pltpu.VMEM)
    return pl.pallas_call(
        kernel,
        in_specs=[pl.BlockSpec(memory_space=pltpu.SMEM)] + [whole] * count,
        out_specs=[whole] * (1 + TERMS),
        out_shape=[jax.ShapeDtypeStruct((count * each, width), F32)] + [jax.ShapeDtypeStruct((1, width), F32)] * (TERMS - 1)
        + [jax.ShapeDtypeStruct((1, 128), F32)],
        cost_estimate=small_cost(),
        name="last_small",
    )(index, *blocks)


def finish_rows(mixer_terms, picked, gating, attended, grad_rows, gain_one, gain_two, square, routed_square, mine, ways):
    rows, width = picked.shape
    own = rows // ways

    def kernel(
        mine_ref,
        terms_ref,
        picked_ref,
        gating_ref,
        attended_ref,
        rows_ref,
        one_ref,
        two_ref,
        square_ref,
        routed_ref,
        new_ref,
        score_ref,
        small_ref,
    ):
        branch = attended_ref[...]
        for k in range(ways):
            branch = branch + terms_ref[k].astype(F32)
        values = picked_ref[...].astype(F32)
        gate = gating_ref[...]
        new_ref[...] = (values + gate * branch).astype(BF)
        along = jnp.sum(rows_ref[...].astype(F32) * branch, axis=-1, keepdims=True)
        score = along * gate * (1.0 - gate)
        score_ref[...] = score
        small_ref[0:1, :] = jnp.sum(score * values, axis=0, keepdims=True)
        small_ref[1:2, :] = one_ref[...]
        small_ref[2:3, :] = two_ref[...]
        lane = lax.broadcasted_iota(jnp.int32, (1, width), 1)
        both = jnp.where(lane == 0, square_ref[:, 0:1], routed_ref[:, 0:1] * (1.0 / ways))
        small_ref[3:4, :] = jnp.where(lane < 2, both, 0.0)

    def block(shape):
        return pl.BlockSpec(shape, lambda i, m: (m[0], 0))

    def fixed(shape):
        return pl.BlockSpec(shape, lambda i, m: (0, 0))

    return pl.pallas_call(
        kernel,
        grid_spec=pltpu.PrefetchScalarGridSpec(
            num_scalar_prefetch=1,
            grid=(1,),
            in_specs=[pl.BlockSpec(mixer_terms.shape, lambda i, m: (0, 0, 0))]
            + [block((own, width)), block((own, 1)), fixed((own, width)), block((own, width))]
            + [fixed((1, width))] * 2
            + [fixed((1, 128))] * 2,
            out_specs=[fixed((own, width)), fixed((own, 1)), fixed((4, width))],
        ),
        out_shape=[
            jax.ShapeDtypeStruct((own, width), BF),
            jax.ShapeDtypeStruct((own, 1), F32),
            jax.ShapeDtypeStruct((4, width), F32),
        ],
        cost_estimate=cost_of(10),
        name="finish_rows",
    )(mine, mixer_terms, picked, gating, attended, grad_rows, gain_one, gain_two, square, routed_square)


def finish_input(terms, grad_rows, score, router, mine, ways):
    rows, width = grad_rows.shape
    own = rows // ways

    def kernel(mine_ref, terms_ref, rows_ref, score_ref, router_ref, out_ref):
        total = rows_ref[...].astype(F32) + score_ref[...] * router_ref[...].astype(F32)
        for k in range(ways):
            total = total + terms_ref[k].astype(F32)
        for k in range(ways):
            out_ref[k] = total.astype(BF)

    def fixed(shape):
        return pl.BlockSpec(shape, lambda i, m: (0,) * len(shape))

    return pl.pallas_call(
        kernel,
        grid_spec=pltpu.PrefetchScalarGridSpec(
            num_scalar_prefetch=1,
            grid=(1,),
            in_specs=[
                fixed((ways, own, width)),
                pl.BlockSpec((own, width), lambda i, m: (m[0], 0)),
                fixed((own, 1)),
                fixed((1, width)),
            ],
            out_specs=fixed((ways, own, width)),
        ),
        out_shape=jax.ShapeDtypeStruct((ways, own, width), BF),
        cost_estimate=small_cost(),
        name="finish_input",
    )(mine, terms, grad_rows, score, router)


def split_kept(count, order):
    keys = [0]
    for bit in reversed(order):
        keys = keys + [k ^ bit for k in keys]
    return keys


def per_device(
    tokens,
    route_offset,
    unit_sequence,
    cotangent,
    router_weight,
    first_gain,
    second_gain,
    qkv_weight,
    out_weight,
    up_weight,
    down_weight,
):
    rows_local, width = tokens.shape
    routed = route_offset.shape[1]
    ways = lax.axis_size("tensor")
    copies = lax.axis_size("dp")
    mine = lax.axis_index("tensor")
    part = lax.axis_index("dp")
    mine_array = jnp.reshape(mine, (1,)).astype(jnp.int32)
    part_array = jnp.reshape(part, (1,)).astype(jnp.int32)
    ladder = [1 << b for b in range(1, copies.bit_length() - 1)]
    order_a = [1] + ladder
    order_b = [1] + ladder[::-1]
    keys_a = split_kept(copies, order_a)
    keys_b = split_kept(copies, order_b)

    tie = lax.optimization_barrier
    own_rows = routed // ways
    heads_width = out_weight.shape[0]
    hidden = up_weight.shape[1]
    by_swaps = copies == 8
    bit_x, bit_y = 2, 4
    shares = (1.0 / (rows_local * copies), 1.0 / (routed * copies))

    quarter = part & 3
    piece_rows = heads_width // 4
    piece = lax.dynamic_slice_in_dim(out_weight, quarter * piece_rows, piece_rows, 0)
    here = to_all(jnp.broadcast_to(piece[None], (ways,) + piece.shape))

    picked = pick_rows(tokens, route_offset, ways)
    first_low, qkv, probs, head_out = attend(picked, first_gain[None], qkv_weight, unit_sequence, ways)
    here, head_out = tie((here, head_out))

    heads = to_all(head_out)
    beside = swap(here, "dp", bit_x)
    cotangent, router_weight, second_gain, here, head_out = tie(
        (cotangent, router_weight, second_gain, here, head_out)
    )
    weight_row = router_weight[None]
    grad_rows = pick_only(cotangent, route_offset, ways)
    beside, here, grad_rows = tie((beside, here, grad_rows))
    across = swap(jnp.stack([here, beside]), "dp", 1)
    gating, routed_square, grad_mixer, grad_act = act_grads(picked, weight_row, grad_rows, down_weight)
    square = score_sums(tokens, weight_row, mine_array, ways)
    heads, across, grad_act, grad_mixer, square = tie((heads, across, grad_act, grad_mixer, square))
    attended, second_low, activated, grad_pre, hidden_part, attended_part, second_gain_part, head_sent = feed_forward(
        heads,
        here,
        beside,
        across,
        picked,
        second_gain[None],
        up_weight,
        grad_act,
        grad_mixer,
        part_array,
        mine_array,
        ways,
    )

    head_terms = to_all(head_sent)
    wide = hidden // 2
    narrow = heads_width * ways // 4
    if by_swaps:
        kept, *leaving = core_grads(
            activated, grad_mixer, second_low, grad_pre, heads, attended_part, part_array, keys_a, keys_b
        )
        wide_a, wide_b, narrow_a, narrow_b = (swap(array, "dp", 1) for array in leaving)
        activated, kept = tie((activated, kept))
    else:
        down_part = dot(activated, grad_mixer, TN).astype(BF)
        up_part = dot(second_low, grad_pre, TN).astype(BF)
        out_parts = jnp.stack([dot(heads[k], attended_part, TN).astype(BF) for k in range(ways)])
    mixer_part = dot(activated, down_weight, NN).astype(BF).reshape(ways, own_rows, width)
    if by_swaps:
        wide_a, wide_b, narrow_a, narrow_b, mixer_part = tie((wide_a, wide_b, narrow_a, narrow_b, mixer_part))
        kept, leave_a, leave_b = halving_sums(kept, (wide_a, narrow_a), (wide_b, narrow_b), wide, narrow)
        got_a, got_b = swap(leave_a, "dp", bit_x), swap(leave_b, "dp", bit_y)
        head_terms, mixer_part, kept = tie((head_terms, mixer_part, kept))
    else:
        head_terms, mixer_part = tie((head_terms, mixer_part))

    mixer_terms = to_all(mixer_part)
    grad_projected, first_gain_part, input_part = attend_back(
        head_terms, qkv, probs, qkv_weight, picked, first_gain[None], hidden_part
    )
    qkv_part = qkv_part_of(first_low, grad_projected)
    input_part = input_part.reshape(ways, own_rows, width)
    if by_swaps:
        got_a, got_b, qkv_part, input_part = tie((got_a, got_b, qkv_part, input_part))
        kept, leave_a, leave_b = halving_sums(kept, (got_a,), (got_b,), wide // 2, narrow // 2)
        mixer_terms, input_part, qkv_part, kept, leave_a, leave_b = tie(
            (mixer_terms, input_part, qkv_part, kept, leave_a, leave_b)
        )
    else:
        mixer_terms, input_part, qkv_part = tie((mixer_terms, input_part, qkv_part))

    input_terms = to_all(input_part)
    if by_swaps:
        got_a, got_b = swap(leave_a, "dp", bit_y), swap(leave_b, "dp", bit_x)
        qkv_got = swap(qkv_part, "dp", 1)
    new_own, grad_score, small = finish_rows(
        mixer_terms,
        picked,
        gating,
        attended,
        grad_rows,
        first_gain_part,
        second_gain_part,
        square,
        routed_square,
        mine_array,
        ways,
    )
    if by_swaps:
        got_a, got_b, new_own = tie((got_a, got_b, new_own))
        lane_a, lane_b, sent = owned_sums(kept, got_a, got_b, new_own, small, wide // 4, ways)
        got_a, got_b = swap(lane_a, "dp", bit_y), swap(lane_b, "dp", bit_x)
        qkv_part, qkv_got, lane_a, lane_b, sent = tie((qkv_part, qkv_got, lane_a, lane_b, sent))
        qkv_a, qkv_b = core_sums(qkv_part, qkv_got)
        input_terms, sent, got_a, got_b, qkv_a, qkv_b = tie((input_terms, sent, got_a, got_b, qkv_a, qkv_b))
    else:
        sent = jnp.concatenate([new_own, split_sums(small)])
        sent = jnp.broadcast_to(sent[None], (ways,) + sent.shape)
        input_terms, sent = tie((input_terms, sent))

    fresh = to_all(sent)
    if by_swaps:
        more_a = [swap(array, "dp", bit_x) for array in (lane_a, got_a)]
        more_b = [swap(array, "dp", bit_y) for array in (lane_b, got_b)]
    last = finish_input(input_terms, grad_rows, grad_score, weight_row, mine_array, ways)
    spots = jnp.stack([mine ^ k for k in range(ways)]).astype(jnp.int32)
    cotangent, last = tie((cotangent, last))
    early = merge_rows(cotangent, route_offset, last, spots[:1])
    if by_swaps:
        more_a, more_b, early, qkv_a, qkv_b = tie((more_a, more_b, early, qkv_a, qkv_b))
        qkv_a_got, qkv_b_got = swap(qkv_a, "dp", bit_y), swap(qkv_b, "dp", bit_x)
        down_near, up_near = gather_blocks([lane_a, got_a] + more_a, [lane_b, got_b] + more_b)
        down_far, up_far = swap(down_near, "dp", 1), swap(up_near, "dp", 1)

        def gathered(order):
            keys = [0]
            for bit in order:
                keys = keys + [k ^ bit for k in keys]
            return jnp.stack([part ^ k for k in keys]).astype(jnp.int32)

        each = hidden // copies

        def by_block(array):
            return array.reshape(-1, each, width)

        down_grad, up_grad = spread_rows(
            by_block(down_near),
            by_block(down_far),
            by_block(up_near),
            by_block(up_far),
            gathered([bit_y, bit_x, 1]),
            gathered([bit_x, bit_y, 1]),
        )
        fresh, last, down_grad, up_grad = tie((fresh, last, down_grad, up_grad))
    else:
        fresh, last = tie((fresh, last))

    input_rows = to_all(last)
    if by_swaps:
        blocks = [first_small(fresh, own_rows)]
        more = [swap(array, "dp", bit_x) for array in blocks]
        qkv_a_got, qkv_b_got, blocks = tie((qkv_a_got, qkv_b_got, blocks))
        qkv_a, qkv_b = lane_sums(qkv_a, qkv_a_got, qkv_b, qkv_b_got)
        more, qkv_a, qkv_b = tie((more, qkv_a, qkv_b))
        blocks = blocks + more
        more = [swap(array, "dp", bit_y) for array in blocks]
        more, qkv_a, qkv_b = tie((more, qkv_a, qkv_b))
        qkv_a_got, qkv_b_got = swap(qkv_a, "dp", bit_x), swap(qkv_b, "dp", bit_y)
        blocks = blocks + more
        more = [swap(array, "dp", 1) for array in blocks]
        fresh, qkv_a, qkv_b, blocks = tie((fresh, qkv_a, qkv_b, blocks))
    output = merge_rows(tokens, route_offset, fresh, spots)
    if by_swaps:
        more, output = tie((more, output))
        out_grad, *small = last_small(blocks + more, gathered([bit_x, bit_y, 1]), shares)
        qkv_a_got, qkv_b_got, out_grad = tie((qkv_a_got, qkv_b_got, out_grad))
        qkv_grad = spread_qkv(qkv_a, qkv_a_got, qkv_b, qkv_b_got, qkv_weight.shape[2])
        input_rows, early, out_grad, small, output, qkv_grad = tie(
            (input_rows, early, out_grad, small, output, qkv_grad)
        )
    input_grad = merge_rows(cotangent, route_offset, input_rows, spots[1:], early)
    if not by_swaps:
        small = sum(joined_sums(fresh[k, own_rows:]) for k in range(ways))
        small = lax.psum(small, "dp")
        small = [small[n : n + 1] for n in range(TERMS)]
        small[3] = small[3][:, :128] * jnp.array((shares + (0.0,) * 126,), F32)
        down_grad, up_grad, qkv_sum, out_sum = (
            lax.psum(v, "dp").astype(F32) for v in (down_part, up_part, qkv_part, out_parts)
        )
        out_grad = jnp.sum(to_all(out_sum.astype(BF)).astype(F32), axis=0)
        qkv_grad = qkv_sum.reshape(3, -1, width).transpose(0, 2, 1)
    router_grad, first_gain_grad, second_gain_grad = (small[n].reshape(width) for n in range(3))
    score_stats = small[3][0, :2]
    return (
        output,
        input_grad,
        router_grad,
        first_gain_grad,
        second_gain_grad,
        qkv_grad,
        out_grad,
        up_grad,
        down_grad,
        score_stats,
    )


def solution(mesh):
    placed = (
        P("dp", None),
        P("dp", None),
        P("dp", None),
        P("dp", None),
        P(),
        P(),
        P(),
        P(None, None, "tensor"),
        P("tensor", None),
        P(None, "tensor"),
        P("tensor", None),
    )
    return jax.shard_map(
        per_device,
        mesh=mesh,
        in_specs=placed,
        out_specs=(
            P("dp", None),
            P("dp", None),
            P(),
            P(),
            P(),
            P(None, None, "tensor"),
            P("tensor", None),
            P(None, "tensor"),
            P("tensor", None),
            P(),
        ),
        check_vma=False,
    )
```

time: 276 us -> 239 us (0.87)
  waiting for transfers between devices: 71.3 us -> 49.6 us
  local copies, waits for them, and re-layouts: 42.2 us -> 22.6 us
  starting transfers between devices: 45.1 us -> 52.5 us
    all_to_all x7, waiting for transfers between devices: 52 us -> 23.1 us  [to_all(): return lax.all_to_all(blocks, 'tensor', 0, 0, tiled=True)]
    unnamed x112 -> x94, local copies, waits for them, and re-layouts: 37.5 us -> 18.2 us
    ppermute x18 -> x30, starting transfers between devices: 12.8 us -> 21.3 us  [swap(): return lax.ppermute(values, axis, [(i, i ^ bits) for i in range(size)])]
    ppermute x18 -> x30, waiting for transfers between devices: 19.4 us -> 26.5 us  [swap(): return lax.ppermute(values, axis, [(i, i ^ bits) for i in range(size)])]
    pallas_call x14 -> x13, Pallas kernels: 50.9 us -> 54.1 us  [the longest x2 17.7 us: staged(): pl.pallas_call(kernel, in_specs=[pl.BlockSpec(memory_space=pltpu.SMEM)] *...]
  transfers between devices with their start and end apart: 25 -> 37, of which waited for: 12 -> 21; matrix products, arithmetic and copies ran while one was open for 3% -> 3% of each run, Pallas kernels for 32% -> 37%
where the time goes in v3:
time: 239 us; the launch traced here: 237 us
  Pallas kernels  107 us (45%)
  starting transfers between devices  52.5 us (22%)
  waiting for transfers between devices  49.6 us (21%)
  local copies, waits for them, and re-layouts  22.6 us (9%)
    all_to_all x7, starting transfers between devices, to_all(): return lax.all_to_all(blocks, 'tensor', 0, 0, tiled=True)  31.2 us
    ppermute x30, waiting for transfers between devices, swap(): return lax.ppermute(values, axis, [(i, i ^ bits) for i in range(size)])  26.5 us
    all_to_all x7, waiting for transfers between devices, to_all(): return lax.all_to_all(blocks, 'tensor', 0, 0, tiled=True)  23.1 us
    ppermute x30, starting transfers between devices, swap(): return lax.ppermute(values, axis, [(i, i ^ bits) for i in range(size)])  21.3 us
    pallas_call x3, Pallas kernels, merge_rows(): pl.pallas_call(kernel, grid_spec=grid_spec, out_shape=jax.ShapeDtypeStruc...  20.9 us
    unnamed x94, local copies, waits for them, and re-layouts  18.2 us
    pallas_call x2, Pallas kernels, staged(): pl.pallas_call(kernel, in_specs=[pl.BlockSpec(memory_space=pltpu.SMEM)] *...  17.7 us
    pallas_call x1, Pallas kernels, spread_rows(): pl.pallas_call(kernel, grid_spec=pltpu.PrefetchScalarGridSpec(num_scalar_...  8.28 us
  transfers between devices with their start and end apart: 37, of which 21 were waited for; matrix products, arithmetic and copies ran while one was open for 3% of the time, Pallas kernels for 37%

profile of v3, /device:TPU:0, one launch (start us, length us, event | category | flops | bytes accessed | tf_op | source)
XLA Modules:
  0.0 237.5 jit_solution(8127890203583728901)
XLA Ops:
  2.6 6.3 %all-to-all-start = ((bf16[4,64,1024]{2,1,0:T(8,128)(2,1)}), bf16[4,64,1024]{2,1,0:T(8,128)(2,1)S(1)}, u32[]{:S(2)}, u32[]{:S(2)}) async-start(bf16[4,64,1024]{2,1,0:T(8,128)(2,1)} %broadcast_in_dim.16), calls=%async_computation | async-start | bytes 1048576 | tf_op jit(solution)/shard_map/all_to_all | solution.py:26
  8.9 5.9 %pick_rows.1.refs_0_.picked_ref.refs_6_ = bf16[512,1024]{1,0:T(8,128)(2,1)} custom-call(bf16[4096,1024]{1,0:T(8,128)(2,1)} %base_ref.7, s32[1,512]{1,0:T(1,128)} %offset_ref.9), custom_call_target="tpu_custom_call" | custom-call | flops 1024 | bytes 1024 | tf_op jit(solution)/shard_map/pick_rows/pallas_call | solution.py:126
  15.4 7.2 %attend.1 = (bf16[512,1024]{1,0:T(8,128)(2,1)}, bf16[3,512,256]{2,1,0:T(8,128)(2,1)}, bf16[4,512,512]{2,1,0:T(8,128)(2,1)}, bf16[4,512,256]{2,1,0:T(8,128)(2,1)}) custom-call(bf16[512,1024]{1,0:T(8,128)(2,1)} %pick_rows.1.refs_0_.picked_ref.refs_6_, bf16[1,1024]{1,0:T(2,128)(2,1)} %broadcast_in_dim.17.refs_1_.gain_ref, bf16[3,1024,256]{2,1,0:T(8,128)(2,1)} %weight_ref.1, ...), custom_call_target="tpu_custom_call" | custom-call | flops 1024 | bytes 1024 | tf_op jit(solution)/shard_map/attend/pallas_call | solution.py:86
  24.9 4.4 %all-to-all-start.1 = ((bf16[4,512,256]{2,1,0:T(8,128)(2,1)}), bf16[4,512,256]{2,1,0:T(8,128)(2,1)S(1)}, u32[]{:S(2)}, u32[]{:S(2)}) async-start(bf16[4,512,256]{2,1,0:T(8,128)(2,1)} %get-tuple-element.155), calls=%async_computation.1 | async-start | bytes 2097152 | tf_op jit(solution)/shard_map/all_to_all | solution.py:26
  29.3 6.0 %pick_only.1.rows_ref = bf16[512,1024]{1,0:T(8,128)(2,1)} custom-call(bf16[4096,1024]{1,0:T(8,128)(2,1)} %base_ref.8, s32[1,512]{1,0:T(1,128)} %offset_ref.9), custom_call_target="tpu_custom_call" | custom-call | flops 1024 | bytes 1024 | tf_op jit(solution)/shard_map/pick_only/pallas_call | solution.py:179
  38.0 2.6 %score_sums.1.square_ref = f32[1,128]{1,0:T(1,128)} custom-call(s32[1]{0:T(128)} %bitcast.1.mine_ref.refs_1_.part_ref, bf16[4096,1024]{1,0:T(8,128)(2,1)} %base_ref.7, bf16[1,1024]{1,0:T(2,128)(2,1)} %broadcast_in_dim.18.router_ref), custom_call_target="tpu_custom_call" | custom-call | flops 1024 | bytes 1024 | tf_op jit(solution)/shard_map/score_sums/pallas_call | solution.py:146
  41.2 5.1 %act_grads.1 = (f32[512,1]{1,0:T(8,128)}, f32[1,128]{1,0:T(1,128)}, bf16[512,1024]{1,0:T(8,128)(2,1)}, f32[512,1024]{1,0:T(8,128)}) custom-call(bf16[512,1024]{1,0:T(8,128)(2,1)} %pick_rows.1.refs_0_.picked_ref.refs_6_, bf16[1,1024]{1,0:T(2,128)(2,1)} %broadcast_in_dim.18.router_ref, bf16[512,1024]{1,0:T(8,128)(2,1)} %pick_only.1.rows_ref, ...), custom_call_target="tpu_custom_call" | custom-call | flops 1024 | bytes 1024 | tf_op jit(solution)/shard_map/act_grads/pallas_call | solution.py:388
  46.3 7.8 %all-to-all-done.1.refs_2_.heads_ref = bf16[4,512,256]{2,1,0:T(8,128)(2,1)S(1)} async-done(((bf16[4,512,256]{2,1,0:T(8,128)(2,1)}), bf16[4,512,256]{2,1,0:T(8,128)(2,1)S(1)}, u32[]{:S(2)}, u32[]{:S(2)}) %all-to-all-start.1) | async-done | bytes 1048608 | tf_op jit(solution)/shard_map/all_to_all | solution.py:26
  55.1 10.5 %feed_forward.1 = (f32[128,1024]{1,0:T(8,128)}, bf16[512,1024]{1,0:T(8,128)(2,1)}, bf16[512,1024]{1,0:T(8,128)(2,1)}, bf16[512,1024]{1,0:T(8,128)(2,1)}, bf16[51...) custom-call(s32[1]{0:T(128)} %bitcast.refs_0_.part_ref, ...), custom_call_target="tpu_custom_call" | custom-call | flops 1024 | bytes 1024 | tf_op jit(solution)/shard_map/feed_forward/pallas_call | solution.py:86
  65.7 4.6 %all-to-all-start.2 = ((bf16[4,512,256]{2,1,0:T(8,128)(2,1)}), bf16[4,512,256]{2,1,0:T(8,128)(2,1)}, u32[]{:S(2)}, u32[]{:S(2)}) async-start(bf16[4,512,256]{2,1,0:T(8,128)(2,1)} %get-tuple-element.170), calls=%async_computation.2 | async-start | bytes 2097152 | tf_op jit(solution)/shard_map/all_to_all | solution.py:26
  75.3 3.9 %core_grads.1 = (bf16[2,768,1024]{2,1,0:T(8,128)(2,1)S(1)}, bf16[512,1024]{1,0:T(8,128)(2,1)S(1)}, bf16[512,1024]{1,0:T(8,128)(2,1)S(1)}, bf16[256,1024]{1,0:T(8,128)(2,1)S(1)}, bf16[256,1024]{1,0:T(8,128)(2,1)S(1)}) custom-call(s32[1]{0:T(128)} %bitcast.refs_0_.part_ref, bf16[512,1024]{1,0:T(8,128)(2,1)S(1)} %copy-done.11, bf16[512,1024]{1,0:T(8,128)(2,1)S(1)} %copy-done.6, ...), custom_call_target="tpu_custom_call" | custom-call | flops 1024 | bytes 1024 | tf_op jit(solution)/shard_map/core_grads/pallas_call | solution.py:604
  80.2 2.2 convolution_convert_fusion
  82.5 1.6 collective-permute-done.4.refs_1_
  88.5 6.9 %all-to-all-done.2.head_ref = bf16[4,512,256]{2,1,0:T(8,128)(2,1)} async-done(((bf16[4,512,256]{2,1,0:T(8,128)(2,1)}), bf16[4,512,256]{2,1,0:T(8,128)(2,1)}, u32[]{:S(2)}, u32[]{:S(2)}) %all-to-all-start.2) | async-done | bytes 1048608 | tf_op jit(solution)/shard_map/all_to_all | solution.py:26
  95.4 4.2 %all-to-all-start.3 = ((bf16[4,128,1024]{2,1,0:T(8,128)(2,1)}), bf16[4,128,1024]{2,1,0:T(8,128)(2,1)}, u32[]{:S(2)}, u32[]{:S(2)}) async-start(bf16[4,128,1024]{2,1,0:T(8,128)(2,1)} %bitcast.33), calls=%async_computation.3 | async-start | bytes 2097152 | tf_op jit(solution)/shard_map/all_to_all | solution.py:26
  100.2 1.5 collective-permute-start.7
  101.8 1.6 copy-done.7
  104.6 6.7 %attend_back.1 = (bf16[3,512,256]{2,1,0:T(8,128)(2,1)S(1)}, f32[1,1024]{1,0:T(1,128)S(1)}, bf16[512,1024]{1,0:T(8,128)(2,1)}) custom-call(bf16[4,512,256]{2,1,0:T(8,128)(2,1)} %all-to-all-done.2.head_ref, bf16[3,512,256]{2,1,0:T(8,128)(2,1)S(1)} %copy-done.16, bf16[4,512,512]{2,1,0:T(8,128)(2,1)S(1)} %copy-done.7, bf16[3,1024,256]{2,1,0:T(8,128)(2,1)S(1)} %copy-done.5, ...), custom_call_target="tpu_custom_call" | custom-call | flops 1024 | bytes 1024 | tf_op jit(solution)/shard_map/attend_back/pallas_call | solution.py:468
  112.8 3.7 %qkv_part.1.rows_ref = bf16[768,1024]{1,0:T(8,128)(2,1)} custom-call(bf16[512,1024]{1,0:T(8,128)(2,1)} %get-tuple-element.191.low_ref, bf16[3,512,256]{2,1,0:T(8,128)(2,1)} %copy-done.20), custom_call_target="tpu_custom_call" | custom-call | flops 1024 | bytes 1024 | tf_op jit(solution)/shard_map/qkv_part/pallas_call | solution.py:532
  116.5 2.0 collective-permute-done.6.refs_0_
  118.8 1.7 halving_sums.3
  121.4 3.5 %all-to-all-done.3.terms_ref = bf16[4,128,1024]{2,1,0:T(8,128)(2,1)} async-done(((bf16[4,128,1024]{2,1,0:T(8,128)(2,1)}), bf16[4,128,1024]{2,1,0:T(8,128)(2,1)}, u32[]{:S(2)}, u32[]{:S(2)}) %all-to-all-start.3) | async-done | bytes 1048608 | tf_op jit(solution)/shard_map/all_to_all | solution.py:26
  124.9 3.8 %all-to-all-start.4 = ((bf16[4,128,1024]{2,1,0:T(8,128)(2,1)}), bf16[4,128,1024]{2,1,0:T(8,128)(2,1)S(1)}, u32[]{:S(2)}, u32[]{:S(2)}) async-start(bf16[4,128,1024]{2,1,0:T(8,128)(2,1)} %bitcast.5), calls=%async_computation.4 | async-start | bytes 2097152 | tf_op jit(solution)/shard_map/all_to_all | solution.py:26
  128.7 1.6 collective-permute-start.9
  130.8 2.6 %finish_rows.1 = (bf16[128,1024]{1,0:T(8,128)(2,1)}, f32[128,1]{1,0:T(8,128)}, f32[4,1024]{1,0:T(4,128)}) custom-call(s32[1]{0:T(128)} %bitcast.1.mine_ref.refs_1_.part_ref, bf16[4,128,1024]{2,1,0:T(8,128)(2,1)} %all-to-all-done.3.terms_ref, bf16[512,1024]{1,0:T(8,128)(2,1)} %pick_rows.1.refs_0_.picked_ref.refs_6_, f32[512,1]{1,0:T(8,128)} %get-tuple-element.212.gating_ref, ...), custom_call_target="tpu_custom_call" | custom-call | flops 1024 | bytes 30000000 | tf_op jit(solution)/shard_map/finish_rows/pallas_call | solution.py:839
  133.5 6.9 %collective-permute-done.9.a_got = bf16[192,1024]{1,0:T(8,128)(2,1)} collective-permute-done((bf16[192,1024]{1,0:T(8,128)(2,1)S(1)}, bf16[192,1024]{1,0:T(8,128)(2,1)}, u32[]{:S(2)}, u32[]{:S(2)}) %collective-permute-start.9) | collective-permute-done | bytes 393248 | tf_op jit(solution)/shard_map/ppermute | solution.py:22
  141.6 2.8 %owned_sums.1 = (bf16[128,1024]{1,0:T(8,128)(2,1)}, bf16[128,1024]{1,0:T(8,128)(2,1)}, bf16[4,168,1024]{2,1,0:T(8,128)(2,1)}) custom-call(bf16[2,192,1024]{2,1,0:T(8,128)(2,1)} %copy-done.19, bf16[192,1024]{1,0:T(8,128)(2,1)} %collective-permute-done.9.a_got, bf16[192,1024]{1,0:T(8,128)(2,1)} %collective-permute-done.10.b_got, ...), custom_call_target="tpu_custom_call" | custom-call | flops 1024 | bytes 1024 | tf_op jit(solution)/shard_map/owned_sums/pallas_call | solution.py:669
  146.6 3.2 %core_sums.1 = (bf16[384,1024]{1,0:T(8,128)(2,1)}, bf16[384,1024]{1,0:T(8,128)(2,1)}) custom-call(bf16[768,1024]{1,0:T(8,128)(2,1)} %qkv_part.1.rows_ref, bf16[768,1024]{1,0:T(8,128)(2,1)} %copy-done.30), custom_call_target="tpu_custom_call" | custom-call | flops 1024 | bytes 1024 | tf_op jit(solution)/shard_map/core_sums/pallas_call | solution.py:688
  149.8 2.4 %collective-permute-done.11.refs_1_ = bf16[128,1024]{1,0:T(8,128)(2,1)S(1)} collective-permute-done((bf16[128,1024]{1,0:T(8,128)(2,1)}, bf16[128,1024]{1,0:T(8,128)(2,1)S(1)}, u32[]{:S(2)}, u32[]{:S(2)}) %collective-permute-start.11) | collective-permute-done | bytes 262176 | tf_op jit(solution)/shard_map/ppermute | solution.py:22
  152.7 2.4 %all-to-all-done.4.terms_ref = bf16[4,128,1024]{2,1,0:T(8,128)(2,1)S(1)} async-done(((bf16[4,128,1024]{2,1,0:T(8,128)(2,1)}), bf16[4,128,1024]{2,1,0:T(8,128)(2,1)S(1)}, u32[]{:S(2)}, u32[]{:S(2)}) %all-to-all-start.4) | async-done | bytes 1048608 | tf_op jit(solution)/shard_map/all_to_all | solution.py:26
  155.1 3.5 %all-to-all-start.5 = ((bf16[4,168,1024]{2,1,0:T(8,128)(2,1)}), bf16[4,168,1024]{2,1,0:T(8,128)(2,1)S(1)}, u32[]{:S(2)}, u32[]{:S(2)}) async-start(bf16[4,168,1024]{2,1,0:T(8,128)(2,1)} %get-tuple-element.231), calls=%async_computation.5 | async-start | bytes 2752512 | tf_op jit(solution)/shard_map/all_to_all | solution.py:26
  159.3 1.5 collective-permute-start.15
  162.8 2.6 %finish_input.1.piece_ref = bf16[4,128,1024]{2,1,0:T(8,128)(2,1)} custom-call(s32[1]{0:T(128)} %bitcast.1.mine_ref.refs_1_.part_ref, bf16[4,128,1024]{2,1,0:T(8,128)(2,1)} %copy-done.27, bf16[512,1024]{1,0:T(8,128)(2,1)} %pick_only.1.rows_ref, f32[128,1]{1,0:T(8,128)} %get-tuple-element.233.score_ref, bf16[1,1024]{1,0:T(2,128)(2,1)} %broadcast_in_dim.18.router_ref), custom_call_target="tpu_custom_call" | custom-call | flops 1024 | bytes 1024 | tf_op jit(solution)/shard_map/finish_input/pallas_call | solution.py:874
  165.3 3.6 %merge_rows.3.rest_0_ = bf16[4096,1024]{1,0:T(8,128)(2,1)} custom-call(s32[1]{0:T(128)} %bitcast.1.mine_ref.refs_1_.part_ref, bf16[4096,1024]{1,0:T(8,128)(2,1)} %base_ref.8, s32[1,512]{1,0:T(1,128)} %offset_ref.9, bf16[4,128,1024]{2,1,0:T(8,128)(2,1)} %finish_input.1.piece_ref), custom_call_target="tpu_custom_call" | custom-call | flops 1024 | bytes 1024 | tf_op jit(solution)/shard_map/merge_rows/pallas_call | solution.py:223
  169.0 3.4 %collective-permute-done.14.refs_3_ = bf16[128,1024]{1,0:T(8,128)(2,1)} collective-permute-done((bf16[128,1024]{1,0:T(8,128)(2,1)S(1)}, bf16[128,1024]{1,0:T(8,128)(2,1)}, u32[]{:S(2)}, u32[]{:S(2)}) %collective-permute-start.14) | collective-permute-done | bytes 262176 | tf_op jit(solution)/shard_map/ppermute | solution.py:22
  172.6 2.9 %gather_blocks.1 = (bf16[512,1024]{1,0:T(8,128)(2,1)}, bf16[512,1024]{1,0:T(8,128)(2,1)}) custom-call(bf16[128,1024]{1,0:T(8,128)(2,1)} %get-tuple-element.235.refs_0_, bf16[128,1024]{1,0:T(8,128)(2,1)} %copy-done.37, bf16[128,1024]{1,0:T(8,128)(2,1)} %collective-permute-done.13.refs_2_, bf16[128,1024]{1,0:T(8,128)(2,1)} %collective-permute-done.14.refs_3_, ...), custom_call_target="tpu_custom_call" | custom-call | flops 1024 | bytes 1024 | tf_op jit(solution)/shard_map/gather_blocks/pallas_call | solution.py:724
  176.0 1.5 collective-permute-start.19
  181.6 8.3 %spread_rows.1 = (f32[1024,1024]{1,0:T(8,128)}, f32[1024,1024]{1,0:T(8,128)}) custom-call(s32[8]{0:T(128)} %stack.79.down_index, s32[8]{0:T(128)} %stack.80.up_index.index_ref, bf16[4,128,1024]{2,1,0:T(8,128)(2,1)} %bitcast.29, bf16[4,128,1024]{2,1,0:T(8,128)(2,1)} %bitcast.31, bf16[4,128,1024]{2,1,0:T(8,128)(2,1)} %bitcast.30, bf16[4,128,1024]{2,1,0:T(8,128)(2,1)} %bitcast.32), custom_call_target="tpu_custom_call" | custom-call | flops 1024 | bytes 1024 | tf_op jit(solution)/shard_map/spread_rows/pallas_call | solution.py:505
  189.9 1.6 all-to-all-done.5.got_ref.piece_ref
  191.5 4.2 %all-to-all-start.6 = ((bf16[4,128,1024]{2,1,0:T(8,128)(2,1)}), bf16[4,128,1024]{2,1,0:T(8,128)(2,1)}, u32[]{:S(2)}, u32[]{:S(2)}) async-start(bf16[4,128,1024]{2,1,0:T(8,128)(2,1)} %finish_input.1.piece_ref), calls=%async_computation.6 | async-start | bytes 2097152 | tf_op jit(solution)/shard_map/all_to_all | solution.py:26
  195.8 2.0 first_small.1.refs_0_
  198.4 1.5 collective-permute-start.21
  199.9 3.2 %lane_sums.1 = (bf16[384,1024]{1,0:T(8,128)(2,1)}, bf16[384,1024]{1,0:T(8,128)(2,1)}) custom-call(bf16[384,1024]{1,0:T(8,128)(2,1)} %get-tuple-element.252.a_ref, bf16[384,1024]{1,0:T(8,128)(2,1)} %collective-permute-done.19.a_got, bf16[384,1024]{1,0:T(8,128)(2,1)} %get-tuple-element.253.b_ref, bf16[384,1024]{1,0:T(8,128)(2,1)} %collective-permute-done.20.b_got), custom_call_target="tpu_custom_call" | custom-call | flops 1024 | bytes 1024 | tf_op jit(solution)/shard_map/lane_sums/pallas_call | solution.py:704
  204.0 3.5 %collective-permute-done.23.refs_3_ = bf16[40,1024]{1,0:T(8,128)(2,1)S(1)} collective-permute-done((bf16[40,1024]{1,0:T(8,128)(2,1)S(1)}, bf16[40,1024]{1,0:T(8,128)(2,1)S(1)}, u32[]{:S(2)}, u32[]{:S(2)}) %collective-permute-start.23) | collective-permute-done | bytes 81952 | tf_op jit(solution)/shard_map/ppermute | solution.py:22
  211.7 9.0 %merge_rows.4 = bf16[4096,1024]{1,0:T(8,128)(2,1)} custom-call(s32[4]{0:T(128)} %pad_add_fusion.part_ref, bf16[4096,1024]{1,0:T(8,128)(2,1)} %base_ref.7, s32[1,512]{1,0:T(1,128)} %offset_ref.9, bf16[4,168,1024]{2,1,0:T(8,128)(2,1)} %copy-done.25), custom_call_target="tpu_custom_call" | custom-call | flops 1024 | bytes 1024 | tf_op jit(solution)/shard_map/merge_rows/pallas_call | solution.py:223
  221.5 2.3 last_small.1
  226.1 2.5 %spread_qkv.1 = f32[3,1024,256]{2,1,0:T(8,128)} custom-call(bf16[384,1024]{1,0:T(8,128)(2,1)S(1)} %copy-done.17, bf16[384,1024]{1,0:T(8,128)(2,1)S(1)} %collective-permute-done.24.a_got, bf16[384,1024]{1,0:T(8,128)(2,1)S(1)} %copy-done.18, bf16[384,1024]{1,0:T(8,128)(2,1)S(1)} %collective-permute-done.25.b_got), custom_call_target="tpu_custom_call" | custom-call | flops 1024 | bytes 1024 | tf_op jit(solution)/shard_map/spread_qkv/pallas_call | solution.py:555
  229.2 8.3 %merge_rows.5 = bf16[4096,1024]{1,0:T(8,128)(2,1)} custom-call(s32[3]{0:T(128)} %pad_add_fusion.1.part_ref, bf16[4096,1024]{1,0:T(8,128)(2,1)} %base_ref.8, s32[1,512]{1,0:T(1,128)} %offset_ref.9, bf16[4,128,1024]{2,1,0:T(8,128)(2,1)} %all-to-all-done.6.piece_ref, bf16[4096,1024]{1,0:T(8,128)(2,1)} %merge_rows.3.rest_0_), custom_call_target="tpu_custom_call", output_to_operand_aliasing={{}: (4, {})} | custom-call | flops 1024 | bytes 1024 | tf_op jit(solution)/shard_map/merge_rows/pallas_call | solution.py:223
  (156 shorter events, 45.0 us)
Async XLA Ops:
  2.6 20.8 %all-to-all-start = ((bf16[4,64,1024]{2,1,0:T(8,128)(2,1)}), bf16[4,64,1024]{2,1,0:T(8,128)(2,1)S(1)}, u32[]{:S(2)}, u32[]{:S(2)}) async-start(bf16[4,64,1024]{2,1,0:T(8,128)(2,1)} %broadcast_in_dim.16), calls=%async_computation | async-start | bytes 1048576 | tf_op jit(solution)/shard_map/all_to_all | solution.py:26
  23.4 12.9 %copy-start.26 = (bf16[4,64,1024]{2,1,0:T(8,128)(2,1)}, bf16[4,64,1024]{2,1,0:T(8,128)(2,1)S(1)}, u32[]{:S(2)}) copy-start(bf16[4,64,1024]{2,1,0:T(8,128)(2,1)S(1)} %all-to-all-done.refs_3_) | copy-start | bytes 1572868
  23.4 12.9 %collective-permute-start = (bf16[4,64,1024]{2,1,0:T(8,128)(2,1)S(1)}, bf16[4,64,1024]{2,1,0:T(8,128)(2,1)S(1)}, u32[]{:S(2)}, u32[]{:S(2)}) collective-permute-start(bf16[4,64,1024]{2,1,0:T(8,128)(2,1)S(1)} %all-to-all-done.refs_3_), channel_id=1, source_target_pairs={{0,8},{4,12},{8,0},{12,4},{16,24},{20,28},{24,16},{28,20},{1,9},{5... | collective-permute-start | bytes 1572872 | tf_op jit(solution)/shard_map/ppermute | solution.py:22
  24.9 29.3 %all-to-all-start.1 = ((bf16[4,512,256]{2,1,0:T(8,128)(2,1)}), bf16[4,512,256]{2,1,0:T(8,128)(2,1)S(1)}, u32[]{:S(2)}, u32[]{:S(2)}) async-start(bf16[4,512,256]{2,1,0:T(8,128)(2,1)} %get-tuple-element.155), calls=%async_computation.1 | async-start | bytes 2097152 | tf_op jit(solution)/shard_map/all_to_all | solution.py:26
  37.4 8.9 %collective-permute-start.1 = (bf16[2,4,64,1024]{3,2,1,0:T(8,128)(2,1)}, bf16[2,4,64,1024]{3,2,1,0:T(8,128)(2,1)S(1)}, u32[]{:S(2)}, u32[]{:S(2)}) collective-permute-start(bf16[2,4,64,1024]{3,2,1,0:T(8,128)(2,1)} %pad_maximum_fusion), channel_id=1, source_target_pairs={{0,4},{4,0},{8,12},{12,8},{16,20},{20,16},{24,28},{28,24},{1,5},{5... | collective-permute-start | bytes 3145736 | tf_op jit(solution)/shard_map/ppermute | solution.py:22
  65.7 29.7 %all-to-all-start.2 = ((bf16[4,512,256]{2,1,0:T(8,128)(2,1)}), bf16[4,512,256]{2,1,0:T(8,128)(2,1)}, u32[]{:S(2)}, u32[]{:S(2)}) async-start(bf16[4,512,256]{2,1,0:T(8,128)(2,1)} %get-tuple-element.170), calls=%async_computation.2 | async-start | bytes 2097152 | tf_op jit(solution)/shard_map/all_to_all | solution.py:26
  79.1 5.7 %collective-permute-start.2 = (bf16[512,1024]{1,0:T(8,128)(2,1)S(1)}, bf16[512,1024]{1,0:T(8,128)(2,1)S(1)}, u32[]{:S(2)}, u32[]{:S(2)}) collective-permute-start(bf16[512,1024]{1,0:T(8,128)(2,1)S(1)} %get-tuple-element.175), channel_id=1, source_target_pairs={{0,4},{4,0},{8,12},{12,8},{16,20},{20,16},{24,28},{28,24},{1,5},{5... | collective-permute-start | bytes 3145736 | tf_op jit(solution)/shard_map/ppermute | solution.py:22
  79.2 5.7 %collective-permute-start.3 = (bf16[512,1024]{1,0:T(8,128)(2,1)S(1)}, bf16[512,1024]{1,0:T(8,128)(2,1)S(1)}, u32[]{:S(2)}, u32[]{:S(2)}) collective-permute-start(bf16[512,1024]{1,0:T(8,128)(2,1)S(1)} %get-tuple-element.176), channel_id=1, source_target_pairs={{0,4},{4,0},{8,12},{12,8},{16,20},{20,16},{24,28},{28,24},{1,5},{5... | collective-permute-start | bytes 3145736 | tf_op jit(solution)/shard_map/ppermute | solution.py:22
  79.7 4.4 %collective-permute-start.4 = (bf16[256,1024]{1,0:T(8,128)(2,1)S(1)}, bf16[256,1024]{1,0:T(8,128)(2,1)S(1)}, u32[]{:S(2)}, u32[]{:S(2)}) collective-permute-start(bf16[256,1024]{1,0:T(8,128)(2,1)S(1)} %get-tuple-element.177), channel_id=1, source_target_pairs={{0,4},{4,0},{8,12},{12,8},{16,20},{20,16},{24,28},{28,24},{1,5},{5... | collective-permute-start | bytes 1572872 | tf_op jit(solution)/shard_map/ppermute | solution.py:22
  79.8 5.1 %collective-permute-start.5 = (bf16[256,1024]{1,0:T(8,128)(2,1)S(1)}, bf16[256,1024]{1,0:T(8,128)(2,1)S(1)}, u32[]{:S(2)}, u32[]{:S(2)}) collective-permute-start(bf16[256,1024]{1,0:T(8,128)(2,1)S(1)} %get-tuple-element.178), channel_id=1, source_target_pairs={{0,4},{4,0},{8,12},{12,8},{16,20},{20,16},{24,28},{28,24},{1,5},{5... | collective-permute-start | bytes 1572872 | tf_op jit(solution)/shard_map/ppermute | solution.py:22
  84.9 16.9 %copy-start.5 = (bf16[3,1024,256]{2,1,0:T(8,128)(2,1)S(1)}, bf16[3,1024,256]{2,1,0:T(8,128)(2,1)}, u32[]{:S(2)}) copy-start(bf16[3,1024,256]{2,1,0:T(8,128)(2,1)} %weight_ref.1) | copy-start | bytes 4718596
  88.5 13.3 %copy-start.2 = (bf16[512,1024]{1,0:T(8,128)(2,1)S(1)}, bf16[512,1024]{1,0:T(8,128)(2,1)}, u32[]{:S(2)}) copy-start(bf16[512,1024]{1,0:T(8,128)(2,1)} %pick_rows.1.refs_0_.picked_ref.refs_6_) | copy-start | bytes 3145732
  88.5 13.3 %copy-start.16 = (bf16[3,512,256]{2,1,0:T(8,128)(2,1)S(1)}, bf16[3,512,256]{2,1,0:T(8,128)(2,1)}, u32[]{:S(2)}) copy-start(bf16[3,512,256]{2,1,0:T(8,128)(2,1)} %get-tuple-element.193.qkv_ref) | copy-start | bytes 2359300
  88.5 13.3 %copy-start.21 = (bf16[1,1024]{1,0:T(2,128)(2,1)S(1)}, bf16[1,1024]{1,0:T(2,128)(2,1)}, u32[]{:S(2)}) copy-start(bf16[1,1024]{1,0:T(2,128)(2,1)} %broadcast_in_dim.17.refs_1_.gain_ref) | copy-start | bytes 6148
  95.4 29.5 %all-to-all-start.3 = ((bf16[4,128,1024]{2,1,0:T(8,128)(2,1)}), bf16[4,128,1024]{2,1,0:T(8,128)(2,1)}, u32[]{:S(2)}, u32[]{:S(2)}) async-start(bf16[4,128,1024]{2,1,0:T(8,128)(2,1)} %bitcast.33), calls=%async_computation.3 | async-start | bytes 2097152 | tf_op jit(solution)/shard_map/all_to_all | solution.py:26
  99.6 18.9 %collective-permute-start.6 = (bf16[384,1024]{1,0:T(8,128)(2,1)}, bf16[384,1024]{1,0:T(8,128)(2,1)}, u32[]{:S(2)}, u32[]{:S(2)}) collective-permute-start(bf16[384,1024]{1,0:T(8,128)(2,1)} %copy-done.24), channel_id=1, source_target_pairs={{0,8},{4,12},{8,0},{12,4},{16,24},{20,28},{24,16},{28,20},{1,9},{5... | collective-permute-start | bytes 2359304 | tf_op jit(solution)/shard_map/ppermute | solution.py:22
  100.2 18.5 %collective-permute-start.7 = (bf16[384,1024]{1,0:T(8,128)(2,1)}, bf16[384,1024]{1,0:T(8,128)(2,1)}, u32[]{:S(2)}, u32[]{:S(2)}) collective-permute-start(bf16[384,1024]{1,0:T(8,128)(2,1)} %copy-done.23), channel_id=1, source_target_pairs={{0,16},{4,20},{8,24},{12,28},{16,0},{20,4},{24,8},{28,12},{1,17},{... | collective-permute-start | bytes 2359304 | tf_op jit(solution)/shard_map/ppermute | solution.py:22
  124.9 20.5 %collective-permute-start.8 = (bf16[768,1024]{1,0:T(8,128)(2,1)}, bf16[768,1024]{1,0:T(8,128)(2,1)S(1)}, u32[]{:S(2)}, u32[]{:S(2)}) collective-permute-start(bf16[768,1024]{1,0:T(8,128)(2,1)} %qkv_part.1.rows_ref), channel_id=1, source_target_pairs={{0,4},{4,0},{8,12},{12,8},{16,20},{20,16},{24,28},{28,24},{1,5},{5... | collective-permute-start | bytes 4718600 | tf_op jit(solution)/shard_map/ppermute | solution.py:22
  124.9 30.2 %all-to-all-start.4 = ((bf16[4,128,1024]{2,1,0:T(8,128)(2,1)}), bf16[4,128,1024]{2,1,0:T(8,128)(2,1)S(1)}, u32[]{:S(2)}, u32[]{:S(2)}) async-start(bf16[4,128,1024]{2,1,0:T(8,128)(2,1)} %bitcast.5), calls=%async_computation.4 | async-start | bytes 2097152 | tf_op jit(solution)/shard_map/all_to_all | solution.py:26
  128.7 11.7 %collective-permute-start.9 = (bf16[192,1024]{1,0:T(8,128)(2,1)S(1)}, bf16[192,1024]{1,0:T(8,128)(2,1)}, u32[]{:S(2)}, u32[]{:S(2)}) collective-permute-start(bf16[192,1024]{1,0:T(8,128)(2,1)S(1)} %get-tuple-element.209), channel_id=1, source_target_pairs={{0,16},{4,20},{8,24},{12,28},{16,0},{20,4},{24,8},{28,12},{1,17},{... | collective-permute-start | bytes 1179656 | tf_op jit(solution)/shard_map/ppermute | solution.py:22
  130.3 11.4 %collective-permute-start.10 = (bf16[192,1024]{1,0:T(8,128)(2,1)S(1)}, bf16[192,1024]{1,0:T(8,128)(2,1)}, u32[]{:S(2)}, u32[]{:S(2)}) collective-permute-start(bf16[192,1024]{1,0:T(8,128)(2,1)S(1)} %get-tuple-element.210), channel_id=1, source_target_pairs={{0,8},{4,12},{8,0},{12,4},{16,24},{20,28},{24,16},{28,20},{1,9},{5... | collective-permute-start | bytes 1179656 | tf_op jit(solution)/shard_map/ppermute | solution.py:22
  144.4 7.8 %collective-permute-start.11 = (bf16[128,1024]{1,0:T(8,128)(2,1)}, bf16[128,1024]{1,0:T(8,128)(2,1)S(1)}, u32[]{:S(2)}, u32[]{:S(2)}) collective-permute-start(bf16[128,1024]{1,0:T(8,128)(2,1)} %get-tuple-element.235.refs_0_), channel_id=1, source_target_pairs={{0,16},{4,20},{8,24},{12,28},{16,0},{20,4},{24,8},{28,12},{1,17},{... | collective-permute-start | bytes 786440 | tf_op jit(solution)/shard_map/ppermute | solution.py:22
  144.9 7.7 %collective-permute-start.12 = (bf16[128,1024]{1,0:T(8,128)(2,1)}, bf16[128,1024]{1,0:T(8,128)(2,1)}, u32[]{:S(2)}, u32[]{:S(2)}) collective-permute-start(bf16[128,1024]{1,0:T(8,128)(2,1)} %get-tuple-element.237.refs_4_), channel_id=1, source_target_pairs={{0,8},{4,12},{8,0},{12,4},{16,24},{20,28},{24,16},{28,20},{1,9},{5... | collective-permute-start | bytes 786440 | tf_op jit(solution)/shard_map/ppermute | solution.py:22
  152.2 13.1 %copy-start.37 = (bf16[128,1024]{1,0:T(8,128)(2,1)}, bf16[128,1024]{1,0:T(8,128)(2,1)S(1)}, u32[]{:S(2)}) copy-start(bf16[128,1024]{1,0:T(8,128)(2,1)S(1)} %collective-permute-done.11.refs_1_) | copy-start | bytes 786436
  155.1 36.4 %all-to-all-start.5 = ((bf16[4,168,1024]{2,1,0:T(8,128)(2,1)}), bf16[4,168,1024]{2,1,0:T(8,128)(2,1)S(1)}, u32[]{:S(2)}, u32[]{:S(2)}) async-start(bf16[4,168,1024]{2,1,0:T(8,128)(2,1)} %get-tuple-element.231), calls=%async_computation.5 | async-start | bytes 2752512 | tf_op jit(solution)/shard_map/all_to_all | solution.py:26
  158.7 10.3 %collective-permute-start.13 = (bf16[128,1024]{1,0:T(8,128)(2,1)S(1)}, bf16[128,1024]{1,0:T(8,128)(2,1)}, u32[]{:S(2)}, u32[]{:S(2)}) collective-permute-start(bf16[128,1024]{1,0:T(8,128)(2,1)S(1)} %copy-done.35), channel_id=1, source_target_pairs={{0,8},{4,12},{8,0},{12,4},{16,24},{20,28},{24,16},{28,20},{1,9},{5... | collective-permute-start | bytes 786440 | tf_op jit(solution)/shard_map/ppermute | solution.py:22
  159.3 9.7 %collective-permute-start.15 = (bf16[128,1024]{1,0:T(8,128)(2,1)S(1)}, bf16[128,1024]{1,0:T(8,128)(2,1)}, u32[]{:S(2)}, u32[]{:S(2)}) collective-permute-start(bf16[128,1024]{1,0:T(8,128)(2,1)S(1)} %copy-done.36), channel_id=1, source_target_pairs={{0,16},{4,20},{8,24},{12,28},{16,0},{20,4},{24,8},{28,12},{1,17},{... | collective-permute-start | bytes 786440 | tf_op jit(solution)/shard_map/ppermute | solution.py:22
  160.8 11.6 %collective-permute-start.14 = (bf16[128,1024]{1,0:T(8,128)(2,1)S(1)}, bf16[128,1024]{1,0:T(8,128)(2,1)}, u32[]{:S(2)}, u32[]{:S(2)}) collective-permute-start(bf16[128,1024]{1,0:T(8,128)(2,1)S(1)} %collective-permute-done.11.refs_1_), channel_id=1, source_target_pairs={{0,8},{4,12},{8,0},{12,4},{16,24},{20,28},{24,16},{28,20},{1,9},{5... | collective-permute-start | bytes 786440 | tf_op jit(solution)/shard_map/ppermute | solution.py:22
  162.3 10.4 %collective-permute-start.16 = (bf16[128,1024]{1,0:T(8,128)(2,1)}, bf16[128,1024]{1,0:T(8,128)(2,1)}, u32[]{:S(2)}, u32[]{:S(2)}) collective-permute-start(bf16[128,1024]{1,0:T(8,128)(2,1)} %collective-permute-done.12.refs_5_), channel_id=1, source_target_pairs={{0,16},{4,20},{8,24},{12,28},{16,0},{20,4},{24,8},{28,12},{1,17},{... | collective-permute-start | bytes 786440 | tf_op jit(solution)/shard_map/ppermute | solution.py:22
  175.5 4.7 %collective-permute-start.17 = (bf16[512,1024]{1,0:T(8,128)(2,1)}, bf16[512,1024]{1,0:T(8,128)(2,1)S(1)}, u32[]{:S(2)}, u32[]{:S(2)}) collective-permute-start(bf16[512,1024]{1,0:T(8,128)(2,1)} %get-tuple-element.246), channel_id=1, source_target_pairs={{0,4},{4,0},{8,12},{12,8},{16,20},{20,16},{24,28},{28,24},{1,5},{5... | collective-permute-start | bytes 3145736 | tf_op jit(solution)/shard_map/ppermute | solution.py:22
  175.5 4.7 %collective-permute-start.18 = (bf16[512,1024]{1,0:T(8,128)(2,1)}, bf16[512,1024]{1,0:T(8,128)(2,1)S(1)}, u32[]{:S(2)}, u32[]{:S(2)}) collective-permute-start(bf16[512,1024]{1,0:T(8,128)(2,1)} %get-tuple-element.247), channel_id=1, source_target_pairs={{0,4},{4,0},{8,12},{12,8},{16,20},{20,16},{24,28},{28,24},{1,5},{5... | collective-permute-start | bytes 3145736 | tf_op jit(solution)/shard_map/ppermute | solution.py:22
  176.0 22.3 %collective-permute-start.19 = (bf16[384,1024]{1,0:T(8,128)(2,1)}, bf16[384,1024]{1,0:T(8,128)(2,1)}, u32[]{:S(2)}, u32[]{:S(2)}) collective-permute-start(bf16[384,1024]{1,0:T(8,128)(2,1)} %get-tuple-element.252.a_ref), channel_id=1, source_target_pairs={{0,16},{4,20},{8,24},{12,28},{16,0},{20,4},{24,8},{28,12},{1,17},{... | collective-permute-start | bytes 2359304 | tf_op jit(solution)/shard_map/ppermute | solution.py:22
  177.6 20.8 %collective-permute-start.20 = (bf16[384,1024]{1,0:T(8,128)(2,1)}, bf16[384,1024]{1,0:T(8,128)(2,1)}, u32[]{:S(2)}, u32[]{:S(2)}) collective-permute-start(bf16[384,1024]{1,0:T(8,128)(2,1)} %get-tuple-element.253.b_ref), channel_id=1, source_target_pairs={{0,8},{4,12},{8,0},{12,4},{16,24},{20,28},{24,16},{28,20},{1,9},{5... | collective-permute-start | bytes 2359304 | tf_op jit(solution)/shard_map/ppermute | solution.py:22
  191.5 37.2 %all-to-all-start.6 = ((bf16[4,128,1024]{2,1,0:T(8,128)(2,1)}), bf16[4,128,1024]{2,1,0:T(8,128)(2,1)}, u32[]{:S(2)}, u32[]{:S(2)}) async-start(bf16[4,128,1024]{2,1,0:T(8,128)(2,1)} %finish_input.1.piece_ref), calls=%async_computation.6 | async-start | bytes 2097152 | tf_op jit(solution)/shard_map/all_to_all | solution.py:26
  197.8 5.2 %collective-permute-start.22 = (bf16[40,1024]{1,0:T(8,128)(2,1)}, bf16[40,1024]{1,0:T(8,128)(2,1)S(1)}, u32[]{:S(2)}, u32[]{:S(2)}) collective-permute-start(bf16[40,1024]{1,0:T(8,128)(2,1)} %first_small.1.refs_0_), channel_id=1, source_target_pairs={{0,8},{4,12},{8,0},{12,4},{16,24},{20,28},{24,16},{28,20},{1,9},{5... | collective-permute-start | bytes 245768 | tf_op jit(solution)/shard_map/ppermute | solution.py:22
  198.4 5.6 %collective-permute-start.21 = (bf16[40,1024]{1,0:T(8,128)(2,1)}, bf16[40,1024]{1,0:T(8,128)(2,1)S(1)}, u32[]{:S(2)}, u32[]{:S(2)}) collective-permute-start(bf16[40,1024]{1,0:T(8,128)(2,1)} %first_small.1.refs_0_), channel_id=1, source_target_pairs={{0,16},{4,20},{8,24},{12,28},{16,0},{20,4},{24,8},{28,12},{1,17},{... | collective-permute-start | bytes 245768 | tf_op jit(solution)/shard_map/ppermute | solution.py:22
  203.1 17.7 %copy-start.38 = (bf16[40,1024]{1,0:T(8,128)(2,1)}, bf16[40,1024]{1,0:T(8,128)(2,1)S(1)}, u32[]{:S(2)}) copy-start(bf16[40,1024]{1,0:T(8,128)(2,1)S(1)} %collective-permute-done.22.refs_1_) | copy-start | bytes 245764
  203.1 4.4 %collective-permute-start.23 = (bf16[40,1024]{1,0:T(8,128)(2,1)S(1)}, bf16[40,1024]{1,0:T(8,128)(2,1)S(1)}, u32[]{:S(2)}, u32[]{:S(2)}) collective-permute-start(bf16[40,1024]{1,0:T(8,128)(2,1)S(1)} %collective-permute-done.22.refs_1_), channel_id=1, source_target_pairs={{0,16},{4,20},{8,24},{12,28},{16,0},{20,4},{24,8},{28,12},{1,17},{... | collective-permute-start | bytes 245768 | tf_op jit(solution)/shard_map/ppermute | solution.py:22
  204.0 16.8 %copy-start.39 = (bf16[40,1024]{1,0:T(8,128)(2,1)}, bf16[40,1024]{1,0:T(8,128)(2,1)S(1)}, u32[]{:S(2)}) copy-start(bf16[40,1024]{1,0:T(8,128)(2,1)S(1)} %collective-permute-done.21.refs_2_) | copy-start | bytes 245764
  207.5 13.3 %copy-start.40 = (bf16[40,1024]{1,0:T(8,128)(2,1)}, bf16[40,1024]{1,0:T(8,128)(2,1)S(1)}, u32[]{:S(2)}) copy-start(bf16[40,1024]{1,0:T(8,128)(2,1)S(1)} %collective-permute-done.23.refs_3_) | copy-start | bytes 245764
  207.5 17.4 %collective-permute-start.24 = (bf16[384,1024]{1,0:T(8,128)(2,1)}, bf16[384,1024]{1,0:T(8,128)(2,1)S(1)}, u32[]{:S(2)}, u32[]{:S(2)}) collective-permute-start(bf16[384,1024]{1,0:T(8,128)(2,1)} %get-tuple-element.283.a_ref), channel_id=1, source_target_pairs={{0,8},{4,12},{8,0},{12,4},{16,24},{20,28},{24,16},{28,20},{1,9},{5... | collective-permute-start | bytes 2359304 | tf_op jit(solution)/shard_map/ppermute | solution.py:22
  209.0 17.1 %collective-permute-start.25 = (bf16[384,1024]{1,0:T(8,128)(2,1)}, bf16[384,1024]{1,0:T(8,128)(2,1)S(1)}, u32[]{:S(2)}, u32[]{:S(2)}) collective-permute-start(bf16[384,1024]{1,0:T(8,128)(2,1)} %get-tuple-element.285.b_ref), channel_id=1, source_target_pairs={{0,16},{4,20},{8,24},{12,28},{16,0},{20,4},{24,8},{28,12},{1,17},{... | collective-permute-start | bytes 2359304 | tf_op jit(solution)/shard_map/ppermute | solution.py:22
  209.5 1.3 collective-permute-start.26
  210.1 10.7 %collective-permute-start.27 = (bf16[40,1024]{1,0:T(8,128)(2,1)S(1)}, bf16[40,1024]{1,0:T(8,128)(2,1)}, u32[]{:S(2)}, u32[]{:S(2)}) collective-permute-start(bf16[40,1024]{1,0:T(8,128)(2,1)S(1)} %collective-permute-done.22.refs_1_), channel_id=1, source_target_pairs={{0,4},{4,0},{8,12},{12,8},{16,20},{20,16},{24,28},{28,24},{1,5},{5... | collective-permute-start | bytes 245768 | tf_op jit(solution)/shard_map/ppermute | solution.py:22
  210.6 10.2 %collective-permute-start.28 = (bf16[40,1024]{1,0:T(8,128)(2,1)S(1)}, bf16[40,1024]{1,0:T(8,128)(2,1)}, u32[]{:S(2)}, u32[]{:S(2)}) collective-permute-start(bf16[40,1024]{1,0:T(8,128)(2,1)S(1)} %collective-permute-done.21.refs_2_), channel_id=1, source_target_pairs={{0,4},{4,0},{8,12},{12,8},{16,20},{20,16},{24,28},{28,24},{1,5},{5... | collective-permute-start | bytes 245768 | tf_op jit(solution)/shard_map/ppermute | solution.py:22
  210.8 10.0 %collective-permute-start.29 = (bf16[40,1024]{1,0:T(8,128)(2,1)S(1)}, bf16[40,1024]{1,0:T(8,128)(2,1)S(1)}, u32[]{:S(2)}, u32[]{:S(2)}) collective-permute-start(bf16[40,1024]{1,0:T(8,128)(2,1)S(1)} %collective-permute-done.23.refs_3_), channel_id=1, source_target_pairs={{0,4},{4,0},{8,12},{12,8},{16,20},{20,16},{24,28},{28,24},{1,5},{5... | collective-permute-start | bytes 245768 | tf_op jit(solution)/shard_map/ppermute | solution.py:22
  211.7 14.4 %copy-start.17 = (bf16[384,1024]{1,0:T(8,128)(2,1)S(1)}, bf16[384,1024]{1,0:T(8,128)(2,1)}, u32[]{:S(2)}) copy-start(bf16[384,1024]{1,0:T(8,128)(2,1)} %get-tuple-element.283.a_ref) | copy-start | bytes 2359300
  211.7 14.4 %copy-start.18 = (bf16[384,1024]{1,0:T(8,128)(2,1)S(1)}, bf16[384,1024]{1,0:T(8,128)(2,1)}, u32[]{:S(2)}) copy-start(bf16[384,1024]{1,0:T(8,128)(2,1)} %get-tuple-element.285.b_ref) | copy-start | bytes 2359300
  (36 other events, 130.0 us)

commit v4 on v3

--- a/solution.py
+++ b/solution.py
@@ -100,14 +100,15 @@
 
 def pick_rows(base, offsets, ways):
     rows, width = base.shape
-    chunks = 2 * ways
+    chunks = ways
     block = rows // chunks
+    groups = block // GROUP
     sub = 256
     sub_groups = sub // GROUP
 
     def kernel(base_ref, offset_ref, picked_ref, held, sems):
         def load(n):
-            part = pl.ds(n * block, block)
+            part = pl.ds(pl.multiple_of(n * block, block), block)
             return pltpu.make_async_copy(base_ref.at[part], held.at[part], sems.at[n])
 
         for n in range(chunks):
@@ -115,12 +116,18 @@
         local = lax.broadcasted_iota(jnp.int32, (sub, sub_groups), 0) - GROUP * lax.broadcasted_iota(
             jnp.int32, (sub, sub_groups), 1
         )
-        for n in range(chunks):
+
+        def step(n, carry):
             load(n).wait()
-            for s in range(n * block // sub, (n + 1) * block // sub):
-                to = slice(s * sub_groups, (s + 1) * sub_groups)
-                chosen = (local == offset_ref[:, to]).astype(F32).astype(BF)
-                picked_ref[to, :] = dot(chosen, held[s * sub : (s + 1) * sub, :], TN).astype(BF)
+            offsets = offset_ref[:, pl.ds(pl.multiple_of(n * groups, groups), groups)]
+            for s in range(block // sub):
+                chosen = (local == offsets[:, s * sub_groups : (s + 1) * sub_groups]).astype(F32).astype(BF)
+                rows_in = held[pl.ds(pl.multiple_of(n * block + s * sub, sub), sub), :]
+                to = pl.ds(pl.multiple_of(n * groups + s * sub_groups, sub_groups), sub_groups)
+                picked_ref[to, :] = dot(chosen, rows_in, TN).astype(BF)
+            return carry
+
+        lax.fori_loop(0, chunks, step, 0)
 
     whole = pl.BlockSpec(memory_space=pltpu.VMEM)
     return pl.pallas_call(
@@ -535,6 +542,7 @@
         out_specs=whole,
         out_shape=jax.ShapeDtypeStruct((3 * part_width, width), BF),
         cost_estimate=small_cost(),
+        compiler_params=pltpu.CompilerParams(vmem_limit_bytes=12 << 20),
         name="qkv_part",
     )(first_low, grads)
 
@@ -672,6 +680,7 @@
         out_specs=[whole] * 3,
         out_shape=[lane_shape, lane_shape, jax.ShapeDtypeStruct((ways, depth, width), BF)],
         cost_estimate=small_cost(),
+        compiler_params=pltpu.CompilerParams(vmem_limit_bytes=10 << 20),
         name="owned_sums",
     )(keep, got_a, got_b, fresh, small)
 
@@ -691,6 +700,7 @@
         out_specs=[whole] * 2,
         out_shape=[jax.ShapeDtypeStruct((third, width), BF)] * 2,
         cost_estimate=small_cost(),
+        compiler_params=pltpu.CompilerParams(vmem_limit_bytes=10 << 20),
         name="core_sums",
     )(rows, other)
 
@@ -707,6 +717,7 @@
         out_specs=[whole] * 2,
         out_shape=[jax.ShapeDtypeStruct(lane_a.shape, BF)] * 2,
         cost_estimate=small_cost(),
+        compiler_params=pltpu.CompilerParams(vmem_limit_bytes=12 << 20),
         name="lane_sums",
     )(lane_a, got_a, lane_b, got_b)
 
@@ -727,6 +738,7 @@
         out_specs=[whole] * 2,
         out_shape=[jax.ShapeDtypeStruct((count * wide, width), BF)] * 2,
         cost_estimate=small_cost(),
+        compiler_params=pltpu.CompilerParams(vmem_limit_bytes=10 << 20),
         name="gather_blocks",
     )(*blocks_a, *blocks_b)
 
@@ -761,6 +773,7 @@
         out_specs=whole,
         out_shape=jax.ShapeDtypeStruct((each + GAP, width), BF),
         cost_estimate=small_cost(),
+        compiler_params=pltpu.CompilerParams(vmem_limit_bytes=8 << 20),
         name="first_small",
     )(received)
 
@@ -791,6 +804,7 @@
         out_shape=[jax.ShapeDtypeStruct((count * each, width), F32)] + [jax.ShapeDtypeStruct((1, width), F32)] * (TERMS - 1)
         + [jax.ShapeDtypeStruct((1, 128), F32)],
         cost_estimate=small_cost(),
+        compiler_params=pltpu.CompilerParams(vmem_limit_bytes=10 << 20),
         name="last_small",
     )(index, *blocks)
 
@@ -886,6 +900,7 @@
         ),
         out_shape=jax.ShapeDtypeStruct((ways, own, width), BF),
         cost_estimate=small_cost(),
+        compiler_params=pltpu.CompilerParams(vmem_limit_bytes=8 << 20),
         name="finish_input",
     )(mine, terms, grad_rows, score, router)
 
@@ -1080,21 +1095,23 @@
         more, qkv_a, qkv_b = tie((more, qkv_a, qkv_b))
         blocks = blocks + more
         more = [swap(array, "dp", bit_y) for array in blocks]
-        more, qkv_a, qkv_b = tie((more, qkv_a, qkv_b))
+        fresh, blocks = tie((fresh, blocks))
+    output = merge_rows(tokens, route_offset, fresh, spots[: ways // 2])
+    if by_swaps:
+        more, output, qkv_a, qkv_b = tie((more, output, qkv_a, qkv_b))
         qkv_a_got, qkv_b_got = swap(qkv_a, "dp", bit_x), swap(qkv_b, "dp", bit_y)
         blocks = blocks + more
         more = [swap(array, "dp", 1) for array in blocks]
-        fresh, qkv_a, qkv_b, blocks = tie((fresh, qkv_a, qkv_b, blocks))
-    output = merge_rows(tokens, route_offset, fresh, spots)
+        fresh, blocks, qkv_a = tie((fresh, blocks, qkv_a))
+    output = merge_rows(tokens, route_offset, fresh, spots[ways // 2 :], output)
     if by_swaps:
         more, output = tie((more, output))
         out_grad, *small = last_small(blocks + more, gathered([bit_x, bit_y, 1]), shares)
-        qkv_a_got, qkv_b_got, out_grad = tie((qkv_a_got, qkv_b_got, out_grad))
+        input_rows, early, output, out_grad, small = tie((input_rows, early, output, out_grad, small))
+    input_grad = merge_rows(cotangent, route_offset, input_rows, spots[1:], early)
+    if by_swaps:
+        qkv_a_got, qkv_b_got, input_grad = tie((qkv_a_got, qkv_b_got, input_grad))
         qkv_grad = spread_qkv(qkv_a, qkv_a_got, qkv_b, qkv_b_got, qkv_weight.shape[2])
-        input_rows, early, out_grad, small, output, qkv_grad = tie(
-            (input_rows, early, out_grad, small, output, qkv_grad)
-        )
-    input_grad = merge_rows(cotangent, route_offset, input_rows, spots[1:], early)
     if not by_swaps:
         small = sum(joined_sums(fresh[k, own_rows:]) for k in range(ways))
         small = lax.psum(small, "dp")

time: 239 us -> 235 us (0.983)
  Pallas kernels: 107 us -> 96.1 us
  waiting for transfers between devices: 49.6 us -> 53.1 us
    ppermute x30, waiting for transfers between devices: 26.5 us -> 29.4 us  [swap(): return lax.ppermute(values, axis, [(i, i ^ bits) for i in range(size)])]
    pallas_call x1, Pallas kernels: 3.72 us -> 1.01 us  [qkv_part_of(): pl.pallas_call(kernel, in_specs=[whole] * 2, out_specs=whole, out_shape=j...]
    unnamed x94 -> x96, local copies, waits for them, and re-layouts: 18.2 us -> 19.5 us
    pallas_call x3 -> x4, Pallas kernels: 20.9 us -> 22 us  [merge_rows(): pl.pallas_call(kernel, grid_spec=grid_spec, out_shape=jax.ShapeDtypeStruc...]
  transfers between devices with their start and end apart: 37 -> 37, of which waited for: 21 -> 23; matrix products, arithmetic and copies ran while one was open for 3% -> 4% of each run, Pallas kernels for 37% -> 35%
where the time goes in v4:
time: 235 us; the launch traced here: 233 us
  Pallas kernels  96.1 us (41%)
  starting transfers between devices  53.8 us (23%)
  waiting for transfers between devices  53.1 us (23%)
  local copies, waits for them, and re-layouts  24 us (10%)
  other arithmetic  2.9 us (1%)
    all_to_all x7, starting transfers between devices, to_all(): return lax.all_to_all(blocks, 'tensor', 0, 0, tiled=True)  31 us
    ppermute x30, waiting for transfers between devices, swap(): return lax.ppermute(values, axis, [(i, i ^ bits) for i in range(size)])  29.4 us
    all_to_all x7, waiting for transfers between devices, to_all(): return lax.all_to_all(blocks, 'tensor', 0, 0, tiled=True)  23.7 us
    ppermute x30, starting transfers between devices, swap(): return lax.ppermute(values, axis, [(i, i ^ bits) for i in range(size)])  22.8 us
    pallas_call x4, Pallas kernels, merge_rows(): pl.pallas_call(kernel, grid_spec=grid_spec, out_shape=jax.ShapeDtypeStruc...  22 us
    unnamed x96, local copies, waits for them, and re-layouts  19.5 us
    pallas_call x2, Pallas kernels, staged(): pl.pallas_call(kernel, in_specs=[pl.BlockSpec(memory_space=pltpu.SMEM)] *...  17.7 us
    pallas_call x1, Pallas kernels, spread_rows(): pl.pallas_call(kernel, grid_spec=pltpu.PrefetchScalarGridSpec(num_scalar_...  8.29 us
  transfers between devices with their start and end apart: 37, of which 23 were waited for; matrix products, arithmetic and copies ran while one was open for 4% of the time, Pallas kernels for 35%

profile of v4, /device:TPU:0, one launch (start us, length us, event | category | flops | bytes accessed | tf_op | source)
XLA Modules:
  0.0 233.2 jit_solution(3983918740241363823)
XLA Ops:
  2.6 6.3 %all-to-all-start = ((bf16[4,64,1024]{2,1,0:T(8,128)(2,1)}), bf16[4,64,1024]{2,1,0:T(8,128)(2,1)S(1)}, u32[]{:S(2)}, u32[]{:S(2)}) async-start(bf16[4,64,1024]{2,1,0:T(8,128)(2,1)} %broadcast_in_dim.16), calls=%async_computation | async-start | bytes 1048576 | tf_op jit(solution)/shard_map/all_to_all | solution.py:26
  8.9 5.7 %pick_rows.1.refs_0_.picked_ref.refs_6_ = bf16[512,1024]{1,0:T(8,128)(2,1)} custom-call(bf16[4096,1024]{1,0:T(8,128)(2,1)} %base_ref.9, s32[1,512]{1,0:T(1,128)} %offset_ref.11), custom_call_target="tpu_custom_call" | custom-call | flops 1024 | bytes 1024 | tf_op jit(solution)/shard_map/pick_rows/pallas_call | solution.py:133
  15.2 7.2 %attend.1 = (bf16[512,1024]{1,0:T(8,128)(2,1)}, bf16[3,512,256]{2,1,0:T(8,128)(2,1)}, bf16[4,512,512]{2,1,0:T(8,128)(2,1)}, bf16[4,512,256]{2,1,0:T(8,128)(2,1)}) custom-call(bf16[512,1024]{1,0:T(8,128)(2,1)} %pick_rows.1.refs_0_.picked_ref.refs_6_, bf16[1,1024]{1,0:T(2,128)(2,1)} %broadcast_in_dim.17.refs_1_.gain_ref, bf16[3,1024,256]{2,1,0:T(8,128)(2,1)} %weight_ref.1, ...), custom_call_target="tpu_custom_call" | custom-call | flops 1024 | bytes 1024 | tf_op jit(solution)/shard_map/attend/pallas_call | solution.py:86
  23.4 1.5 collective-permute-start
  24.9 4.2 %all-to-all-start.1 = ((bf16[4,512,256]{2,1,0:T(8,128)(2,1)}), bf16[4,512,256]{2,1,0:T(8,128)(2,1)S(1)}, u32[]{:S(2)}, u32[]{:S(2)}) async-start(bf16[4,512,256]{2,1,0:T(8,128)(2,1)} %get-tuple-element.157), calls=%async_computation.1 | async-start | bytes 2097152 | tf_op jit(solution)/shard_map/all_to_all | solution.py:26
  29.1 6.0 %pick_only.1.rows_ref = bf16[512,1024]{1,0:T(8,128)(2,1)} custom-call(bf16[4096,1024]{1,0:T(8,128)(2,1)} %base_ref.10, s32[1,512]{1,0:T(1,128)} %offset_ref.11), custom_call_target="tpu_custom_call" | custom-call | flops 1024 | bytes 1024 | tf_op jit(solution)/shard_map/pick_only/pallas_call | solution.py:186
  38.0 2.6 %score_sums.1.square_ref = f32[1,128]{1,0:T(1,128)} custom-call(s32[1]{0:T(128)} %bitcast.1.mine_ref.refs_1_.part_ref, bf16[4096,1024]{1,0:T(8,128)(2,1)} %base_ref.9, bf16[1,1024]{1,0:T(2,128)(2,1)} %broadcast_in_dim.18.router_ref), custom_call_target="tpu_custom_call" | custom-call | flops 1024 | bytes 1024 | tf_op jit(solution)/shard_map/score_sums/pallas_call | solution.py:153
  41.2 5.1 %act_grads.1 = (f32[512,1]{1,0:T(8,128)}, f32[1,128]{1,0:T(1,128)}, bf16[512,1024]{1,0:T(8,128)(2,1)}, f32[512,1024]{1,0:T(8,128)}) custom-call(bf16[512,1024]{1,0:T(8,128)(2,1)} %pick_rows.1.refs_0_.picked_ref.refs_6_, bf16[1,1024]{1,0:T(2,128)(2,1)} %broadcast_in_dim.18.router_ref, bf16[512,1024]{1,0:T(8,128)(2,1)} %pick_only.1.rows_ref, ...), custom_call_target="tpu_custom_call" | custom-call | flops 1024 | bytes 1024 | tf_op jit(solution)/shard_map/act_grads/pallas_call | solution.py:395
  46.4 7.6 %all-to-all-done.1.refs_2_.heads_ref = bf16[4,512,256]{2,1,0:T(8,128)(2,1)S(1)} async-done(((bf16[4,512,256]{2,1,0:T(8,128)(2,1)}), bf16[4,512,256]{2,1,0:T(8,128)(2,1)S(1)}, u32[]{:S(2)}, u32[]{:S(2)}) %all-to-all-start.1) | async-done | bytes 1048608 | tf_op jit(solution)/shard_map/all_to_all | solution.py:26
  55.0 10.5 %feed_forward.1 = (f32[128,1024]{1,0:T(8,128)}, bf16[512,1024]{1,0:T(8,128)(2,1)}, bf16[512,1024]{1,0:T(8,128)(2,1)}, bf16[512,1024]{1,0:T(8,128)(2,1)}, bf16[51...) custom-call(s32[1]{0:T(128)} %bitcast.refs_0_.part_ref, ...), custom_call_target="tpu_custom_call" | custom-call | flops 1024 | bytes 1024 | tf_op jit(solution)/shard_map/feed_forward/pallas_call | solution.py:86
  65.5 4.6 %all-to-all-start.2 = ((bf16[4,512,256]{2,1,0:T(8,128)(2,1)}), bf16[4,512,256]{2,1,0:T(8,128)(2,1)}, u32[]{:S(2)}, u32[]{:S(2)}) async-start(bf16[4,512,256]{2,1,0:T(8,128)(2,1)} %get-tuple-element.172), calls=%async_computation.2 | async-start | bytes 2097152 | tf_op jit(solution)/shard_map/all_to_all | solution.py:26
  75.1 3.9 %core_grads.1 = (bf16[2,768,1024]{2,1,0:T(8,128)(2,1)S(1)}, bf16[512,1024]{1,0:T(8,128)(2,1)S(1)}, bf16[512,1024]{1,0:T(8,128)(2,1)S(1)}, bf16[256,1024]{1,0:T(8,128)(2,1)S(1)}, bf16[256,1024]{1,0:T(8,128)(2,1)S(1)}) custom-call(s32[1]{0:T(128)} %bitcast.refs_0_.part_ref, bf16[512,1024]{1,0:T(8,128)(2,1)S(1)} %copy-done.16, bf16[512,1024]{1,0:T(8,128)(2,1)S(1)} %copy-done.8, ...), custom_call_target="tpu_custom_call" | custom-call | flops 1024 | bytes 1024 | tf_op jit(solution)/shard_map/core_grads/pallas_call | solution.py:612
  80.0 2.2 convolution_convert_fusion
  82.2 1.6 collective-permute-done.4.refs_1_
  88.4 6.8 %all-to-all-done.2.head_ref = bf16[4,512,256]{2,1,0:T(8,128)(2,1)} async-done(((bf16[4,512,256]{2,1,0:T(8,128)(2,1)}), bf16[4,512,256]{2,1,0:T(8,128)(2,1)}, u32[]{:S(2)}, u32[]{:S(2)}) %all-to-all-start.2) | async-done | bytes 1048608 | tf_op jit(solution)/shard_map/all_to_all | solution.py:26
  95.2 4.2 %all-to-all-start.3 = ((bf16[4,128,1024]{2,1,0:T(8,128)(2,1)}), bf16[4,128,1024]{2,1,0:T(8,128)(2,1)}, u32[]{:S(2)}, u32[]{:S(2)}) async-start(bf16[4,128,1024]{2,1,0:T(8,128)(2,1)} %bitcast.32), calls=%async_computation.3 | async-start | bytes 2097152 | tf_op jit(solution)/shard_map/all_to_all | solution.py:26
  100.0 1.5 collective-permute-start.7
  101.6 1.6 copy-done.9
  104.4 5.8 %attend_back.1 = (bf16[3,512,256]{2,1,0:T(8,128)(2,1)S(1)}, f32[1,1024]{1,0:T(1,128)S(1)}, bf16[512,1024]{1,0:T(8,128)(2,1)S(1)}) custom-call(bf16[4,512,256]{2,1,0:T(8,128)(2,1)} %all-to-all-done.2.head_ref, bf16[3,512,256]{2,1,0:T(8,128)(2,1)S(1)} %copy-done.23, bf16[4,512,512]{2,1,0:T(8,128)(2,1)S(1)} %copy-done.9, bf16[3,1024,256]{2,1,0:T(8,128)(2,1)S(1)} %copy-done.7, ...), custom_call_target="tpu_custom_call" | custom-call | flops 1024 | bytes 1024 | tf_op jit(solution)/shard_map/attend_back/pallas_call | solution.py:475
  111.2 7.0 %collective-permute-done.6.refs_0_ = bf16[384,1024]{1,0:T(8,128)(2,1)S(1)} collective-permute-done((bf16[384,1024]{1,0:T(8,128)(2,1)}, bf16[384,1024]{1,0:T(8,128)(2,1)S(1)}, u32[]{:S(2)}, u32[]{:S(2)}) %collective-permute-start.6) | collective-permute-done | bytes 786464 | tf_op jit(solution)/shard_map/ppermute | solution.py:22
  120.3 4.4 %all-to-all-done.3.terms_ref = bf16[4,128,1024]{2,1,0:T(8,128)(2,1)} async-done(((bf16[4,128,1024]{2,1,0:T(8,128)(2,1)}), bf16[4,128,1024]{2,1,0:T(8,128)(2,1)}, u32[]{:S(2)}, u32[]{:S(2)}) %all-to-all-start.3) | async-done | bytes 1048608 | tf_op jit(solution)/shard_map/all_to_all | solution.py:26
  124.7 3.8 %all-to-all-start.4 = ((bf16[4,128,1024]{2,1,0:T(8,128)(2,1)}), bf16[4,128,1024]{2,1,0:T(8,128)(2,1)S(1)}, u32[]{:S(2)}, u32[]{:S(2)}) async-start(bf16[4,128,1024]{2,1,0:T(8,128)(2,1)} %bitcast.29), calls=%async_computation.4 | async-start | bytes 2097152 | tf_op jit(solution)/shard_map/all_to_all | solution.py:26
  129.1 1.5 collective-permute-start.9
  130.6 2.6 %finish_rows.1 = (bf16[128,1024]{1,0:T(8,128)(2,1)}, f32[128,1]{1,0:T(8,128)}, f32[4,1024]{1,0:T(4,128)}) custom-call(s32[1]{0:T(128)} %bitcast.1.mine_ref.refs_1_.part_ref, bf16[4,128,1024]{2,1,0:T(8,128)(2,1)} %all-to-all-done.3.terms_ref, bf16[512,1024]{1,0:T(8,128)(2,1)} %pick_rows.1.refs_0_.picked_ref.refs_6_, f32[512,1]{1,0:T(8,128)} %get-tuple-element.214.gating_ref, ...), custom_call_target="tpu_custom_call" | custom-call | flops 1024 | bytes 30000000 | tf_op jit(solution)/shard_map/finish_rows/pallas_call | solution.py:853
  133.3 7.1 %collective-permute-done.10.b_got = bf16[192,1024]{1,0:T(8,128)(2,1)} collective-permute-done((bf16[192,1024]{1,0:T(8,128)(2,1)}, bf16[192,1024]{1,0:T(8,128)(2,1)}, u32[]{:S(2)}, u32[]{:S(2)}) %collective-permute-start.10) | collective-permute-done | bytes 393248 | tf_op jit(solution)/shard_map/ppermute | solution.py:22
  143.7 1.6 collective-permute-start.11
  145.3 1.5 collective-permute-start.12
  146.8 2.8 %core_sums.1 = (bf16[384,1024]{1,0:T(8,128)(2,1)}, bf16[384,1024]{1,0:T(8,128)(2,1)}) custom-call(bf16[768,1024]{1,0:T(8,128)(2,1)S(1)} %qkv_part.1.rows_ref, bf16[768,1024]{1,0:T(8,128)(2,1)} %collective-permute-done.8.other_ref), custom_call_target="tpu_custom_call" | custom-call | flops 1024 | bytes 1024 | tf_op jit(solution)/shard_map/core_sums/pallas_call | solution.py:697
  149.5 1.9 collective-permute-done.11.refs_1_
  152.8 2.1 all-to-all-done.4.terms_ref
  154.9 3.5 %all-to-all-start.5 = ((bf16[4,168,1024]{2,1,0:T(8,128)(2,1)}), bf16[4,168,1024]{2,1,0:T(8,128)(2,1)S(1)}, u32[]{:S(2)}, u32[]{:S(2)}) async-start(bf16[4,168,1024]{2,1,0:T(8,128)(2,1)} %copy-done.12), calls=%async_computation.5 | async-start | bytes 2752512 | tf_op jit(solution)/shard_map/all_to_all | solution.py:26
  159.0 1.5 collective-permute-start.16
  160.6 1.5 collective-permute-start.13
  163.8 3.6 %merge_rows.4.rest_0_ = bf16[4096,1024]{1,0:T(8,128)(2,1)} custom-call(s32[1]{0:T(128)} %bitcast.1.mine_ref.refs_1_.part_ref, bf16[4096,1024]{1,0:T(8,128)(2,1)} %base_ref.10, s32[1,512]{1,0:T(1,128)} %offset_ref.11, bf16[4,128,1024]{2,1,0:T(8,128)(2,1)} %finish_input.1.piece_ref), custom_call_target="tpu_custom_call" | custom-call | flops 1024 | bytes 1024 | tf_op jit(solution)/shard_map/merge_rows/pallas_call | solution.py:230
  168.6 3.8 %collective-permute-done.13.refs_2_ = bf16[128,1024]{1,0:T(8,128)(2,1)} collective-permute-done((bf16[128,1024]{1,0:T(8,128)(2,1)}, bf16[128,1024]{1,0:T(8,128)(2,1)}, u32[]{:S(2)}, u32[]{:S(2)}) %collective-permute-start.13) | collective-permute-done | bytes 262176 | tf_op jit(solution)/shard_map/ppermute | solution.py:22
  177.5 1.5 collective-permute-start.19
  179.0 1.5 collective-permute-start.20
  181.8 8.3 %spread_rows.1 = (f32[1024,1024]{1,0:T(8,128)}, f32[1024,1024]{1,0:T(8,128)}) custom-call(s32[8]{0:T(128)} %stack.81.down_index, s32[8]{0:T(128)} %stack.82.up_index.index_ref, bf16[4,128,1024]{2,1,0:T(8,128)(2,1)} %bitcast.27, bf16[4,128,1024]{2,1,0:T(8,128)(2,1)} %bitcast.14.far_ref, bf16[4,128,1024]{2,1,0:T(8,128)(2,1)} %bitcast.28, ...), custom_call_target="tpu_custom_call" | custom-call | flops 1024 | bytes 1024 | tf_op jit(solution)/shard_map/spread_rows/pallas_call | solution.py:512
  191.3 4.2 %all-to-all-start.6 = ((bf16[4,128,1024]{2,1,0:T(8,128)(2,1)}), bf16[4,128,1024]{2,1,0:T(8,128)(2,1)}, u32[]{:S(2)}, u32[]{:S(2)}) async-start(bf16[4,128,1024]{2,1,0:T(8,128)(2,1)} %finish_input.1.piece_ref), calls=%async_computation.6 | async-start | bytes 2097152 | tf_op jit(solution)/shard_map/all_to_all | solution.py:26
  197.3 2.1 collective-permute-done.20.b_got
  199.4 2.2 lane_sums.1
  201.7 2.1 collective-permute-start.25
  204.3 5.1 %merge_rows.5.rest_0_ = bf16[4096,1024]{1,0:T(8,128)(2,1)} custom-call(s32[2]{0:T(128)} %pad_add_fusion.part_ref, bf16[4096,1024]{1,0:T(8,128)(2,1)} %base_ref.9, s32[1,512]{1,0:T(1,128)} %offset_ref.11, bf16[4,168,1024]{2,1,0:T(8,128)(2,1)} %copy-done.3), custom_call_target="tpu_custom_call" | custom-call | flops 1024 | bytes 1024 | tf_op jit(solution)/shard_map/merge_rows/pallas_call | solution.py:230
  209.4 1.6 collective-permute-start.28
  213.3 5.2 %merge_rows.6 = bf16[4096,1024]{1,0:T(8,128)(2,1)} custom-call(s32[2]{0:T(128)} %pad_add_fusion.1.part_ref, bf16[4096,1024]{1,0:T(8,128)(2,1)} %base_ref.9, s32[1,512]{1,0:T(1,128)} %offset_ref.11, bf16[4,168,1024]{2,1,0:T(8,128)(2,1)} %copy-done.3, bf16[4096,1024]{1,0:T(8,128)(2,1)} %merge_rows.5.rest_0_), custom_call_target="tpu_custom_call", output_to_operand_aliasing={{}: (4, {})} | custom-call | flops 1024 | bytes 1024 | tf_op jit(solution)/shard_map/merge_rows/pallas_call | solution.py:230
  218.6 1.6 last_small.1
  220.9 8.1 %merge_rows.7 = bf16[4096,1024]{1,0:T(8,128)(2,1)} custom-call(s32[3]{0:T(128)} %pad_add_fusion.2.part_ref, bf16[4096,1024]{1,0:T(8,128)(2,1)} %base_ref.10, s32[1,512]{1,0:T(1,128)} %offset_ref.11, bf16[4,128,1024]{2,1,0:T(8,128)(2,1)} %all-to-all-done.6.piece_ref, bf16[4096,1024]{1,0:T(8,128)(2,1)} %merge_rows.4.rest_0_), custom_call_target="tpu_custom_call", output_to_operand_aliasing={{}: (4, {})} | custom-call | flops 1024 | bytes 1024 | tf_op jit(solution)/shard_map/merge_rows/pallas_call | solution.py:230
  229.6 3.7 %spread_qkv.1 = f32[3,1024,256]{2,1,0:T(8,128)} custom-call(bf16[384,1024]{1,0:T(8,128)(2,1)S(1)} %get-tuple-element.295.a_ref, bf16[384,1024]{1,0:T(8,128)(2,1)S(1)} %collective-permute-done.28.a_got, bf16[384,1024]{1,0:T(8,128)(2,1)S(1)} %get-tuple-element.288.b_ref, bf16[384,1024]{1,0:T(8,128)(2,1)} %collective-permute-done.29.b_got), custom_call_target="tpu_custom_call" | custom-call | flops 1024 | bytes 1024 | tf_op jit(solution)/shard_map/spread_qkv/pallas_call | solution.py:563
  (160 shorter events, 45.7 us)
Async XLA Ops:
  2.6 20.8 %all-to-all-start = ((bf16[4,64,1024]{2,1,0:T(8,128)(2,1)}), bf16[4,64,1024]{2,1,0:T(8,128)(2,1)S(1)}, u32[]{:S(2)}, u32[]{:S(2)}) async-start(bf16[4,64,1024]{2,1,0:T(8,128)(2,1)} %broadcast_in_dim.16), calls=%async_computation | async-start | bytes 1048576 | tf_op jit(solution)/shard_map/all_to_all | solution.py:26
  23.4 12.9 %copy-start.41 = (bf16[4,64,1024]{2,1,0:T(8,128)(2,1)}, bf16[4,64,1024]{2,1,0:T(8,128)(2,1)S(1)}, u32[]{:S(2)}) copy-start(bf16[4,64,1024]{2,1,0:T(8,128)(2,1)S(1)} %all-to-all-done.refs_3_) | copy-start | bytes 1572868
  23.4 12.9 %collective-permute-start = (bf16[4,64,1024]{2,1,0:T(8,128)(2,1)S(1)}, bf16[4,64,1024]{2,1,0:T(8,128)(2,1)S(1)}, u32[]{:S(2)}, u32[]{:S(2)}) collective-permute-start(bf16[4,64,1024]{2,1,0:T(8,128)(2,1)S(1)} %all-to-all-done.refs_3_), channel_id=1, source_target_pairs={{0,8},{4,12},{8,0},{12,4},{16,24},{20,28},{24,16},{28,20},{1,9},{5... | collective-permute-start | bytes 1572872 | tf_op jit(solution)/shard_map/ppermute | solution.py:22
  24.9 29.1 %all-to-all-start.1 = ((bf16[4,512,256]{2,1,0:T(8,128)(2,1)}), bf16[4,512,256]{2,1,0:T(8,128)(2,1)S(1)}, u32[]{:S(2)}, u32[]{:S(2)}) async-start(bf16[4,512,256]{2,1,0:T(8,128)(2,1)} %get-tuple-element.157), calls=%async_computation.1 | async-start | bytes 2097152 | tf_op jit(solution)/shard_map/all_to_all | solution.py:26
  37.4 9.0 %collective-permute-start.1 = (bf16[2,4,64,1024]{3,2,1,0:T(8,128)(2,1)}, bf16[2,4,64,1024]{3,2,1,0:T(8,128)(2,1)S(1)}, u32[]{:S(2)}, u32[]{:S(2)}) collective-permute-start(bf16[2,4,64,1024]{3,2,1,0:T(8,128)(2,1)} %pad_maximum_fusion), channel_id=1, source_target_pairs={{0,4},{4,0},{8,12},{12,8},{16,20},{20,16},{24,28},{28,24},{1,5},{5... | collective-permute-start | bytes 3145736 | tf_op jit(solution)/shard_map/ppermute | solution.py:22
  65.5 29.7 %all-to-all-start.2 = ((bf16[4,512,256]{2,1,0:T(8,128)(2,1)}), bf16[4,512,256]{2,1,0:T(8,128)(2,1)}, u32[]{:S(2)}, u32[]{:S(2)}) async-start(bf16[4,512,256]{2,1,0:T(8,128)(2,1)} %get-tuple-element.172), calls=%async_computation.2 | async-start | bytes 2097152 | tf_op jit(solution)/shard_map/all_to_all | solution.py:26
  78.9 5.7 %collective-permute-start.2 = (bf16[512,1024]{1,0:T(8,128)(2,1)S(1)}, bf16[512,1024]{1,0:T(8,128)(2,1)S(1)}, u32[]{:S(2)}, u32[]{:S(2)}) collective-permute-start(bf16[512,1024]{1,0:T(8,128)(2,1)S(1)} %get-tuple-element.177), channel_id=1, source_target_pairs={{0,4},{4,0},{8,12},{12,8},{16,20},{20,16},{24,28},{28,24},{1,5},{5... | collective-permute-start | bytes 3145736 | tf_op jit(solution)/shard_map/ppermute | solution.py:22
  79.0 5.7 %collective-permute-start.3 = (bf16[512,1024]{1,0:T(8,128)(2,1)S(1)}, bf16[512,1024]{1,0:T(8,128)(2,1)S(1)}, u32[]{:S(2)}, u32[]{:S(2)}) collective-permute-start(bf16[512,1024]{1,0:T(8,128)(2,1)S(1)} %get-tuple-element.178), channel_id=1, source_target_pairs={{0,4},{4,0},{8,12},{12,8},{16,20},{20,16},{24,28},{28,24},{1,5},{5... | collective-permute-start | bytes 3145736 | tf_op jit(solution)/shard_map/ppermute | solution.py:22
  79.5 4.4 %collective-permute-start.4 = (bf16[256,1024]{1,0:T(8,128)(2,1)S(1)}, bf16[256,1024]{1,0:T(8,128)(2,1)S(1)}, u32[]{:S(2)}, u32[]{:S(2)}) collective-permute-start(bf16[256,1024]{1,0:T(8,128)(2,1)S(1)} %get-tuple-element.179), channel_id=1, source_target_pairs={{0,4},{4,0},{8,12},{12,8},{16,20},{20,16},{24,28},{28,24},{1,5},{5... | collective-permute-start | bytes 1572872 | tf_op jit(solution)/shard_map/ppermute | solution.py:22
  79.6 5.1 %collective-permute-start.5 = (bf16[256,1024]{1,0:T(8,128)(2,1)S(1)}, bf16[256,1024]{1,0:T(8,128)(2,1)S(1)}, u32[]{:S(2)}, u32[]{:S(2)}) collective-permute-start(bf16[256,1024]{1,0:T(8,128)(2,1)S(1)} %get-tuple-element.180), channel_id=1, source_target_pairs={{0,4},{4,0},{8,12},{12,8},{16,20},{20,16},{24,28},{28,24},{1,5},{5... | collective-permute-start | bytes 1572872 | tf_op jit(solution)/shard_map/ppermute | solution.py:22
  84.6 16.9 %copy-start.7 = (bf16[3,1024,256]{2,1,0:T(8,128)(2,1)S(1)}, bf16[3,1024,256]{2,1,0:T(8,128)(2,1)}, u32[]{:S(2)}) copy-start(bf16[3,1024,256]{2,1,0:T(8,128)(2,1)} %weight_ref.1) | copy-start | bytes 4718596
  88.4 13.2 %copy-start.2 = (bf16[512,1024]{1,0:T(8,128)(2,1)S(1)}, bf16[512,1024]{1,0:T(8,128)(2,1)}, u32[]{:S(2)}) copy-start(bf16[512,1024]{1,0:T(8,128)(2,1)} %pick_rows.1.refs_0_.picked_ref.refs_6_) | copy-start | bytes 3145732
  88.4 13.2 %copy-start.23 = (bf16[3,512,256]{2,1,0:T(8,128)(2,1)S(1)}, bf16[3,512,256]{2,1,0:T(8,128)(2,1)}, u32[]{:S(2)}) copy-start(bf16[3,512,256]{2,1,0:T(8,128)(2,1)} %get-tuple-element.195.qkv_ref) | copy-start | bytes 2359300
  88.4 13.2 %copy-start.33 = (bf16[1,1024]{1,0:T(2,128)(2,1)S(1)}, bf16[1,1024]{1,0:T(2,128)(2,1)}, u32[]{:S(2)}) copy-start(bf16[1,1024]{1,0:T(2,128)(2,1)} %broadcast_in_dim.17.refs_1_.gain_ref) | copy-start | bytes 6148
  95.2 29.5 %all-to-all-start.3 = ((bf16[4,128,1024]{2,1,0:T(8,128)(2,1)}), bf16[4,128,1024]{2,1,0:T(8,128)(2,1)}, u32[]{:S(2)}, u32[]{:S(2)}) async-start(bf16[4,128,1024]{2,1,0:T(8,128)(2,1)} %bitcast.32), calls=%async_computation.3 | async-start | bytes 2097152 | tf_op jit(solution)/shard_map/all_to_all | solution.py:26
  99.4 18.8 %collective-permute-start.6 = (bf16[384,1024]{1,0:T(8,128)(2,1)}, bf16[384,1024]{1,0:T(8,128)(2,1)S(1)}, u32[]{:S(2)}, u32[]{:S(2)}) collective-permute-start(bf16[384,1024]{1,0:T(8,128)(2,1)} %copy-done.38), channel_id=1, source_target_pairs={{0,8},{4,12},{8,0},{12,4},{16,24},{20,28},{24,16},{28,20},{1,9},{5... | collective-permute-start | bytes 2359304 | tf_op jit(solution)/shard_map/ppermute | solution.py:22
  100.0 18.4 %collective-permute-start.7 = (bf16[384,1024]{1,0:T(8,128)(2,1)}, bf16[384,1024]{1,0:T(8,128)(2,1)S(1)}, u32[]{:S(2)}, u32[]{:S(2)}) collective-permute-start(bf16[384,1024]{1,0:T(8,128)(2,1)} %copy-done.37), channel_id=1, source_target_pairs={{0,16},{4,20},{8,24},{12,28},{16,0},{20,4},{24,8},{28,12},{1,17},{... | collective-permute-start | bytes 2359304 | tf_op jit(solution)/shard_map/ppermute | solution.py:22
  110.2 8.3 %copy-start.36 = (f32[1,1024]{1,0:T(1,128)}, f32[1,1024]{1,0:T(1,128)S(1)}, u32[]{:S(2)}) copy-start(f32[1,1024]{1,0:T(1,128)S(1)} %get-tuple-element.216.one_ref) | copy-start | bytes 12292
  110.2 8.3 %copy-start.11 = (bf16[2,384,1024]{2,1,0:T(8,128)(2,1)S(1)}, bf16[2,384,1024]{2,1,0:T(8,128)(2,1)}, u32[]{:S(2)}) copy-start(bf16[2,384,1024]{2,1,0:T(8,128)(2,1)} %copy-done.10) | copy-start | bytes 4718596
  124.7 22.1 %collective-permute-start.8 = (bf16[768,1024]{1,0:T(8,128)(2,1)S(1)}, bf16[768,1024]{1,0:T(8,128)(2,1)}, u32[]{:S(2)}, u32[]{:S(2)}) collective-permute-start(bf16[768,1024]{1,0:T(8,128)(2,1)S(1)} %qkv_part.1.rows_ref), channel_id=1, source_target_pairs={{0,4},{4,0},{8,12},{12,8},{16,20},{20,16},{24,28},{28,24},{1,5},{5... | collective-permute-start | bytes 4718600 | tf_op jit(solution)/shard_map/ppermute | solution.py:22
  124.7 30.2 %all-to-all-start.4 = ((bf16[4,128,1024]{2,1,0:T(8,128)(2,1)}), bf16[4,128,1024]{2,1,0:T(8,128)(2,1)S(1)}, u32[]{:S(2)}, u32[]{:S(2)}) async-start(bf16[4,128,1024]{2,1,0:T(8,128)(2,1)} %bitcast.29), calls=%async_computation.4 | async-start | bytes 2097152 | tf_op jit(solution)/shard_map/all_to_all | solution.py:26
  128.5 11.9 %collective-permute-start.10 = (bf16[192,1024]{1,0:T(8,128)(2,1)}, bf16[192,1024]{1,0:T(8,128)(2,1)}, u32[]{:S(2)}, u32[]{:S(2)}) collective-permute-start(bf16[192,1024]{1,0:T(8,128)(2,1)} %copy-done.40), channel_id=1, source_target_pairs={{0,8},{4,12},{8,0},{12,4},{16,24},{20,28},{24,16},{28,20},{1,9},{5... | collective-permute-start | bytes 1179656 | tf_op jit(solution)/shard_map/ppermute | solution.py:22
  129.1 11.6 %collective-permute-start.9 = (bf16[192,1024]{1,0:T(8,128)(2,1)}, bf16[192,1024]{1,0:T(8,128)(2,1)}, u32[]{:S(2)}, u32[]{:S(2)}) collective-permute-start(bf16[192,1024]{1,0:T(8,128)(2,1)} %copy-done.39), channel_id=1, source_target_pairs={{0,16},{4,20},{8,24},{12,28},{16,0},{20,4},{24,8},{28,12},{1,17},{... | collective-permute-start | bytes 1179656 | tf_op jit(solution)/shard_map/ppermute | solution.py:22
  143.7 7.8 %collective-permute-start.11 = (bf16[128,1024]{1,0:T(8,128)(2,1)S(1)}, bf16[128,1024]{1,0:T(8,128)(2,1)S(1)}, u32[]{:S(2)}, u32[]{:S(2)}) collective-permute-start(bf16[128,1024]{1,0:T(8,128)(2,1)S(1)} %get-tuple-element.237.refs_0_), channel_id=1, source_target_pairs={{0,16},{4,20},{8,24},{12,28},{16,0},{20,4},{24,8},{28,12},{1,17},{... | collective-permute-start | bytes 786440 | tf_op jit(solution)/shard_map/ppermute | solution.py:22
  145.3 7.5 %collective-permute-start.12 = (bf16[128,1024]{1,0:T(8,128)(2,1)S(1)}, bf16[128,1024]{1,0:T(8,128)(2,1)}, u32[]{:S(2)}, u32[]{:S(2)}) collective-permute-start(bf16[128,1024]{1,0:T(8,128)(2,1)S(1)} %get-tuple-element.239.refs_4_), channel_id=1, source_target_pairs={{0,8},{4,12},{8,0},{12,4},{16,24},{20,28},{24,16},{28,20},{1,9},{5... | collective-permute-start | bytes 786440 | tf_op jit(solution)/shard_map/ppermute | solution.py:22
  149.5 13.0 %copy-start.4 = (bf16[512,1024]{1,0:T(8,128)(2,1)S(1)}, bf16[512,1024]{1,0:T(8,128)(2,1)}, u32[]{:S(2)}) copy-start(bf16[512,1024]{1,0:T(8,128)(2,1)} %pick_only.1.rows_ref) | copy-start | bytes 3145732
  149.5 13.0 %copy-start.31 = (bf16[1,1024]{1,0:T(2,128)(2,1)S(1)}, bf16[1,1024]{1,0:T(2,128)(2,1)}, u32[]{:S(2)}) copy-start(bf16[1,1024]{1,0:T(2,128)(2,1)} %broadcast_in_dim.18.router_ref) | copy-start | bytes 6148
  149.5 13.0 %copy-start.32 = (f32[128,1]{1,0:T(8,128)S(1)}, f32[128,1]{1,0:T(8,128)}, u32[]{:S(2)}) copy-start(f32[128,1]{1,0:T(8,128)} %get-tuple-element.235.score_ref) | copy-start | bytes 1540
  154.9 36.4 %all-to-all-start.5 = ((bf16[4,168,1024]{2,1,0:T(8,128)(2,1)}), bf16[4,168,1024]{2,1,0:T(8,128)(2,1)S(1)}, u32[]{:S(2)}, u32[]{:S(2)}) async-start(bf16[4,168,1024]{2,1,0:T(8,128)(2,1)} %copy-done.12), calls=%async_computation.5 | async-start | bytes 2752512 | tf_op jit(solution)/shard_map/all_to_all | solution.py:26
  158.4 9.6 %collective-permute-start.14 = (bf16[128,1024]{1,0:T(8,128)(2,1)}, bf16[128,1024]{1,0:T(8,128)(2,1)}, u32[]{:S(2)}, u32[]{:S(2)}) collective-permute-start(bf16[128,1024]{1,0:T(8,128)(2,1)} %copy-done.29), channel_id=1, source_target_pairs={{0,8},{4,12},{8,0},{12,4},{16,24},{20,28},{24,16},{28,20},{1,9},{5... | collective-permute-start | bytes 786440 | tf_op jit(solution)/shard_map/ppermute | solution.py:22
  159.0 9.6 %collective-permute-start.16 = (bf16[128,1024]{1,0:T(8,128)(2,1)}, bf16[128,1024]{1,0:T(8,128)(2,1)}, u32[]{:S(2)}, u32[]{:S(2)}) collective-permute-start(bf16[128,1024]{1,0:T(8,128)(2,1)} %collective-permute-done.12.refs_5_), channel_id=1, source_target_pairs={{0,16},{4,20},{8,24},{12,28},{16,0},{20,4},{24,8},{28,12},{1,17},{... | collective-permute-start | bytes 786440 | tf_op jit(solution)/shard_map/ppermute | solution.py:22
  160.6 11.8 %collective-permute-start.13 = (bf16[128,1024]{1,0:T(8,128)(2,1)}, bf16[128,1024]{1,0:T(8,128)(2,1)}, u32[]{:S(2)}, u32[]{:S(2)}) collective-permute-start(bf16[128,1024]{1,0:T(8,128)(2,1)} %copy-done.25), channel_id=1, source_target_pairs={{0,8},{4,12},{8,0},{12,4},{16,24},{20,28},{24,16},{28,20},{1,9},{5... | collective-permute-start | bytes 786440 | tf_op jit(solution)/shard_map/ppermute | solution.py:22
  162.0 10.6 %collective-permute-start.15 = (bf16[128,1024]{1,0:T(8,128)(2,1)}, bf16[128,1024]{1,0:T(8,128)(2,1)}, u32[]{:S(2)}, u32[]{:S(2)}) collective-permute-start(bf16[128,1024]{1,0:T(8,128)(2,1)} %copy-done.27), channel_id=1, source_target_pairs={{0,16},{4,20},{8,24},{12,28},{16,0},{20,4},{24,8},{28,12},{1,17},{... | collective-permute-start | bytes 786440 | tf_op jit(solution)/shard_map/ppermute | solution.py:22
  176.9 4.9 %collective-permute-start.17 = (bf16[512,1024]{1,0:T(8,128)(2,1)S(1)}, bf16[512,1024]{1,0:T(8,128)(2,1)}, u32[]{:S(2)}, u32[]{:S(2)}) collective-permute-start(bf16[512,1024]{1,0:T(8,128)(2,1)S(1)} %get-tuple-element.248), channel_id=1, source_target_pairs={{0,4},{4,0},{8,12},{12,8},{16,20},{20,16},{24,28},{28,24},{1,5},{5... | collective-permute-start | bytes 3145736 | tf_op jit(solution)/shard_map/ppermute | solution.py:22
  177.0 4.8 %collective-permute-start.18 = (bf16[512,1024]{1,0:T(8,128)(2,1)S(1)}, bf16[512,1024]{1,0:T(8,128)(2,1)}, u32[]{:S(2)}, u32[]{:S(2)}) collective-permute-start(bf16[512,1024]{1,0:T(8,128)(2,1)S(1)} %get-tuple-element.249), channel_id=1, source_target_pairs={{0,4},{4,0},{8,12},{12,8},{16,20},{20,16},{24,28},{28,24},{1,5},{5... | collective-permute-start | bytes 3145736 | tf_op jit(solution)/shard_map/ppermute | solution.py:22
  177.5 19.8 %collective-permute-start.19 = (bf16[384,1024]{1,0:T(8,128)(2,1)}, bf16[384,1024]{1,0:T(8,128)(2,1)}, u32[]{:S(2)}, u32[]{:S(2)}) collective-permute-start(bf16[384,1024]{1,0:T(8,128)(2,1)} %get-tuple-element.255.a_ref), channel_id=1, source_target_pairs={{0,16},{4,20},{8,24},{12,28},{16,0},{20,4},{24,8},{28,12},{1,17},{... | collective-permute-start | bytes 2359304 | tf_op jit(solution)/shard_map/ppermute | solution.py:22
  179.0 20.4 %collective-permute-start.20 = (bf16[384,1024]{1,0:T(8,128)(2,1)}, bf16[384,1024]{1,0:T(8,128)(2,1)}, u32[]{:S(2)}, u32[]{:S(2)}) collective-permute-start(bf16[384,1024]{1,0:T(8,128)(2,1)} %get-tuple-element.256.b_ref), channel_id=1, source_target_pairs={{0,8},{4,12},{8,0},{12,4},{16,24},{20,28},{24,16},{28,20},{1,9},{5... | collective-permute-start | bytes 2359304 | tf_op jit(solution)/shard_map/ppermute | solution.py:22
  191.3 10.3 %copy-start.3 = (bf16[4,168,1024]{2,1,0:T(8,128)(2,1)}, bf16[4,168,1024]{2,1,0:T(8,128)(2,1)S(1)}, u32[]{:S(2)}) copy-start(bf16[4,168,1024]{2,1,0:T(8,128)(2,1)S(1)} %all-to-all-done.5.got_ref.piece_ref) | copy-start | bytes 4128772
  191.3 29.6 %all-to-all-start.6 = ((bf16[4,128,1024]{2,1,0:T(8,128)(2,1)}), bf16[4,128,1024]{2,1,0:T(8,128)(2,1)}, u32[]{:S(2)}, u32[]{:S(2)}) async-start(bf16[4,128,1024]{2,1,0:T(8,128)(2,1)} %finish_input.1.piece_ref), calls=%async_computation.6 | async-start | bytes 2097152 | tf_op jit(solution)/shard_map/all_to_all | solution.py:26
  195.6 6.0 %collective-permute-start.21 = (bf16[40,1024]{1,0:T(8,128)(2,1)S(1)}, bf16[40,1024]{1,0:T(8,128)(2,1)S(1)}, u32[]{:S(2)}, u32[]{:S(2)}) collective-permute-start(bf16[40,1024]{1,0:T(8,128)(2,1)S(1)} %first_small.1.refs_0_), channel_id=1, source_target_pairs={{0,8},{4,12},{8,0},{12,4},{16,24},{20,28},{24,16},{28,20},{1,9},{5... | collective-permute-start | bytes 245768 | tf_op jit(solution)/shard_map/ppermute | solution.py:22
  199.4 10.0 %collective-permute-start.24 = (bf16[40,1024]{1,0:T(8,128)(2,1)S(1)}, bf16[40,1024]{1,0:T(8,128)(2,1)S(1)}, u32[]{:S(2)}, u32[]{:S(2)}) collective-permute-start(bf16[40,1024]{1,0:T(8,128)(2,1)S(1)} %first_small.1.refs_0_), channel_id=1, source_target_pairs={{0,16},{4,20},{8,24},{12,28},{16,0},{20,4},{24,8},{28,12},{1,17},{... | collective-permute-start | bytes 245768 | tf_op jit(solution)/shard_map/ppermute | solution.py:22
  201.7 7.7 %collective-permute-start.25 = (bf16[40,1024]{1,0:T(8,128)(2,1)S(1)}, bf16[40,1024]{1,0:T(8,128)(2,1)S(1)}, u32[]{:S(2)}, u32[]{:S(2)}) collective-permute-start(bf16[40,1024]{1,0:T(8,128)(2,1)S(1)} %collective-permute-done.21.refs_1_), channel_id=1, source_target_pairs={{0,16},{4,20},{8,24},{12,28},{16,0},{20,4},{24,8},{28,12},{1,17},{... | collective-permute-start | bytes 245768 | tf_op jit(solution)/shard_map/ppermute | solution.py:22
  209.4 19.6 %collective-permute-start.28 = (bf16[384,1024]{1,0:T(8,128)(2,1)S(1)}, bf16[384,1024]{1,0:T(8,128)(2,1)S(1)}, u32[]{:S(2)}, u32[]{:S(2)}) collective-permute-start(bf16[384,1024]{1,0:T(8,128)(2,1)S(1)} %get-tuple-element.295.a_ref), channel_id=1, source_target_pairs={{0,8},{4,12},{8,0},{12,4},{16,24},{20,28},{24,16},{28,20},{1,9},{5... | collective-permute-start | bytes 2359304 | tf_op jit(solution)/shard_map/ppermute | solution.py:22
  211.0 18.1 %collective-permute-start.29 = (bf16[384,1024]{1,0:T(8,128)(2,1)S(1)}, bf16[384,1024]{1,0:T(8,128)(2,1)}, u32[]{:S(2)}, u32[]{:S(2)}) collective-permute-start(bf16[384,1024]{1,0:T(8,128)(2,1)S(1)} %get-tuple-element.288.b_ref), channel_id=1, source_target_pairs={{0,16},{4,20},{8,24},{12,28},{16,0},{20,4},{24,8},{28,12},{1,17},{... | collective-permute-start | bytes 2359304 | tf_op jit(solution)/shard_map/ppermute | solution.py:22
  211.1 1.3 collective-permute-start.22
  211.7 6.8 %collective-permute-start.23 = (bf16[40,1024]{1,0:T(8,128)(2,1)S(1)}, bf16[40,1024]{1,0:T(8,128)(2,1)S(1)}, u32[]{:S(2)}, u32[]{:S(2)}) collective-permute-start(bf16[40,1024]{1,0:T(8,128)(2,1)S(1)} %collective-permute-done.21.refs_1_), channel_id=1, source_target_pairs={{0,4},{4,0},{8,12},{12,8},{16,20},{20,16},{24,28},{28,24},{1,5},{5... | collective-permute-start | bytes 245768 | tf_op jit(solution)/shard_map/ppermute | solution.py:22
  212.2 6.3 %collective-permute-start.26 = (bf16[40,1024]{1,0:T(8,128)(2,1)S(1)}, bf16[40,1024]{1,0:T(8,128)(2,1)S(1)}, u32[]{:S(2)}, u32[]{:S(2)}) collective-permute-start(bf16[40,1024]{1,0:T(8,128)(2,1)S(1)} %collective-permute-done.24.refs_2_), channel_id=1, source_target_pairs={{0,4},{4,0},{8,12},{12,8},{16,20},{20,16},{24,28},{28,24},{1,5},{5... | collective-permute-start | bytes 245768 | tf_op jit(solution)/shard_map/ppermute | solution.py:22
  212.4 6.1 %collective-permute-start.27 = (bf16[40,1024]{1,0:T(8,128)(2,1)S(1)}, bf16[40,1024]{1,0:T(8,128)(2,1)S(1)}, u32[]{:S(2)}, u32[]{:S(2)}) collective-permute-start(bf16[40,1024]{1,0:T(8,128)(2,1)S(1)} %collective-permute-done.25.refs_3_), channel_id=1, source_target_pairs={{0,4},{4,0},{8,12},{12,8},{16,20},{20,16},{24,28},{28,24},{1,5},{5... | collective-permute-start | bytes 245768 | tf_op jit(solution)/shard_map/ppermute | solution.py:22
  (37 other events, 106.1 us)

commit v5 on v4

--- a/solution.py
+++ b/solution.py
@@ -194,7 +194,7 @@
     )(base, offsets)
 
 
-def merge_rows(base, offsets, pieces, parts, held_out=None):
+def merge_rows(base, offsets, pieces, mine, which, held_out=None):
     rows, width = base.shape
     ways, depth, _ = pieces.shape
     count = rows // ways
@@ -202,6 +202,8 @@
     kept = [] if held_out is None else [held_out]
     sub = 256
     sub_groups = sub // GROUP
+
+    first = which.start
 
     def kernel(part_ref, base_ref, offset_ref, piece_ref, *rest):
         out_ref = rest[-1]
@@ -218,14 +220,14 @@
 
     grid_spec = pltpu.PrefetchScalarGridSpec(
         num_scalar_prefetch=1,
-        grid=(parts.shape[0],),
+        grid=(len(which),),
         in_specs=[
-            pl.BlockSpec((count, width), lambda i, p: (p[i], 0)),
-            pl.BlockSpec((1, groups), lambda i, p: (0, p[i])),
-            pl.BlockSpec((1, depth, width), lambda i, p: (p[i], 0, 0)),
+            pl.BlockSpec((count, width), lambda i, m: (m[0] ^ (i + first), 0)),
+            pl.BlockSpec((1, groups), lambda i, m: (0, m[0] ^ (i + first))),
+            pl.BlockSpec((1, depth, width), lambda i, m: (m[0] ^ (i + first), 0, 0)),
         ]
         + [pl.BlockSpec(memory_space=pl.ANY)] * len(kept),
-        out_specs=pl.BlockSpec((count, width), lambda i, p: (p[i], 0)),
+        out_specs=pl.BlockSpec((count, width), lambda i, m: (m[0] ^ (i + first), 0)),
     )
     return pl.pallas_call(
         kernel,
@@ -234,7 +236,7 @@
         input_output_aliases={4: 0} if kept else {},
         cost_estimate=small_cost(),
         name="merge_rows",
-    )(parts, base, offsets, pieces, *kept)
+    )(mine, base, offsets, pieces, *kept)
 
 
 def attend(picked, gain, weight, seq_row, ways):
@@ -244,7 +246,7 @@
     block = min(256, rows)
 
     def body(load, store, outs, scalars, scratch):
-        low_ref, qkv_ref, probs_ref, out_ref = outs
+        low_ref, qkv_ref, out_ref, *probs_refs = outs
         values = load(0)[...].astype(F32)
         low_ref[...] = (values * inverse_rms(values) * load(1)[...].astype(F32)).astype(BF)
         store(0)
@@ -255,8 +257,8 @@
         sequence = load(3)[...].astype(F32)
         column = jnp.broadcast_to(sequence, (128, rows)).T[:, :1]
         lane_head = lax.broadcasted_iota(jnp.int32, (1, heads_width), 1) // HEAD_DIM
-        for start in range(0, rows, block):
-            stop = start + block
+        for n in reversed(range(rows // block)):
+            start, stop = n * block, (n + 1) * block
             query = qkv_ref[0, start:stop, :] * BF(HEAD_DIM ** (-0.5))
             order = lax.broadcasted_iota(jnp.int32, (block, stop), 0) + start
             keys = lax.broadcasted_iota(jnp.int32, (block, stop), 1)
@@ -268,13 +270,12 @@
                 logits = jnp.where(allowed, dot(query, key, NT), mask_fill)
                 raised = jnp.exp(logits - jnp.max(logits, axis=-1, keepdims=True))
                 probs = (raised * (1.0 / jnp.sum(raised, axis=-1, keepdims=True))).astype(BF)
-                probs_ref[head, start:stop, :stop] = probs
-                if stop < rows:
-                    probs_ref[head, start:stop, stop:] = jnp.zeros((block, rows - stop), BF)
+                probs_refs[n][head] = probs
                 value = jnp.where(here, qkv_ref[2, :stop, :], BF(0))
                 total = total + dot(probs, value, NN)
             for k in range(ways):
                 out_ref[k, start:stop, :] = total.astype(BF)
+            store(3 + n)
 
     return staged(
         "attend",
@@ -284,19 +285,19 @@
         [
             ((rows, width), BF),
             ((3, rows, heads_width), BF),
-            ((heads, rows, rows), BF),
             ((ways, rows, heads_width), BF),
-        ],
+        ]
+        + [((heads, block, (n + 1) * block), BF) for n in range(rows // block)],
         [],
         60,
         small_cost(),
     )
 
 
-def feed_forward(heads, here, beside, across, picked, gain, up, grad_act, grad_mixer, part, mine, ways):
+def feed_forward(heads, own_weight, quarters, picked, gain, up, grad_act, grad_mixer, part, mine, ways):
     rows, width = picked.shape
     hidden = up.shape[1]
-    sub = min(256, hidden)
+    sub = min(512, hidden)
     count, _, heads_width = heads.shape
     piece = heads_width // 4
     own = rows // ways
@@ -309,22 +310,23 @@
         total, state, weights = scratch
         quarter = part_ref[0] & 3
         heads_ref = load(0)
-        here_ref, beside_ref, across_ref = load(1), load(2), load(3)
-        for n, source in enumerate((here_ref, across_ref.at[0], beside_ref, across_ref.at[1])):
+        weights[0] = load(1)[...]
+        for n in range(4):
             start = pl.multiple_of((quarter ^ n) * piece, piece)
-            for k in range(count):
-                weights[k, pl.ds(start, piece), :] = source[k]
-        attended = dot(heads_ref[0], weights[0], NN)
+            source = load(2 + n)
+            for k in range(1, count):
+                weights[k, pl.ds(start, piece), :] = source[k - 1]
+        attended = dot(heads_ref[mine_ref[0]], weights[0], NN)
         for k in range(1, count):
-            attended = attended + dot(heads_ref[k], weights[k], NN)
+            attended = attended + dot(heads_ref[mine_ref[0] ^ k], weights[k], NN)
         total[...] = attended
         attended_ref[...] = total[pl.ds(pl.multiple_of(mine_ref[0] * own, own), own), :]
-        state_in = load(4)[...].astype(F32) + attended
+        state_in = load(6)[...].astype(F32) + attended
         state[...] = state_in
-        gain_row = load(5)[...].astype(F32)
+        gain_row = load(7)[...].astype(F32)
         low_ref[...] = (state_in * inverse_rms(state_in) * gain_row).astype(BF)
         store(0, 1)
-        up_ref, act_grad_ref = load(6), load(7)
+        up_ref, act_grad_ref = load(8), load(9)
         for s in range(hidden // sub):
             lanes = slice(s * sub, (s + 1) * sub)
             value = dot(low_ref[...], up_ref[:, lanes], NN)
@@ -350,16 +352,16 @@
         along = jnp.mean(scaled * normal, axis=-1, keepdims=True)
         back = inverse * (scaled - normal * along)
         hidden_ref[...] = back.astype(BF)
-        part_out_ref[...] = (back + load(8)[...].astype(F32) * (1.0 / count)).astype(BF)
+        part_out_ref[...] = (back + load(10)[...].astype(F32) * (1.0 / count)).astype(BF)
         store(4, 5, 6)
         for k in range(count):
-            sent_ref[k] = dot(part_out_ref[...], weights[k], NT).astype(BF)
+            sent_ref[mine_ref[0] ^ k] = dot(part_out_ref[...], weights[k], NT).astype(BF)
 
     return staged(
         "feed_forward",
         body,
         [part, mine],
-        [heads, here, beside, across, picked, gain, up, grad_act, grad_mixer],
+        [heads, own_weight, *quarters, picked, gain, up, grad_act, grad_mixer],
         [
             ((own, width), F32),
             ((rows, width), BF),
@@ -417,17 +419,13 @@
     def kernel(
         head_ref,
         qkv_ref,
-        probs_ref,
         weight_ref,
         picked_ref,
         gain_ref,
         hidden_ref,
-        grads_ref,
-        gain_part_ref,
-        result,
-        grad_key,
-        grad_value,
+        *rest,
     ):
+        probs_refs, (grads_ref, gain_part_ref, result, grad_key, grad_value) = rest[: len(probs)], rest[len(probs) :]
         lane_head = lax.broadcasted_iota(jnp.int32, (1, heads_width), 1) // HEAD_DIM
         for start in reversed(range(0, rows, block)):
             stop = start + block
@@ -444,7 +442,7 @@
                 here = lane_head == head
                 value = jnp.where(here, qkv_ref[2, :stop, :], BF(0))
                 key = jnp.where(here, qkv_ref[1, :stop, :], BF(0))
-                low = probs_ref[head, here_rows, :stop]
+                low = probs_refs[start // block][head]
                 weighted = low.astype(F32) * dot(grad_head, value, NT)
                 row_sum = jnp.sum(weighted, axis=-1, keepdims=True)
                 slopes = (weighted - low.astype(F32) * row_sum).astype(BF)
@@ -474,7 +472,7 @@
     whole = pl.BlockSpec(memory_space=pltpu.VMEM)
     return pl.pallas_call(
         kernel,
-        in_specs=[whole] * 7,
+        in_specs=[whole] * (6 + len(probs)),
         out_specs=[whole] * 3,
         out_shape=[
             jax.ShapeDtypeStruct((3, rows, heads_width), BF),
@@ -488,42 +486,46 @@
         cost_estimate=small_cost(),
         compiler_params=pltpu.CompilerParams(vmem_limit_bytes=20 << 20),
         name="attend_back",
-    )(head_terms, qkv, probs, weight, picked, gain, hidden_part)
-
-
-def spread_rows(down_near, down_far, up_near, up_far, index_down, index_up):
-    half, rows, width = down_near.shape
-
-    def kernel(down_index, up_index, down_ref, far_ref, up_ref, up_far_ref, down_out, up_out):
-        near = pl.program_id(0) < half
-
-        @pl.when(near)
-        def _():
-            down_out[...] = down_ref[0].astype(F32)
-            up_out[...] = up_ref[0].astype(F32)
-
-        @pl.when(jnp.logical_not(near))
-        def _():
-            down_out[...] = far_ref[0].astype(F32)
-            up_out[...] = up_far_ref[0].astype(F32)
-
-    first = pl.BlockSpec((1, rows, width), lambda i, d, u: (jnp.minimum(i, half - 1), 0, 0))
-    second = pl.BlockSpec((1, rows, width), lambda i, d, u: (jnp.maximum(i - half, 0), 0, 0))
+    )(head_terms, qkv, weight, picked, gain, hidden_part, *probs)
+
+
+def spread_rows(down, up, order_down, order_up, part):
+    count = len(down)
+    wide, width = down[0].shape
+    rows = wide // (2 ** len(order_down) // count)
+    each = wide // rows
+
+    def kernel(part_ref, *refs):
+        down_out, up_out = refs[2 * count :]
+        for n in range(count):
+
+            @pl.when(pl.program_id(0) // each == n)
+            def _():
+                down_out[...] = refs[n][...].astype(F32)
+                up_out[...] = refs[count + n][...].astype(F32)
+
+    def source(n):
+        return pl.BlockSpec((rows, width), lambda i, p: (jnp.clip(i - n * each, 0, each - 1), 0))
+
+    def target(order):
+        def place(i, p):
+            key = sum((i >> n & 1) * bit for n, bit in enumerate(order))
+            return p[0] ^ key, 0
+
+        return pl.BlockSpec((rows, width), place)
+
     return pl.pallas_call(
         kernel,
         grid_spec=pltpu.PrefetchScalarGridSpec(
-            num_scalar_prefetch=2,
-            grid=(2 * half,),
-            in_specs=[first, second, first, second],
-            out_specs=[
-                pl.BlockSpec((rows, width), lambda i, d, u: (d[i], 0)),
-                pl.BlockSpec((rows, width), lambda i, d, u: (u[i], 0)),
-            ],
+            num_scalar_prefetch=1,
+            grid=(count * each,),
+            in_specs=[source(n) for n in range(count)] * 2,
+            out_specs=[target(order_down), target(order_up)],
         ),
-        out_shape=[jax.ShapeDtypeStruct((2 * half * rows, width), F32)] * 2,
+        out_shape=[jax.ShapeDtypeStruct((count * wide, width), F32)] * 2,
         cost_estimate=small_cost(),
         name="spread_rows",
-    )(index_down, index_up, down_near, down_far, up_near, up_far)
+    )(part, *down, *up)
 
 
 def qkv_part_of(first_low, grads):
@@ -778,12 +780,12 @@
     )(received)
 
 
-def last_small(blocks, index, shares):
+def last_small(blocks, keys, part, shares):
     depth, width = blocks[0].shape
     each = depth - GAP
     count = len(blocks)
 
-    def kernel(index_ref, *refs):
+    def kernel(part_ref, *refs):
         out_ref, small_refs = refs[count], refs[count + 1 :]
         total = joined_sums(refs[0][each:, :])
         for n in range(1, count):
@@ -793,7 +795,7 @@
         lane = lax.broadcasted_iota(jnp.int32, (1, 128), 1)
         small_refs[TERMS - 1][...] = total[TERMS - 1 :, :128] * jnp.where(lane == 0, shares[0], shares[1])
         for n in range(count):
-            start = pl.multiple_of(index_ref[n] * each, each)
+            start = pl.multiple_of((part_ref[0] ^ keys[n]) * each, each)
             out_ref[pl.ds(start, each), :] = refs[n][:each, :].astype(F32)
 
     whole = pl.BlockSpec(memory_space=pltpu.VMEM)
@@ -806,7 +808,7 @@
         cost_estimate=small_cost(),
         compiler_params=pltpu.CompilerParams(vmem_limit_bytes=10 << 20),
         name="last_small",
-    )(index, *blocks)
+    )(part, *blocks)
 
 
 def finish_rows(mixer_terms, picked, gating, attended, grad_rows, gain_one, gain_two, square, routed_square, mine, ways):
@@ -950,29 +952,29 @@
     quarter = part & 3
     piece_rows = heads_width // 4
     piece = lax.dynamic_slice_in_dim(out_weight, quarter * piece_rows, piece_rows, 0)
-    here = to_all(jnp.broadcast_to(piece[None], (ways,) + piece.shape))
+    here = [swap(piece, "tensor", k) for k in range(1, ways)]
 
     picked = pick_rows(tokens, route_offset, ways)
-    first_low, qkv, probs, head_out = attend(picked, first_gain[None], qkv_weight, unit_sequence, ways)
+    first_low, qkv, head_out, *probs = attend(picked, first_gain[None], qkv_weight, unit_sequence, ways)
     here, head_out = tie((here, head_out))
 
     heads = to_all(head_out)
-    beside = swap(here, "dp", bit_x)
+    here = jnp.stack(here)
+    beside, across = swap(here, "dp", bit_x), swap(here, "dp", 1)
     cotangent, router_weight, second_gain, here, head_out = tie(
         (cotangent, router_weight, second_gain, here, head_out)
     )
     weight_row = router_weight[None]
     grad_rows = pick_only(cotangent, route_offset, ways)
-    beside, here, grad_rows = tie((beside, here, grad_rows))
-    across = swap(jnp.stack([here, beside]), "dp", 1)
+    beside, across, here, grad_rows = tie((beside, across, here, grad_rows))
+    quarters = [here, across, beside, swap(beside, "dp", 1)]
     gating, routed_square, grad_mixer, grad_act = act_grads(picked, weight_row, grad_rows, down_weight)
     square = score_sums(tokens, weight_row, mine_array, ways)
-    heads, across, grad_act, grad_mixer, square = tie((heads, across, grad_act, grad_mixer, square))
+    heads, quarters, grad_act, grad_mixer, square = tie((heads, quarters, grad_act, grad_mixer, square))
     attended, second_low, activated, grad_pre, hidden_part, attended_part, second_gain_part, head_sent = feed_forward(
         heads,
-        here,
-        beside,
-        across,
+        out_weight,
+        quarters,
         picked,
         second_gain[None],
         up_weight,
@@ -1054,33 +1056,25 @@
         more_a = [swap(array, "dp", bit_x) for array in (lane_a, got_a)]
         more_b = [swap(array, "dp", bit_y) for array in (lane_b, got_b)]
     last = finish_input(input_terms, grad_rows, grad_score, weight_row, mine_array, ways)
-    spots = jnp.stack([mine ^ k for k in range(ways)]).astype(jnp.int32)
     cotangent, last = tie((cotangent, last))
-    early = merge_rows(cotangent, route_offset, last, spots[:1])
+    early = merge_rows(cotangent, route_offset, last, mine_array, range(1))
     if by_swaps:
         more_a, more_b, early, qkv_a, qkv_b = tie((more_a, more_b, early, qkv_a, qkv_b))
         qkv_a_got, qkv_b_got = swap(qkv_a, "dp", bit_y), swap(qkv_b, "dp", bit_x)
-        down_near, up_near = gather_blocks([lane_a, got_a] + more_a, [lane_b, got_b] + more_b)
-        down_far, up_far = swap(down_near, "dp", 1), swap(up_near, "dp", 1)
+        down_one, up_one = gather_blocks([lane_a, got_a], [lane_b, got_b])
+        down_two, up_two = gather_blocks(more_a, more_b)
+        down_near, up_near = [down_one, down_two], [up_one, up_two]
+        down_far = [swap(array, "dp", 1) for array in down_near]
+        up_far = [swap(array, "dp", 1) for array in up_near]
 
         def gathered(order):
             keys = [0]
             for bit in order:
                 keys = keys + [k ^ bit for k in keys]
-            return jnp.stack([part ^ k for k in keys]).astype(jnp.int32)
-
-        each = hidden // copies
-
-        def by_block(array):
-            return array.reshape(-1, each, width)
+            return keys
 
         down_grad, up_grad = spread_rows(
-            by_block(down_near),
-            by_block(down_far),
-            by_block(up_near),
-            by_block(up_far),
-            gathered([bit_y, bit_x, 1]),
-            gathered([bit_x, bit_y, 1]),
+            down_near + down_far, up_near + up_far, [bit_y, bit_x, 1], [bit_x, bit_y, 1], part_array
         )
         fresh, last, down_grad, up_grad = tie((fresh, last, down_grad, up_grad))
     else:
@@ -1096,19 +1090,20 @@
         blocks = blocks + more
         more = [swap(array, "dp", bit_y) for array in blocks]
         fresh, blocks = tie((fresh, blocks))
-    output = merge_rows(tokens, route_offset, fresh, spots[: ways // 2])
+    output = merge_rows(tokens, route_offset, fresh, mine_array, range(ways // 2))
     if by_swaps:
         more, output, qkv_a, qkv_b = tie((more, output, qkv_a, qkv_b))
         qkv_a_got, qkv_b_got = swap(qkv_a, "dp", bit_x), swap(qkv_b, "dp", bit_y)
         blocks = blocks + more
         more = [swap(array, "dp", 1) for array in blocks]
         fresh, blocks, qkv_a = tie((fresh, blocks, qkv_a))
-    output = merge_rows(tokens, route_offset, fresh, spots[ways // 2 :], output)
+    output = merge_rows(tokens, route_offset, fresh, mine_array, range(ways // 2, ways), output)
     if by_swaps:
         more, output = tie((more, output))
-        out_grad, *small = last_small(blocks + more, gathered([bit_x, bit_y, 1]), shares)
+        out_grad, *small = last_small(blocks + more, gathered([bit_x, bit_y, 1]), part_array, shares)
+        small[3] = small[3][:, :2]
         input_rows, early, output, out_grad, small = tie((input_rows, early, output, out_grad, small))
-    input_grad = merge_rows(cotangent, route_offset, input_rows, spots[1:], early)
+    input_grad = merge_rows(cotangent, route_offset, input_rows, mine_array, range(1, ways), early)
     if by_swaps:
         qkv_a_got, qkv_b_got, input_grad = tie((qkv_a_got, qkv_b_got, input_grad))
         qkv_grad = spread_qkv(qkv_a, qkv_a_got, qkv_b, qkv_b_got, qkv_weight.shape[2])
@@ -1116,14 +1111,14 @@
         small = sum(joined_sums(fresh[k, own_rows:]) for k in range(ways))
         small = lax.psum(small, "dp")
         small = [small[n : n + 1] for n in range(TERMS)]
-        small[3] = small[3][:, :128] * jnp.array((shares + (0.0,) * 126,), F32)
+        small[3] = small[3][:, :2] * jnp.array((shares,), F32)
         down_grad, up_grad, qkv_sum, out_sum = (
             lax.psum(v, "dp").astype(F32) for v in (down_part, up_part, qkv_part, out_parts)
         )
         out_grad = jnp.sum(to_all(out_sum.astype(BF)).astype(F32), axis=0)
         qkv_grad = qkv_sum.reshape(3, -1, width).transpose(0, 2, 1)
     router_grad, first_gain_grad, second_gain_grad = (small[n].reshape(width) for n in range(3))
-    score_stats = small[3][0, :2]
+    score_stats = small[3].reshape(2)
     return (
         output,
         input_grad,

time: 235 us -> 229 us (0.974)
  waiting for transfers between devices: 53.1 us -> 46.6 us
  local copies, waits for them, and re-layouts: 24 us -> 28.5 us
  Pallas kernels: 96.1 us -> 92.3 us
  starting transfers between devices: 53.8 us -> 56.8 us
  other arithmetic: 2.9 us -> 0.05 us
    ppermute x30 -> x36, starting transfers between devices: 22.8 us -> 31.2 us  [swap(): return lax.ppermute(values, axis, [(i, i ^ bits) for i in range(size)])]
    ppermute x30 -> x36, waiting for transfers between devices: 29.4 us -> 21.5 us  [swap(): return lax.ppermute(values, axis, [(i, i ^ bits) for i in range(size)])]
    unnamed x96 -> x114, local copies, waits for them, and re-layouts: 19.5 us -> 25.7 us
    all_to_all x7 -> x6, starting transfers between devices: 31 us -> 25.5 us  [to_all(): return lax.all_to_all(blocks, 'tensor', 0, 0, tiled=True)]
    another operation x4 -> x1, other arithmetic: 2.9 us -> 0.05 us  [per_device(): here = jnp.stack(here)]
    all_to_all x7 -> x6, waiting for transfers between devices: 23.7 us -> 25.1 us  [to_all(): return lax.all_to_all(blocks, 'tensor', 0, 0, tiled=True)]
  transfers between devices with their start and end apart: 37 -> 42, of which waited for: 23 -> 15; matrix products, arithmetic and copies ran while one was open for 4% -> 2% of each run, Pallas kernels for 35% -> 35%
where the time goes in v5:
time: 229 us; the launch traced here: 228 us
  Pallas kernels  92.3 us (40%)
  starting transfers between devices  56.8 us (25%)
  waiting for transfers between devices  46.6 us (20%)
  local copies, waits for them, and re-layouts  28.5 us (12%)
    ppermute x36, starting transfers between devices, swap(): return lax.ppermute(values, axis, [(i, i ^ bits) for i in range(size)])  31.2 us
    unnamed x114, local copies, waits for them, and re-layouts  25.7 us
    all_to_all x6, starting transfers between devices, to_all(): return lax.all_to_all(blocks, 'tensor', 0, 0, tiled=True)  25.5 us
    all_to_all x6, waiting for transfers between devices, to_all(): return lax.all_to_all(blocks, 'tensor', 0, 0, tiled=True)  25.1 us
    ppermute x36, waiting for transfers between devices, swap(): return lax.ppermute(values, axis, [(i, i ^ bits) for i in range(size)])  21.5 us
    pallas_call x4, Pallas kernels, merge_rows(): pl.pallas_call(kernel, grid_spec=grid_spec, out_shape=jax.ShapeDtypeStruc...  20 us
    pallas_call x2, Pallas kernels, staged(): pl.pallas_call(kernel, in_specs=[pl.BlockSpec(memory_space=pltpu.SMEM)] *...  16.5 us
    pallas_call x1, Pallas kernels, spread_rows(): pl.pallas_call(kernel, grid_spec=pltpu.PrefetchScalarGridSpec(num_scalar_...  7.98 us
  transfers between devices with their start and end apart: 42, of which 15 were waited for; matrix products, arithmetic and copies ran while one was open for 2% of the time, Pallas kernels for 35%

profile of v5, /device:TPU:0, one launch (start us, length us, event | category | flops | bytes accessed | tf_op | source)
XLA Modules:
  0.0 227.6 jit_solution(5773743596885432615)
XLA Ops:
  1.6 3.1 %collective-permute-start = (bf16[64,1024]{1,0:T(8,128)(2,1)S(1)}, bf16[64,1024]{1,0:T(8,128)(2,1)S(1)}, u32[]{:S(2)}, u32[]{:S(2)}) collective-permute-start(bf16[64,1024]{1,0:T(8,128)(2,1)S(1)} %constant_dynamic-slice_fusion), channel_id=1, source_target_pairs={{0,1},{1,0},{2,3},{3,2},{4,5},{5,4},{6,7},{7,6},{8,9},{9,8},{10,11... | collective-permute-start | bytes 393224 | tf_op jit(solution)/shard_map/ppermute | solution.py:22
  4.7 2.6 %collective-permute-start.1 = (bf16[64,1024]{1,0:T(8,128)(2,1)S(1)}, bf16[64,1024]{1,0:T(8,128)(2,1)S(1)}, u32[]{:S(2)}, u32[]{:S(2)}) collective-permute-start(bf16[64,1024]{1,0:T(8,128)(2,1)S(1)} %constant_dynamic-slice_fusion), channel_id=1, source_target_pairs={{0,2},{1,3},{2,0},{3,1},{4,6},{5,7},{6,4},{7,5},{8,10},{9,11},{10,... | collective-permute-start | bytes 393224 | tf_op jit(solution)/shard_map/ppermute | solution.py:22
  7.3 5.7 %pick_rows.1.refs_0_.picked_ref.refs_8_ = bf16[512,1024]{1,0:T(8,128)(2,1)} custom-call(bf16[4096,1024]{1,0:T(8,128)(2,1)} %base_ref.9, s32[1,512]{1,0:T(1,128)} %offset_ref.11), custom_call_target="tpu_custom_call" | custom-call | flops 1024 | bytes 1024 | tf_op jit(solution)/shard_map/pick_rows/pallas_call | solution.py:133
  13.6 6.6 %attend.1 = (bf16[512,1024]{1,0:T(8,128)(2,1)}, bf16[3,512,256]{2,1,0:T(8,128)(2,1)}, bf16[4,512,256]{2,1,0:T(8,128)(2,1)}, bf16[4,256,256]{2,1,0:T(8,128)(2,1)}, bf16[4,256,512]{2,1,0:T(8,128)(2,1)}) custom-call(bf16[512,1024]{1,0:T(8,128)(2,1)} %pick_rows.1.refs_0_.picked_ref.refs_8_, bf16[1,1024]{1,0:T(2,128)(2,1)} %broadcast_in_dim.10.refs_1_.gain_ref, ...), custom_call_target="tpu_custom_call" | custom-call | flops 1024 | bytes 1024 | tf_op jit(solution)/shard_map/attend/pallas_call | solution.py:86
  20.2 5.1 %all-to-all-start = ((bf16[4,512,256]{2,1,0:T(8,128)(2,1)}), bf16[4,512,256]{2,1,0:T(8,128)(2,1)S(1)}, u32[]{:S(2)}, u32[]{:S(2)}) async-start(bf16[4,512,256]{2,1,0:T(8,128)(2,1)} %get-tuple-element.166), calls=%async_computation | async-start | bytes 2097152 | tf_op jit(solution)/shard_map/all_to_all | solution.py:26
  25.4 1.6 collective-permute-start.3
  26.9 6.0 %pick_only.1.rows_ref = bf16[512,1024]{1,0:T(8,128)(2,1)} custom-call(bf16[4096,1024]{1,0:T(8,128)(2,1)} %base_ref.10, s32[1,512]{1,0:T(1,128)} %offset_ref.11), custom_call_target="tpu_custom_call" | custom-call | flops 1024 | bytes 1024 | tf_op jit(solution)/shard_map/pick_only/pallas_call | solution.py:186
  32.9 2.3 collective-permute-done.3.refs_6_
  36.0 2.6 %score_sums.1.square_ref = f32[1,128]{1,0:T(1,128)} custom-call(s32[1]{0:T(128)} %bitcast.1.mine_ref.refs_1_.part_ref, bf16[4096,1024]{1,0:T(8,128)(2,1)} %base_ref.9, bf16[1,1024]{1,0:T(2,128)(2,1)} %broadcast_in_dim.11.router_ref), custom_call_target="tpu_custom_call" | custom-call | flops 1024 | bytes 1024 | tf_op jit(solution)/shard_map/score_sums/pallas_call | solution.py:153
  39.2 5.1 %act_grads.1 = (f32[512,1]{1,0:T(8,128)}, f32[1,128]{1,0:T(1,128)}, bf16[512,1024]{1,0:T(8,128)(2,1)}, f32[512,1024]{1,0:T(8,128)}) custom-call(bf16[512,1024]{1,0:T(8,128)(2,1)} %pick_rows.1.refs_0_.picked_ref.refs_8_, bf16[1,1024]{1,0:T(2,128)(2,1)} %broadcast_in_dim.11.router_ref, bf16[512,1024]{1,0:T(8,128)(2,1)} %pick_only.1.rows_ref, ...), custom_call_target="tpu_custom_call" | custom-call | flops 1024 | bytes 1024 | tf_op jit(solution)/shard_map/act_grads/pallas_call | solution.py:397
  44.4 5.8 %all-to-all-done.refs_2_.heads_ref = bf16[4,512,256]{2,1,0:T(8,128)(2,1)S(1)} async-done(((bf16[4,512,256]{2,1,0:T(8,128)(2,1)}), bf16[4,512,256]{2,1,0:T(8,128)(2,1)S(1)}, u32[]{:S(2)}, u32[]{:S(2)}) %all-to-all-start) | async-done | bytes 1048608 | tf_op jit(solution)/shard_map/all_to_all | solution.py:26
  51.1 9.9 %feed_forward.1 = (f32[128,1024]{1,0:T(8,128)}, bf16[512,1024]{1,0:T(8,128)(2,1)}, bf16[512,1024]{1,0:T(8,128)(2,1)}, bf16[512,1024]{1,0:T(8,128)(2,1)}, bf16[51...) custom-call(s32[1]{0:T(128)} %bitcast.refs_0_.part_ref, ...), custom_call_target="tpu_custom_call" | custom-call | flops 1024 | bytes 1024 | tf_op jit(solution)/shard_map/feed_forward/pallas_call | solution.py:86
  61.1 4.6 %all-to-all-start.1 = ((bf16[4,512,256]{2,1,0:T(8,128)(2,1)}), bf16[4,512,256]{2,1,0:T(8,128)(2,1)}, u32[]{:S(2)}, u32[]{:S(2)}) async-start(bf16[4,512,256]{2,1,0:T(8,128)(2,1)} %get-tuple-element.187), calls=%async_computation.1 | async-start | bytes 2097152 | tf_op jit(solution)/shard_map/all_to_all | solution.py:26
  70.7 3.9 %core_grads.1 = (bf16[2,768,1024]{2,1,0:T(8,128)(2,1)S(1)}, bf16[512,1024]{1,0:T(8,128)(2,1)S(1)}, bf16[512,1024]{1,0:T(8,128)(2,1)S(1)}, bf16[256,1024]{1,0:T(8,128)(2,1)S(1)}, bf16[256,1024]{1,0:T(8,128)(2,1)S(1)}) custom-call(s32[1]{0:T(128)} %bitcast.refs_0_.part_ref, bf16[512,1024]{1,0:T(8,128)(2,1)S(1)} %copy-done.10, bf16[512,1024]{1,0:T(8,128)(2,1)S(1)} %copy-done.6, ...), custom_call_target="tpu_custom_call" | custom-call | flops 1024 | bytes 1024 | tf_op jit(solution)/shard_map/core_grads/pallas_call | solution.py:614
  75.6 2.2 convolution_convert_fusion
  77.8 1.6 collective-permute-done.8.refs_1_
  84.0 6.8 %all-to-all-done.1.head_ref = bf16[4,512,256]{2,1,0:T(8,128)(2,1)} async-done(((bf16[4,512,256]{2,1,0:T(8,128)(2,1)}), bf16[4,512,256]{2,1,0:T(8,128)(2,1)}, u32[]{:S(2)}, u32[]{:S(2)}) %all-to-all-start.1) | async-done | bytes 1048608 | tf_op jit(solution)/shard_map/all_to_all | solution.py:26
  90.8 4.2 %all-to-all-start.2 = ((bf16[4,128,1024]{2,1,0:T(8,128)(2,1)}), bf16[4,128,1024]{2,1,0:T(8,128)(2,1)}, u32[]{:S(2)}, u32[]{:S(2)}) async-start(bf16[4,128,1024]{2,1,0:T(8,128)(2,1)} %bitcast.15), calls=%async_computation.2 | async-start | bytes 2097152 | tf_op jit(solution)/shard_map/all_to_all | solution.py:26
  95.0 1.6 collective-permute-start.10
  96.6 1.5 collective-permute-start.11
  101.6 5.8 %attend_back.1 = (bf16[3,512,256]{2,1,0:T(8,128)(2,1)S(1)}, f32[1,1024]{1,0:T(1,128)S(1)}, bf16[512,1024]{1,0:T(8,128)(2,1)S(1)}) custom-call(bf16[4,512,256]{2,1,0:T(8,128)(2,1)} %all-to-all-done.1.head_ref, bf16[3,512,256]{2,1,0:T(8,128)(2,1)S(1)} %copy-done.19, bf16[3,1024,256]{2,1,0:T(8,128)(2,1)S(1)} %copy-done.5, bf16[512,1024]{1,0:T(8,128)(2,1)S(1)} %copy-done, ...), custom_call_target="tpu_custom_call" | custom-call | flops 1024 | bytes 1024 | tf_op jit(solution)/shard_map/attend_back/pallas_call | solution.py:473
  108.5 5.3 %collective-permute-done.10.refs_0_ = bf16[384,1024]{1,0:T(8,128)(2,1)S(1)} collective-permute-done((bf16[384,1024]{1,0:T(8,128)(2,1)}, bf16[384,1024]{1,0:T(8,128)(2,1)S(1)}, u32[]{:S(2)}, u32[]{:S(2)}) %collective-permute-start.10) | collective-permute-done | bytes 786464 | tf_op jit(solution)/shard_map/ppermute | solution.py:22
  116.9 3.4 %all-to-all-done.2.terms_ref = bf16[4,128,1024]{2,1,0:T(8,128)(2,1)} async-done(((bf16[4,128,1024]{2,1,0:T(8,128)(2,1)}), bf16[4,128,1024]{2,1,0:T(8,128)(2,1)}, u32[]{:S(2)}, u32[]{:S(2)}) %all-to-all-start.2) | async-done | bytes 1048608 | tf_op jit(solution)/shard_map/all_to_all | solution.py:26
  120.3 3.8 %all-to-all-start.3 = ((bf16[4,128,1024]{2,1,0:T(8,128)(2,1)}), bf16[4,128,1024]{2,1,0:T(8,128)(2,1)S(1)}, u32[]{:S(2)}, u32[]{:S(2)}) async-start(bf16[4,128,1024]{2,1,0:T(8,128)(2,1)} %bitcast.14), calls=%async_computation.3 | async-start | bytes 2097152 | tf_op jit(solution)/shard_map/all_to_all | solution.py:26
  124.1 1.6 collective-permute-start.13
  127.2 2.6 %finish_rows.1 = (bf16[128,1024]{1,0:T(8,128)(2,1)}, f32[128,1]{1,0:T(8,128)}, f32[4,1024]{1,0:T(4,128)}) custom-call(s32[1]{0:T(128)} %bitcast.1.mine_ref.refs_1_.part_ref, bf16[4,128,1024]{2,1,0:T(8,128)(2,1)} %all-to-all-done.2.terms_ref, bf16[512,1024]{1,0:T(8,128)(2,1)} %pick_rows.1.refs_0_.picked_ref.refs_8_, f32[512,1]{1,0:T(8,128)} %get-tuple-element.230.gating_ref, ...), custom_call_target="tpu_custom_call" | custom-call | flops 1024 | bytes 30000000 | tf_op jit(solution)/shard_map/finish_rows/pallas_call | solution.py:855
  129.8 6.2 %collective-permute-done.13.a_got = bf16[192,1024]{1,0:T(8,128)(2,1)} collective-permute-done((bf16[192,1024]{1,0:T(8,128)(2,1)}, bf16[192,1024]{1,0:T(8,128)(2,1)}, u32[]{:S(2)}, u32[]{:S(2)}) %collective-permute-start.13) | collective-permute-done | bytes 393248 | tf_op jit(solution)/shard_map/ppermute | solution.py:22
  142.4 1.8 core_sums.1
  145.9 2.1 collective-permute-done.15.refs_1_
  148.7 1.8 all-to-all-done.3.terms_ref
  150.5 3.5 %all-to-all-start.4 = ((bf16[4,168,1024]{2,1,0:T(8,128)(2,1)}), bf16[4,168,1024]{2,1,0:T(8,128)(2,1)S(1)}, u32[]{:S(2)}, u32[]{:S(2)}) async-start(bf16[4,168,1024]{2,1,0:T(8,128)(2,1)} %copy-done.9), calls=%async_computation.4 | async-start | bytes 2752512 | tf_op jit(solution)/shard_map/all_to_all | solution.py:26
  154.0 1.6 collective-permute-start.18
  155.6 1.5 collective-permute-start.20
  161.0 1.8 gather_blocks.2
  164.9 3.8 %merge_rows.4.rest_0_ = bf16[4096,1024]{1,0:T(8,128)(2,1)} custom-call(s32[1]{0:T(128)} %bitcast.1.mine_ref.refs_1_.part_ref, bf16[4096,1024]{1,0:T(8,128)(2,1)} %base_ref.10, s32[1,512]{1,0:T(1,128)} %offset_ref.11, bf16[4,128,1024]{2,1,0:T(8,128)(2,1)} %finish_input.1.piece_ref), custom_call_target="tpu_custom_call" | custom-call | flops 1024 | bytes 1024 | tf_op jit(solution)/shard_map/merge_rows/pallas_call | solution.py:232
  171.1 1.5 collective-permute-start.25
  172.6 1.5 collective-permute-start.26
  175.8 8.0 %spread_rows.1 = (f32[1024,1024]{1,0:T(8,128)}, f32[1024,1024]{1,0:T(8,128)}) custom-call(s32[1]{0:T(128)} %bitcast.refs_0_.part_ref, bf16[256,1024]{1,0:T(8,128)(2,1)} %get-tuple-element.257.refs_0_, bf16[256,1024]{1,0:T(8,128)(2,1)} %copy-done.29, bf16[256,1024]{1,0:T(8,128)(2,1)} %collective-permute-done.21.refs_2_, bf16[256,1024]{1,0:T(8,128)(2,1)} %copy-done.50, ...), custom_call_target="tpu_custom_call" | custom-call | flops 1024 | bytes 1024 | tf_op jit(solution)/shard_map/spread_rows/pallas_call | solution.py:517
  183.8 3.2 %all-to-all-done.4.got_ref.piece_ref = bf16[4,168,1024]{2,1,0:T(8,128)(2,1)S(1)} async-done(((bf16[4,168,1024]{2,1,0:T(8,128)(2,1)}), bf16[4,168,1024]{2,1,0:T(8,128)(2,1)S(1)}, u32[]{:S(2)}, u32[]{:S(2)}) %all-to-all-start.4) | async-done | bytes 1376288 | tf_op jit(solution)/shard_map/all_to_all | solution.py:26
  186.9 4.2 %all-to-all-start.5 = ((bf16[4,128,1024]{2,1,0:T(8,128)(2,1)}), bf16[4,128,1024]{2,1,0:T(8,128)(2,1)}, u32[]{:S(2)}, u32[]{:S(2)}) async-start(bf16[4,128,1024]{2,1,0:T(8,128)(2,1)} %finish_input.1.piece_ref), calls=%async_computation.5 | async-start | bytes 2097152 | tf_op jit(solution)/shard_map/all_to_all | solution.py:26
  191.2 1.6 collective-permute-start.27
  192.8 1.5 collective-permute-start.30
  196.6 1.7 lane_sums.1
  198.9 4.4 %merge_rows.5.rest_0_ = bf16[4096,1024]{1,0:T(8,128)(2,1)} custom-call(s32[1]{0:T(128)} %bitcast.1.mine_ref.refs_1_.part_ref, bf16[4096,1024]{1,0:T(8,128)(2,1)} %base_ref.9, s32[1,512]{1,0:T(1,128)} %offset_ref.11, bf16[4,168,1024]{2,1,0:T(8,128)(2,1)} %copy-done.1), custom_call_target="tpu_custom_call" | custom-call | flops 1024 | bytes 1024 | tf_op jit(solution)/shard_map/merge_rows/pallas_call | solution.py:232
  206.9 4.4 %merge_rows.6 = bf16[4096,1024]{1,0:T(8,128)(2,1)} custom-call(s32[1]{0:T(128)} %bitcast.1.mine_ref.refs_1_.part_ref, bf16[4096,1024]{1,0:T(8,128)(2,1)} %base_ref.9, s32[1,512]{1,0:T(1,128)} %offset_ref.11, bf16[4,168,1024]{2,1,0:T(8,128)(2,1)} %copy-done.1, bf16[4096,1024]{1,0:T(8,128)(2,1)} %merge_rows.5.rest_0_), custom_call_target="tpu_custom_call", output_to_operand_aliasing={{}: (4, {})} | custom-call | flops 1024 | bytes 1024 | tf_op jit(solution)/shard_map/merge_rows/pallas_call | solution.py:232
  212.4 4.1 %all-to-all-done.5.piece_ref = bf16[4,128,1024]{2,1,0:T(8,128)(2,1)} async-done(((bf16[4,128,1024]{2,1,0:T(8,128)(2,1)}), bf16[4,128,1024]{2,1,0:T(8,128)(2,1)}, u32[]{:S(2)}, u32[]{:S(2)}) %all-to-all-start.5) | async-done | bytes 1048608 | tf_op jit(solution)/shard_map/all_to_all | solution.py:26
  216.5 7.5 %merge_rows.7 = bf16[4096,1024]{1,0:T(8,128)(2,1)} custom-call(s32[1]{0:T(128)} %bitcast.1.mine_ref.refs_1_.part_ref, bf16[4096,1024]{1,0:T(8,128)(2,1)} %base_ref.10, s32[1,512]{1,0:T(1,128)} %offset_ref.11, bf16[4,128,1024]{2,1,0:T(8,128)(2,1)} %all-to-all-done.5.piece_ref, bf16[4096,1024]{1,0:T(8,128)(2,1)} %merge_rows.4.rest_0_), custom_call_target="tpu_custom_call", output_to_operand_aliasing={{}: (4, {})} | custom-call | flops 1024 | bytes 1024 | tf_op jit(solution)/shard_map/merge_rows/pallas_call | solution.py:232
  224.0 3.7 %spread_qkv.1 = f32[3,1024,256]{2,1,0:T(8,128)} custom-call(bf16[384,1024]{1,0:T(8,128)(2,1)S(1)} %get-tuple-element.313.a_ref, bf16[384,1024]{1,0:T(8,128)(2,1)S(1)} %collective-permute-done.34.a_got, bf16[384,1024]{1,0:T(8,128)(2,1)S(1)} %get-tuple-element.306.b_ref, bf16[384,1024]{1,0:T(8,128)(2,1)} %collective-permute-done.35.b_got), custom_call_target="tpu_custom_call" | custom-call | flops 1024 | bytes 1024 | tf_op jit(solution)/shard_map/spread_qkv/pallas_call | solution.py:565
  (182 shorter events, 49.9 us)
Async XLA Ops:
  1.6 18.6 %collective-permute-start = (bf16[64,1024]{1,0:T(8,128)(2,1)S(1)}, bf16[64,1024]{1,0:T(8,128)(2,1)S(1)}, u32[]{:S(2)}, u32[]{:S(2)}) collective-permute-start(bf16[64,1024]{1,0:T(8,128)(2,1)S(1)} %constant_dynamic-slice_fusion), channel_id=1, source_target_pairs={{0,1},{1,0},{2,3},{3,2},{4,5},{5,4},{6,7},{7,6},{8,9},{9,8},{10,11... | collective-permute-start | bytes 393224 | tf_op jit(solution)/shard_map/ppermute | solution.py:22
  4.7 15.5 %collective-permute-start.1 = (bf16[64,1024]{1,0:T(8,128)(2,1)S(1)}, bf16[64,1024]{1,0:T(8,128)(2,1)S(1)}, u32[]{:S(2)}, u32[]{:S(2)}) collective-permute-start(bf16[64,1024]{1,0:T(8,128)(2,1)S(1)} %constant_dynamic-slice_fusion), channel_id=1, source_target_pairs={{0,2},{1,3},{2,0},{3,1},{4,6},{5,7},{6,4},{7,5},{8,10},{9,11},{10,... | collective-permute-start | bytes 393224 | tf_op jit(solution)/shard_map/ppermute | solution.py:22
  7.3 12.9 %collective-permute-start.2 = (bf16[64,1024]{1,0:T(8,128)(2,1)S(1)}, bf16[64,1024]{1,0:T(8,128)(2,1)S(1)}, u32[]{:S(2)}, u32[]{:S(2)}) collective-permute-start(bf16[64,1024]{1,0:T(8,128)(2,1)S(1)} %constant_dynamic-slice_fusion), channel_id=1, source_target_pairs={{0,3},{1,2},{2,1},{3,0},{4,7},{5,6},{6,5},{7,4},{8,11},{9,10},{10,... | collective-permute-start | bytes 393224 | tf_op jit(solution)/shard_map/ppermute | solution.py:22
  20.2 30.0 %all-to-all-start = ((bf16[4,512,256]{2,1,0:T(8,128)(2,1)}), bf16[4,512,256]{2,1,0:T(8,128)(2,1)S(1)}, u32[]{:S(2)}, u32[]{:S(2)}) async-start(bf16[4,512,256]{2,1,0:T(8,128)(2,1)} %get-tuple-element.166), calls=%async_computation | async-start | bytes 2097152 | tf_op jit(solution)/shard_map/all_to_all | solution.py:26
  25.4 9.8 %collective-permute-start.3 = (bf16[3,64,1024]{2,1,0:T(8,128)(2,1)S(1)}, bf16[3,64,1024]{2,1,0:T(8,128)(2,1)S(1)}, u32[]{:S(2)}, u32[]{:S(2)}) collective-permute-start(bf16[3,64,1024]{2,1,0:T(8,128)(2,1)S(1)} %pad_maximum_fusion.refs_4_), channel_id=1, source_target_pairs={{0,8},{4,12},{8,0},{12,4},{16,24},{20,28},{24,16},{28,20},{1,9},{5... | collective-permute-start | bytes 1179656 | tf_op jit(solution)/shard_map/ppermute | solution.py:22
  26.9 8.3 %collective-permute-start.4 = (bf16[3,64,1024]{2,1,0:T(8,128)(2,1)S(1)}, bf16[3,64,1024]{2,1,0:T(8,128)(2,1)S(1)}, u32[]{:S(2)}, u32[]{:S(2)}) collective-permute-start(bf16[3,64,1024]{2,1,0:T(8,128)(2,1)S(1)} %pad_maximum_fusion.refs_4_), channel_id=1, source_target_pairs={{0,4},{4,0},{8,12},{12,8},{16,20},{20,16},{24,28},{28,24},{1,5},{5... | collective-permute-start | bytes 1179656 | tf_op jit(solution)/shard_map/ppermute | solution.py:22
  35.2 9.2 %collective-permute-start.5 = (bf16[3,64,1024]{2,1,0:T(8,128)(2,1)S(1)}, bf16[3,64,1024]{2,1,0:T(8,128)(2,1)S(1)}, u32[]{:S(2)}, u32[]{:S(2)}) collective-permute-start(bf16[3,64,1024]{2,1,0:T(8,128)(2,1)S(1)} %collective-permute-done.3.refs_6_), channel_id=1, source_target_pairs={{0,4},{4,0},{8,12},{12,8},{16,20},{20,16},{24,28},{28,24},{1,5},{5... | collective-permute-start | bytes 1179656 | tf_op jit(solution)/shard_map/ppermute | solution.py:22
  61.1 29.7 %all-to-all-start.1 = ((bf16[4,512,256]{2,1,0:T(8,128)(2,1)}), bf16[4,512,256]{2,1,0:T(8,128)(2,1)}, u32[]{:S(2)}, u32[]{:S(2)}) async-start(bf16[4,512,256]{2,1,0:T(8,128)(2,1)} %get-tuple-element.187), calls=%async_computation.1 | async-start | bytes 2097152 | tf_op jit(solution)/shard_map/all_to_all | solution.py:26
  74.5 5.7 %collective-permute-start.6 = (bf16[512,1024]{1,0:T(8,128)(2,1)S(1)}, bf16[512,1024]{1,0:T(8,128)(2,1)S(1)}, u32[]{:S(2)}, u32[]{:S(2)}) collective-permute-start(bf16[512,1024]{1,0:T(8,128)(2,1)S(1)} %get-tuple-element.192), channel_id=1, source_target_pairs={{0,4},{4,0},{8,12},{12,8},{16,20},{20,16},{24,28},{28,24},{1,5},{5... | collective-permute-start | bytes 3145736 | tf_op jit(solution)/shard_map/ppermute | solution.py:22
  74.6 5.7 %collective-permute-start.7 = (bf16[512,1024]{1,0:T(8,128)(2,1)S(1)}, bf16[512,1024]{1,0:T(8,128)(2,1)S(1)}, u32[]{:S(2)}, u32[]{:S(2)}) collective-permute-start(bf16[512,1024]{1,0:T(8,128)(2,1)S(1)} %get-tuple-element.193), channel_id=1, source_target_pairs={{0,4},{4,0},{8,12},{12,8},{16,20},{20,16},{24,28},{28,24},{1,5},{5... | collective-permute-start | bytes 3145736 | tf_op jit(solution)/shard_map/ppermute | solution.py:22
  75.1 4.4 %collective-permute-start.8 = (bf16[256,1024]{1,0:T(8,128)(2,1)S(1)}, bf16[256,1024]{1,0:T(8,128)(2,1)S(1)}, u32[]{:S(2)}, u32[]{:S(2)}) collective-permute-start(bf16[256,1024]{1,0:T(8,128)(2,1)S(1)} %get-tuple-element.194), channel_id=1, source_target_pairs={{0,4},{4,0},{8,12},{12,8},{16,20},{20,16},{24,28},{28,24},{1,5},{5... | collective-permute-start | bytes 1572872 | tf_op jit(solution)/shard_map/ppermute | solution.py:22
  75.2 5.1 %collective-permute-start.9 = (bf16[256,1024]{1,0:T(8,128)(2,1)S(1)}, bf16[256,1024]{1,0:T(8,128)(2,1)S(1)}, u32[]{:S(2)}, u32[]{:S(2)}) collective-permute-start(bf16[256,1024]{1,0:T(8,128)(2,1)S(1)} %get-tuple-element.195), channel_id=1, source_target_pairs={{0,4},{4,0},{8,12},{12,8},{16,20},{20,16},{24,28},{28,24},{1,5},{5... | collective-permute-start | bytes 1572872 | tf_op jit(solution)/shard_map/ppermute | solution.py:22
  80.2 17.9 %copy-start.5 = (bf16[3,1024,256]{2,1,0:T(8,128)(2,1)S(1)}, bf16[3,1024,256]{2,1,0:T(8,128)(2,1)}, u32[]{:S(2)}) copy-start(bf16[3,1024,256]{2,1,0:T(8,128)(2,1)} %weight_ref.1) | copy-start | bytes 4718596
  84.0 14.1 %copy-start.19 = (bf16[3,512,256]{2,1,0:T(8,128)(2,1)S(1)}, bf16[3,512,256]{2,1,0:T(8,128)(2,1)}, u32[]{:S(2)}) copy-start(bf16[3,512,256]{2,1,0:T(8,128)(2,1)} %get-tuple-element.210.qkv_ref) | copy-start | bytes 2359300
  84.0 14.1 %copy-start.40 = (bf16[1,1024]{1,0:T(2,128)(2,1)S(1)}, bf16[1,1024]{1,0:T(2,128)(2,1)}, u32[]{:S(2)}) copy-start(bf16[1,1024]{1,0:T(2,128)(2,1)} %broadcast_in_dim.10.refs_1_.gain_ref) | copy-start | bytes 6148
  90.8 29.5 %all-to-all-start.2 = ((bf16[4,128,1024]{2,1,0:T(8,128)(2,1)}), bf16[4,128,1024]{2,1,0:T(8,128)(2,1)}, u32[]{:S(2)}, u32[]{:S(2)}) async-start(bf16[4,128,1024]{2,1,0:T(8,128)(2,1)} %bitcast.15), calls=%async_computation.2 | async-start | bytes 2097152 | tf_op jit(solution)/shard_map/all_to_all | solution.py:26
  95.0 18.8 %collective-permute-start.10 = (bf16[384,1024]{1,0:T(8,128)(2,1)}, bf16[384,1024]{1,0:T(8,128)(2,1)S(1)}, u32[]{:S(2)}, u32[]{:S(2)}) collective-permute-start(bf16[384,1024]{1,0:T(8,128)(2,1)} %copy-done.44), channel_id=1, source_target_pairs={{0,8},{4,12},{8,0},{12,4},{16,24},{20,28},{24,16},{28,20},{1,9},{5... | collective-permute-start | bytes 2359304 | tf_op jit(solution)/shard_map/ppermute | solution.py:22
  96.6 18.4 %collective-permute-start.11 = (bf16[384,1024]{1,0:T(8,128)(2,1)}, bf16[384,1024]{1,0:T(8,128)(2,1)S(1)}, u32[]{:S(2)}, u32[]{:S(2)}) collective-permute-start(bf16[384,1024]{1,0:T(8,128)(2,1)} %copy-done.43), channel_id=1, source_target_pairs={{0,16},{4,20},{8,24},{12,28},{16,0},{20,4},{24,8},{28,12},{1,17},{... | collective-permute-start | bytes 2359304 | tf_op jit(solution)/shard_map/ppermute | solution.py:22
  120.3 22.0 %collective-permute-start.12 = (bf16[768,1024]{1,0:T(8,128)(2,1)S(1)}, bf16[768,1024]{1,0:T(8,128)(2,1)}, u32[]{:S(2)}, u32[]{:S(2)}) collective-permute-start(bf16[768,1024]{1,0:T(8,128)(2,1)S(1)} %qkv_part.1.rows_ref), channel_id=1, source_target_pairs={{0,4},{4,0},{8,12},{12,8},{16,20},{20,16},{24,28},{28,24},{1,5},{5... | collective-permute-start | bytes 4718600 | tf_op jit(solution)/shard_map/ppermute | solution.py:22
  120.3 30.2 %all-to-all-start.3 = ((bf16[4,128,1024]{2,1,0:T(8,128)(2,1)}), bf16[4,128,1024]{2,1,0:T(8,128)(2,1)S(1)}, u32[]{:S(2)}, u32[]{:S(2)}) async-start(bf16[4,128,1024]{2,1,0:T(8,128)(2,1)} %bitcast.14), calls=%async_computation.3 | async-start | bytes 2097152 | tf_op jit(solution)/shard_map/all_to_all | solution.py:26
  124.1 11.9 %collective-permute-start.13 = (bf16[192,1024]{1,0:T(8,128)(2,1)}, bf16[192,1024]{1,0:T(8,128)(2,1)}, u32[]{:S(2)}, u32[]{:S(2)}) collective-permute-start(bf16[192,1024]{1,0:T(8,128)(2,1)} %copy-done.46), channel_id=1, source_target_pairs={{0,16},{4,20},{8,24},{12,28},{16,0},{20,4},{24,8},{28,12},{1,17},{... | collective-permute-start | bytes 1179656 | tf_op jit(solution)/shard_map/ppermute | solution.py:22
  125.7 11.6 %collective-permute-start.14 = (bf16[192,1024]{1,0:T(8,128)(2,1)}, bf16[192,1024]{1,0:T(8,128)(2,1)}, u32[]{:S(2)}, u32[]{:S(2)}) collective-permute-start(bf16[192,1024]{1,0:T(8,128)(2,1)} %copy-done.45), channel_id=1, source_target_pairs={{0,8},{4,12},{8,0},{12,4},{16,24},{20,28},{24,16},{28,20},{1,9},{5... | collective-permute-start | bytes 1179656 | tf_op jit(solution)/shard_map/ppermute | solution.py:22
  140.3 7.7 %collective-permute-start.15 = (bf16[128,1024]{1,0:T(8,128)(2,1)S(1)}, bf16[128,1024]{1,0:T(8,128)(2,1)S(1)}, u32[]{:S(2)}, u32[]{:S(2)}) collective-permute-start(bf16[128,1024]{1,0:T(8,128)(2,1)S(1)} %get-tuple-element.253.refs_0_), channel_id=1, source_target_pairs={{0,16},{4,20},{8,24},{12,28},{16,0},{20,4},{24,8},{28,12},{1,17},{... | collective-permute-start | bytes 786440 | tf_op jit(solution)/shard_map/ppermute | solution.py:22
  140.9 7.8 %collective-permute-start.16 = (bf16[128,1024]{1,0:T(8,128)(2,1)S(1)}, bf16[128,1024]{1,0:T(8,128)(2,1)}, u32[]{:S(2)}, u32[]{:S(2)}) collective-permute-start(bf16[128,1024]{1,0:T(8,128)(2,1)S(1)} %get-tuple-element.255.refs_2_), channel_id=1, source_target_pairs={{0,8},{4,12},{8,0},{12,4},{16,24},{20,28},{24,16},{28,20},{1,9},{5... | collective-permute-start | bytes 786440 | tf_op jit(solution)/shard_map/ppermute | solution.py:22
  145.9 17.7 %copy-start.2 = (bf16[512,1024]{1,0:T(8,128)(2,1)S(1)}, bf16[512,1024]{1,0:T(8,128)(2,1)}, u32[]{:S(2)}) copy-start(bf16[512,1024]{1,0:T(8,128)(2,1)} %pick_only.1.rows_ref) | copy-start | bytes 3145732
  145.9 17.7 %copy-start.38 = (bf16[1,1024]{1,0:T(2,128)(2,1)S(1)}, bf16[1,1024]{1,0:T(2,128)(2,1)}, u32[]{:S(2)}) copy-start(bf16[1,1024]{1,0:T(2,128)(2,1)} %broadcast_in_dim.11.router_ref) | copy-start | bytes 6148
  145.9 17.8 %copy-start.39 = (f32[128,1]{1,0:T(8,128)S(1)}, f32[128,1]{1,0:T(8,128)}, u32[]{:S(2)}) copy-start(f32[128,1]{1,0:T(8,128)} %get-tuple-element.251.score_ref) | copy-start | bytes 1540
  150.5 36.4 %all-to-all-start.4 = ((bf16[4,168,1024]{2,1,0:T(8,128)(2,1)}), bf16[4,168,1024]{2,1,0:T(8,128)(2,1)S(1)}, u32[]{:S(2)}, u32[]{:S(2)}) async-start(bf16[4,168,1024]{2,1,0:T(8,128)(2,1)} %copy-done.9), calls=%async_computation.4 | async-start | bytes 2752512 | tf_op jit(solution)/shard_map/all_to_all | solution.py:26
  154.0 14.6 %collective-permute-start.18 = (bf16[128,1024]{1,0:T(8,128)(2,1)}, bf16[128,1024]{1,0:T(8,128)(2,1)}, u32[]{:S(2)}, u32[]{:S(2)}) collective-permute-start(bf16[128,1024]{1,0:T(8,128)(2,1)} %copy-done.36), channel_id=1, source_target_pairs={{0,8},{4,12},{8,0},{12,4},{16,24},{20,28},{24,16},{28,20},{1,9},{5... | collective-permute-start | bytes 786440 | tf_op jit(solution)/shard_map/ppermute | solution.py:22
  155.6 13.6 %collective-permute-start.20 = (bf16[128,1024]{1,0:T(8,128)(2,1)}, bf16[128,1024]{1,0:T(8,128)(2,1)}, u32[]{:S(2)}, u32[]{:S(2)}) collective-permute-start(bf16[128,1024]{1,0:T(8,128)(2,1)} %collective-permute-done.16.refs_3_), channel_id=1, source_target_pairs={{0,16},{4,20},{8,24},{12,28},{16,0},{20,4},{24,8},{28,12},{1,17},{... | collective-permute-start | bytes 786440 | tf_op jit(solution)/shard_map/ppermute | solution.py:22
  157.1 12.1 %collective-permute-start.17 = (bf16[128,1024]{1,0:T(8,128)(2,1)}, bf16[128,1024]{1,0:T(8,128)(2,1)}, u32[]{:S(2)}, u32[]{:S(2)}) collective-permute-start(bf16[128,1024]{1,0:T(8,128)(2,1)} %copy-done.34), channel_id=1, source_target_pairs={{0,8},{4,12},{8,0},{12,4},{16,24},{20,28},{24,16},{28,20},{1,9},{5... | collective-permute-start | bytes 786440 | tf_op jit(solution)/shard_map/ppermute | solution.py:22
  157.7 11.5 %collective-permute-start.19 = (bf16[128,1024]{1,0:T(8,128)(2,1)}, bf16[128,1024]{1,0:T(8,128)(2,1)}, u32[]{:S(2)}, u32[]{:S(2)}) collective-permute-start(bf16[128,1024]{1,0:T(8,128)(2,1)} %copy-done.32), channel_id=1, source_target_pairs={{0,16},{4,20},{8,24},{12,28},{16,0},{20,4},{24,8},{28,12},{1,17},{... | collective-permute-start | bytes 786440 | tf_op jit(solution)/shard_map/ppermute | solution.py:22
  163.6 8.9 %collective-permute-start.21 = (bf16[256,1024]{1,0:T(8,128)(2,1)}, bf16[256,1024]{1,0:T(8,128)(2,1)}, u32[]{:S(2)}, u32[]{:S(2)}) collective-permute-start(bf16[256,1024]{1,0:T(8,128)(2,1)} %get-tuple-element.257.refs_0_), channel_id=1, source_target_pairs={{0,4},{4,0},{8,12},{12,8},{16,20},{20,16},{24,28},{28,24},{1,5},{5... | collective-permute-start | bytes 1572872 | tf_op jit(solution)/shard_map/ppermute | solution.py:22
  168.7 5.4 %collective-permute-start.23 = (bf16[256,1024]{1,0:T(8,128)(2,1)S(1)}, bf16[256,1024]{1,0:T(8,128)(2,1)S(1)}, u32[]{:S(2)}, u32[]{:S(2)}) collective-permute-start(bf16[256,1024]{1,0:T(8,128)(2,1)S(1)} %copy-done.28), channel_id=1, source_target_pairs={{0,4},{4,0},{8,12},{12,8},{16,20},{20,16},{24,28},{28,24},{1,5},{5... | collective-permute-start | bytes 1572872 | tf_op jit(solution)/shard_map/ppermute | solution.py:22
  170.5 3.6 %collective-permute-start.22 = (bf16[256,1024]{1,0:T(8,128)(2,1)S(1)}, bf16[256,1024]{1,0:T(8,128)(2,1)S(1)}, u32[]{:S(2)}, u32[]{:S(2)}) collective-permute-start(bf16[256,1024]{1,0:T(8,128)(2,1)S(1)} %get-tuple-element.265.refs_1_), channel_id=1, source_target_pairs={{0,4},{4,0},{8,12},{12,8},{16,20},{20,16},{24,28},{28,24},{1,5},{5... | collective-permute-start | bytes 1572872 | tf_op jit(solution)/shard_map/ppermute | solution.py:22
  170.6 5.2 %collective-permute-start.24 = (bf16[256,1024]{1,0:T(8,128)(2,1)S(1)}, bf16[256,1024]{1,0:T(8,128)(2,1)}, u32[]{:S(2)}, u32[]{:S(2)}) collective-permute-start(bf16[256,1024]{1,0:T(8,128)(2,1)S(1)} %get-tuple-element.267.refs_5_), channel_id=1, source_target_pairs={{0,4},{4,0},{8,12},{12,8},{16,20},{20,16},{24,28},{28,24},{1,5},{5... | collective-permute-start | bytes 1572872 | tf_op jit(solution)/shard_map/ppermute | solution.py:22
  171.1 21.7 %collective-permute-start.25 = (bf16[384,1024]{1,0:T(8,128)(2,1)S(1)}, bf16[384,1024]{1,0:T(8,128)(2,1)}, u32[]{:S(2)}, u32[]{:S(2)}) collective-permute-start(bf16[384,1024]{1,0:T(8,128)(2,1)S(1)} %copy-done.21), channel_id=1, source_target_pairs={{0,16},{4,20},{8,24},{12,28},{16,0},{20,4},{24,8},{28,12},{1,17},{... | collective-permute-start | bytes 2359304 | tf_op jit(solution)/shard_map/ppermute | solution.py:22
  172.6 20.2 %collective-permute-start.26 = (bf16[384,1024]{1,0:T(8,128)(2,1)S(1)}, bf16[384,1024]{1,0:T(8,128)(2,1)}, u32[]{:S(2)}, u32[]{:S(2)}) collective-permute-start(bf16[384,1024]{1,0:T(8,128)(2,1)S(1)} %copy-done.24), channel_id=1, source_target_pairs={{0,8},{4,12},{8,0},{12,4},{16,24},{20,28},{24,16},{28,20},{1,9},{5... | collective-permute-start | bytes 2359304 | tf_op jit(solution)/shard_map/ppermute | solution.py:22
  186.9 29.6 %all-to-all-start.5 = ((bf16[4,128,1024]{2,1,0:T(8,128)(2,1)}), bf16[4,128,1024]{2,1,0:T(8,128)(2,1)}, u32[]{:S(2)}, u32[]{:S(2)}) async-start(bf16[4,128,1024]{2,1,0:T(8,128)(2,1)} %finish_input.1.piece_ref), calls=%async_computation.5 | async-start | bytes 2097152 | tf_op jit(solution)/shard_map/all_to_all | solution.py:26
  191.2 7.1 %collective-permute-start.27 = (bf16[40,1024]{1,0:T(8,128)(2,1)S(1)}, bf16[40,1024]{1,0:T(8,128)(2,1)S(1)}, u32[]{:S(2)}, u32[]{:S(2)}) collective-permute-start(bf16[40,1024]{1,0:T(8,128)(2,1)S(1)} %first_small.1.refs_0_), channel_id=1, source_target_pairs={{0,8},{4,12},{8,0},{12,4},{16,24},{20,28},{24,16},{28,20},{1,9},{5... | collective-permute-start | bytes 245768 | tf_op jit(solution)/shard_map/ppermute | solution.py:22
  192.8 10.5 %collective-permute-start.30 = (bf16[40,1024]{1,0:T(8,128)(2,1)S(1)}, bf16[40,1024]{1,0:T(8,128)(2,1)S(1)}, u32[]{:S(2)}, u32[]{:S(2)}) collective-permute-start(bf16[40,1024]{1,0:T(8,128)(2,1)S(1)} %first_small.1.refs_0_), channel_id=1, source_target_pairs={{0,16},{4,20},{8,24},{12,28},{16,0},{20,4},{24,8},{28,12},{1,17},{... | collective-permute-start | bytes 245768 | tf_op jit(solution)/shard_map/ppermute | solution.py:22
  198.3 5.0 %collective-permute-start.31 = (bf16[40,1024]{1,0:T(8,128)(2,1)S(1)}, bf16[40,1024]{1,0:T(8,128)(2,1)S(1)}, u32[]{:S(2)}, u32[]{:S(2)}) collective-permute-start(bf16[40,1024]{1,0:T(8,128)(2,1)S(1)} %collective-permute-done.27.refs_1_), channel_id=1, source_target_pairs={{0,16},{4,20},{8,24},{12,28},{16,0},{20,4},{24,8},{28,12},{1,17},{... | collective-permute-start | bytes 245768 | tf_op jit(solution)/shard_map/ppermute | solution.py:22
  203.3 20.6 %collective-permute-start.34 = (bf16[384,1024]{1,0:T(8,128)(2,1)S(1)}, bf16[384,1024]{1,0:T(8,128)(2,1)S(1)}, u32[]{:S(2)}, u32[]{:S(2)}) collective-permute-start(bf16[384,1024]{1,0:T(8,128)(2,1)S(1)} %get-tuple-element.313.a_ref), channel_id=1, source_target_pairs={{0,8},{4,12},{8,0},{12,4},{16,24},{20,28},{24,16},{28,20},{1,9},{5... | collective-permute-start | bytes 2359304 | tf_op jit(solution)/shard_map/ppermute | solution.py:22
  204.0 20.0 %collective-permute-start.35 = (bf16[384,1024]{1,0:T(8,128)(2,1)S(1)}, bf16[384,1024]{1,0:T(8,128)(2,1)}, u32[]{:S(2)}, u32[]{:S(2)}) collective-permute-start(bf16[384,1024]{1,0:T(8,128)(2,1)S(1)} %get-tuple-element.306.b_ref), channel_id=1, source_target_pairs={{0,16},{4,20},{8,24},{12,28},{16,0},{20,4},{24,8},{28,12},{1,17},{... | collective-permute-start | bytes 2359304 | tf_op jit(solution)/shard_map/ppermute | solution.py:22
  205.4 1.3 collective-permute-start.28
  205.4 5.8 %collective-permute-start.29 = (bf16[40,1024]{1,0:T(8,128)(2,1)S(1)}, bf16[40,1024]{1,0:T(8,128)(2,1)S(1)}, u32[]{:S(2)}, u32[]{:S(2)}) collective-permute-start(bf16[40,1024]{1,0:T(8,128)(2,1)S(1)} %collective-permute-done.27.refs_1_), channel_id=1, source_target_pairs={{0,4},{4,0},{8,12},{12,8},{16,20},{20,16},{24,28},{28,24},{1,5},{5... | collective-permute-start | bytes 245768 | tf_op jit(solution)/shard_map/ppermute | solution.py:22
  205.9 5.3 %collective-permute-start.32 = (bf16[40,1024]{1,0:T(8,128)(2,1)S(1)}, bf16[40,1024]{1,0:T(8,128)(2,1)S(1)}, u32[]{:S(2)}, u32[]{:S(2)}) collective-permute-start(bf16[40,1024]{1,0:T(8,128)(2,1)S(1)} %collective-permute-done.30.refs_2_), channel_id=1, source_target_pairs={{0,4},{4,0},{8,12},{12,8},{16,20},{20,16},{24,28},{28,24},{1,5},{5... | collective-permute-start | bytes 245768 | tf_op jit(solution)/shard_map/ppermute | solution.py:22
  206.7 4.6 %collective-permute-start.33 = (bf16[40,1024]{1,0:T(8,128)(2,1)S(1)}, bf16[40,1024]{1,0:T(8,128)(2,1)S(1)}, u32[]{:S(2)}, u32[]{:S(2)}) collective-permute-start(bf16[40,1024]{1,0:T(8,128)(2,1)S(1)} %collective-permute-done.31.refs_3_), channel_id=1, source_target_pairs={{0,4},{4,0},{8,12},{12,8},{16,20},{20,16},{24,28},{28,24},{1,5},{5... | collective-permute-start | bytes 245768 | tf_op jit(solution)/shard_map/ppermute | solution.py:22
  (51 other events, 179.0 us)

commit v6 on v5

--- a/solution.py
+++ b/solution.py
@@ -528,49 +528,57 @@
     )(part, *down, *up)
 
 
-def qkv_part_of(first_low, grads):
+def qkv_part_of(first_low, grads, part):
     rows, width = first_low.shape
     part_width = grads.shape[2]
-
-    def kernel(low_ref, grads_ref, out_ref):
+    half = 3 * part_width // 2
+
+    def kernel(part_ref, low_ref, grads_ref, keep_ref, send_ref, full):
         for n in range(3):
             product = dot(grads_ref[n], low_ref[...], TN)
-            out_ref[n * part_width : (n + 1) * part_width, :] = product.astype(BF)
-
-    whole = pl.BlockSpec(memory_space=pltpu.VMEM)
-    return pl.pallas_call(
-        kernel,
-        in_specs=[whole] * 2,
-        out_specs=whole,
-        out_shape=jax.ShapeDtypeStruct((3 * part_width, width), BF),
-        cost_estimate=small_cost(),
-        compiler_params=pltpu.CompilerParams(vmem_limit_bytes=12 << 20),
+            full[n * part_width : (n + 1) * part_width, :] = product.astype(BF)
+        core = part_ref[0] & 1
+        for target, which in ((keep_ref, core), (send_ref, 1 - core)):
+            target[...] = full[pl.ds(pl.multiple_of(which * half, half), half), :]
+
+    whole = pl.BlockSpec(memory_space=pltpu.VMEM)
+    return pl.pallas_call(
+        kernel,
+        in_specs=[pl.BlockSpec(memory_space=pltpu.SMEM)] + [whole] * 2,
+        out_specs=[whole] * 2,
+        out_shape=[jax.ShapeDtypeStruct((half, width), BF)] * 2,
+        scratch_shapes=[pltpu.VMEM((2 * half, width), BF)],
+        cost_estimate=small_cost(),
+        compiler_params=pltpu.CompilerParams(vmem_limit_bytes=14 << 20),
         name="qkv_part",
-    )(first_low, grads)
-
-
-def spread_qkv(lane_a, got_a, lane_b, got_b, part_width):
-    rows, width = lane_a.shape
+    )(part, first_low, grads)
+
+
+def spread_qkv(near, far, part, part_width):
+    rows, width = near.shape
     tile = 128
-
-    def kernel(a_ref, a_got, b_ref, b_got, out_ref):
-        for n in range(2 * rows // tile):
-            start = n * tile % rows
-            ref, got = (a_ref, a_got) if n * tile < rows else (b_ref, b_got)
-            lane, column = divmod(n * tile, part_width)
-            piece = ref[start : start + tile, :].astype(F32) + got[start : start + tile, :].astype(F32)
-            out_ref[lane, :, column : column + tile] = piece.T
-
-    whole = pl.BlockSpec(memory_space=pltpu.VMEM)
-    return pl.pallas_call(
-        kernel,
-        in_specs=[whole] * 4,
+    count = rows // tile
+    many = part_width // tile
+
+    def kernel(part_ref, near_ref, far_ref, out_ref):
+        core = part_ref[0] & 1
+        for ref, which in ((near_ref, core), (far_ref, 1 - core)):
+            for n in range(count):
+                spot = which * count + n
+                column = pl.multiple_of(spot % many * tile, tile)
+                piece = ref[n * tile : (n + 1) * tile, :].astype(F32)
+                out_ref[spot // many, :, pl.ds(column, tile)] = piece.T
+
+    whole = pl.BlockSpec(memory_space=pltpu.VMEM)
+    return pl.pallas_call(
+        kernel,
+        in_specs=[pl.BlockSpec(memory_space=pltpu.SMEM)] + [whole] * 2,
         out_specs=whole,
         out_shape=jax.ShapeDtypeStruct((2 * rows // part_width, width, part_width), F32),
         cost_estimate=small_cost(),
-        compiler_params=pltpu.CompilerParams(vmem_limit_bytes=16 << 20),
+        compiler_params=pltpu.CompilerParams(vmem_limit_bytes=14 << 20),
         name="spread_qkv",
-    )(lane_a, got_a, lane_b, got_b)
+    )(part, near, far)
 
 
 def core_grads(activated, grad_mixer, second_low, grad_pre, heads, attended_part, part, keys_a, keys_b):
@@ -721,6 +729,25 @@
         cost_estimate=small_cost(),
         compiler_params=pltpu.CompilerParams(vmem_limit_bytes=12 << 20),
         name="lane_sums",
+    )(lane_a, got_a, lane_b, got_b)
+
+
+def joined_lanes(lane_a, got_a, lane_b, got_b):
+    rows, width = lane_a.shape
+
+    def kernel(a_ref, a_got, b_ref, b_got, out_ref):
+        out_ref[:rows, :] = plus(a_ref[...], a_got[...])
+        out_ref[rows:, :] = plus(b_ref[...], b_got[...])
+
+    whole = pl.BlockSpec(memory_space=pltpu.VMEM)
+    return pl.pallas_call(
+        kernel,
+        in_specs=[whole] * 4,
+        out_specs=whole,
+        out_shape=jax.ShapeDtypeStruct((2 * rows, width), BF),
+        cost_estimate=small_cost(),
+        compiler_params=pltpu.CompilerParams(vmem_limit_bytes=10 << 20),
+        name="joined_lanes",
     )(lane_a, got_a, lane_b, got_b)
 
 
@@ -1011,10 +1038,10 @@
     grad_projected, first_gain_part, input_part = attend_back(
         head_terms, qkv, probs, qkv_weight, picked, first_gain[None], hidden_part
     )
-    qkv_part = qkv_part_of(first_low, grad_projected)
+    qkv_part, qkv_leaving = qkv_part_of(first_low, grad_projected, part_array)
     input_part = input_part.reshape(ways, own_rows, width)
     if by_swaps:
-        got_a, got_b, qkv_part, input_part = tie((got_a, got_b, qkv_part, input_part))
+        got_a, got_b, qkv_part, qkv_leaving, input_part = tie((got_a, got_b, qkv_part, qkv_leaving, input_part))
         kept, leave_a, leave_b = halving_sums(kept, (got_a,), (got_b,), wide // 2, narrow // 2)
         mixer_terms, input_part, qkv_part, kept, leave_a, leave_b = tie(
             (mixer_terms, input_part, qkv_part, kept, leave_a, leave_b)
@@ -1025,7 +1052,7 @@
     input_terms = to_all(input_part)
     if by_swaps:
         got_a, got_b = swap(leave_a, "dp", bit_y), swap(leave_b, "dp", bit_x)
-        qkv_got = swap(qkv_part, "dp", 1)
+        qkv_got = swap(qkv_leaving, "dp", 1)
     new_own, grad_score, small = finish_rows(
         mixer_terms,
         picked,
@@ -1086,34 +1113,39 @@
         more = [swap(array, "dp", bit_x) for array in blocks]
         qkv_a_got, qkv_b_got, blocks = tie((qkv_a_got, qkv_b_got, blocks))
         qkv_a, qkv_b = lane_sums(qkv_a, qkv_a_got, qkv_b, qkv_b_got)
-        more, qkv_a, qkv_b = tie((more, qkv_a, qkv_b))
+        qkv_a_got, qkv_b_got = swap(qkv_a, "dp", bit_x), swap(qkv_b, "dp", bit_y)
+        fresh, blocks, qkv_a, qkv_b = tie((fresh, blocks, qkv_a, qkv_b))
+    output = merge_rows(tokens, route_offset, fresh, mine_array, range(ways // 2))
+    if by_swaps:
+        more, qkv_a_got, qkv_b_got, output = tie((more, qkv_a_got, qkv_b_got, output))
+        qkv_near = joined_lanes(qkv_a, qkv_a_got, qkv_b, qkv_b_got)
+        qkv_far = swap(qkv_near, "dp", 1)
         blocks = blocks + more
         more = [swap(array, "dp", bit_y) for array in blocks]
-        fresh, blocks = tie((fresh, blocks))
-    output = merge_rows(tokens, route_offset, fresh, mine_array, range(ways // 2))
+        fresh, blocks, qkv_near = tie((fresh, blocks, qkv_near))
+    output = merge_rows(tokens, route_offset, fresh, mine_array, range(ways // 2, ways), output)
     if by_swaps:
-        more, output, qkv_a, qkv_b = tie((more, output, qkv_a, qkv_b))
-        qkv_a_got, qkv_b_got = swap(qkv_a, "dp", bit_x), swap(qkv_b, "dp", bit_y)
+        more, qkv_far, output = tie((more, qkv_far, output))
         blocks = blocks + more
         more = [swap(array, "dp", 1) for array in blocks]
-        fresh, blocks, qkv_a = tie((fresh, blocks, qkv_a))
-    output = merge_rows(tokens, route_offset, fresh, mine_array, range(ways // 2, ways), output)
-    if by_swaps:
-        more, output = tie((more, output))
+        qkv_near, blocks = tie((qkv_near, blocks))
+        qkv_grad = spread_qkv(qkv_near, qkv_far, part_array, qkv_weight.shape[2])
+        more, qkv_grad = tie((more, qkv_grad))
         out_grad, *small = last_small(blocks + more, gathered([bit_x, bit_y, 1]), part_array, shares)
         small[3] = small[3][:, :2]
-        input_rows, early, output, out_grad, small = tie((input_rows, early, output, out_grad, small))
+        input_rows, early, output, out_grad, small, qkv_grad = tie(
+            (input_rows, early, output, out_grad, small, qkv_grad)
+        )
     input_grad = merge_rows(cotangent, route_offset, input_rows, mine_array, range(1, ways), early)
-    if by_swaps:
-        qkv_a_got, qkv_b_got, input_grad = tie((qkv_a_got, qkv_b_got, input_grad))
-        qkv_grad = spread_qkv(qkv_a, qkv_a_got, qkv_b, qkv_b_got, qkv_weight.shape[2])
     if not by_swaps:
+        swapped = jnp.concatenate([qkv_leaving, qkv_part])
+        qkv_whole = jnp.where(part & 1 == 0, jnp.concatenate([qkv_part, qkv_leaving]), swapped)
         small = sum(joined_sums(fresh[k, own_rows:]) for k in range(ways))
         small = lax.psum(small, "dp")
         small = [small[n : n + 1] for n in range(TERMS)]
         small[3] = small[3][:, :2] * jnp.array((shares,), F32)
         down_grad, up_grad, qkv_sum, out_sum = (
-            lax.psum(v, "dp").astype(F32) for v in (down_part, up_part, qkv_part, out_parts)
+            lax.psum(v, "dp").astype(F32) for v in (down_part, up_part, qkv_whole, out_parts)
         )
         out_grad = jnp.sum(to_all(out_sum.astype(BF)).astype(F32), axis=0)
         qkv_grad = qkv_sum.reshape(3, -1, width).transpose(0, 2, 1)

time: 229 us -> 224 us (0.978)
  local copies, waits for them, and re-layouts: 28.5 us -> 25.4 us
    all_to_all x6, waiting for transfers between devices: 25.1 us -> 17.9 us  [to_all(): return lax.all_to_all(blocks, 'tensor', 0, 0, tiled=True)]
    ppermute x36 -> x37, waiting for transfers between devices: 21.5 us -> 26.4 us  [swap(): return lax.ppermute(values, axis, [(i, i ^ bits) for i in range(size)])]
    unnamed x114 -> x106, local copies, waits for them, and re-layouts: 25.7 us -> 22.7 us
    pallas_call x2 -> x3, Pallas kernels: 4.69 us -> 3.48 us  [the longest x1 2.14 us: spread_qkv(): pl.pallas_call(kernel, in_specs=[pl.BlockSpec(memory_space=pltpu.SMEM)] +...]
    ppermute x36 -> x37, starting transfers between devices: 31.2 us -> 31.4 us  [swap(): return lax.ppermute(values, axis, [(i, i ^ bits) for i in range(size)])]
  transfers between devices with their start and end apart: 42 -> 43, of which waited for: 15 -> 15; matrix products, arithmetic and copies ran while one was open for 2% -> 2% of each run, Pallas kernels for 35% -> 33%
where the time goes in v6:
time: 224 us; the launch traced here: 222 us
  Pallas kernels  90.9 us (41%)
  starting transfers between devices  58.1 us (26%)
  waiting for transfers between devices  44.4 us (20%)
  local copies, waits for them, and re-layouts  25.4 us (11%)
    ppermute x37, starting transfers between devices, swap(): return lax.ppermute(values, axis, [(i, i ^ bits) for i in range(size)])  31.4 us
    all_to_all x6, starting transfers between devices, to_all(): return lax.all_to_all(blocks, 'tensor', 0, 0, tiled=True)  26.7 us
    ppermute x37, waiting for transfers between devices, swap(): return lax.ppermute(values, axis, [(i, i ^ bits) for i in range(size)])  26.4 us
    unnamed x106, local copies, waits for them, and re-layouts  22.7 us
    pallas_call x4, Pallas kernels, merge_rows(): pl.pallas_call(kernel, grid_spec=grid_spec, out_shape=jax.ShapeDtypeStruc...  19.9 us
    all_to_all x6, waiting for transfers between devices, to_all(): return lax.all_to_all(blocks, 'tensor', 0, 0, tiled=True)  17.9 us
    pallas_call x2, Pallas kernels, staged(): pl.pallas_call(kernel, in_specs=[pl.BlockSpec(memory_space=pltpu.SMEM)] *...  16.5 us
    pallas_call x1, Pallas kernels, spread_rows(): pl.pallas_call(kernel, grid_spec=pltpu.PrefetchScalarGridSpec(num_scalar_...  7.99 us
  transfers between devices with their start and end apart: 43, of which 15 were waited for; matrix products, arithmetic and copies ran while one was open for 2% of the time, Pallas kernels for 33%

profile of v6, /device:TPU:0, one launch (start us, length us, event | category | flops | bytes accessed | tf_op | source)
XLA Modules:
  0.0 222.2 jit_solution(6450980477754884319)
XLA Ops:
  1.6 5.1 %collective-permute-start.2 = (bf16[64,1024]{1,0:T(8,128)(2,1)S(1)}, bf16[64,1024]{1,0:T(8,128)(2,1)S(1)}, u32[]{:S(2)}, u32[]{:S(2)}) collective-permute-start(bf16[64,1024]{1,0:T(8,128)(2,1)S(1)} %constant_dynamic-slice_fusion), channel_id=1, source_target_pairs={{0,3},{1,2},{2,1},{3,0},{4,7},{5,6},{6,5},{7,4},{8,11},{9,10},{10,... | collective-permute-start | bytes 393224 | tf_op jit(solution)/shard_map/ppermute | solution.py:22
  7.3 5.7 %pick_rows.1.refs_0_.picked_ref.refs_8_ = bf16[512,1024]{1,0:T(8,128)(2,1)} custom-call(bf16[4096,1024]{1,0:T(8,128)(2,1)} %base_ref.9, s32[1,512]{1,0:T(1,128)} %offset_ref.11), custom_call_target="tpu_custom_call" | custom-call | flops 1024 | bytes 1024 | tf_op jit(solution)/shard_map/pick_rows/pallas_call | solution.py:133
  13.7 6.6 %attend.1 = (bf16[512,1024]{1,0:T(8,128)(2,1)}, bf16[3,512,256]{2,1,0:T(8,128)(2,1)}, bf16[4,512,256]{2,1,0:T(8,128)(2,1)}, bf16[4,256,256]{2,1,0:T(8,128)(2,1)}, bf16[4,256,512]{2,1,0:T(8,128)(2,1)}) custom-call(bf16[512,1024]{1,0:T(8,128)(2,1)} %pick_rows.1.refs_0_.picked_ref.refs_8_, bf16[1,1024]{1,0:T(2,128)(2,1)} %broadcast_in_dim.10.refs_1_.gain_ref, ...), custom_call_target="tpu_custom_call" | custom-call | flops 1024 | bytes 1024 | tf_op jit(solution)/shard_map/attend/pallas_call | solution.py:86
  20.3 5.0 %all-to-all-start = ((bf16[4,512,256]{2,1,0:T(8,128)(2,1)}), bf16[4,512,256]{2,1,0:T(8,128)(2,1)S(1)}, u32[]{:S(2)}, u32[]{:S(2)}) async-start(bf16[4,512,256]{2,1,0:T(8,128)(2,1)} %get-tuple-element.171), calls=%async_computation | async-start | bytes 2097152 | tf_op jit(solution)/shard_map/all_to_all | solution.py:26
  25.4 1.6 collective-permute-start.3
  27.0 6.0 %pick_only.1.rows_ref = bf16[512,1024]{1,0:T(8,128)(2,1)} custom-call(bf16[4096,1024]{1,0:T(8,128)(2,1)} %base_ref.10, s32[1,512]{1,0:T(1,128)} %offset_ref.11), custom_call_target="tpu_custom_call" | custom-call | flops 1024 | bytes 1024 | tf_op jit(solution)/shard_map/pick_only/pallas_call | solution.py:186
  33.0 4.0 %collective-permute-done.3.refs_6_ = bf16[3,64,1024]{2,1,0:T(8,128)(2,1)S(1)} collective-permute-done((bf16[3,64,1024]{2,1,0:T(8,128)(2,1)S(1)}, bf16[3,64,1024]{2,1,0:T(8,128)(2,1)S(1)}, u32[]{:S(2)}, u32[]{:S(2)}) %collective-permute-start.3) | collective-permute-done | bytes 393248 | tf_op jit(solution)/shard_map/ppermute | solution.py:22
  37.6 2.6 %score_sums.1.square_ref = f32[1,128]{1,0:T(1,128)} custom-call(s32[1]{0:T(128)} %bitcast.1.mine_ref.refs_1_.part_ref, bf16[4096,1024]{1,0:T(8,128)(2,1)} %base_ref.9, bf16[1,1024]{1,0:T(2,128)(2,1)} %broadcast_in_dim.11.router_ref), custom_call_target="tpu_custom_call" | custom-call | flops 1024 | bytes 1024 | tf_op jit(solution)/shard_map/score_sums/pallas_call | solution.py:153
  40.9 5.1 %act_grads.1 = (f32[512,1]{1,0:T(8,128)}, f32[1,128]{1,0:T(1,128)}, bf16[512,1024]{1,0:T(8,128)(2,1)}, f32[512,1024]{1,0:T(8,128)}) custom-call(bf16[512,1024]{1,0:T(8,128)(2,1)} %pick_rows.1.refs_0_.picked_ref.refs_8_, bf16[1,1024]{1,0:T(2,128)(2,1)} %broadcast_in_dim.11.router_ref, bf16[512,1024]{1,0:T(8,128)(2,1)} %pick_only.1.rows_ref, ...), custom_call_target="tpu_custom_call" | custom-call | flops 1024 | bytes 1024 | tf_op jit(solution)/shard_map/act_grads/pallas_call | solution.py:397
  46.0 4.2 %all-to-all-done.refs_2_.heads_ref = bf16[4,512,256]{2,1,0:T(8,128)(2,1)S(1)} async-done(((bf16[4,512,256]{2,1,0:T(8,128)(2,1)}), bf16[4,512,256]{2,1,0:T(8,128)(2,1)S(1)}, u32[]{:S(2)}, u32[]{:S(2)}) %all-to-all-start) | async-done | bytes 1048608 | tf_op jit(solution)/shard_map/all_to_all | solution.py:26
  51.1 9.9 %feed_forward.1 = (f32[128,1024]{1,0:T(8,128)}, bf16[512,1024]{1,0:T(8,128)(2,1)}, bf16[512,1024]{1,0:T(8,128)(2,1)}, bf16[512,1024]{1,0:T(8,128)(2,1)}, bf16[51...) custom-call(s32[1]{0:T(128)} %bitcast.refs_0_.part_ref, ...), custom_call_target="tpu_custom_call" | custom-call | flops 1024 | bytes 1024 | tf_op jit(solution)/shard_map/feed_forward/pallas_call | solution.py:86
  61.1 4.6 %all-to-all-start.1 = ((bf16[4,512,256]{2,1,0:T(8,128)(2,1)}), bf16[4,512,256]{2,1,0:T(8,128)(2,1)}, u32[]{:S(2)}, u32[]{:S(2)}) async-start(bf16[4,512,256]{2,1,0:T(8,128)(2,1)} %get-tuple-element.192), calls=%async_computation.1 | async-start | bytes 2097152 | tf_op jit(solution)/shard_map/all_to_all | solution.py:26
  70.7 3.9 %core_grads.1 = (bf16[2,768,1024]{2,1,0:T(8,128)(2,1)S(1)}, bf16[512,1024]{1,0:T(8,128)(2,1)S(1)}, bf16[512,1024]{1,0:T(8,128)(2,1)S(1)}, bf16[256,1024]{1,0:T(8,128)(2,1)S(1)}, bf16[256,1024]{1,0:T(8,128)(2,1)S(1)}) custom-call(s32[1]{0:T(128)} %bitcast.refs_0_.part_ref, bf16[512,1024]{1,0:T(8,128)(2,1)S(1)} %copy-done.10, bf16[512,1024]{1,0:T(8,128)(2,1)S(1)} %copy-done.6, ...), custom_call_target="tpu_custom_call" | custom-call | flops 1024 | bytes 1024 | tf_op jit(solution)/shard_map/core_grads/pallas_call | solution.py:622
  75.6 2.2 %convolution_convert_fusion = bf16[512,1024]{1,0:T(8,128)(2,1)} fusion(bf16[512,1024]{1,0:T(8,128)(2,1)S(1)} %copy-done.11, bf16[1024,1024]{1,0:T(8,128)(2,1)S(1)} %copy-done.43), kind=kOutput, calls=%fused_computation | convolution fusion | flops 1074266112 | bytes 4194304 | tf_op jit(solution)/shard_map/dot_general | solution.py:17
  77.9 1.6 collective-permute-done.8.refs_1_
  84.0 6.8 %all-to-all-done.1.head_ref = bf16[4,512,256]{2,1,0:T(8,128)(2,1)} async-done(((bf16[4,512,256]{2,1,0:T(8,128)(2,1)}), bf16[4,512,256]{2,1,0:T(8,128)(2,1)}, u32[]{:S(2)}, u32[]{:S(2)}) %all-to-all-start.1) | async-done | bytes 1048608 | tf_op jit(solution)/shard_map/all_to_all | solution.py:26
  90.8 4.2 %all-to-all-start.2 = ((bf16[4,128,1024]{2,1,0:T(8,128)(2,1)}), bf16[4,128,1024]{2,1,0:T(8,128)(2,1)}, u32[]{:S(2)}, u32[]{:S(2)}) async-start(bf16[4,128,1024]{2,1,0:T(8,128)(2,1)} %bitcast.14), calls=%async_computation.2 | async-start | bytes 2097152 | tf_op jit(solution)/shard_map/all_to_all | solution.py:26
  95.0 1.6 collective-permute-start.10
  96.6 1.5 collective-permute-start.11
  101.6 6.7 %attend_back.1 = (bf16[3,512,256]{2,1,0:T(8,128)(2,1)S(1)}, f32[1,1024]{1,0:T(1,128)S(1)}, bf16[512,1024]{1,0:T(8,128)(2,1)}) custom-call(bf16[4,512,256]{2,1,0:T(8,128)(2,1)} %all-to-all-done.1.head_ref, bf16[3,512,256]{2,1,0:T(8,128)(2,1)S(1)} %copy-done.18, bf16[3,1024,256]{2,1,0:T(8,128)(2,1)S(1)} %copy-done.5, bf16[512,1024]{1,0:T(8,128)(2,1)S(1)} %copy-done, ...), custom_call_target="tpu_custom_call" | custom-call | flops 1024 | bytes 1024 | tf_op jit(solution)/shard_map/attend_back/pallas_call | solution.py:473
  110.4 3.4 %collective-permute-done.10.refs_0_ = bf16[384,1024]{1,0:T(8,128)(2,1)S(1)} collective-permute-done((bf16[384,1024]{1,0:T(8,128)(2,1)}, bf16[384,1024]{1,0:T(8,128)(2,1)S(1)}, u32[]{:S(2)}, u32[]{:S(2)}) %collective-permute-start.10) | collective-permute-done | bytes 786464 | tf_op jit(solution)/shard_map/ppermute | solution.py:22
  116.9 3.4 %all-to-all-done.2.terms_ref = bf16[4,128,1024]{2,1,0:T(8,128)(2,1)} async-done(((bf16[4,128,1024]{2,1,0:T(8,128)(2,1)}), bf16[4,128,1024]{2,1,0:T(8,128)(2,1)}, u32[]{:S(2)}, u32[]{:S(2)}) %all-to-all-start.2) | async-done | bytes 1048608 | tf_op jit(solution)/shard_map/all_to_all | solution.py:26
  120.3 3.8 %all-to-all-start.3 = ((bf16[4,128,1024]{2,1,0:T(8,128)(2,1)}), bf16[4,128,1024]{2,1,0:T(8,128)(2,1)S(1)}, u32[]{:S(2)}, u32[]{:S(2)}) async-start(bf16[4,128,1024]{2,1,0:T(8,128)(2,1)} %bitcast.6), calls=%async_computation.3 | async-start | bytes 2097152 | tf_op jit(solution)/shard_map/all_to_all | solution.py:26
  124.2 1.6 collective-permute-start.13
  125.8 1.5 collective-permute-start.14
  127.3 2.6 %finish_rows.1 = (bf16[128,1024]{1,0:T(8,128)(2,1)}, f32[128,1]{1,0:T(8,128)}, f32[4,1024]{1,0:T(4,128)}) custom-call(s32[1]{0:T(128)} %bitcast.1.mine_ref.refs_1_.part_ref, bf16[4,128,1024]{2,1,0:T(8,128)(2,1)} %all-to-all-done.2.terms_ref, bf16[512,1024]{1,0:T(8,128)(2,1)} %pick_rows.1.refs_0_.picked_ref.refs_8_, f32[512,1]{1,0:T(8,128)} %get-tuple-element.238.gating_ref, ...), custom_call_target="tpu_custom_call" | custom-call | flops 1024 | bytes 30000000 | tf_op jit(solution)/shard_map/finish_rows/pallas_call | solution.py:882
  129.9 6.0 %collective-permute-done.13.a_got = bf16[192,1024]{1,0:T(8,128)(2,1)S(1)} collective-permute-done((bf16[192,1024]{1,0:T(8,128)(2,1)}, bf16[192,1024]{1,0:T(8,128)(2,1)S(1)}, u32[]{:S(2)}, u32[]{:S(2)}) %collective-permute-start.13) | collective-permute-done | bytes 393248 | tf_op jit(solution)/shard_map/ppermute | solution.py:22
  135.9 1.3 collective-permute-done.14.b_got
  141.7 1.5 collective-permute-start.16
  145.3 3.6 %collective-permute-done.15.refs_1_ = bf16[128,1024]{1,0:T(8,128)(2,1)} collective-permute-done((bf16[128,1024]{1,0:T(8,128)(2,1)S(1)}, bf16[128,1024]{1,0:T(8,128)(2,1)}, u32[]{:S(2)}, u32[]{:S(2)}) %collective-permute-start.15) | collective-permute-done | bytes 262176 | tf_op jit(solution)/shard_map/ppermute | solution.py:22
  149.2 4.8 %all-to-all-start.4 = ((bf16[4,168,1024]{2,1,0:T(8,128)(2,1)}), bf16[4,168,1024]{2,1,0:T(8,128)(2,1)S(1)}, u32[]{:S(2)}, u32[]{:S(2)}) async-start(bf16[4,168,1024]{2,1,0:T(8,128)(2,1)} %copy-done.9), calls=%async_computation.4 | async-start | bytes 2752512 | tf_op jit(solution)/shard_map/all_to_all | solution.py:26
  154.0 1.5 collective-permute-start.17
  155.5 1.4 collective-permute-start.19
  160.0 1.9 gather_blocks.2
  163.9 3.7 %merge_rows.4.rest_0_ = bf16[4096,1024]{1,0:T(8,128)(2,1)} custom-call(s32[1]{0:T(128)} %bitcast.1.mine_ref.refs_1_.part_ref, bf16[4096,1024]{1,0:T(8,128)(2,1)} %base_ref.10, s32[1,512]{1,0:T(1,128)} %offset_ref.11, bf16[4,128,1024]{2,1,0:T(8,128)(2,1)} %finish_input.1.piece_ref), custom_call_target="tpu_custom_call" | custom-call | flops 1024 | bytes 1024 | tf_op jit(solution)/shard_map/merge_rows/pallas_call | solution.py:232
  170.0 1.4 collective-permute-start.25
  171.4 1.5 collective-permute-start.26
  174.5 8.0 %spread_rows.1 = (f32[1024,1024]{1,0:T(8,128)}, f32[1024,1024]{1,0:T(8,128)}) custom-call(s32[1]{0:T(128)} %bitcast.refs_0_.part_ref, bf16[256,1024]{1,0:T(8,128)(2,1)} %get-tuple-element.265.refs_0_, bf16[256,1024]{1,0:T(8,128)(2,1)} %copy-done.22, bf16[256,1024]{1,0:T(8,128)(2,1)} %collective-permute-done.21.refs_2_, bf16[256,1024]{1,0:T(8,128)(2,1)} %copy-done.46, ...), custom_call_target="tpu_custom_call" | custom-call | flops 1024 | bytes 1024 | tf_op jit(solution)/shard_map/spread_rows/pallas_call | solution.py:517
  182.5 2.7 %all-to-all-done.4.got_ref.piece_ref = bf16[4,168,1024]{2,1,0:T(8,128)(2,1)S(1)} async-done(((bf16[4,168,1024]{2,1,0:T(8,128)(2,1)}), bf16[4,168,1024]{2,1,0:T(8,128)(2,1)S(1)}, u32[]{:S(2)}, u32[]{:S(2)}) %all-to-all-start.4) | async-done | bytes 1376288 | tf_op jit(solution)/shard_map/all_to_all | solution.py:26
  185.2 4.3 %all-to-all-start.5 = ((bf16[4,128,1024]{2,1,0:T(8,128)(2,1)}), bf16[4,128,1024]{2,1,0:T(8,128)(2,1)}, u32[]{:S(2)}, u32[]{:S(2)}) async-start(bf16[4,128,1024]{2,1,0:T(8,128)(2,1)} %finish_input.1.piece_ref), calls=%async_computation.5 | async-start | bytes 2097152 | tf_op jit(solution)/shard_map/all_to_all | solution.py:26
  190.9 1.6 collective-permute-start.29
  192.5 1.3 collective-permute-start.30
  194.3 4.4 %merge_rows.5.rest_0_ = bf16[4096,1024]{1,0:T(8,128)(2,1)} custom-call(s32[1]{0:T(128)} %bitcast.1.mine_ref.refs_1_.part_ref, bf16[4096,1024]{1,0:T(8,128)(2,1)} %base_ref.9, s32[1,512]{1,0:T(1,128)} %offset_ref.11, bf16[4,168,1024]{2,1,0:T(8,128)(2,1)} %copy-done.1), custom_call_target="tpu_custom_call" | custom-call | flops 1024 | bytes 1024 | tf_op jit(solution)/shard_map/merge_rows/pallas_call | solution.py:232
  198.7 4.1 %collective-permute-done.28.refs_1_ = bf16[40,1024]{1,0:T(8,128)(2,1)S(1)} collective-permute-done((bf16[40,1024]{1,0:T(8,128)(2,1)S(1)}, bf16[40,1024]{1,0:T(8,128)(2,1)S(1)}, u32[]{:S(2)}, u32[]{:S(2)}) %collective-permute-start.28) | collective-permute-done | bytes 81952 | tf_op jit(solution)/shard_map/ppermute | solution.py:22
  203.1 1.4 collective-permute-start.27
  205.7 4.4 %merge_rows.6 = bf16[4096,1024]{1,0:T(8,128)(2,1)} custom-call(s32[1]{0:T(128)} %bitcast.1.mine_ref.refs_1_.part_ref, bf16[4096,1024]{1,0:T(8,128)(2,1)} %base_ref.9, s32[1,512]{1,0:T(1,128)} %offset_ref.11, bf16[4,168,1024]{2,1,0:T(8,128)(2,1)} %copy-done.1, bf16[4096,1024]{1,0:T(8,128)(2,1)} %merge_rows.5.rest_0_), custom_call_target="tpu_custom_call", output_to_operand_aliasing={{}: (4, {})} | custom-call | flops 1024 | bytes 1024 | tf_op jit(solution)/shard_map/merge_rows/pallas_call | solution.py:232
  210.6 2.1 spread_qkv.1
  214.8 7.5 %merge_rows.7 = bf16[4096,1024]{1,0:T(8,128)(2,1)} custom-call(s32[1]{0:T(128)} %bitcast.1.mine_ref.refs_1_.part_ref, bf16[4096,1024]{1,0:T(8,128)(2,1)} %base_ref.10, s32[1,512]{1,0:T(1,128)} %offset_ref.11, bf16[4,128,1024]{2,1,0:T(8,128)(2,1)} %all-to-all-done.5.piece_ref, bf16[4096,1024]{1,0:T(8,128)(2,1)} %merge_rows.4.rest_0_), custom_call_target="tpu_custom_call", output_to_operand_aliasing={{}: (4, {})} | custom-call | flops 1024 | bytes 1024 | tf_op jit(solution)/shard_map/merge_rows/pallas_call | solution.py:232
  (177 shorter events, 45.5 us)
Async XLA Ops:
  1.6 18.7 %collective-permute-start.2 = (bf16[64,1024]{1,0:T(8,128)(2,1)S(1)}, bf16[64,1024]{1,0:T(8,128)(2,1)S(1)}, u32[]{:S(2)}, u32[]{:S(2)}) collective-permute-start(bf16[64,1024]{1,0:T(8,128)(2,1)S(1)} %constant_dynamic-slice_fusion), channel_id=1, source_target_pairs={{0,3},{1,2},{2,1},{3,0},{4,7},{5,6},{6,5},{7,4},{8,11},{9,10},{10,... | collective-permute-start | bytes 393224 | tf_op jit(solution)/shard_map/ppermute | solution.py:22
  6.7 13.5 %collective-permute-start.1 = (bf16[64,1024]{1,0:T(8,128)(2,1)S(1)}, bf16[64,1024]{1,0:T(8,128)(2,1)S(1)}, u32[]{:S(2)}, u32[]{:S(2)}) collective-permute-start(bf16[64,1024]{1,0:T(8,128)(2,1)S(1)} %constant_dynamic-slice_fusion), channel_id=1, source_target_pairs={{0,2},{1,3},{2,0},{3,1},{4,6},{5,7},{6,4},{7,5},{8,10},{9,11},{10,... | collective-permute-start | bytes 393224 | tf_op jit(solution)/shard_map/ppermute | solution.py:22
  6.7 13.6 %collective-permute-start = (bf16[64,1024]{1,0:T(8,128)(2,1)S(1)}, bf16[64,1024]{1,0:T(8,128)(2,1)S(1)}, u32[]{:S(2)}, u32[]{:S(2)}) collective-permute-start(bf16[64,1024]{1,0:T(8,128)(2,1)S(1)} %constant_dynamic-slice_fusion), channel_id=1, source_target_pairs={{0,1},{1,0},{2,3},{3,2},{4,5},{5,4},{6,7},{7,6},{8,9},{9,8},{10,11... | collective-permute-start | bytes 393224 | tf_op jit(solution)/shard_map/ppermute | solution.py:22
  20.3 29.9 %all-to-all-start = ((bf16[4,512,256]{2,1,0:T(8,128)(2,1)}), bf16[4,512,256]{2,1,0:T(8,128)(2,1)S(1)}, u32[]{:S(2)}, u32[]{:S(2)}) async-start(bf16[4,512,256]{2,1,0:T(8,128)(2,1)} %get-tuple-element.171), calls=%async_computation | async-start | bytes 2097152 | tf_op jit(solution)/shard_map/all_to_all | solution.py:26
  25.4 7.6 %collective-permute-start.4 = (bf16[3,64,1024]{2,1,0:T(8,128)(2,1)S(1)}, bf16[3,64,1024]{2,1,0:T(8,128)(2,1)S(1)}, u32[]{:S(2)}, u32[]{:S(2)}) collective-permute-start(bf16[3,64,1024]{2,1,0:T(8,128)(2,1)S(1)} %pad_maximum_fusion.refs_4_), channel_id=1, source_target_pairs={{0,4},{4,0},{8,12},{12,8},{16,20},{20,16},{24,28},{28,24},{1,5},{5... | collective-permute-start | bytes 1179656 | tf_op jit(solution)/shard_map/ppermute | solution.py:22
  25.4 11.5 %collective-permute-start.3 = (bf16[3,64,1024]{2,1,0:T(8,128)(2,1)S(1)}, bf16[3,64,1024]{2,1,0:T(8,128)(2,1)S(1)}, u32[]{:S(2)}, u32[]{:S(2)}) collective-permute-start(bf16[3,64,1024]{2,1,0:T(8,128)(2,1)S(1)} %pad_maximum_fusion.refs_4_), channel_id=1, source_target_pairs={{0,8},{4,12},{8,0},{12,4},{16,24},{20,28},{24,16},{28,20},{1,9},{5... | collective-permute-start | bytes 1179656 | tf_op jit(solution)/shard_map/ppermute | solution.py:22
  37.0 9.0 %collective-permute-start.5 = (bf16[3,64,1024]{2,1,0:T(8,128)(2,1)S(1)}, bf16[3,64,1024]{2,1,0:T(8,128)(2,1)S(1)}, u32[]{:S(2)}, u32[]{:S(2)}) collective-permute-start(bf16[3,64,1024]{2,1,0:T(8,128)(2,1)S(1)} %collective-permute-done.3.refs_6_), channel_id=1, source_target_pairs={{0,4},{4,0},{8,12},{12,8},{16,20},{20,16},{24,28},{28,24},{1,5},{5... | collective-permute-start | bytes 1179656 | tf_op jit(solution)/shard_map/ppermute | solution.py:22
  61.1 29.7 %all-to-all-start.1 = ((bf16[4,512,256]{2,1,0:T(8,128)(2,1)}), bf16[4,512,256]{2,1,0:T(8,128)(2,1)}, u32[]{:S(2)}, u32[]{:S(2)}) async-start(bf16[4,512,256]{2,1,0:T(8,128)(2,1)} %get-tuple-element.192), calls=%async_computation.1 | async-start | bytes 2097152 | tf_op jit(solution)/shard_map/all_to_all | solution.py:26
  74.5 5.7 %collective-permute-start.6 = (bf16[512,1024]{1,0:T(8,128)(2,1)S(1)}, bf16[512,1024]{1,0:T(8,128)(2,1)S(1)}, u32[]{:S(2)}, u32[]{:S(2)}) collective-permute-start(bf16[512,1024]{1,0:T(8,128)(2,1)S(1)} %get-tuple-element.197), channel_id=1, source_target_pairs={{0,4},{4,0},{8,12},{12,8},{16,20},{20,16},{24,28},{28,24},{1,5},{5... | collective-permute-start | bytes 3145736 | tf_op jit(solution)/shard_map/ppermute | solution.py:22
  74.6 5.7 %collective-permute-start.7 = (bf16[512,1024]{1,0:T(8,128)(2,1)S(1)}, bf16[512,1024]{1,0:T(8,128)(2,1)S(1)}, u32[]{:S(2)}, u32[]{:S(2)}) collective-permute-start(bf16[512,1024]{1,0:T(8,128)(2,1)S(1)} %get-tuple-element.198), channel_id=1, source_target_pairs={{0,4},{4,0},{8,12},{12,8},{16,20},{20,16},{24,28},{28,24},{1,5},{5... | collective-permute-start | bytes 3145736 | tf_op jit(solution)/shard_map/ppermute | solution.py:22
  75.1 4.4 %collective-permute-start.8 = (bf16[256,1024]{1,0:T(8,128)(2,1)S(1)}, bf16[256,1024]{1,0:T(8,128)(2,1)S(1)}, u32[]{:S(2)}, u32[]{:S(2)}) collective-permute-start(bf16[256,1024]{1,0:T(8,128)(2,1)S(1)} %get-tuple-element.199), channel_id=1, source_target_pairs={{0,4},{4,0},{8,12},{12,8},{16,20},{20,16},{24,28},{28,24},{1,5},{5... | collective-permute-start | bytes 1572872 | tf_op jit(solution)/shard_map/ppermute | solution.py:22
  75.2 5.1 %collective-permute-start.9 = (bf16[256,1024]{1,0:T(8,128)(2,1)S(1)}, bf16[256,1024]{1,0:T(8,128)(2,1)S(1)}, u32[]{:S(2)}, u32[]{:S(2)}) collective-permute-start(bf16[256,1024]{1,0:T(8,128)(2,1)S(1)} %get-tuple-element.200), channel_id=1, source_target_pairs={{0,4},{4,0},{8,12},{12,8},{16,20},{20,16},{24,28},{28,24},{1,5},{5... | collective-permute-start | bytes 1572872 | tf_op jit(solution)/shard_map/ppermute | solution.py:22
  80.3 17.9 %copy-start.5 = (bf16[3,1024,256]{2,1,0:T(8,128)(2,1)S(1)}, bf16[3,1024,256]{2,1,0:T(8,128)(2,1)}, u32[]{:S(2)}) copy-start(bf16[3,1024,256]{2,1,0:T(8,128)(2,1)} %weight_ref.1) | copy-start | bytes 4718596
  84.0 14.1 %copy-start.35 = (bf16[1,1024]{1,0:T(2,128)(2,1)S(1)}, bf16[1,1024]{1,0:T(2,128)(2,1)}, u32[]{:S(2)}) copy-start(bf16[1,1024]{1,0:T(2,128)(2,1)} %broadcast_in_dim.10.refs_1_.gain_ref) | copy-start | bytes 6148
  90.8 29.5 %all-to-all-start.2 = ((bf16[4,128,1024]{2,1,0:T(8,128)(2,1)}), bf16[4,128,1024]{2,1,0:T(8,128)(2,1)}, u32[]{:S(2)}, u32[]{:S(2)}) async-start(bf16[4,128,1024]{2,1,0:T(8,128)(2,1)} %bitcast.14), calls=%async_computation.2 | async-start | bytes 2097152 | tf_op jit(solution)/shard_map/all_to_all | solution.py:26
  95.0 18.8 %collective-permute-start.10 = (bf16[384,1024]{1,0:T(8,128)(2,1)}, bf16[384,1024]{1,0:T(8,128)(2,1)S(1)}, u32[]{:S(2)}, u32[]{:S(2)}) collective-permute-start(bf16[384,1024]{1,0:T(8,128)(2,1)} %copy-done.40), channel_id=1, source_target_pairs={{0,8},{4,12},{8,0},{12,4},{16,24},{20,28},{24,16},{28,20},{1,9},{5... | collective-permute-start | bytes 2359304 | tf_op jit(solution)/shard_map/ppermute | solution.py:22
  96.6 18.4 %collective-permute-start.11 = (bf16[384,1024]{1,0:T(8,128)(2,1)}, bf16[384,1024]{1,0:T(8,128)(2,1)S(1)}, u32[]{:S(2)}, u32[]{:S(2)}) collective-permute-start(bf16[384,1024]{1,0:T(8,128)(2,1)} %copy-done.39), channel_id=1, source_target_pairs={{0,16},{4,20},{8,24},{12,28},{16,0},{20,4},{24,8},{28,12},{1,17},{... | collective-permute-start | bytes 2359304 | tf_op jit(solution)/shard_map/ppermute | solution.py:22
  120.3 28.9 %all-to-all-start.3 = ((bf16[4,128,1024]{2,1,0:T(8,128)(2,1)}), bf16[4,128,1024]{2,1,0:T(8,128)(2,1)S(1)}, u32[]{:S(2)}, u32[]{:S(2)}) async-start(bf16[4,128,1024]{2,1,0:T(8,128)(2,1)} %bitcast.6), calls=%async_computation.3 | async-start | bytes 2097152 | tf_op jit(solution)/shard_map/all_to_all | solution.py:26
  124.1 19.1 %collective-permute-start.12 = (bf16[384,1024]{1,0:T(8,128)(2,1)}, bf16[384,1024]{1,0:T(8,128)(2,1)}, u32[]{:S(2)}, u32[]{:S(2)}) collective-permute-start(bf16[384,1024]{1,0:T(8,128)(2,1)} %copy-done.38), channel_id=1, source_target_pairs={{0,4},{4,0},{8,12},{12,8},{16,20},{20,16},{24,28},{28,24},{1,5},{5... | collective-permute-start | bytes 2359304 | tf_op jit(solution)/shard_map/ppermute | solution.py:22
  124.2 11.7 %collective-permute-start.13 = (bf16[192,1024]{1,0:T(8,128)(2,1)}, bf16[192,1024]{1,0:T(8,128)(2,1)S(1)}, u32[]{:S(2)}, u32[]{:S(2)}) collective-permute-start(bf16[192,1024]{1,0:T(8,128)(2,1)} %copy-done.42), channel_id=1, source_target_pairs={{0,16},{4,20},{8,24},{12,28},{16,0},{20,4},{24,8},{28,12},{1,17},{... | collective-permute-start | bytes 1179656 | tf_op jit(solution)/shard_map/ppermute | solution.py:22
  125.8 11.5 %collective-permute-start.14 = (bf16[192,1024]{1,0:T(8,128)(2,1)}, bf16[192,1024]{1,0:T(8,128)(2,1)}, u32[]{:S(2)}, u32[]{:S(2)}) collective-permute-start(bf16[192,1024]{1,0:T(8,128)(2,1)} %copy-done.41), channel_id=1, source_target_pairs={{0,8},{4,12},{8,0},{12,4},{16,24},{20,28},{24,16},{28,20},{1,9},{5... | collective-permute-start | bytes 1179656 | tf_op jit(solution)/shard_map/ppermute | solution.py:22
  141.2 7.7 %collective-permute-start.15 = (bf16[128,1024]{1,0:T(8,128)(2,1)S(1)}, bf16[128,1024]{1,0:T(8,128)(2,1)}, u32[]{:S(2)}, u32[]{:S(2)}) collective-permute-start(bf16[128,1024]{1,0:T(8,128)(2,1)S(1)} %get-tuple-element.261.refs_0_), channel_id=1, source_target_pairs={{0,16},{4,20},{8,24},{12,28},{16,0},{20,4},{24,8},{28,12},{1,17},{... | collective-permute-start | bytes 786440 | tf_op jit(solution)/shard_map/ppermute | solution.py:22
  141.7 7.5 %collective-permute-start.16 = (bf16[128,1024]{1,0:T(8,128)(2,1)S(1)}, bf16[128,1024]{1,0:T(8,128)(2,1)}, u32[]{:S(2)}, u32[]{:S(2)}) collective-permute-start(bf16[128,1024]{1,0:T(8,128)(2,1)S(1)} %get-tuple-element.263.refs_2_), channel_id=1, source_target_pairs={{0,8},{4,12},{8,0},{12,4},{16,24},{20,28},{24,16},{28,20},{1,9},{5... | collective-permute-start | bytes 786440 | tf_op jit(solution)/shard_map/ppermute | solution.py:22
  145.3 17.3 %copy-start.2 = (bf16[512,1024]{1,0:T(8,128)(2,1)S(1)}, bf16[512,1024]{1,0:T(8,128)(2,1)}, u32[]{:S(2)}) copy-start(bf16[512,1024]{1,0:T(8,128)(2,1)} %pick_only.1.rows_ref) | copy-start | bytes 3145732
  145.3 17.3 %copy-start.33 = (bf16[1,1024]{1,0:T(2,128)(2,1)S(1)}, bf16[1,1024]{1,0:T(2,128)(2,1)}, u32[]{:S(2)}) copy-start(bf16[1,1024]{1,0:T(2,128)(2,1)} %broadcast_in_dim.11.router_ref) | copy-start | bytes 6148
  145.3 17.3 %copy-start.34 = (f32[128,1]{1,0:T(8,128)S(1)}, f32[128,1]{1,0:T(8,128)}, u32[]{:S(2)}) copy-start(f32[128,1]{1,0:T(8,128)} %get-tuple-element.259.score_ref) | copy-start | bytes 1540
  149.2 36.0 %all-to-all-start.4 = ((bf16[4,168,1024]{2,1,0:T(8,128)(2,1)}), bf16[4,168,1024]{2,1,0:T(8,128)(2,1)S(1)}, u32[]{:S(2)}, u32[]{:S(2)}) async-start(bf16[4,168,1024]{2,1,0:T(8,128)(2,1)} %copy-done.9), calls=%async_computation.4 | async-start | bytes 2752512 | tf_op jit(solution)/shard_map/all_to_all | solution.py:26
  154.0 13.6 %collective-permute-start.17 = (bf16[128,1024]{1,0:T(8,128)(2,1)}, bf16[128,1024]{1,0:T(8,128)(2,1)}, u32[]{:S(2)}, u32[]{:S(2)}) collective-permute-start(bf16[128,1024]{1,0:T(8,128)(2,1)} %copy-done.31), channel_id=1, source_target_pairs={{0,8},{4,12},{8,0},{12,4},{16,24},{20,28},{24,16},{28,20},{1,9},{5... | collective-permute-start | bytes 786440 | tf_op jit(solution)/shard_map/ppermute | solution.py:22
  155.5 12.6 %collective-permute-start.19 = (bf16[128,1024]{1,0:T(8,128)(2,1)}, bf16[128,1024]{1,0:T(8,128)(2,1)}, u32[]{:S(2)}, u32[]{:S(2)}) collective-permute-start(bf16[128,1024]{1,0:T(8,128)(2,1)} %copy-done.29), channel_id=1, source_target_pairs={{0,16},{4,20},{8,24},{12,28},{16,0},{20,4},{24,8},{28,12},{1,17},{... | collective-permute-start | bytes 786440 | tf_op jit(solution)/shard_map/ppermute | solution.py:22
  156.9 11.2 %collective-permute-start.18 = (bf16[128,1024]{1,0:T(8,128)(2,1)}, bf16[128,1024]{1,0:T(8,128)(2,1)}, u32[]{:S(2)}, u32[]{:S(2)}) collective-permute-start(bf16[128,1024]{1,0:T(8,128)(2,1)} %collective-permute-done.15.refs_1_), channel_id=1, source_target_pairs={{0,8},{4,12},{8,0},{12,4},{16,24},{20,28},{24,16},{28,20},{1,9},{5... | collective-permute-start | bytes 786440 | tf_op jit(solution)/shard_map/ppermute | solution.py:22
  157.5 10.6 %collective-permute-start.20 = (bf16[128,1024]{1,0:T(8,128)(2,1)}, bf16[128,1024]{1,0:T(8,128)(2,1)}, u32[]{:S(2)}, u32[]{:S(2)}) collective-permute-start(bf16[128,1024]{1,0:T(8,128)(2,1)} %collective-permute-done.16.refs_3_), channel_id=1, source_target_pairs={{0,16},{4,20},{8,24},{12,28},{16,0},{20,4},{24,8},{28,12},{1,17},{... | collective-permute-start | bytes 786440 | tf_op jit(solution)/shard_map/ppermute | solution.py:22
  162.6 8.8 %collective-permute-start.21 = (bf16[256,1024]{1,0:T(8,128)(2,1)}, bf16[256,1024]{1,0:T(8,128)(2,1)}, u32[]{:S(2)}, u32[]{:S(2)}) collective-permute-start(bf16[256,1024]{1,0:T(8,128)(2,1)} %get-tuple-element.265.refs_0_), channel_id=1, source_target_pairs={{0,4},{4,0},{8,12},{12,8},{16,20},{20,16},{24,28},{28,24},{1,5},{5... | collective-permute-start | bytes 1572872 | tf_op jit(solution)/shard_map/ppermute | solution.py:22
  167.6 5.3 %collective-permute-start.23 = (bf16[256,1024]{1,0:T(8,128)(2,1)S(1)}, bf16[256,1024]{1,0:T(8,128)(2,1)S(1)}, u32[]{:S(2)}, u32[]{:S(2)}) collective-permute-start(bf16[256,1024]{1,0:T(8,128)(2,1)S(1)} %copy-done.21), channel_id=1, source_target_pairs={{0,4},{4,0},{8,12},{12,8},{16,20},{20,16},{24,28},{28,24},{1,5},{5... | collective-permute-start | bytes 1572872 | tf_op jit(solution)/shard_map/ppermute | solution.py:22
  169.4 3.5 %collective-permute-start.22 = (bf16[256,1024]{1,0:T(8,128)(2,1)S(1)}, bf16[256,1024]{1,0:T(8,128)(2,1)S(1)}, u32[]{:S(2)}, u32[]{:S(2)}) collective-permute-start(bf16[256,1024]{1,0:T(8,128)(2,1)S(1)} %get-tuple-element.273.refs_1_), channel_id=1, source_target_pairs={{0,4},{4,0},{8,12},{12,8},{16,20},{20,16},{24,28},{28,24},{1,5},{5... | collective-permute-start | bytes 1572872 | tf_op jit(solution)/shard_map/ppermute | solution.py:22
  169.5 5.0 %collective-permute-start.24 = (bf16[256,1024]{1,0:T(8,128)(2,1)S(1)}, bf16[256,1024]{1,0:T(8,128)(2,1)}, u32[]{:S(2)}, u32[]{:S(2)}) collective-permute-start(bf16[256,1024]{1,0:T(8,128)(2,1)S(1)} %get-tuple-element.275.refs_5_), channel_id=1, source_target_pairs={{0,4},{4,0},{8,12},{12,8},{16,20},{20,16},{24,28},{28,24},{1,5},{5... | collective-permute-start | bytes 1572872 | tf_op jit(solution)/shard_map/ppermute | solution.py:22
  170.0 19.6 %collective-permute-start.25 = (bf16[192,1024]{1,0:T(8,128)(2,1)S(1)}, bf16[192,1024]{1,0:T(8,128)(2,1)}, u32[]{:S(2)}, u32[]{:S(2)}) collective-permute-start(bf16[192,1024]{1,0:T(8,128)(2,1)S(1)} %copy-done.25), channel_id=1, source_target_pairs={{0,16},{4,20},{8,24},{12,28},{16,0},{20,4},{24,8},{28,12},{1,17},{... | collective-permute-start | bytes 1179656 | tf_op jit(solution)/shard_map/ppermute | solution.py:22
  171.4 18.2 %collective-permute-start.26 = (bf16[192,1024]{1,0:T(8,128)(2,1)}, bf16[192,1024]{1,0:T(8,128)(2,1)}, u32[]{:S(2)}, u32[]{:S(2)}) collective-permute-start(bf16[192,1024]{1,0:T(8,128)(2,1)} %copy-done.26), channel_id=1, source_target_pairs={{0,8},{4,12},{8,0},{12,4},{16,24},{20,28},{24,16},{28,20},{1,9},{5... | collective-permute-start | bytes 1179656 | tf_op jit(solution)/shard_map/ppermute | solution.py:22
  185.2 29.5 %all-to-all-start.5 = ((bf16[4,128,1024]{2,1,0:T(8,128)(2,1)}), bf16[4,128,1024]{2,1,0:T(8,128)(2,1)}, u32[]{:S(2)}, u32[]{:S(2)}) async-start(bf16[4,128,1024]{2,1,0:T(8,128)(2,1)} %finish_input.1.piece_ref), calls=%async_computation.5 | async-start | bytes 2097152 | tf_op jit(solution)/shard_map/all_to_all | solution.py:26
  190.9 11.9 %collective-permute-start.29 = (bf16[192,1024]{1,0:T(8,128)(2,1)S(1)}, bf16[192,1024]{1,0:T(8,128)(2,1)S(1)}, u32[]{:S(2)}, u32[]{:S(2)}) collective-permute-start(bf16[192,1024]{1,0:T(8,128)(2,1)S(1)} %get-tuple-element.291.a_ref), channel_id=1, source_target_pairs={{0,8},{4,12},{8,0},{12,4},{16,24},{20,28},{24,16},{28,20},{1,9},{5... | collective-permute-start | bytes 1179656 | tf_op jit(solution)/shard_map/ppermute | solution.py:22
  192.5 10.3 %collective-permute-start.30 = (bf16[192,1024]{1,0:T(8,128)(2,1)S(1)}, bf16[192,1024]{1,0:T(8,128)(2,1)S(1)}, u32[]{:S(2)}, u32[]{:S(2)}) collective-permute-start(bf16[192,1024]{1,0:T(8,128)(2,1)S(1)} %get-tuple-element.293.b_ref), channel_id=1, source_target_pairs={{0,16},{4,20},{8,24},{12,28},{16,0},{20,4},{24,8},{28,12},{1,17},{... | collective-permute-start | bytes 1179656 | tf_op jit(solution)/shard_map/ppermute | solution.py:22
  193.8 9.0 %collective-permute-start.28 = (bf16[40,1024]{1,0:T(8,128)(2,1)S(1)}, bf16[40,1024]{1,0:T(8,128)(2,1)S(1)}, u32[]{:S(2)}, u32[]{:S(2)}) collective-permute-start(bf16[40,1024]{1,0:T(8,128)(2,1)S(1)} %first_small.1.refs_0_), channel_id=1, source_target_pairs={{0,8},{4,12},{8,0},{12,4},{16,24},{20,28},{24,16},{28,20},{1,9},{5... | collective-permute-start | bytes 245768 | tf_op jit(solution)/shard_map/ppermute | solution.py:22
  203.0 7.1 %collective-permute-start.32 = (bf16[384,1024]{1,0:T(8,128)(2,1)S(1)}, bf16[384,1024]{1,0:T(8,128)(2,1)S(1)}, u32[]{:S(2)}, u32[]{:S(2)}) collective-permute-start(bf16[384,1024]{1,0:T(8,128)(2,1)S(1)} %joined_lanes.1.near_ref), channel_id=1, source_target_pairs={{0,4},{4,0},{8,12},{12,8},{16,20},{20,16},{24,28},{28,24},{1,5},{5... | collective-permute-start | bytes 2359304 | tf_op jit(solution)/shard_map/ppermute | solution.py:22
  203.1 7.0 %collective-permute-start.27 = (bf16[40,1024]{1,0:T(8,128)(2,1)S(1)}, bf16[40,1024]{1,0:T(8,128)(2,1)S(1)}, u32[]{:S(2)}, u32[]{:S(2)}) collective-permute-start(bf16[40,1024]{1,0:T(8,128)(2,1)S(1)} %first_small.1.refs_0_), channel_id=1, source_target_pairs={{0,16},{4,20},{8,24},{12,28},{16,0},{20,4},{24,8},{28,12},{1,17},{... | collective-permute-start | bytes 245768 | tf_op jit(solution)/shard_map/ppermute | solution.py:22
  204.4 5.6 %collective-permute-start.31 = (bf16[40,1024]{1,0:T(8,128)(2,1)S(1)}, bf16[40,1024]{1,0:T(8,128)(2,1)S(1)}, u32[]{:S(2)}, u32[]{:S(2)}) collective-permute-start(bf16[40,1024]{1,0:T(8,128)(2,1)S(1)} %collective-permute-done.28.refs_1_), channel_id=1, source_target_pairs={{0,16},{4,20},{8,24},{12,28},{16,0},{20,4},{24,8},{28,12},{1,17},{... | collective-permute-start | bytes 245768 | tf_op jit(solution)/shard_map/ppermute | solution.py:22
  205.1 7.6 %collective-permute-start.33 = (bf16[40,1024]{1,0:T(8,128)(2,1)S(1)}, bf16[40,1024]{1,0:T(8,128)(2,1)S(1)}, u32[]{:S(2)}, u32[]{:S(2)}) collective-permute-start(bf16[40,1024]{1,0:T(8,128)(2,1)S(1)} %first_small.1.refs_0_), channel_id=1, source_target_pairs={{0,4},{4,0},{8,12},{12,8},{16,20},{20,16},{24,28},{28,24},{1,5},{5... | collective-permute-start | bytes 245768 | tf_op jit(solution)/shard_map/ppermute | solution.py:22
  205.1 7.6 %collective-permute-start.34 = (bf16[40,1024]{1,0:T(8,128)(2,1)S(1)}, bf16[40,1024]{1,0:T(8,128)(2,1)S(1)}, u32[]{:S(2)}, u32[]{:S(2)}) collective-permute-start(bf16[40,1024]{1,0:T(8,128)(2,1)S(1)} %collective-permute-done.28.refs_1_), channel_id=1, source_target_pairs={{0,4},{4,0},{8,12},{12,8},{16,20},{20,16},{24,28},{28,24},{1,5},{5... | collective-permute-start | bytes 245768 | tf_op jit(solution)/shard_map/ppermute | solution.py:22
  210.1 2.7 %collective-permute-start.35 = (bf16[40,1024]{1,0:T(8,128)(2,1)S(1)}, bf16[40,1024]{1,0:T(8,128)(2,1)S(1)}, u32[]{:S(2)}, u32[]{:S(2)}) collective-permute-start(bf16[40,1024]{1,0:T(8,128)(2,1)S(1)} %collective-permute-done.27.refs_2_), channel_id=1, source_target_pairs={{0,4},{4,0},{8,12},{12,8},{16,20},{20,16},{24,28},{28,24},{1,5},{5... | collective-permute-start | bytes 245768 | tf_op jit(solution)/shard_map/ppermute | solution.py:22
  210.1 2.7 %collective-permute-start.36 = (bf16[40,1024]{1,0:T(8,128)(2,1)S(1)}, bf16[40,1024]{1,0:T(8,128)(2,1)S(1)}, u32[]{:S(2)}, u32[]{:S(2)}) collective-permute-start(bf16[40,1024]{1,0:T(8,128)(2,1)S(1)} %collective-permute-done.31.refs_3_), channel_id=1, source_target_pairs={{0,4},{4,0},{8,12},{12,8},{16,20},{20,16},{24,28},{28,24},{1,5},{5... | collective-permute-start | bytes 245768 | tf_op jit(solution)/shard_map/ppermute | solution.py:22
  (48 other events, 190.0 us)

commit v7 on v6

--- a/solution.py
+++ b/solution.py
@@ -235,8 +235,76 @@
         out_shape=jax.ShapeDtypeStruct((rows, width), BF),
         input_output_aliases={4: 0} if kept else {},
         cost_estimate=small_cost(),
+        compiler_params=pltpu.CompilerParams(vmem_limit_bytes=52 << 20),
         name="merge_rows",
     )(mine, base, offsets, pieces, *kept)
+
+
+def hold_rows(base, mine, which, ways):
+    rows, width = base.shape
+    count = rows // ways
+    first = which.start
+
+    def kernel(mine_ref, base_ref, out_ref):
+        out_ref[0] = base_ref[...]
+
+    return pl.pallas_call(
+        kernel,
+        grid_spec=pltpu.PrefetchScalarGridSpec(
+            num_scalar_prefetch=1,
+            grid=(len(which),),
+            in_specs=[pl.BlockSpec((count, width), lambda i, m: (m[0] ^ (i + first), 0))],
+            out_specs=pl.BlockSpec((1, count, width), lambda i, m: (i, 0, 0)),
+        ),
+        out_shape=jax.ShapeDtypeStruct((len(which), count, width), BF),
+        cost_estimate=small_cost(),
+        compiler_params=pltpu.CompilerParams(vmem_limit_bytes=52 << 20),
+        name="hold_rows",
+    )(mine, base)
+
+
+def merge_held(held, offsets, pieces, mine, which, out):
+    rows, width = out.shape
+    ways, depth, _ = pieces.shape
+    count = rows // ways
+    groups = count // GROUP
+    sub = 256
+    sub_groups = sub // GROUP
+
+    first = which.start
+
+    def kernel(part_ref, base_ref, offset_ref, piece_ref, old_ref, out_ref):
+        local = lax.broadcasted_iota(jnp.int32, (sub, sub_groups), 0) - GROUP * lax.broadcasted_iota(
+            jnp.int32, (sub, sub_groups), 1
+        )
+        for s in range(count // sub):
+            here = slice(s * sub, (s + 1) * sub)
+            to = slice(s * sub_groups, (s + 1) * sub_groups)
+            chosen = (local == offset_ref[:, to]).astype(F32)
+            hit = jnp.sum(chosen, axis=1, keepdims=True) > 0.5
+            spread = dot(chosen.astype(BF), piece_ref[0, to, :], NN)
+            out_ref[here, :] = jnp.where(hit, spread, base_ref[pl.program_id(0), here, :].astype(F32)).astype(BF)
+
+    grid_spec = pltpu.PrefetchScalarGridSpec(
+        num_scalar_prefetch=1,
+        grid=(len(which),),
+        in_specs=[
+            pl.BlockSpec(memory_space=pltpu.VMEM),
+            pl.BlockSpec((1, groups), lambda i, m: (0, m[0] ^ (i + first))),
+            pl.BlockSpec((1, depth, width), lambda i, m: (m[0] ^ (i + first), 0, 0)),
+            pl.BlockSpec(memory_space=pl.ANY),
+        ],
+        out_specs=pl.BlockSpec((count, width), lambda i, m: (m[0] ^ (i + first), 0)),
+    )
+    return pl.pallas_call(
+        kernel,
+        grid_spec=grid_spec,
+        out_shape=jax.ShapeDtypeStruct((rows, width), BF),
+        input_output_aliases={4: 0},
+        cost_estimate=small_cost(),
+        compiler_params=pltpu.CompilerParams(vmem_limit_bytes=24 << 20),
+        name="merge_held",
+    )(mine, held, offsets, pieces, out)
 
 
 def attend(picked, gain, weight, seq_row, ways):
@@ -297,7 +365,7 @@
 def feed_forward(heads, own_weight, quarters, picked, gain, up, grad_act, grad_mixer, part, mine, ways):
     rows, width = picked.shape
     hidden = up.shape[1]
-    sub = min(512, hidden)
+    sub = min(1024, hidden)
     count, _, heads_width = heads.shape
     piece = heads_width // 4
     own = rows // ways
@@ -1116,8 +1184,11 @@
         qkv_a_got, qkv_b_got = swap(qkv_a, "dp", bit_x), swap(qkv_b, "dp", bit_y)
         fresh, blocks, qkv_a, qkv_b = tie((fresh, blocks, qkv_a, qkv_b))
     output = merge_rows(tokens, route_offset, fresh, mine_array, range(ways // 2))
+    cotangent, output = tie((cotangent, output))
+    held = hold_rows(cotangent, mine_array, range(1, ways), ways)
+    held = pltpu.with_memory_space_constraint(held, pltpu.VMEM)
     if by_swaps:
-        more, qkv_a_got, qkv_b_got, output = tie((more, qkv_a_got, qkv_b_got, output))
+        more, qkv_a_got, qkv_b_got, output, held = tie((more, qkv_a_got, qkv_b_got, output, held))
         qkv_near = joined_lanes(qkv_a, qkv_a_got, qkv_b, qkv_b_got)
         qkv_far = swap(qkv_near, "dp", 1)
         blocks = blocks + more
@@ -1133,10 +1204,10 @@
         more, qkv_grad = tie((more, qkv_grad))
         out_grad, *small = last_small(blocks + more, gathered([bit_x, bit_y, 1]), part_array, shares)
         small[3] = small[3][:, :2]
-        input_rows, early, output, out_grad, small, qkv_grad = tie(
-            (input_rows, early, output, out_grad, small, qkv_grad)
+        input_rows, early, output, held, out_grad, small, qkv_grad = tie(
+            (input_rows, early, output, held, out_grad, small, qkv_grad)
         )
-    input_grad = merge_rows(cotangent, route_offset, input_rows, mine_array, range(1, ways), early)
+    input_grad = merge_held(held, route_offset, input_rows, mine_array, range(1, ways), early)
     if not by_swaps:
         swapped = jnp.concatenate([qkv_leaving, qkv_part])
         qkv_whole = jnp.where(part & 1 == 0, jnp.concatenate([qkv_part, qkv_leaving]), swapped)

time: 224 us -> 223 us (level)
  local copies, waits for them, and re-layouts: 25.4 us -> 30.6 us
  waiting for transfers between devices: 44.4 us -> 39.3 us
    pallas_call x0 -> x2, Pallas kernels: none -> 10.5 us  [the longest x1 6.47 us: hold_rows(): pl.pallas_call(kernel, grid_spec=pltpu.PrefetchScalarGridSpec(num_scalar_...]
    pallas_call x4 -> x3, Pallas kernels: 19.9 us -> 12.3 us  [merge_rows(): pl.pallas_call(kernel, grid_spec=grid_spec, out_shape=jax.ShapeDtypeStruc...]
    ppermute x37, waiting for transfers between devices: 26.4 us -> 19.2 us  [swap(): return lax.ppermute(values, axis, [(i, i ^ bits) for i in range(size)])]
    unnamed x106 -> x112, local copies, waits for them, and re-layouts: 22.7 us -> 27.8 us
  transfers between devices with their start and end apart: 43 -> 43, of which waited for: 15 -> 14; matrix products, arithmetic and copies ran while one was open for 2% -> 2% of each run, Pallas kernels for 33% -> 35%
where the time goes in v7:
time: 223 us; the launch traced here: 222 us
  Pallas kernels  92.1 us (41%)
  starting transfers between devices  56.2 us (25%)
  waiting for transfers between devices  39.3 us (18%)
  local copies, waits for them, and re-layouts  30.6 us (14%)
  matrix products  2.23 us (1%)
    ppermute x37, starting transfers between devices, swap(): return lax.ppermute(values, axis, [(i, i ^ bits) for i in range(size)])  31.1 us
    unnamed x112, local copies, waits for them, and re-layouts  27.8 us
    all_to_all x6, starting transfers between devices, to_all(): return lax.all_to_all(blocks, 'tensor', 0, 0, tiled=True)  25.1 us
    all_to_all x6, waiting for transfers between devices, to_all(): return lax.all_to_all(blocks, 'tensor', 0, 0, tiled=True)  20 us
    ppermute x37, waiting for transfers between devices, swap(): return lax.ppermute(values, axis, [(i, i ^ bits) for i in range(size)])  19.2 us
    pallas_call x2, Pallas kernels, staged(): pl.pallas_call(kernel, in_specs=[pl.BlockSpec(memory_space=pltpu.SMEM)] *...  16.1 us
    pallas_call x3, Pallas kernels, merge_rows(): pl.pallas_call(kernel, grid_spec=grid_spec, out_shape=jax.ShapeDtypeStruc...  12.3 us
    pallas_call x1, Pallas kernels, spread_rows(): pl.pallas_call(kernel, grid_spec=pltpu.PrefetchScalarGridSpec(num_scalar_...  7.99 us
  transfers between devices with their start and end apart: 43, of which 14 were waited for; matrix products, arithmetic and copies ran while one was open for 2% of the time, Pallas kernels for 35%

profile of v7, /device:TPU:0, one launch (start us, length us, event | category | flops | bytes accessed | tf_op | source)
XLA Modules:
  0.0 221.6 jit_solution(16116978133842507127)
XLA Ops:
  1.6 5.1 %collective-permute-start.2 = (bf16[64,1024]{1,0:T(8,128)(2,1)S(1)}, bf16[64,1024]{1,0:T(8,128)(2,1)S(1)}, u32[]{:S(2)}, u32[]{:S(2)}) collective-permute-start(bf16[64,1024]{1,0:T(8,128)(2,1)S(1)} %constant_dynamic-slice_fusion), channel_id=1, source_target_pairs={{0,3},{1,2},{2,1},{3,0},{4,7},{5,6},{6,5},{7,4},{8,11},{9,10},{10,... | collective-permute-start | bytes 393224 | tf_op jit(solution)/shard_map/ppermute | solution.py:22
  7.3 5.7 %pick_rows.1.refs_0_.picked_ref.refs_8_ = bf16[512,1024]{1,0:T(8,128)(2,1)} custom-call(bf16[4096,1024]{1,0:T(8,128)(2,1)} %base_ref.10, s32[1,512]{1,0:T(1,128)} %offset_ref.11), custom_call_target="tpu_custom_call" | custom-call | flops 1024 | bytes 1024 | tf_op jit(solution)/shard_map/pick_rows/pallas_call | solution.py:133
  13.7 6.6 %attend.1 = (bf16[512,1024]{1,0:T(8,128)(2,1)}, bf16[3,512,256]{2,1,0:T(8,128)(2,1)}, bf16[4,512,256]{2,1,0:T(8,128)(2,1)}, bf16[4,256,256]{2,1,0:T(8,128)(2,1)}, bf16[4,256,512]{2,1,0:T(8,128)(2,1)}) custom-call(bf16[512,1024]{1,0:T(8,128)(2,1)} %pick_rows.1.refs_0_.picked_ref.refs_8_, bf16[1,1024]{1,0:T(2,128)(2,1)} %broadcast_in_dim.10.refs_1_.gain_ref, ...), custom_call_target="tpu_custom_call" | custom-call | flops 1024 | bytes 1024 | tf_op jit(solution)/shard_map/attend/pallas_call | solution.py:86
  20.3 5.0 %all-to-all-start = ((bf16[4,512,256]{2,1,0:T(8,128)(2,1)}), bf16[4,512,256]{2,1,0:T(8,128)(2,1)S(1)}, u32[]{:S(2)}, u32[]{:S(2)}) async-start(bf16[4,512,256]{2,1,0:T(8,128)(2,1)} %get-tuple-element.175), calls=%async_computation | async-start | bytes 2097152 | tf_op jit(solution)/shard_map/all_to_all | solution.py:26
  25.4 1.6 collective-permute-start.3
  27.0 6.0 %pick_only.1.rows_ref = bf16[512,1024]{1,0:T(8,128)(2,1)} custom-call(bf16[4096,1024]{1,0:T(8,128)(2,1)} %base_ref.9, s32[1,512]{1,0:T(1,128)} %offset_ref.11), custom_call_target="tpu_custom_call" | custom-call | flops 1024 | bytes 1024 | tf_op jit(solution)/shard_map/pick_only/pallas_call | solution.py:186
  33.0 4.0 %collective-permute-done.3.refs_6_ = bf16[3,64,1024]{2,1,0:T(8,128)(2,1)S(1)} collective-permute-done((bf16[3,64,1024]{2,1,0:T(8,128)(2,1)S(1)}, bf16[3,64,1024]{2,1,0:T(8,128)(2,1)S(1)}, u32[]{:S(2)}, u32[]{:S(2)}) %collective-permute-start.3) | collective-permute-done | bytes 393248 | tf_op jit(solution)/shard_map/ppermute | solution.py:22
  37.6 2.7 %score_sums.1.square_ref = f32[1,128]{1,0:T(1,128)} custom-call(s32[1]{0:T(128)} %bitcast.1.mine_ref.refs_1_.part_ref, bf16[4096,1024]{1,0:T(8,128)(2,1)} %base_ref.10, bf16[1,1024]{1,0:T(2,128)(2,1)} %broadcast_in_dim.11.router_ref), custom_call_target="tpu_custom_call" | custom-call | flops 1024 | bytes 1024 | tf_op jit(solution)/shard_map/score_sums/pallas_call | solution.py:153
  40.9 5.1 %act_grads.1 = (f32[512,1]{1,0:T(8,128)}, f32[1,128]{1,0:T(1,128)}, bf16[512,1024]{1,0:T(8,128)(2,1)}, f32[512,1024]{1,0:T(8,128)}) custom-call(bf16[512,1024]{1,0:T(8,128)(2,1)} %pick_rows.1.refs_0_.picked_ref.refs_8_, bf16[1,1024]{1,0:T(2,128)(2,1)} %broadcast_in_dim.11.router_ref, bf16[512,1024]{1,0:T(8,128)(2,1)} %pick_only.1.rows_ref, ...), custom_call_target="tpu_custom_call" | custom-call | flops 1024 | bytes 1024 | tf_op jit(solution)/shard_map/act_grads/pallas_call | solution.py:465
  46.1 4.1 %all-to-all-done.refs_2_.heads_ref = bf16[4,512,256]{2,1,0:T(8,128)(2,1)S(1)} async-done(((bf16[4,512,256]{2,1,0:T(8,128)(2,1)}), bf16[4,512,256]{2,1,0:T(8,128)(2,1)S(1)}, u32[]{:S(2)}, u32[]{:S(2)}) %all-to-all-start) | async-done | bytes 1048608 | tf_op jit(solution)/shard_map/all_to_all | solution.py:26
  51.2 9.5 %feed_forward.1 = (f32[128,1024]{1,0:T(8,128)}, bf16[512,1024]{1,0:T(8,128)(2,1)}, bf16[512,1024]{1,0:T(8,128)(2,1)}, bf16[512,1024]{1,0:T(8,128)(2,1)}, bf16[51...) custom-call(s32[1]{0:T(128)} %bitcast.refs_0_.part_ref, ...), custom_call_target="tpu_custom_call" | custom-call | flops 1024 | bytes 1024 | tf_op jit(solution)/shard_map/feed_forward/pallas_call | solution.py:86
  60.7 4.5 %all-to-all-start.1 = ((bf16[4,512,256]{2,1,0:T(8,128)(2,1)}), bf16[4,512,256]{2,1,0:T(8,128)(2,1)}, u32[]{:S(2)}, u32[]{:S(2)}) async-start(bf16[4,512,256]{2,1,0:T(8,128)(2,1)} %get-tuple-element.196), calls=%async_computation.1 | async-start | bytes 2097152 | tf_op jit(solution)/shard_map/all_to_all | solution.py:26
  71.3 3.9 %core_grads.1 = (bf16[2,768,1024]{2,1,0:T(8,128)(2,1)S(1)}, bf16[512,1024]{1,0:T(8,128)(2,1)S(1)}, bf16[512,1024]{1,0:T(8,128)(2,1)S(1)}, bf16[256,1024]{1,0:T(8,128)(2,1)S(1)}, bf16[256,1024]{1,0:T(8,128)(2,1)S(1)}) custom-call(s32[1]{0:T(128)} %bitcast.refs_0_.part_ref, bf16[512,1024]{1,0:T(8,128)(2,1)S(1)} %copy-done.10, bf16[512,1024]{1,0:T(8,128)(2,1)S(1)} %copy-done.6, ...), custom_call_target="tpu_custom_call" | custom-call | flops 1024 | bytes 1024 | tf_op jit(solution)/shard_map/core_grads/pallas_call | solution.py:690
  76.3 2.2 %convolution_convert_fusion = bf16[512,1024]{1,0:T(8,128)(2,1)} fusion(bf16[512,1024]{1,0:T(8,128)(2,1)S(1)} %copy-done.11, bf16[1024,1024]{1,0:T(8,128)(2,1)S(1)} %copy-done.45), kind=kOutput, calls=%fused_computation | convolution fusion | flops 1074266112 | bytes 4194304 | tf_op jit(solution)/shard_map/dot_general | solution.py:17
  78.5 1.6 collective-permute-done.8.refs_1_
  84.7 5.6 %all-to-all-done.1.head_ref = bf16[4,512,256]{2,1,0:T(8,128)(2,1)} async-done(((bf16[4,512,256]{2,1,0:T(8,128)(2,1)}), bf16[4,512,256]{2,1,0:T(8,128)(2,1)}, u32[]{:S(2)}, u32[]{:S(2)}) %all-to-all-start.1) | async-done | bytes 1048608 | tf_op jit(solution)/shard_map/all_to_all | solution.py:26
  90.3 4.2 %all-to-all-start.2 = ((bf16[4,128,1024]{2,1,0:T(8,128)(2,1)}), bf16[4,128,1024]{2,1,0:T(8,128)(2,1)}, u32[]{:S(2)}, u32[]{:S(2)}) async-start(bf16[4,128,1024]{2,1,0:T(8,128)(2,1)} %bitcast.14), calls=%async_computation.2 | async-start | bytes 2097152 | tf_op jit(solution)/shard_map/all_to_all | solution.py:26
  94.5 1.6 collective-permute-start.10
  96.1 1.5 collective-permute-start.11
  101.1 6.8 %attend_back.1 = (bf16[3,512,256]{2,1,0:T(8,128)(2,1)S(1)}, f32[1,1024]{1,0:T(1,128)S(1)}, bf16[512,1024]{1,0:T(8,128)(2,1)}) custom-call(bf16[4,512,256]{2,1,0:T(8,128)(2,1)} %all-to-all-done.1.head_ref, bf16[3,512,256]{2,1,0:T(8,128)(2,1)S(1)} %copy-done.18, bf16[3,1024,256]{2,1,0:T(8,128)(2,1)S(1)} %copy-done.5, bf16[512,1024]{1,0:T(8,128)(2,1)S(1)} %copy-done, ...), custom_call_target="tpu_custom_call" | custom-call | flops 1024 | bytes 1024 | tf_op jit(solution)/shard_map/attend_back/pallas_call | solution.py:541
  107.9 2.0 qkv_part.1
  110.8 2.5 %collective-permute-done.10.refs_0_ = bf16[384,1024]{1,0:T(8,128)(2,1)S(1)} collective-permute-done((bf16[384,1024]{1,0:T(8,128)(2,1)}, bf16[384,1024]{1,0:T(8,128)(2,1)S(1)}, u32[]{:S(2)}, u32[]{:S(2)}) %collective-permute-start.10) | collective-permute-done | bytes 786464 | tf_op jit(solution)/shard_map/ppermute | solution.py:22
  115.5 4.3 %all-to-all-done.2.terms_ref = bf16[4,128,1024]{2,1,0:T(8,128)(2,1)} async-done(((bf16[4,128,1024]{2,1,0:T(8,128)(2,1)}), bf16[4,128,1024]{2,1,0:T(8,128)(2,1)}, u32[]{:S(2)}, u32[]{:S(2)}) %all-to-all-start.2) | async-done | bytes 1048608 | tf_op jit(solution)/shard_map/all_to_all | solution.py:26
  119.8 3.8 %all-to-all-start.3 = ((bf16[4,128,1024]{2,1,0:T(8,128)(2,1)}), bf16[4,128,1024]{2,1,0:T(8,128)(2,1)S(1)}, u32[]{:S(2)}, u32[]{:S(2)}) async-start(bf16[4,128,1024]{2,1,0:T(8,128)(2,1)} %bitcast.6), calls=%async_computation.3 | async-start | bytes 2097152 | tf_op jit(solution)/shard_map/all_to_all | solution.py:26
  123.6 1.6 collective-permute-start.13
  125.2 1.5 collective-permute-start.14
  126.7 2.6 %finish_rows.1 = (bf16[128,1024]{1,0:T(8,128)(2,1)}, f32[128,1]{1,0:T(8,128)}, f32[4,1024]{1,0:T(4,128)}) custom-call(s32[1]{0:T(128)} %bitcast.1.mine_ref.refs_1_.part_ref, bf16[4,128,1024]{2,1,0:T(8,128)(2,1)} %all-to-all-done.2.terms_ref, bf16[512,1024]{1,0:T(8,128)(2,1)} %pick_rows.1.refs_0_.picked_ref.refs_8_, f32[512,1]{1,0:T(8,128)} %get-tuple-element.242.gating_ref, ...), custom_call_target="tpu_custom_call" | custom-call | flops 1024 | bytes 30000000 | tf_op jit(solution)/shard_map/finish_rows/pallas_call | solution.py:950
  129.4 6.0 %collective-permute-done.13.a_got = bf16[192,1024]{1,0:T(8,128)(2,1)S(1)} collective-permute-done((bf16[192,1024]{1,0:T(8,128)(2,1)}, bf16[192,1024]{1,0:T(8,128)(2,1)S(1)}, u32[]{:S(2)}, u32[]{:S(2)}) %collective-permute-start.13) | collective-permute-done | bytes 393248 | tf_op jit(solution)/shard_map/ppermute | solution.py:22
  139.9 1.5 collective-permute-start.16
  142.5 1.3 core_sums.1
  145.3 1.6 collective-permute-done.15.refs_1_
  148.5 4.1 %all-to-all-start.4 = ((bf16[4,168,1024]{2,1,0:T(8,128)(2,1)}), bf16[4,168,1024]{2,1,0:T(8,128)(2,1)S(1)}, u32[]{:S(2)}, u32[]{:S(2)}) async-start(bf16[4,168,1024]{2,1,0:T(8,128)(2,1)} %copy-done.9), calls=%async_computation.4 | async-start | bytes 2752512 | tf_op jit(solution)/shard_map/all_to_all | solution.py:26
  152.6 1.5 collective-permute-start.17
  161.9 3.7 %merge_rows.3.old_ref = bf16[4096,1024]{1,0:T(8,128)(2,1)} custom-call(s32[1]{0:T(128)} %bitcast.1.mine_ref.refs_1_.part_ref, bf16[4096,1024]{1,0:T(8,128)(2,1)} %base_ref.9, s32[1,512]{1,0:T(1,128)S(1)} %copy-done.37, bf16[4,128,1024]{2,1,0:T(8,128)(2,1)} %finish_input.1.piece_ref), custom_call_target="tpu_custom_call" | custom-call | flops 1024 | bytes 1024 | tf_op jit(solution)/shard_map/merge_rows/pallas_call | solution.py:232
  167.2 1.5 collective-permute-start.25
  171.2 8.0 %spread_rows.1 = (f32[1024,1024]{1,0:T(8,128)}, f32[1024,1024]{1,0:T(8,128)}) custom-call(s32[1]{0:T(128)} %bitcast.refs_0_.part_ref, bf16[256,1024]{1,0:T(8,128)(2,1)} %copy-done.22, bf16[256,1024]{1,0:T(8,128)(2,1)} %copy-done.24, bf16[256,1024]{1,0:T(8,128)(2,1)} %copy-done.47, bf16[256,1024]{1,0:T(8,128)(2,1)} %copy-done.49, ...), custom_call_target="tpu_custom_call" | custom-call | flops 1024 | bytes 1024 | tf_op jit(solution)/shard_map/spread_rows/pallas_call | solution.py:585
  179.2 5.2 %all-to-all-done.4.got_ref.piece_ref = bf16[4,168,1024]{2,1,0:T(8,128)(2,1)S(1)} async-done(((bf16[4,168,1024]{2,1,0:T(8,128)(2,1)}), bf16[4,168,1024]{2,1,0:T(8,128)(2,1)S(1)}, u32[]{:S(2)}, u32[]{:S(2)}) %all-to-all-start.4) | async-done | bytes 1376288 | tf_op jit(solution)/shard_map/all_to_all | solution.py:26
  184.4 3.5 %all-to-all-start.5 = ((bf16[4,128,1024]{2,1,0:T(8,128)(2,1)}), bf16[4,128,1024]{2,1,0:T(8,128)(2,1)S(1)}, u32[]{:S(2)}, u32[]{:S(2)}) async-start(bf16[4,128,1024]{2,1,0:T(8,128)(2,1)} %finish_input.1.piece_ref), calls=%async_computation.5 | async-start | bytes 2097152 | tf_op jit(solution)/shard_map/all_to_all | solution.py:26
  188.0 1.3 lane_sums.1
  189.3 1.6 collective-permute-start.29
  190.8 1.5 collective-permute-start.30
  192.9 4.3 %merge_rows.4.rest_0_ = bf16[4096,1024]{1,0:T(8,128)(2,1)} custom-call(s32[1]{0:T(128)} %bitcast.1.mine_ref.refs_1_.part_ref, bf16[4096,1024]{1,0:T(8,128)(2,1)} %base_ref.10, s32[1,512]{1,0:T(1,128)S(1)} %copy-done.37, bf16[4,168,1024]{2,1,0:T(8,128)(2,1)S(1)} %all-to-all-done.4.got_ref.piece_ref), custom_call_target="tpu_custom_call" | custom-call | flops 1024 | bytes 1024 | tf_op jit(solution)/shard_map/merge_rows/pallas_call | solution.py:232
  197.2 6.5 %hold_rows.1.base_ref = bf16[3,1024,1024]{2,1,0:T(8,128)(2,1)} custom-call(s32[1]{0:T(128)} %bitcast.1.mine_ref.refs_1_.part_ref, bf16[4096,1024]{1,0:T(8,128)(2,1)} %base_ref.9), custom_call_target="tpu_custom_call" | custom-call | flops 1024 | bytes 1024 | tf_op jit(solution)/shard_map/hold_rows/pallas_call | solution.py:251
  204.6 1.5 collective-permute-start.31
  206.6 4.3 %merge_rows.5 = bf16[4096,1024]{1,0:T(8,128)(2,1)} custom-call(s32[1]{0:T(128)} %bitcast.1.mine_ref.refs_1_.part_ref, bf16[4096,1024]{1,0:T(8,128)(2,1)} %base_ref.10, s32[1,512]{1,0:T(1,128)S(1)} %copy-done.37, bf16[4,168,1024]{2,1,0:T(8,128)(2,1)S(1)} %all-to-all-done.4.got_ref.piece_ref, ...), custom_call_target="tpu_custom_call", output_to_operand_aliasing={{}: (4, {})} | custom-call | flops 1024 | bytes 1024 | tf_op jit(solution)/shard_map/merge_rows/pallas_call | solution.py:232
  211.5 2.1 spread_qkv.1
  214.8 2.8 %copy-done.1 = bf16[3,1024,1024]{2,1,0:T(8,128)(2,1)S(1)} copy-done((bf16[3,1024,1024]{2,1,0:T(8,128)(2,1)S(1)}, bf16[3,1024,1024]{2,1,0:T(8,128)(2,1)}, u32[]{:S(2)}) %copy-start.1) | copy-done | bytes 6291480
  217.5 4.0 %merge_held.1 = bf16[4096,1024]{1,0:T(8,128)(2,1)} custom-call(s32[1]{0:T(128)} %bitcast.1.mine_ref.refs_1_.part_ref, bf16[3,1024,1024]{2,1,0:T(8,128)(2,1)S(1)} %copy-done.1, s32[1,512]{1,0:T(1,128)S(1)} %copy-done.37, bf16[4,128,1024]{2,1,0:T(8,128)(2,1)S(1)} %all-to-all-done.5.piece_ref, ...), custom_call_target="tpu_custom_call", output_to_operand_aliasing={{}: (4, {})} | custom-call | flops 1024 | bytes 1024 | tf_op jit(solution)/shard_map/merge_held/pallas_call | solution.py:299
  (184 shorter events, 47.0 us)
Async XLA Ops:
  1.6 18.7 %collective-permute-start.2 = (bf16[64,1024]{1,0:T(8,128)(2,1)S(1)}, bf16[64,1024]{1,0:T(8,128)(2,1)S(1)}, u32[]{:S(2)}, u32[]{:S(2)}) collective-permute-start(bf16[64,1024]{1,0:T(8,128)(2,1)S(1)} %constant_dynamic-slice_fusion), channel_id=1, source_target_pairs={{0,3},{1,2},{2,1},{3,0},{4,7},{5,6},{6,5},{7,4},{8,11},{9,10},{10,... | collective-permute-start | bytes 393224 | tf_op jit(solution)/shard_map/ppermute | solution.py:22
  6.7 13.5 %collective-permute-start.1 = (bf16[64,1024]{1,0:T(8,128)(2,1)S(1)}, bf16[64,1024]{1,0:T(8,128)(2,1)S(1)}, u32[]{:S(2)}, u32[]{:S(2)}) collective-permute-start(bf16[64,1024]{1,0:T(8,128)(2,1)S(1)} %constant_dynamic-slice_fusion), channel_id=1, source_target_pairs={{0,2},{1,3},{2,0},{3,1},{4,6},{5,7},{6,4},{7,5},{8,10},{9,11},{10,... | collective-permute-start | bytes 393224 | tf_op jit(solution)/shard_map/ppermute | solution.py:22
  6.7 13.6 %collective-permute-start = (bf16[64,1024]{1,0:T(8,128)(2,1)S(1)}, bf16[64,1024]{1,0:T(8,128)(2,1)S(1)}, u32[]{:S(2)}, u32[]{:S(2)}) collective-permute-start(bf16[64,1024]{1,0:T(8,128)(2,1)S(1)} %constant_dynamic-slice_fusion), channel_id=1, source_target_pairs={{0,1},{1,0},{2,3},{3,2},{4,5},{5,4},{6,7},{7,6},{8,9},{9,8},{10,11... | collective-permute-start | bytes 393224 | tf_op jit(solution)/shard_map/ppermute | solution.py:22
  20.3 29.9 %all-to-all-start = ((bf16[4,512,256]{2,1,0:T(8,128)(2,1)}), bf16[4,512,256]{2,1,0:T(8,128)(2,1)S(1)}, u32[]{:S(2)}, u32[]{:S(2)}) async-start(bf16[4,512,256]{2,1,0:T(8,128)(2,1)} %get-tuple-element.175), calls=%async_computation | async-start | bytes 2097152 | tf_op jit(solution)/shard_map/all_to_all | solution.py:26
  25.4 7.6 %collective-permute-start.4 = (bf16[3,64,1024]{2,1,0:T(8,128)(2,1)S(1)}, bf16[3,64,1024]{2,1,0:T(8,128)(2,1)S(1)}, u32[]{:S(2)}, u32[]{:S(2)}) collective-permute-start(bf16[3,64,1024]{2,1,0:T(8,128)(2,1)S(1)} %pad_maximum_fusion.refs_4_), channel_id=1, source_target_pairs={{0,4},{4,0},{8,12},{12,8},{16,20},{20,16},{24,28},{28,24},{1,5},{5... | collective-permute-start | bytes 1179656 | tf_op jit(solution)/shard_map/ppermute | solution.py:22
  25.4 11.5 %collective-permute-start.3 = (bf16[3,64,1024]{2,1,0:T(8,128)(2,1)S(1)}, bf16[3,64,1024]{2,1,0:T(8,128)(2,1)S(1)}, u32[]{:S(2)}, u32[]{:S(2)}) collective-permute-start(bf16[3,64,1024]{2,1,0:T(8,128)(2,1)S(1)} %pad_maximum_fusion.refs_4_), channel_id=1, source_target_pairs={{0,8},{4,12},{8,0},{12,4},{16,24},{20,28},{24,16},{28,20},{1,9},{5... | collective-permute-start | bytes 1179656 | tf_op jit(solution)/shard_map/ppermute | solution.py:22
  37.0 9.1 %collective-permute-start.5 = (bf16[3,64,1024]{2,1,0:T(8,128)(2,1)S(1)}, bf16[3,64,1024]{2,1,0:T(8,128)(2,1)S(1)}, u32[]{:S(2)}, u32[]{:S(2)}) collective-permute-start(bf16[3,64,1024]{2,1,0:T(8,128)(2,1)S(1)} %collective-permute-done.3.refs_6_), channel_id=1, source_target_pairs={{0,4},{4,0},{8,12},{12,8},{16,20},{20,16},{24,28},{28,24},{1,5},{5... | collective-permute-start | bytes 1179656 | tf_op jit(solution)/shard_map/ppermute | solution.py:22
  60.7 29.6 %all-to-all-start.1 = ((bf16[4,512,256]{2,1,0:T(8,128)(2,1)}), bf16[4,512,256]{2,1,0:T(8,128)(2,1)}, u32[]{:S(2)}, u32[]{:S(2)}) async-start(bf16[4,512,256]{2,1,0:T(8,128)(2,1)} %get-tuple-element.196), calls=%async_computation.1 | async-start | bytes 2097152 | tf_op jit(solution)/shard_map/all_to_all | solution.py:26
  75.2 5.7 %collective-permute-start.6 = (bf16[512,1024]{1,0:T(8,128)(2,1)S(1)}, bf16[512,1024]{1,0:T(8,128)(2,1)S(1)}, u32[]{:S(2)}, u32[]{:S(2)}) collective-permute-start(bf16[512,1024]{1,0:T(8,128)(2,1)S(1)} %get-tuple-element.201), channel_id=1, source_target_pairs={{0,4},{4,0},{8,12},{12,8},{16,20},{20,16},{24,28},{28,24},{1,5},{5... | collective-permute-start | bytes 3145736 | tf_op jit(solution)/shard_map/ppermute | solution.py:22
  75.3 5.7 %collective-permute-start.7 = (bf16[512,1024]{1,0:T(8,128)(2,1)S(1)}, bf16[512,1024]{1,0:T(8,128)(2,1)S(1)}, u32[]{:S(2)}, u32[]{:S(2)}) collective-permute-start(bf16[512,1024]{1,0:T(8,128)(2,1)S(1)} %get-tuple-element.202), channel_id=1, source_target_pairs={{0,4},{4,0},{8,12},{12,8},{16,20},{20,16},{24,28},{28,24},{1,5},{5... | collective-permute-start | bytes 3145736 | tf_op jit(solution)/shard_map/ppermute | solution.py:22
  75.8 4.4 %collective-permute-start.8 = (bf16[256,1024]{1,0:T(8,128)(2,1)S(1)}, bf16[256,1024]{1,0:T(8,128)(2,1)S(1)}, u32[]{:S(2)}, u32[]{:S(2)}) collective-permute-start(bf16[256,1024]{1,0:T(8,128)(2,1)S(1)} %get-tuple-element.203), channel_id=1, source_target_pairs={{0,4},{4,0},{8,12},{12,8},{16,20},{20,16},{24,28},{28,24},{1,5},{5... | collective-permute-start | bytes 1572872 | tf_op jit(solution)/shard_map/ppermute | solution.py:22
  75.9 5.1 %collective-permute-start.9 = (bf16[256,1024]{1,0:T(8,128)(2,1)S(1)}, bf16[256,1024]{1,0:T(8,128)(2,1)S(1)}, u32[]{:S(2)}, u32[]{:S(2)}) collective-permute-start(bf16[256,1024]{1,0:T(8,128)(2,1)S(1)} %get-tuple-element.204), channel_id=1, source_target_pairs={{0,4},{4,0},{8,12},{12,8},{16,20},{20,16},{24,28},{28,24},{1,5},{5... | collective-permute-start | bytes 1572872 | tf_op jit(solution)/shard_map/ppermute | solution.py:22
  80.9 16.7 %copy-start = (bf16[512,1024]{1,0:T(8,128)(2,1)S(1)}, bf16[512,1024]{1,0:T(8,128)(2,1)}, u32[]{:S(2)}) copy-start(bf16[512,1024]{1,0:T(8,128)(2,1)} %pick_rows.1.refs_0_.picked_ref.refs_8_) | copy-start | bytes 3145732
  80.9 16.7 %copy-start.5 = (bf16[3,1024,256]{2,1,0:T(8,128)(2,1)S(1)}, bf16[3,1024,256]{2,1,0:T(8,128)(2,1)}, u32[]{:S(2)}) copy-start(bf16[3,1024,256]{2,1,0:T(8,128)(2,1)} %weight_ref.1) | copy-start | bytes 4718596
  90.3 29.5 %all-to-all-start.2 = ((bf16[4,128,1024]{2,1,0:T(8,128)(2,1)}), bf16[4,128,1024]{2,1,0:T(8,128)(2,1)}, u32[]{:S(2)}, u32[]{:S(2)}) async-start(bf16[4,128,1024]{2,1,0:T(8,128)(2,1)} %bitcast.14), calls=%async_computation.2 | async-start | bytes 2097152 | tf_op jit(solution)/shard_map/all_to_all | solution.py:26
  94.5 18.8 %collective-permute-start.10 = (bf16[384,1024]{1,0:T(8,128)(2,1)}, bf16[384,1024]{1,0:T(8,128)(2,1)S(1)}, u32[]{:S(2)}, u32[]{:S(2)}) collective-permute-start(bf16[384,1024]{1,0:T(8,128)(2,1)} %copy-done.44), channel_id=1, source_target_pairs={{0,8},{4,12},{8,0},{12,4},{16,24},{20,28},{24,16},{28,20},{1,9},{5... | collective-permute-start | bytes 2359304 | tf_op jit(solution)/shard_map/ppermute | solution.py:22
  96.1 18.4 %collective-permute-start.11 = (bf16[384,1024]{1,0:T(8,128)(2,1)}, bf16[384,1024]{1,0:T(8,128)(2,1)S(1)}, u32[]{:S(2)}, u32[]{:S(2)}) collective-permute-start(bf16[384,1024]{1,0:T(8,128)(2,1)} %copy-done.43), channel_id=1, source_target_pairs={{0,16},{4,20},{8,24},{12,28},{16,0},{20,4},{24,8},{28,12},{1,17},{... | collective-permute-start | bytes 2359304 | tf_op jit(solution)/shard_map/ppermute | solution.py:22
  119.8 28.7 %all-to-all-start.3 = ((bf16[4,128,1024]{2,1,0:T(8,128)(2,1)}), bf16[4,128,1024]{2,1,0:T(8,128)(2,1)S(1)}, u32[]{:S(2)}, u32[]{:S(2)}) async-start(bf16[4,128,1024]{2,1,0:T(8,128)(2,1)} %bitcast.6), calls=%async_computation.3 | async-start | bytes 2097152 | tf_op jit(solution)/shard_map/all_to_all | solution.py:26
  123.6 17.8 %collective-permute-start.12 = (bf16[384,1024]{1,0:T(8,128)(2,1)}, bf16[384,1024]{1,0:T(8,128)(2,1)}, u32[]{:S(2)}, u32[]{:S(2)}) collective-permute-start(bf16[384,1024]{1,0:T(8,128)(2,1)} %get-tuple-element.237), channel_id=1, source_target_pairs={{0,4},{4,0},{8,12},{12,8},{16,20},{20,16},{24,28},{28,24},{1,5},{5... | collective-permute-start | bytes 2359304 | tf_op jit(solution)/shard_map/ppermute | solution.py:22
  123.6 11.7 %collective-permute-start.13 = (bf16[192,1024]{1,0:T(8,128)(2,1)}, bf16[192,1024]{1,0:T(8,128)(2,1)S(1)}, u32[]{:S(2)}, u32[]{:S(2)}) collective-permute-start(bf16[192,1024]{1,0:T(8,128)(2,1)} %get-tuple-element.239), channel_id=1, source_target_pairs={{0,16},{4,20},{8,24},{12,28},{16,0},{20,4},{24,8},{28,12},{1,17},{... | collective-permute-start | bytes 1179656 | tf_op jit(solution)/shard_map/ppermute | solution.py:22
  125.2 11.2 %collective-permute-start.14 = (bf16[192,1024]{1,0:T(8,128)(2,1)S(1)}, bf16[192,1024]{1,0:T(8,128)(2,1)S(1)}, u32[]{:S(2)}, u32[]{:S(2)}) collective-permute-start(bf16[192,1024]{1,0:T(8,128)(2,1)S(1)} %get-tuple-element.240), channel_id=1, source_target_pairs={{0,8},{4,12},{8,0},{12,4},{16,24},{20,28},{24,16},{28,20},{1,9},{5... | collective-permute-start | bytes 1179656 | tf_op jit(solution)/shard_map/ppermute | solution.py:22
  138.1 22.5 %copy-start.38 = (bf16[1,1024]{1,0:T(2,128)(2,1)S(1)}, bf16[1,1024]{1,0:T(2,128)(2,1)}, u32[]{:S(2)}) copy-start(bf16[1,1024]{1,0:T(2,128)(2,1)} %broadcast_in_dim.11.router_ref) | copy-start | bytes 6148
  138.1 22.5 %copy-start.39 = (f32[128,1]{1,0:T(8,128)S(1)}, f32[128,1]{1,0:T(8,128)}, u32[]{:S(2)}) copy-start(f32[128,1]{1,0:T(8,128)} %get-tuple-element.263.score_ref) | copy-start | bytes 1540
  139.4 21.2 %copy-start.2 = (bf16[512,1024]{1,0:T(8,128)(2,1)S(1)}, bf16[512,1024]{1,0:T(8,128)(2,1)}, u32[]{:S(2)}) copy-start(bf16[512,1024]{1,0:T(8,128)(2,1)} %pick_only.1.rows_ref) | copy-start | bytes 3145732
  139.4 7.5 %collective-permute-start.15 = (bf16[128,1024]{1,0:T(8,128)(2,1)S(1)}, bf16[128,1024]{1,0:T(8,128)(2,1)S(1)}, u32[]{:S(2)}, u32[]{:S(2)}) collective-permute-start(bf16[128,1024]{1,0:T(8,128)(2,1)S(1)} %get-tuple-element.265.refs_0_), channel_id=1, source_target_pairs={{0,16},{4,20},{8,24},{12,28},{16,0},{20,4},{24,8},{28,12},{1,17},{... | collective-permute-start | bytes 786440 | tf_op jit(solution)/shard_map/ppermute | solution.py:22
  139.9 7.7 %collective-permute-start.16 = (bf16[128,1024]{1,0:T(8,128)(2,1)S(1)}, bf16[128,1024]{1,0:T(8,128)(2,1)}, u32[]{:S(2)}, u32[]{:S(2)}) collective-permute-start(bf16[128,1024]{1,0:T(8,128)(2,1)S(1)} %get-tuple-element.267.refs_2_), channel_id=1, source_target_pairs={{0,8},{4,12},{8,0},{12,4},{16,24},{20,28},{24,16},{28,20},{1,9},{5... | collective-permute-start | bytes 786440 | tf_op jit(solution)/shard_map/ppermute | solution.py:22
  148.5 35.9 %all-to-all-start.4 = ((bf16[4,168,1024]{2,1,0:T(8,128)(2,1)}), bf16[4,168,1024]{2,1,0:T(8,128)(2,1)S(1)}, u32[]{:S(2)}, u32[]{:S(2)}) async-start(bf16[4,168,1024]{2,1,0:T(8,128)(2,1)} %copy-done.9), calls=%async_computation.4 | async-start | bytes 2752512 | tf_op jit(solution)/shard_map/all_to_all | solution.py:26
  152.6 13.0 %collective-permute-start.17 = (bf16[128,1024]{1,0:T(8,128)(2,1)}, bf16[128,1024]{1,0:T(8,128)(2,1)S(1)}, u32[]{:S(2)}, u32[]{:S(2)}) collective-permute-start(bf16[128,1024]{1,0:T(8,128)(2,1)} %copy-done.35), channel_id=1, source_target_pairs={{0,8},{4,12},{8,0},{12,4},{16,24},{20,28},{24,16},{28,20},{1,9},{5... | collective-permute-start | bytes 786440 | tf_op jit(solution)/shard_map/ppermute | solution.py:22
  154.1 12.0 %collective-permute-start.19 = (bf16[128,1024]{1,0:T(8,128)(2,1)}, bf16[128,1024]{1,0:T(8,128)(2,1)S(1)}, u32[]{:S(2)}, u32[]{:S(2)}) collective-permute-start(bf16[128,1024]{1,0:T(8,128)(2,1)} %copy-done.31), channel_id=1, source_target_pairs={{0,16},{4,20},{8,24},{12,28},{16,0},{20,4},{24,8},{28,12},{1,17},{... | collective-permute-start | bytes 786440 | tf_op jit(solution)/shard_map/ppermute | solution.py:22
  155.3 10.9 %collective-permute-start.18 = (bf16[128,1024]{1,0:T(8,128)(2,1)}, bf16[128,1024]{1,0:T(8,128)(2,1)S(1)}, u32[]{:S(2)}, u32[]{:S(2)}) collective-permute-start(bf16[128,1024]{1,0:T(8,128)(2,1)} %copy-done.33), channel_id=1, source_target_pairs={{0,8},{4,12},{8,0},{12,4},{16,24},{20,28},{24,16},{28,20},{1,9},{5... | collective-permute-start | bytes 786440 | tf_op jit(solution)/shard_map/ppermute | solution.py:22
  155.8 10.7 %collective-permute-start.20 = (bf16[128,1024]{1,0:T(8,128)(2,1)}, bf16[128,1024]{1,0:T(8,128)(2,1)S(1)}, u32[]{:S(2)}, u32[]{:S(2)}) collective-permute-start(bf16[128,1024]{1,0:T(8,128)(2,1)} %collective-permute-done.16.refs_3_), channel_id=1, source_target_pairs={{0,16},{4,20},{8,24},{12,28},{16,0},{20,4},{24,8},{28,12},{1,17},{... | collective-permute-start | bytes 786440 | tf_op jit(solution)/shard_map/ppermute | solution.py:22
  160.5 8.2 %collective-permute-start.21 = (bf16[256,1024]{1,0:T(8,128)(2,1)S(1)}, bf16[256,1024]{1,0:T(8,128)(2,1)S(1)}, u32[]{:S(2)}, u32[]{:S(2)}) collective-permute-start(bf16[256,1024]{1,0:T(8,128)(2,1)S(1)} %get-tuple-element.269.refs_0_), channel_id=1, source_target_pairs={{0,4},{4,0},{8,12},{12,8},{16,20},{20,16},{24,28},{28,24},{1,5},{5... | collective-permute-start | bytes 1572872 | tf_op jit(solution)/shard_map/ppermute | solution.py:22
  165.6 4.0 %collective-permute-start.23 = (bf16[256,1024]{1,0:T(8,128)(2,1)S(1)}, bf16[256,1024]{1,0:T(8,128)(2,1)S(1)}, u32[]{:S(2)}, u32[]{:S(2)}) collective-permute-start(bf16[256,1024]{1,0:T(8,128)(2,1)S(1)} %get-tuple-element.278.refs_4_), channel_id=1, source_target_pairs={{0,4},{4,0},{8,12},{12,8},{16,20},{20,16},{24,28},{28,24},{1,5},{5... | collective-permute-start | bytes 1572872 | tf_op jit(solution)/shard_map/ppermute | solution.py:22
  166.6 2.9 %collective-permute-start.22 = (bf16[256,1024]{1,0:T(8,128)(2,1)S(1)}, bf16[256,1024]{1,0:T(8,128)(2,1)S(1)}, u32[]{:S(2)}, u32[]{:S(2)}) collective-permute-start(bf16[256,1024]{1,0:T(8,128)(2,1)S(1)} %get-tuple-element.277.refs_1_), channel_id=1, source_target_pairs={{0,4},{4,0},{8,12},{12,8},{16,20},{20,16},{24,28},{28,24},{1,5},{5... | collective-permute-start | bytes 1572872 | tf_op jit(solution)/shard_map/ppermute | solution.py:22
  166.7 4.4 %collective-permute-start.24 = (bf16[256,1024]{1,0:T(8,128)(2,1)S(1)}, bf16[256,1024]{1,0:T(8,128)(2,1)}, u32[]{:S(2)}, u32[]{:S(2)}) collective-permute-start(bf16[256,1024]{1,0:T(8,128)(2,1)S(1)} %get-tuple-element.279.refs_5_), channel_id=1, source_target_pairs={{0,4},{4,0},{8,12},{12,8},{16,20},{20,16},{24,28},{28,24},{1,5},{5... | collective-permute-start | bytes 1572872 | tf_op jit(solution)/shard_map/ppermute | solution.py:22
  167.2 20.8 %collective-permute-start.25 = (bf16[192,1024]{1,0:T(8,128)(2,1)S(1)}, bf16[192,1024]{1,0:T(8,128)(2,1)}, u32[]{:S(2)}, u32[]{:S(2)}) collective-permute-start(bf16[192,1024]{1,0:T(8,128)(2,1)S(1)} %copy-done.27), channel_id=1, source_target_pairs={{0,16},{4,20},{8,24},{12,28},{16,0},{20,4},{24,8},{28,12},{1,17},{... | collective-permute-start | bytes 1179656 | tf_op jit(solution)/shard_map/ppermute | solution.py:22
  168.7 19.2 %collective-permute-start.26 = (bf16[192,1024]{1,0:T(8,128)(2,1)S(1)}, bf16[192,1024]{1,0:T(8,128)(2,1)}, u32[]{:S(2)}, u32[]{:S(2)}) collective-permute-start(bf16[192,1024]{1,0:T(8,128)(2,1)S(1)} %copy-done.29), channel_id=1, source_target_pairs={{0,8},{4,12},{8,0},{12,4},{16,24},{20,28},{24,16},{28,20},{1,9},{5... | collective-permute-start | bytes 1179656 | tf_op jit(solution)/shard_map/ppermute | solution.py:22
  184.4 30.4 %all-to-all-start.5 = ((bf16[4,128,1024]{2,1,0:T(8,128)(2,1)}), bf16[4,128,1024]{2,1,0:T(8,128)(2,1)S(1)}, u32[]{:S(2)}, u32[]{:S(2)}) async-start(bf16[4,128,1024]{2,1,0:T(8,128)(2,1)} %finish_input.1.piece_ref), calls=%async_computation.5 | async-start | bytes 2097152 | tf_op jit(solution)/shard_map/all_to_all | solution.py:26
  189.3 14.4 %collective-permute-start.29 = (bf16[192,1024]{1,0:T(8,128)(2,1)S(1)}, bf16[192,1024]{1,0:T(8,128)(2,1)S(1)}, u32[]{:S(2)}, u32[]{:S(2)}) collective-permute-start(bf16[192,1024]{1,0:T(8,128)(2,1)S(1)} %get-tuple-element.297.a_ref), channel_id=1, source_target_pairs={{0,8},{4,12},{8,0},{12,4},{16,24},{20,28},{24,16},{28,20},{1,9},{5... | collective-permute-start | bytes 1179656 | tf_op jit(solution)/shard_map/ppermute | solution.py:22
  190.8 12.9 %collective-permute-start.30 = (bf16[192,1024]{1,0:T(8,128)(2,1)S(1)}, bf16[192,1024]{1,0:T(8,128)(2,1)S(1)}, u32[]{:S(2)}, u32[]{:S(2)}) collective-permute-start(bf16[192,1024]{1,0:T(8,128)(2,1)S(1)} %get-tuple-element.299.b_ref), channel_id=1, source_target_pairs={{0,16},{4,20},{8,24},{12,28},{16,0},{20,4},{24,8},{28,12},{1,17},{... | collective-permute-start | bytes 1179656 | tf_op jit(solution)/shard_map/ppermute | solution.py:22
  192.4 11.3 %collective-permute-start.28 = (bf16[40,1024]{1,0:T(8,128)(2,1)S(1)}, bf16[40,1024]{1,0:T(8,128)(2,1)S(1)}, u32[]{:S(2)}, u32[]{:S(2)}) collective-permute-start(bf16[40,1024]{1,0:T(8,128)(2,1)S(1)} %first_small.1.refs_0_), channel_id=1, source_target_pairs={{0,8},{4,12},{8,0},{12,4},{16,24},{20,28},{24,16},{28,20},{1,9},{5... | collective-permute-start | bytes 245768 | tf_op jit(solution)/shard_map/ppermute | solution.py:22
  203.9 7.0 %collective-permute-start.32 = (bf16[384,1024]{1,0:T(8,128)(2,1)S(1)}, bf16[384,1024]{1,0:T(8,128)(2,1)S(1)}, u32[]{:S(2)}, u32[]{:S(2)}) collective-permute-start(bf16[384,1024]{1,0:T(8,128)(2,1)S(1)} %joined_lanes.1.near_ref), channel_id=1, source_target_pairs={{0,4},{4,0},{8,12},{12,8},{16,20},{20,16},{24,28},{28,24},{1,5},{5... | collective-permute-start | bytes 2359304 | tf_op jit(solution)/shard_map/ppermute | solution.py:22
  204.0 6.9 %collective-permute-start.27 = (bf16[40,1024]{1,0:T(8,128)(2,1)S(1)}, bf16[40,1024]{1,0:T(8,128)(2,1)S(1)}, u32[]{:S(2)}, u32[]{:S(2)}) collective-permute-start(bf16[40,1024]{1,0:T(8,128)(2,1)S(1)} %first_small.1.refs_0_), channel_id=1, source_target_pairs={{0,16},{4,20},{8,24},{12,28},{16,0},{20,4},{24,8},{28,12},{1,17},{... | collective-permute-start | bytes 245768 | tf_op jit(solution)/shard_map/ppermute | solution.py:22
  204.6 6.4 %collective-permute-start.31 = (bf16[40,1024]{1,0:T(8,128)(2,1)S(1)}, bf16[40,1024]{1,0:T(8,128)(2,1)S(1)}, u32[]{:S(2)}, u32[]{:S(2)}) collective-permute-start(bf16[40,1024]{1,0:T(8,128)(2,1)S(1)} %collective-permute-done.28.refs_1_), channel_id=1, source_target_pairs={{0,16},{4,20},{8,24},{12,28},{16,0},{20,4},{24,8},{28,12},{1,17},{... | collective-permute-start | bytes 245768 | tf_op jit(solution)/shard_map/ppermute | solution.py:22
  206.1 7.6 %collective-permute-start.33 = (bf16[40,1024]{1,0:T(8,128)(2,1)S(1)}, bf16[40,1024]{1,0:T(8,128)(2,1)S(1)}, u32[]{:S(2)}, u32[]{:S(2)}) collective-permute-start(bf16[40,1024]{1,0:T(8,128)(2,1)S(1)} %first_small.1.refs_0_), channel_id=1, source_target_pairs={{0,4},{4,0},{8,12},{12,8},{16,20},{20,16},{24,28},{28,24},{1,5},{5... | collective-permute-start | bytes 245768 | tf_op jit(solution)/shard_map/ppermute | solution.py:22
  206.1 7.6 %collective-permute-start.34 = (bf16[40,1024]{1,0:T(8,128)(2,1)S(1)}, bf16[40,1024]{1,0:T(8,128)(2,1)S(1)}, u32[]{:S(2)}, u32[]{:S(2)}) collective-permute-start(bf16[40,1024]{1,0:T(8,128)(2,1)S(1)} %collective-permute-done.28.refs_1_), channel_id=1, source_target_pairs={{0,4},{4,0},{8,12},{12,8},{16,20},{20,16},{24,28},{28,24},{1,5},{5... | collective-permute-start | bytes 245768 | tf_op jit(solution)/shard_map/ppermute | solution.py:22
  210.9 2.7 %collective-permute-start.35 = (bf16[40,1024]{1,0:T(8,128)(2,1)S(1)}, bf16[40,1024]{1,0:T(8,128)(2,1)S(1)}, u32[]{:S(2)}, u32[]{:S(2)}) collective-permute-start(bf16[40,1024]{1,0:T(8,128)(2,1)S(1)} %collective-permute-done.27.refs_2_), channel_id=1, source_target_pairs={{0,4},{4,0},{8,12},{12,8},{16,20},{20,16},{24,28},{28,24},{1,5},{5... | collective-permute-start | bytes 245768 | tf_op jit(solution)/shard_map/ppermute | solution.py:22
  211.0 2.7 %collective-permute-start.36 = (bf16[40,1024]{1,0:T(8,128)(2,1)S(1)}, bf16[40,1024]{1,0:T(8,128)(2,1)S(1)}, u32[]{:S(2)}, u32[]{:S(2)}) collective-permute-start(bf16[40,1024]{1,0:T(8,128)(2,1)S(1)} %collective-permute-done.31.refs_3_), channel_id=1, source_target_pairs={{0,4},{4,0},{8,12},{12,8},{16,20},{20,16},{24,28},{28,24},{1,5},{5... | collective-permute-start | bytes 245768 | tf_op jit(solution)/shard_map/ppermute | solution.py:22
  (51 other events, 220.8 us)

commit v8 on v6

--- a/solution.py
+++ b/solution.py
@@ -297,7 +297,7 @@
 def feed_forward(heads, own_weight, quarters, picked, gain, up, grad_act, grad_mixer, part, mine, ways):
     rows, width = picked.shape
     hidden = up.shape[1]
-    sub = min(512, hidden)
+    sub = min(1024, hidden)
     count, _, heads_width = heads.shape
     piece = heads_width // 4
     own = rows // ways

time: 224 us -> 223 us (level)
  no operation moved by 1% of the time
where the time goes in v8:
time: 223 us; the launch traced here: 222 us
  Pallas kernels  90.5 us (41%)
  starting transfers between devices  58.1 us (26%)
  waiting for transfers between devices  44.3 us (20%)
  local copies, waits for them, and re-layouts  25.4 us (11%)
  matrix products  2.23 us (1%)
    ppermute x37, starting transfers between devices, swap(): return lax.ppermute(values, axis, [(i, i ^ bits) for i in range(size)])  31.4 us
    all_to_all x6, starting transfers between devices, to_all(): return lax.all_to_all(blocks, 'tensor', 0, 0, tiled=True)  26.7 us
    ppermute x37, waiting for transfers between devices, swap(): return lax.ppermute(values, axis, [(i, i ^ bits) for i in range(size)])  26.4 us
    unnamed x106, local copies, waits for them, and re-layouts  22.7 us
    pallas_call x4, Pallas kernels, merge_rows(): pl.pallas_call(kernel, grid_spec=grid_spec, out_shape=jax.ShapeDtypeStruc...  19.9 us
    all_to_all x6, waiting for transfers between devices, to_all(): return lax.all_to_all(blocks, 'tensor', 0, 0, tiled=True)  17.9 us
    pallas_call x2, Pallas kernels, staged(): pl.pallas_call(kernel, in_specs=[pl.BlockSpec(memory_space=pltpu.SMEM)] *...  16 us
    pallas_call x1, Pallas kernels, spread_rows(): pl.pallas_call(kernel, grid_spec=pltpu.PrefetchScalarGridSpec(num_scalar_...  7.99 us
  transfers between devices with their start and end apart: 43, of which 15 were waited for; matrix products, arithmetic and copies ran while one was open for 2% of the time, Pallas kernels for 33%

profile of v8, /device:TPU:0, one launch (start us, length us, event | category | flops | bytes accessed | tf_op | source)
XLA Modules:
  0.0 221.7 jit_solution(16377694888437892793)
XLA Ops:
  1.6 5.1 %collective-permute-start.2 = (bf16[64,1024]{1,0:T(8,128)(2,1)S(1)}, bf16[64,1024]{1,0:T(8,128)(2,1)S(1)}, u32[]{:S(2)}, u32[]{:S(2)}) collective-permute-start(bf16[64,1024]{1,0:T(8,128)(2,1)S(1)} %constant_dynamic-slice_fusion), channel_id=1, source_target_pairs={{0,3},{1,2},{2,1},{3,0},{4,7},{5,6},{6,5},{7,4},{8,11},{9,10},{10,... | collective-permute-start | bytes 393224 | tf_op jit(solution)/shard_map/ppermute | solution.py:22
  7.3 5.7 %pick_rows.1.refs_0_.picked_ref.refs_8_ = bf16[512,1024]{1,0:T(8,128)(2,1)} custom-call(bf16[4096,1024]{1,0:T(8,128)(2,1)} %base_ref.9, s32[1,512]{1,0:T(1,128)} %offset_ref.11), custom_call_target="tpu_custom_call" | custom-call | flops 1024 | bytes 1024 | tf_op jit(solution)/shard_map/pick_rows/pallas_call | solution.py:133
  13.7 6.6 %attend.1 = (bf16[512,1024]{1,0:T(8,128)(2,1)}, bf16[3,512,256]{2,1,0:T(8,128)(2,1)}, bf16[4,512,256]{2,1,0:T(8,128)(2,1)}, bf16[4,256,256]{2,1,0:T(8,128)(2,1)}, bf16[4,256,512]{2,1,0:T(8,128)(2,1)}) custom-call(bf16[512,1024]{1,0:T(8,128)(2,1)} %pick_rows.1.refs_0_.picked_ref.refs_8_, bf16[1,1024]{1,0:T(2,128)(2,1)} %broadcast_in_dim.10.refs_1_.gain_ref, ...), custom_call_target="tpu_custom_call" | custom-call | flops 1024 | bytes 1024 | tf_op jit(solution)/shard_map/attend/pallas_call | solution.py:86
  20.3 5.0 %all-to-all-start = ((bf16[4,512,256]{2,1,0:T(8,128)(2,1)}), bf16[4,512,256]{2,1,0:T(8,128)(2,1)S(1)}, u32[]{:S(2)}, u32[]{:S(2)}) async-start(bf16[4,512,256]{2,1,0:T(8,128)(2,1)} %get-tuple-element.171), calls=%async_computation | async-start | bytes 2097152 | tf_op jit(solution)/shard_map/all_to_all | solution.py:26
  25.4 1.6 collective-permute-start.3
  27.0 6.0 %pick_only.1.rows_ref = bf16[512,1024]{1,0:T(8,128)(2,1)} custom-call(bf16[4096,1024]{1,0:T(8,128)(2,1)} %base_ref.10, s32[1,512]{1,0:T(1,128)} %offset_ref.11), custom_call_target="tpu_custom_call" | custom-call | flops 1024 | bytes 1024 | tf_op jit(solution)/shard_map/pick_only/pallas_call | solution.py:186
  33.0 4.0 %collective-permute-done.3.refs_6_ = bf16[3,64,1024]{2,1,0:T(8,128)(2,1)S(1)} collective-permute-done((bf16[3,64,1024]{2,1,0:T(8,128)(2,1)S(1)}, bf16[3,64,1024]{2,1,0:T(8,128)(2,1)S(1)}, u32[]{:S(2)}, u32[]{:S(2)}) %collective-permute-start.3) | collective-permute-done | bytes 393248 | tf_op jit(solution)/shard_map/ppermute | solution.py:22
  37.6 2.6 %score_sums.1.square_ref = f32[1,128]{1,0:T(1,128)} custom-call(s32[1]{0:T(128)} %bitcast.1.mine_ref.refs_1_.part_ref, bf16[4096,1024]{1,0:T(8,128)(2,1)} %base_ref.9, bf16[1,1024]{1,0:T(2,128)(2,1)} %broadcast_in_dim.11.router_ref), custom_call_target="tpu_custom_call" | custom-call | flops 1024 | bytes 1024 | tf_op jit(solution)/shard_map/score_sums/pallas_call | solution.py:153
  40.9 5.1 %act_grads.1 = (f32[512,1]{1,0:T(8,128)}, f32[1,128]{1,0:T(1,128)}, bf16[512,1024]{1,0:T(8,128)(2,1)}, f32[512,1024]{1,0:T(8,128)}) custom-call(bf16[512,1024]{1,0:T(8,128)(2,1)} %pick_rows.1.refs_0_.picked_ref.refs_8_, bf16[1,1024]{1,0:T(2,128)(2,1)} %broadcast_in_dim.11.router_ref, bf16[512,1024]{1,0:T(8,128)(2,1)} %pick_only.1.rows_ref, ...), custom_call_target="tpu_custom_call" | custom-call | flops 1024 | bytes 1024 | tf_op jit(solution)/shard_map/act_grads/pallas_call | solution.py:397
  46.0 4.2 %all-to-all-done.refs_2_.heads_ref = bf16[4,512,256]{2,1,0:T(8,128)(2,1)S(1)} async-done(((bf16[4,512,256]{2,1,0:T(8,128)(2,1)}), bf16[4,512,256]{2,1,0:T(8,128)(2,1)S(1)}, u32[]{:S(2)}, u32[]{:S(2)}) %all-to-all-start) | async-done | bytes 1048608 | tf_op jit(solution)/shard_map/all_to_all | solution.py:26
  51.1 9.5 %feed_forward.1 = (f32[128,1024]{1,0:T(8,128)}, bf16[512,1024]{1,0:T(8,128)(2,1)}, bf16[512,1024]{1,0:T(8,128)(2,1)}, bf16[512,1024]{1,0:T(8,128)(2,1)}, bf16[51...) custom-call(s32[1]{0:T(128)} %bitcast.refs_0_.part_ref, ...), custom_call_target="tpu_custom_call" | custom-call | flops 1024 | bytes 1024 | tf_op jit(solution)/shard_map/feed_forward/pallas_call | solution.py:86
  60.6 4.6 %all-to-all-start.1 = ((bf16[4,512,256]{2,1,0:T(8,128)(2,1)}), bf16[4,512,256]{2,1,0:T(8,128)(2,1)}, u32[]{:S(2)}, u32[]{:S(2)}) async-start(bf16[4,512,256]{2,1,0:T(8,128)(2,1)} %get-tuple-element.192), calls=%async_computation.1 | async-start | bytes 2097152 | tf_op jit(solution)/shard_map/all_to_all | solution.py:26
  70.2 3.9 %core_grads.1 = (bf16[2,768,1024]{2,1,0:T(8,128)(2,1)S(1)}, bf16[512,1024]{1,0:T(8,128)(2,1)S(1)}, bf16[512,1024]{1,0:T(8,128)(2,1)S(1)}, bf16[256,1024]{1,0:T(8,128)(2,1)S(1)}, bf16[256,1024]{1,0:T(8,128)(2,1)S(1)}) custom-call(s32[1]{0:T(128)} %bitcast.refs_0_.part_ref, bf16[512,1024]{1,0:T(8,128)(2,1)S(1)} %copy-done.10, bf16[512,1024]{1,0:T(8,128)(2,1)S(1)} %copy-done.6, ...), custom_call_target="tpu_custom_call" | custom-call | flops 1024 | bytes 1024 | tf_op jit(solution)/shard_map/core_grads/pallas_call | solution.py:622
  75.1 2.2 %convolution_convert_fusion = bf16[512,1024]{1,0:T(8,128)(2,1)} fusion(bf16[512,1024]{1,0:T(8,128)(2,1)S(1)} %copy-done.11, bf16[1024,1024]{1,0:T(8,128)(2,1)S(1)} %copy-done.43), kind=kOutput, calls=%fused_computation | convolution fusion | flops 1074266112 | bytes 4194304 | tf_op jit(solution)/shard_map/dot_general | solution.py:17
  77.4 1.6 collective-permute-done.8.refs_1_
  83.6 6.8 %all-to-all-done.1.head_ref = bf16[4,512,256]{2,1,0:T(8,128)(2,1)} async-done(((bf16[4,512,256]{2,1,0:T(8,128)(2,1)}), bf16[4,512,256]{2,1,0:T(8,128)(2,1)}, u32[]{:S(2)}, u32[]{:S(2)}) %all-to-all-start.1) | async-done | bytes 1048608 | tf_op jit(solution)/shard_map/all_to_all | solution.py:26
  90.3 4.2 %all-to-all-start.2 = ((bf16[4,128,1024]{2,1,0:T(8,128)(2,1)}), bf16[4,128,1024]{2,1,0:T(8,128)(2,1)}, u32[]{:S(2)}, u32[]{:S(2)}) async-start(bf16[4,128,1024]{2,1,0:T(8,128)(2,1)} %bitcast.14), calls=%async_computation.2 | async-start | bytes 2097152 | tf_op jit(solution)/shard_map/all_to_all | solution.py:26
  94.6 1.6 collective-permute-start.10
  96.1 1.5 collective-permute-start.11
  101.1 6.7 %attend_back.1 = (bf16[3,512,256]{2,1,0:T(8,128)(2,1)S(1)}, f32[1,1024]{1,0:T(1,128)S(1)}, bf16[512,1024]{1,0:T(8,128)(2,1)}) custom-call(bf16[4,512,256]{2,1,0:T(8,128)(2,1)} %all-to-all-done.1.head_ref, bf16[3,512,256]{2,1,0:T(8,128)(2,1)S(1)} %copy-done.18, bf16[3,1024,256]{2,1,0:T(8,128)(2,1)S(1)} %copy-done.5, bf16[512,1024]{1,0:T(8,128)(2,1)S(1)} %copy-done, ...), custom_call_target="tpu_custom_call" | custom-call | flops 1024 | bytes 1024 | tf_op jit(solution)/shard_map/attend_back/pallas_call | solution.py:473
  109.9 3.4 %collective-permute-done.10.refs_0_ = bf16[384,1024]{1,0:T(8,128)(2,1)S(1)} collective-permute-done((bf16[384,1024]{1,0:T(8,128)(2,1)}, bf16[384,1024]{1,0:T(8,128)(2,1)S(1)}, u32[]{:S(2)}, u32[]{:S(2)}) %collective-permute-start.10) | collective-permute-done | bytes 786464 | tf_op jit(solution)/shard_map/ppermute | solution.py:22
  116.4 3.4 %all-to-all-done.2.terms_ref = bf16[4,128,1024]{2,1,0:T(8,128)(2,1)} async-done(((bf16[4,128,1024]{2,1,0:T(8,128)(2,1)}), bf16[4,128,1024]{2,1,0:T(8,128)(2,1)}, u32[]{:S(2)}, u32[]{:S(2)}) %all-to-all-start.2) | async-done | bytes 1048608 | tf_op jit(solution)/shard_map/all_to_all | solution.py:26
  119.8 3.8 %all-to-all-start.3 = ((bf16[4,128,1024]{2,1,0:T(8,128)(2,1)}), bf16[4,128,1024]{2,1,0:T(8,128)(2,1)S(1)}, u32[]{:S(2)}, u32[]{:S(2)}) async-start(bf16[4,128,1024]{2,1,0:T(8,128)(2,1)} %bitcast.6), calls=%async_computation.3 | async-start | bytes 2097152 | tf_op jit(solution)/shard_map/all_to_all | solution.py:26
  123.7 1.6 collective-permute-start.13
  125.3 1.5 collective-permute-start.14
  126.8 2.6 %finish_rows.1 = (bf16[128,1024]{1,0:T(8,128)(2,1)}, f32[128,1]{1,0:T(8,128)}, f32[4,1024]{1,0:T(4,128)}) custom-call(s32[1]{0:T(128)} %bitcast.1.mine_ref.refs_1_.part_ref, bf16[4,128,1024]{2,1,0:T(8,128)(2,1)} %all-to-all-done.2.terms_ref, bf16[512,1024]{1,0:T(8,128)(2,1)} %pick_rows.1.refs_0_.picked_ref.refs_8_, f32[512,1]{1,0:T(8,128)} %get-tuple-element.238.gating_ref, ...), custom_call_target="tpu_custom_call" | custom-call | flops 1024 | bytes 30000000 | tf_op jit(solution)/shard_map/finish_rows/pallas_call | solution.py:882
  129.4 6.0 %collective-permute-done.13.a_got = bf16[192,1024]{1,0:T(8,128)(2,1)S(1)} collective-permute-done((bf16[192,1024]{1,0:T(8,128)(2,1)}, bf16[192,1024]{1,0:T(8,128)(2,1)S(1)}, u32[]{:S(2)}, u32[]{:S(2)}) %collective-permute-start.13) | collective-permute-done | bytes 393248 | tf_op jit(solution)/shard_map/ppermute | solution.py:22
  135.4 1.3 collective-permute-done.14.b_got
  141.3 1.5 collective-permute-start.16
  144.8 3.6 %collective-permute-done.15.refs_1_ = bf16[128,1024]{1,0:T(8,128)(2,1)} collective-permute-done((bf16[128,1024]{1,0:T(8,128)(2,1)S(1)}, bf16[128,1024]{1,0:T(8,128)(2,1)}, u32[]{:S(2)}, u32[]{:S(2)}) %collective-permute-start.15) | collective-permute-done | bytes 262176 | tf_op jit(solution)/shard_map/ppermute | solution.py:22
  148.7 4.8 %all-to-all-start.4 = ((bf16[4,168,1024]{2,1,0:T(8,128)(2,1)}), bf16[4,168,1024]{2,1,0:T(8,128)(2,1)S(1)}, u32[]{:S(2)}, u32[]{:S(2)}) async-start(bf16[4,168,1024]{2,1,0:T(8,128)(2,1)} %copy-done.9), calls=%async_computation.4 | async-start | bytes 2752512 | tf_op jit(solution)/shard_map/all_to_all | solution.py:26
  153.5 1.5 collective-permute-start.17
  155.0 1.4 collective-permute-start.19
  159.5 1.9 gather_blocks.2
  163.4 3.7 %merge_rows.4.rest_0_ = bf16[4096,1024]{1,0:T(8,128)(2,1)} custom-call(s32[1]{0:T(128)} %bitcast.1.mine_ref.refs_1_.part_ref, bf16[4096,1024]{1,0:T(8,128)(2,1)} %base_ref.10, s32[1,512]{1,0:T(1,128)} %offset_ref.11, bf16[4,128,1024]{2,1,0:T(8,128)(2,1)} %finish_input.1.piece_ref), custom_call_target="tpu_custom_call" | custom-call | flops 1024 | bytes 1024 | tf_op jit(solution)/shard_map/merge_rows/pallas_call | solution.py:232
  169.5 1.4 collective-permute-start.25
  170.9 1.5 collective-permute-start.26
  174.0 8.0 %spread_rows.1 = (f32[1024,1024]{1,0:T(8,128)}, f32[1024,1024]{1,0:T(8,128)}) custom-call(s32[1]{0:T(128)} %bitcast.refs_0_.part_ref, bf16[256,1024]{1,0:T(8,128)(2,1)} %get-tuple-element.265.refs_0_, bf16[256,1024]{1,0:T(8,128)(2,1)} %copy-done.22, bf16[256,1024]{1,0:T(8,128)(2,1)} %collective-permute-done.21.refs_2_, bf16[256,1024]{1,0:T(8,128)(2,1)} %copy-done.46, ...), custom_call_target="tpu_custom_call" | custom-call | flops 1024 | bytes 1024 | tf_op jit(solution)/shard_map/spread_rows/pallas_call | solution.py:517
  182.0 2.7 %all-to-all-done.4.got_ref.piece_ref = bf16[4,168,1024]{2,1,0:T(8,128)(2,1)S(1)} async-done(((bf16[4,168,1024]{2,1,0:T(8,128)(2,1)}), bf16[4,168,1024]{2,1,0:T(8,128)(2,1)S(1)}, u32[]{:S(2)}, u32[]{:S(2)}) %all-to-all-start.4) | async-done | bytes 1376288 | tf_op jit(solution)/shard_map/all_to_all | solution.py:26
  184.7 4.3 %all-to-all-start.5 = ((bf16[4,128,1024]{2,1,0:T(8,128)(2,1)}), bf16[4,128,1024]{2,1,0:T(8,128)(2,1)}, u32[]{:S(2)}, u32[]{:S(2)}) async-start(bf16[4,128,1024]{2,1,0:T(8,128)(2,1)} %finish_input.1.piece_ref), calls=%async_computation.5 | async-start | bytes 2097152 | tf_op jit(solution)/shard_map/all_to_all | solution.py:26
  190.4 1.6 collective-permute-start.29
  192.0 1.3 collective-permute-start.30
  193.8 4.4 %merge_rows.5.rest_0_ = bf16[4096,1024]{1,0:T(8,128)(2,1)} custom-call(s32[1]{0:T(128)} %bitcast.1.mine_ref.refs_1_.part_ref, bf16[4096,1024]{1,0:T(8,128)(2,1)} %base_ref.9, s32[1,512]{1,0:T(1,128)} %offset_ref.11, bf16[4,168,1024]{2,1,0:T(8,128)(2,1)} %copy-done.1), custom_call_target="tpu_custom_call" | custom-call | flops 1024 | bytes 1024 | tf_op jit(solution)/shard_map/merge_rows/pallas_call | solution.py:232
  198.2 4.1 %collective-permute-done.28.refs_1_ = bf16[40,1024]{1,0:T(8,128)(2,1)S(1)} collective-permute-done((bf16[40,1024]{1,0:T(8,128)(2,1)S(1)}, bf16[40,1024]{1,0:T(8,128)(2,1)S(1)}, u32[]{:S(2)}, u32[]{:S(2)}) %collective-permute-start.28) | collective-permute-done | bytes 81952 | tf_op jit(solution)/shard_map/ppermute | solution.py:22
  202.6 1.4 collective-permute-start.27
  205.2 4.4 %merge_rows.6 = bf16[4096,1024]{1,0:T(8,128)(2,1)} custom-call(s32[1]{0:T(128)} %bitcast.1.mine_ref.refs_1_.part_ref, bf16[4096,1024]{1,0:T(8,128)(2,1)} %base_ref.9, s32[1,512]{1,0:T(1,128)} %offset_ref.11, bf16[4,168,1024]{2,1,0:T(8,128)(2,1)} %copy-done.1, bf16[4096,1024]{1,0:T(8,128)(2,1)} %merge_rows.5.rest_0_), custom_call_target="tpu_custom_call", output_to_operand_aliasing={{}: (4, {})} | custom-call | flops 1024 | bytes 1024 | tf_op jit(solution)/shard_map/merge_rows/pallas_call | solution.py:232
  210.2 2.1 spread_qkv.1
  214.3 7.5 %merge_rows.7 = bf16[4096,1024]{1,0:T(8,128)(2,1)} custom-call(s32[1]{0:T(128)} %bitcast.1.mine_ref.refs_1_.part_ref, bf16[4096,1024]{1,0:T(8,128)(2,1)} %base_ref.10, s32[1,512]{1,0:T(1,128)} %offset_ref.11, bf16[4,128,1024]{2,1,0:T(8,128)(2,1)} %all-to-all-done.5.piece_ref, bf16[4096,1024]{1,0:T(8,128)(2,1)} %merge_rows.4.rest_0_), custom_call_target="tpu_custom_call", output_to_operand_aliasing={{}: (4, {})} | custom-call | flops 1024 | bytes 1024 | tf_op jit(solution)/shard_map/merge_rows/pallas_call | solution.py:232
  (177 shorter events, 45.5 us)
Async XLA Ops:
  1.6 18.7 %collective-permute-start.2 = (bf16[64,1024]{1,0:T(8,128)(2,1)S(1)}, bf16[64,1024]{1,0:T(8,128)(2,1)S(1)}, u32[]{:S(2)}, u32[]{:S(2)}) collective-permute-start(bf16[64,1024]{1,0:T(8,128)(2,1)S(1)} %constant_dynamic-slice_fusion), channel_id=1, source_target_pairs={{0,3},{1,2},{2,1},{3,0},{4,7},{5,6},{6,5},{7,4},{8,11},{9,10},{10,... | collective-permute-start | bytes 393224 | tf_op jit(solution)/shard_map/ppermute | solution.py:22
  6.7 13.5 %collective-permute-start.1 = (bf16[64,1024]{1,0:T(8,128)(2,1)S(1)}, bf16[64,1024]{1,0:T(8,128)(2,1)S(1)}, u32[]{:S(2)}, u32[]{:S(2)}) collective-permute-start(bf16[64,1024]{1,0:T(8,128)(2,1)S(1)} %constant_dynamic-slice_fusion), channel_id=1, source_target_pairs={{0,2},{1,3},{2,0},{3,1},{4,6},{5,7},{6,4},{7,5},{8,10},{9,11},{10,... | collective-permute-start | bytes 393224 | tf_op jit(solution)/shard_map/ppermute | solution.py:22
  6.7 13.6 %collective-permute-start = (bf16[64,1024]{1,0:T(8,128)(2,1)S(1)}, bf16[64,1024]{1,0:T(8,128)(2,1)S(1)}, u32[]{:S(2)}, u32[]{:S(2)}) collective-permute-start(bf16[64,1024]{1,0:T(8,128)(2,1)S(1)} %constant_dynamic-slice_fusion), channel_id=1, source_target_pairs={{0,1},{1,0},{2,3},{3,2},{4,5},{5,4},{6,7},{7,6},{8,9},{9,8},{10,11... | collective-permute-start | bytes 393224 | tf_op jit(solution)/shard_map/ppermute | solution.py:22
  20.3 29.9 %all-to-all-start = ((bf16[4,512,256]{2,1,0:T(8,128)(2,1)}), bf16[4,512,256]{2,1,0:T(8,128)(2,1)S(1)}, u32[]{:S(2)}, u32[]{:S(2)}) async-start(bf16[4,512,256]{2,1,0:T(8,128)(2,1)} %get-tuple-element.171), calls=%async_computation | async-start | bytes 2097152 | tf_op jit(solution)/shard_map/all_to_all | solution.py:26
  25.4 7.6 %collective-permute-start.4 = (bf16[3,64,1024]{2,1,0:T(8,128)(2,1)S(1)}, bf16[3,64,1024]{2,1,0:T(8,128)(2,1)S(1)}, u32[]{:S(2)}, u32[]{:S(2)}) collective-permute-start(bf16[3,64,1024]{2,1,0:T(8,128)(2,1)S(1)} %pad_maximum_fusion.refs_4_), channel_id=1, source_target_pairs={{0,4},{4,0},{8,12},{12,8},{16,20},{20,16},{24,28},{28,24},{1,5},{5... | collective-permute-start | bytes 1179656 | tf_op jit(solution)/shard_map/ppermute | solution.py:22
  25.4 11.5 %collective-permute-start.3 = (bf16[3,64,1024]{2,1,0:T(8,128)(2,1)S(1)}, bf16[3,64,1024]{2,1,0:T(8,128)(2,1)S(1)}, u32[]{:S(2)}, u32[]{:S(2)}) collective-permute-start(bf16[3,64,1024]{2,1,0:T(8,128)(2,1)S(1)} %pad_maximum_fusion.refs_4_), channel_id=1, source_target_pairs={{0,8},{4,12},{8,0},{12,4},{16,24},{20,28},{24,16},{28,20},{1,9},{5... | collective-permute-start | bytes 1179656 | tf_op jit(solution)/shard_map/ppermute | solution.py:22
  37.0 9.0 %collective-permute-start.5 = (bf16[3,64,1024]{2,1,0:T(8,128)(2,1)S(1)}, bf16[3,64,1024]{2,1,0:T(8,128)(2,1)S(1)}, u32[]{:S(2)}, u32[]{:S(2)}) collective-permute-start(bf16[3,64,1024]{2,1,0:T(8,128)(2,1)S(1)} %collective-permute-done.3.refs_6_), channel_id=1, source_target_pairs={{0,4},{4,0},{8,12},{12,8},{16,20},{20,16},{24,28},{28,24},{1,5},{5... | collective-permute-start | bytes 1179656 | tf_op jit(solution)/shard_map/ppermute | solution.py:22
  60.6 29.7 %all-to-all-start.1 = ((bf16[4,512,256]{2,1,0:T(8,128)(2,1)}), bf16[4,512,256]{2,1,0:T(8,128)(2,1)}, u32[]{:S(2)}, u32[]{:S(2)}) async-start(bf16[4,512,256]{2,1,0:T(8,128)(2,1)} %get-tuple-element.192), calls=%async_computation.1 | async-start | bytes 2097152 | tf_op jit(solution)/shard_map/all_to_all | solution.py:26
  74.1 5.7 %collective-permute-start.6 = (bf16[512,1024]{1,0:T(8,128)(2,1)S(1)}, bf16[512,1024]{1,0:T(8,128)(2,1)S(1)}, u32[]{:S(2)}, u32[]{:S(2)}) collective-permute-start(bf16[512,1024]{1,0:T(8,128)(2,1)S(1)} %get-tuple-element.197), channel_id=1, source_target_pairs={{0,4},{4,0},{8,12},{12,8},{16,20},{20,16},{24,28},{28,24},{1,5},{5... | collective-permute-start | bytes 3145736 | tf_op jit(solution)/shard_map/ppermute | solution.py:22
  74.1 5.7 %collective-permute-start.7 = (bf16[512,1024]{1,0:T(8,128)(2,1)S(1)}, bf16[512,1024]{1,0:T(8,128)(2,1)S(1)}, u32[]{:S(2)}, u32[]{:S(2)}) collective-permute-start(bf16[512,1024]{1,0:T(8,128)(2,1)S(1)} %get-tuple-element.198), channel_id=1, source_target_pairs={{0,4},{4,0},{8,12},{12,8},{16,20},{20,16},{24,28},{28,24},{1,5},{5... | collective-permute-start | bytes 3145736 | tf_op jit(solution)/shard_map/ppermute | solution.py:22
  74.6 4.4 %collective-permute-start.8 = (bf16[256,1024]{1,0:T(8,128)(2,1)S(1)}, bf16[256,1024]{1,0:T(8,128)(2,1)S(1)}, u32[]{:S(2)}, u32[]{:S(2)}) collective-permute-start(bf16[256,1024]{1,0:T(8,128)(2,1)S(1)} %get-tuple-element.199), channel_id=1, source_target_pairs={{0,4},{4,0},{8,12},{12,8},{16,20},{20,16},{24,28},{28,24},{1,5},{5... | collective-permute-start | bytes 1572872 | tf_op jit(solution)/shard_map/ppermute | solution.py:22
  74.7 5.1 %collective-permute-start.9 = (bf16[256,1024]{1,0:T(8,128)(2,1)S(1)}, bf16[256,1024]{1,0:T(8,128)(2,1)S(1)}, u32[]{:S(2)}, u32[]{:S(2)}) collective-permute-start(bf16[256,1024]{1,0:T(8,128)(2,1)S(1)} %get-tuple-element.200), channel_id=1, source_target_pairs={{0,4},{4,0},{8,12},{12,8},{16,20},{20,16},{24,28},{28,24},{1,5},{5... | collective-permute-start | bytes 1572872 | tf_op jit(solution)/shard_map/ppermute | solution.py:22
  79.8 17.9 %copy-start.5 = (bf16[3,1024,256]{2,1,0:T(8,128)(2,1)S(1)}, bf16[3,1024,256]{2,1,0:T(8,128)(2,1)}, u32[]{:S(2)}) copy-start(bf16[3,1024,256]{2,1,0:T(8,128)(2,1)} %weight_ref.1) | copy-start | bytes 4718596
  83.6 14.1 %copy-start.35 = (bf16[1,1024]{1,0:T(2,128)(2,1)S(1)}, bf16[1,1024]{1,0:T(2,128)(2,1)}, u32[]{:S(2)}) copy-start(bf16[1,1024]{1,0:T(2,128)(2,1)} %broadcast_in_dim.10.refs_1_.gain_ref) | copy-start | bytes 6148
  90.3 29.5 %all-to-all-start.2 = ((bf16[4,128,1024]{2,1,0:T(8,128)(2,1)}), bf16[4,128,1024]{2,1,0:T(8,128)(2,1)}, u32[]{:S(2)}, u32[]{:S(2)}) async-start(bf16[4,128,1024]{2,1,0:T(8,128)(2,1)} %bitcast.14), calls=%async_computation.2 | async-start | bytes 2097152 | tf_op jit(solution)/shard_map/all_to_all | solution.py:26
  94.6 18.8 %collective-permute-start.10 = (bf16[384,1024]{1,0:T(8,128)(2,1)}, bf16[384,1024]{1,0:T(8,128)(2,1)S(1)}, u32[]{:S(2)}, u32[]{:S(2)}) collective-permute-start(bf16[384,1024]{1,0:T(8,128)(2,1)} %copy-done.40), channel_id=1, source_target_pairs={{0,8},{4,12},{8,0},{12,4},{16,24},{20,28},{24,16},{28,20},{1,9},{5... | collective-permute-start | bytes 2359304 | tf_op jit(solution)/shard_map/ppermute | solution.py:22
  96.1 18.4 %collective-permute-start.11 = (bf16[384,1024]{1,0:T(8,128)(2,1)}, bf16[384,1024]{1,0:T(8,128)(2,1)S(1)}, u32[]{:S(2)}, u32[]{:S(2)}) collective-permute-start(bf16[384,1024]{1,0:T(8,128)(2,1)} %copy-done.39), channel_id=1, source_target_pairs={{0,16},{4,20},{8,24},{12,28},{16,0},{20,4},{24,8},{28,12},{1,17},{... | collective-permute-start | bytes 2359304 | tf_op jit(solution)/shard_map/ppermute | solution.py:22
  119.8 28.9 %all-to-all-start.3 = ((bf16[4,128,1024]{2,1,0:T(8,128)(2,1)}), bf16[4,128,1024]{2,1,0:T(8,128)(2,1)S(1)}, u32[]{:S(2)}, u32[]{:S(2)}) async-start(bf16[4,128,1024]{2,1,0:T(8,128)(2,1)} %bitcast.6), calls=%async_computation.3 | async-start | bytes 2097152 | tf_op jit(solution)/shard_map/all_to_all | solution.py:26
  123.6 19.1 %collective-permute-start.12 = (bf16[384,1024]{1,0:T(8,128)(2,1)}, bf16[384,1024]{1,0:T(8,128)(2,1)}, u32[]{:S(2)}, u32[]{:S(2)}) collective-permute-start(bf16[384,1024]{1,0:T(8,128)(2,1)} %copy-done.38), channel_id=1, source_target_pairs={{0,4},{4,0},{8,12},{12,8},{16,20},{20,16},{24,28},{28,24},{1,5},{5... | collective-permute-start | bytes 2359304 | tf_op jit(solution)/shard_map/ppermute | solution.py:22
  123.7 11.7 %collective-permute-start.13 = (bf16[192,1024]{1,0:T(8,128)(2,1)}, bf16[192,1024]{1,0:T(8,128)(2,1)S(1)}, u32[]{:S(2)}, u32[]{:S(2)}) collective-permute-start(bf16[192,1024]{1,0:T(8,128)(2,1)} %copy-done.42), channel_id=1, source_target_pairs={{0,16},{4,20},{8,24},{12,28},{16,0},{20,4},{24,8},{28,12},{1,17},{... | collective-permute-start | bytes 1179656 | tf_op jit(solution)/shard_map/ppermute | solution.py:22
  125.3 11.5 %collective-permute-start.14 = (bf16[192,1024]{1,0:T(8,128)(2,1)}, bf16[192,1024]{1,0:T(8,128)(2,1)}, u32[]{:S(2)}, u32[]{:S(2)}) collective-permute-start(bf16[192,1024]{1,0:T(8,128)(2,1)} %copy-done.41), channel_id=1, source_target_pairs={{0,8},{4,12},{8,0},{12,4},{16,24},{20,28},{24,16},{28,20},{1,9},{5... | collective-permute-start | bytes 1179656 | tf_op jit(solution)/shard_map/ppermute | solution.py:22
  140.8 7.7 %collective-permute-start.15 = (bf16[128,1024]{1,0:T(8,128)(2,1)S(1)}, bf16[128,1024]{1,0:T(8,128)(2,1)}, u32[]{:S(2)}, u32[]{:S(2)}) collective-permute-start(bf16[128,1024]{1,0:T(8,128)(2,1)S(1)} %get-tuple-element.261.refs_0_), channel_id=1, source_target_pairs={{0,16},{4,20},{8,24},{12,28},{16,0},{20,4},{24,8},{28,12},{1,17},{... | collective-permute-start | bytes 786440 | tf_op jit(solution)/shard_map/ppermute | solution.py:22
  141.3 7.5 %collective-permute-start.16 = (bf16[128,1024]{1,0:T(8,128)(2,1)S(1)}, bf16[128,1024]{1,0:T(8,128)(2,1)}, u32[]{:S(2)}, u32[]{:S(2)}) collective-permute-start(bf16[128,1024]{1,0:T(8,128)(2,1)S(1)} %get-tuple-element.263.refs_2_), channel_id=1, source_target_pairs={{0,8},{4,12},{8,0},{12,4},{16,24},{20,28},{24,16},{28,20},{1,9},{5... | collective-permute-start | bytes 786440 | tf_op jit(solution)/shard_map/ppermute | solution.py:22
  144.8 17.3 %copy-start.2 = (bf16[512,1024]{1,0:T(8,128)(2,1)S(1)}, bf16[512,1024]{1,0:T(8,128)(2,1)}, u32[]{:S(2)}) copy-start(bf16[512,1024]{1,0:T(8,128)(2,1)} %pick_only.1.rows_ref) | copy-start | bytes 3145732
  144.8 17.3 %copy-start.33 = (bf16[1,1024]{1,0:T(2,128)(2,1)S(1)}, bf16[1,1024]{1,0:T(2,128)(2,1)}, u32[]{:S(2)}) copy-start(bf16[1,1024]{1,0:T(2,128)(2,1)} %broadcast_in_dim.11.router_ref) | copy-start | bytes 6148
  144.8 17.3 %copy-start.34 = (f32[128,1]{1,0:T(8,128)S(1)}, f32[128,1]{1,0:T(8,128)}, u32[]{:S(2)}) copy-start(f32[128,1]{1,0:T(8,128)} %get-tuple-element.259.score_ref) | copy-start | bytes 1540
  148.7 36.0 %all-to-all-start.4 = ((bf16[4,168,1024]{2,1,0:T(8,128)(2,1)}), bf16[4,168,1024]{2,1,0:T(8,128)(2,1)S(1)}, u32[]{:S(2)}, u32[]{:S(2)}) async-start(bf16[4,168,1024]{2,1,0:T(8,128)(2,1)} %copy-done.9), calls=%async_computation.4 | async-start | bytes 2752512 | tf_op jit(solution)/shard_map/all_to_all | solution.py:26
  153.5 13.6 %collective-permute-start.17 = (bf16[128,1024]{1,0:T(8,128)(2,1)}, bf16[128,1024]{1,0:T(8,128)(2,1)}, u32[]{:S(2)}, u32[]{:S(2)}) collective-permute-start(bf16[128,1024]{1,0:T(8,128)(2,1)} %copy-done.31), channel_id=1, source_target_pairs={{0,8},{4,12},{8,0},{12,4},{16,24},{20,28},{24,16},{28,20},{1,9},{5... | collective-permute-start | bytes 786440 | tf_op jit(solution)/shard_map/ppermute | solution.py:22
  155.0 12.6 %collective-permute-start.19 = (bf16[128,1024]{1,0:T(8,128)(2,1)}, bf16[128,1024]{1,0:T(8,128)(2,1)}, u32[]{:S(2)}, u32[]{:S(2)}) collective-permute-start(bf16[128,1024]{1,0:T(8,128)(2,1)} %copy-done.29), channel_id=1, source_target_pairs={{0,16},{4,20},{8,24},{12,28},{16,0},{20,4},{24,8},{28,12},{1,17},{... | collective-permute-start | bytes 786440 | tf_op jit(solution)/shard_map/ppermute | solution.py:22
  156.4 11.2 %collective-permute-start.18 = (bf16[128,1024]{1,0:T(8,128)(2,1)}, bf16[128,1024]{1,0:T(8,128)(2,1)}, u32[]{:S(2)}, u32[]{:S(2)}) collective-permute-start(bf16[128,1024]{1,0:T(8,128)(2,1)} %collective-permute-done.15.refs_1_), channel_id=1, source_target_pairs={{0,8},{4,12},{8,0},{12,4},{16,24},{20,28},{24,16},{28,20},{1,9},{5... | collective-permute-start | bytes 786440 | tf_op jit(solution)/shard_map/ppermute | solution.py:22
  157.0 10.6 %collective-permute-start.20 = (bf16[128,1024]{1,0:T(8,128)(2,1)}, bf16[128,1024]{1,0:T(8,128)(2,1)}, u32[]{:S(2)}, u32[]{:S(2)}) collective-permute-start(bf16[128,1024]{1,0:T(8,128)(2,1)} %collective-permute-done.16.refs_3_), channel_id=1, source_target_pairs={{0,16},{4,20},{8,24},{12,28},{16,0},{20,4},{24,8},{28,12},{1,17},{... | collective-permute-start | bytes 786440 | tf_op jit(solution)/shard_map/ppermute | solution.py:22
  162.1 8.8 %collective-permute-start.21 = (bf16[256,1024]{1,0:T(8,128)(2,1)}, bf16[256,1024]{1,0:T(8,128)(2,1)}, u32[]{:S(2)}, u32[]{:S(2)}) collective-permute-start(bf16[256,1024]{1,0:T(8,128)(2,1)} %get-tuple-element.265.refs_0_), channel_id=1, source_target_pairs={{0,4},{4,0},{8,12},{12,8},{16,20},{20,16},{24,28},{28,24},{1,5},{5... | collective-permute-start | bytes 1572872 | tf_op jit(solution)/shard_map/ppermute | solution.py:22
  167.1 5.3 %collective-permute-start.23 = (bf16[256,1024]{1,0:T(8,128)(2,1)S(1)}, bf16[256,1024]{1,0:T(8,128)(2,1)S(1)}, u32[]{:S(2)}, u32[]{:S(2)}) collective-permute-start(bf16[256,1024]{1,0:T(8,128)(2,1)S(1)} %copy-done.21), channel_id=1, source_target_pairs={{0,4},{4,0},{8,12},{12,8},{16,20},{20,16},{24,28},{28,24},{1,5},{5... | collective-permute-start | bytes 1572872 | tf_op jit(solution)/shard_map/ppermute | solution.py:22
  168.9 3.5 %collective-permute-start.22 = (bf16[256,1024]{1,0:T(8,128)(2,1)S(1)}, bf16[256,1024]{1,0:T(8,128)(2,1)S(1)}, u32[]{:S(2)}, u32[]{:S(2)}) collective-permute-start(bf16[256,1024]{1,0:T(8,128)(2,1)S(1)} %get-tuple-element.273.refs_1_), channel_id=1, source_target_pairs={{0,4},{4,0},{8,12},{12,8},{16,20},{20,16},{24,28},{28,24},{1,5},{5... | collective-permute-start | bytes 1572872 | tf_op jit(solution)/shard_map/ppermute | solution.py:22
  169.0 5.0 %collective-permute-start.24 = (bf16[256,1024]{1,0:T(8,128)(2,1)S(1)}, bf16[256,1024]{1,0:T(8,128)(2,1)}, u32[]{:S(2)}, u32[]{:S(2)}) collective-permute-start(bf16[256,1024]{1,0:T(8,128)(2,1)S(1)} %get-tuple-element.275.refs_5_), channel_id=1, source_target_pairs={{0,4},{4,0},{8,12},{12,8},{16,20},{20,16},{24,28},{28,24},{1,5},{5... | collective-permute-start | bytes 1572872 | tf_op jit(solution)/shard_map/ppermute | solution.py:22
  169.5 19.6 %collective-permute-start.25 = (bf16[192,1024]{1,0:T(8,128)(2,1)S(1)}, bf16[192,1024]{1,0:T(8,128)(2,1)}, u32[]{:S(2)}, u32[]{:S(2)}) collective-permute-start(bf16[192,1024]{1,0:T(8,128)(2,1)S(1)} %copy-done.25), channel_id=1, source_target_pairs={{0,16},{4,20},{8,24},{12,28},{16,0},{20,4},{24,8},{28,12},{1,17},{... | collective-permute-start | bytes 1179656 | tf_op jit(solution)/shard_map/ppermute | solution.py:22
  170.9 18.2 %collective-permute-start.26 = (bf16[192,1024]{1,0:T(8,128)(2,1)}, bf16[192,1024]{1,0:T(8,128)(2,1)}, u32[]{:S(2)}, u32[]{:S(2)}) collective-permute-start(bf16[192,1024]{1,0:T(8,128)(2,1)} %copy-done.26), channel_id=1, source_target_pairs={{0,8},{4,12},{8,0},{12,4},{16,24},{20,28},{24,16},{28,20},{1,9},{5... | collective-permute-start | bytes 1179656 | tf_op jit(solution)/shard_map/ppermute | solution.py:22
  184.7 29.5 %all-to-all-start.5 = ((bf16[4,128,1024]{2,1,0:T(8,128)(2,1)}), bf16[4,128,1024]{2,1,0:T(8,128)(2,1)}, u32[]{:S(2)}, u32[]{:S(2)}) async-start(bf16[4,128,1024]{2,1,0:T(8,128)(2,1)} %finish_input.1.piece_ref), calls=%async_computation.5 | async-start | bytes 2097152 | tf_op jit(solution)/shard_map/all_to_all | solution.py:26
  190.4 11.9 %collective-permute-start.29 = (bf16[192,1024]{1,0:T(8,128)(2,1)S(1)}, bf16[192,1024]{1,0:T(8,128)(2,1)S(1)}, u32[]{:S(2)}, u32[]{:S(2)}) collective-permute-start(bf16[192,1024]{1,0:T(8,128)(2,1)S(1)} %get-tuple-element.291.a_ref), channel_id=1, source_target_pairs={{0,8},{4,12},{8,0},{12,4},{16,24},{20,28},{24,16},{28,20},{1,9},{5... | collective-permute-start | bytes 1179656 | tf_op jit(solution)/shard_map/ppermute | solution.py:22
  192.0 10.3 %collective-permute-start.30 = (bf16[192,1024]{1,0:T(8,128)(2,1)S(1)}, bf16[192,1024]{1,0:T(8,128)(2,1)S(1)}, u32[]{:S(2)}, u32[]{:S(2)}) collective-permute-start(bf16[192,1024]{1,0:T(8,128)(2,1)S(1)} %get-tuple-element.293.b_ref), channel_id=1, source_target_pairs={{0,16},{4,20},{8,24},{12,28},{16,0},{20,4},{24,8},{28,12},{1,17},{... | collective-permute-start | bytes 1179656 | tf_op jit(solution)/shard_map/ppermute | solution.py:22
  193.3 9.0 %collective-permute-start.28 = (bf16[40,1024]{1,0:T(8,128)(2,1)S(1)}, bf16[40,1024]{1,0:T(8,128)(2,1)S(1)}, u32[]{:S(2)}, u32[]{:S(2)}) collective-permute-start(bf16[40,1024]{1,0:T(8,128)(2,1)S(1)} %first_small.1.refs_0_), channel_id=1, source_target_pairs={{0,8},{4,12},{8,0},{12,4},{16,24},{20,28},{24,16},{28,20},{1,9},{5... | collective-permute-start | bytes 245768 | tf_op jit(solution)/shard_map/ppermute | solution.py:22
  202.5 7.1 %collective-permute-start.32 = (bf16[384,1024]{1,0:T(8,128)(2,1)S(1)}, bf16[384,1024]{1,0:T(8,128)(2,1)S(1)}, u32[]{:S(2)}, u32[]{:S(2)}) collective-permute-start(bf16[384,1024]{1,0:T(8,128)(2,1)S(1)} %joined_lanes.1.near_ref), channel_id=1, source_target_pairs={{0,4},{4,0},{8,12},{12,8},{16,20},{20,16},{24,28},{28,24},{1,5},{5... | collective-permute-start | bytes 2359304 | tf_op jit(solution)/shard_map/ppermute | solution.py:22
  202.6 7.0 %collective-permute-start.27 = (bf16[40,1024]{1,0:T(8,128)(2,1)S(1)}, bf16[40,1024]{1,0:T(8,128)(2,1)S(1)}, u32[]{:S(2)}, u32[]{:S(2)}) collective-permute-start(bf16[40,1024]{1,0:T(8,128)(2,1)S(1)} %first_small.1.refs_0_), channel_id=1, source_target_pairs={{0,16},{4,20},{8,24},{12,28},{16,0},{20,4},{24,8},{28,12},{1,17},{... | collective-permute-start | bytes 245768 | tf_op jit(solution)/shard_map/ppermute | solution.py:22
  204.0 5.6 %collective-permute-start.31 = (bf16[40,1024]{1,0:T(8,128)(2,1)S(1)}, bf16[40,1024]{1,0:T(8,128)(2,1)S(1)}, u32[]{:S(2)}, u32[]{:S(2)}) collective-permute-start(bf16[40,1024]{1,0:T(8,128)(2,1)S(1)} %collective-permute-done.28.refs_1_), channel_id=1, source_target_pairs={{0,16},{4,20},{8,24},{12,28},{16,0},{20,4},{24,8},{28,12},{1,17},{... | collective-permute-start | bytes 245768 | tf_op jit(solution)/shard_map/ppermute | solution.py:22
  204.7 7.6 %collective-permute-start.33 = (bf16[40,1024]{1,0:T(8,128)(2,1)S(1)}, bf16[40,1024]{1,0:T(8,128)(2,1)S(1)}, u32[]{:S(2)}, u32[]{:S(2)}) collective-permute-start(bf16[40,1024]{1,0:T(8,128)(2,1)S(1)} %first_small.1.refs_0_), channel_id=1, source_target_pairs={{0,4},{4,0},{8,12},{12,8},{16,20},{20,16},{24,28},{28,24},{1,5},{5... | collective-permute-start | bytes 245768 | tf_op jit(solution)/shard_map/ppermute | solution.py:22
  204.7 7.6 %collective-permute-start.34 = (bf16[40,1024]{1,0:T(8,128)(2,1)S(1)}, bf16[40,1024]{1,0:T(8,128)(2,1)S(1)}, u32[]{:S(2)}, u32[]{:S(2)}) collective-permute-start(bf16[40,1024]{1,0:T(8,128)(2,1)S(1)} %collective-permute-done.28.refs_1_), channel_id=1, source_target_pairs={{0,4},{4,0},{8,12},{12,8},{16,20},{20,16},{24,28},{28,24},{1,5},{5... | collective-permute-start | bytes 245768 | tf_op jit(solution)/shard_map/ppermute | solution.py:22
  209.6 2.7 %collective-permute-start.35 = (bf16[40,1024]{1,0:T(8,128)(2,1)S(1)}, bf16[40,1024]{1,0:T(8,128)(2,1)S(1)}, u32[]{:S(2)}, u32[]{:S(2)}) collective-permute-start(bf16[40,1024]{1,0:T(8,128)(2,1)S(1)} %collective-permute-done.27.refs_2_), channel_id=1, source_target_pairs={{0,4},{4,0},{8,12},{12,8},{16,20},{20,16},{24,28},{28,24},{1,5},{5... | collective-permute-start | bytes 245768 | tf_op jit(solution)/shard_map/ppermute | solution.py:22
  209.7 2.7 %collective-permute-start.36 = (bf16[40,1024]{1,0:T(8,128)(2,1)S(1)}, bf16[40,1024]{1,0:T(8,128)(2,1)S(1)}, u32[]{:S(2)}, u32[]{:S(2)}) collective-permute-start(bf16[40,1024]{1,0:T(8,128)(2,1)S(1)} %collective-permute-done.31.refs_3_), channel_id=1, source_target_pairs={{0,4},{4,0},{8,12},{12,8},{16,20},{20,16},{24,28},{28,24},{1,5},{5... | collective-permute-start | bytes 245768 | tf_op jit(solution)/shard_map/ppermute | solution.py:22
  (48 other events, 189.9 us)

commit v9 on v8

--- a/solution.py
+++ b/solution.py
@@ -248,7 +248,7 @@
     def body(load, store, outs, scalars, scratch):
         low_ref, qkv_ref, out_ref, *probs_refs = outs
         values = load(0)[...].astype(F32)
-        low_ref[...] = (values * inverse_rms(values) * load(1)[...].astype(F32)).astype(BF)
+        low_ref[...] = (values * inverse_rms(values) * load(1)[...].astype(F32).reshape(1, width)).astype(BF)
         store(0)
         weight_ref = load(2)
         for n in range(3):
@@ -982,7 +982,7 @@
     here = [swap(piece, "tensor", k) for k in range(1, ways)]
 
     picked = pick_rows(tokens, route_offset, ways)
-    first_low, qkv, head_out, *probs = attend(picked, first_gain[None], qkv_weight, unit_sequence, ways)
+    first_low, qkv, head_out, *probs = attend(picked, first_gain, qkv_weight, unit_sequence, ways)
     here, head_out = tie((here, head_out))
 
     heads = to_all(head_out)

time: 223 us -> 223 us (level)
    unnamed x106 -> x104, local copies, waits for them, and re-layouts: 22.7 us -> 22.6 us
where the time goes in v9:
time: 223 us; the launch traced here: 221 us
  Pallas kernels  90.5 us (41%)
  starting transfers between devices  58.1 us (26%)
  waiting for transfers between devices  44.3 us (20%)
  local copies, waits for them, and re-layouts  24.8 us (11%)
  matrix products  2.23 us (1%)
    ppermute x37, starting transfers between devices, swap(): return lax.ppermute(values, axis, [(i, i ^ bits) for i in range(size)])  31.4 us
    all_to_all x6, starting transfers between devices, to_all(): return lax.all_to_all(blocks, 'tensor', 0, 0, tiled=True)  26.7 us
    ppermute x37, waiting for transfers between devices, swap(): return lax.ppermute(values, axis, [(i, i ^ bits) for i in range(size)])  26.4 us
    unnamed x104, local copies, waits for them, and re-layouts  22.6 us
    pallas_call x4, Pallas kernels, merge_rows(): pl.pallas_call(kernel, grid_spec=grid_spec, out_shape=jax.ShapeDtypeStruc...  19.9 us
    all_to_all x6, waiting for transfers between devices, to_all(): return lax.all_to_all(blocks, 'tensor', 0, 0, tiled=True)  17.9 us
    pallas_call x2, Pallas kernels, staged(): pl.pallas_call(kernel, in_specs=[pl.BlockSpec(memory_space=pltpu.SMEM)] *...  16 us
    pallas_call x1, Pallas kernels, spread_rows(): pl.pallas_call(kernel, grid_spec=pltpu.PrefetchScalarGridSpec(num_scalar_...  7.99 us
  transfers between devices with their start and end apart: 43, of which 15 were waited for; matrix products, arithmetic and copies ran while one was open for 2% of the time, Pallas kernels for 33%

profile of v9, /device:TPU:0, one launch (start us, length us, event | category | flops | bytes accessed | tf_op | source)
XLA Modules:
  0.0 221.1 jit_solution(2177297168604909070)
XLA Ops:
  1.6 5.1 %collective-permute-start.2 = (bf16[64,1024]{1,0:T(8,128)(2,1)S(1)}, bf16[64,1024]{1,0:T(8,128)(2,1)S(1)}, u32[]{:S(2)}, u32[]{:S(2)}) collective-permute-start(bf16[64,1024]{1,0:T(8,128)(2,1)S(1)} %constant_dynamic-slice_fusion), channel_id=1, source_target_pairs={{0,3},{1,2},{2,1},{3,0},{4,7},{5,6},{6,5},{7,4},{8,11},{9,10},{10,... | collective-permute-start | bytes 393224 | tf_op jit(solution)/shard_map/ppermute | solution.py:22
  7.3 5.7 %pick_rows.1.refs_0_.picked_ref.refs_8_ = bf16[512,1024]{1,0:T(8,128)(2,1)} custom-call(bf16[4096,1024]{1,0:T(8,128)(2,1)} %base_ref.9, s32[1,512]{1,0:T(1,128)} %offset_ref.11), custom_call_target="tpu_custom_call" | custom-call | flops 1024 | bytes 1024 | tf_op jit(solution)/shard_map/pick_rows/pallas_call | solution.py:133
  13.0 6.6 %attend.1 = (bf16[512,1024]{1,0:T(8,128)(2,1)}, bf16[3,512,256]{2,1,0:T(8,128)(2,1)}, bf16[4,512,256]{2,1,0:T(8,128)(2,1)}, bf16[4,256,256]{2,1,0:T(8,128)(2,1)}, bf16[4,256,512]{2,1,0:T(8,128)(2,1)}) custom-call(bf16[512,1024]{1,0:T(8,128)(2,1)} %pick_rows.1.refs_0_.picked_ref.refs_8_, bf16[1024]{0:T(1024)(128)(2,1)} %refs_1_.1, ...), custom_call_target="tpu_custom_call" | custom-call | flops 1024 | bytes 1024 | tf_op jit(solution)/shard_map/attend/pallas_call | solution.py:86
  19.6 5.0 %all-to-all-start = ((bf16[4,512,256]{2,1,0:T(8,128)(2,1)}), bf16[4,512,256]{2,1,0:T(8,128)(2,1)S(1)}, u32[]{:S(2)}, u32[]{:S(2)}) async-start(bf16[4,512,256]{2,1,0:T(8,128)(2,1)} %get-tuple-element.171), calls=%async_computation | async-start | bytes 2097152 | tf_op jit(solution)/shard_map/all_to_all | solution.py:26
  24.8 1.6 collective-permute-start.3
  26.4 6.0 %pick_only.1.rows_ref = bf16[512,1024]{1,0:T(8,128)(2,1)} custom-call(bf16[4096,1024]{1,0:T(8,128)(2,1)} %base_ref.10, s32[1,512]{1,0:T(1,128)} %offset_ref.11), custom_call_target="tpu_custom_call" | custom-call | flops 1024 | bytes 1024 | tf_op jit(solution)/shard_map/pick_only/pallas_call | solution.py:186
  32.4 4.0 %collective-permute-done.3.refs_6_ = bf16[3,64,1024]{2,1,0:T(8,128)(2,1)S(1)} collective-permute-done((bf16[3,64,1024]{2,1,0:T(8,128)(2,1)S(1)}, bf16[3,64,1024]{2,1,0:T(8,128)(2,1)S(1)}, u32[]{:S(2)}, u32[]{:S(2)}) %collective-permute-start.3) | collective-permute-done | bytes 393248 | tf_op jit(solution)/shard_map/ppermute | solution.py:22
  37.0 2.7 %score_sums.1.square_ref = f32[1,128]{1,0:T(1,128)} custom-call(s32[1]{0:T(128)} %bitcast.1.mine_ref.refs_1_.part_ref, bf16[4096,1024]{1,0:T(8,128)(2,1)} %base_ref.9, bf16[1,1024]{1,0:T(2,128)(2,1)} %broadcast_in_dim.9.router_ref), custom_call_target="tpu_custom_call" | custom-call | flops 1024 | bytes 1024 | tf_op jit(solution)/shard_map/score_sums/pallas_call | solution.py:153
  40.3 5.1 %act_grads.1 = (f32[512,1]{1,0:T(8,128)}, f32[1,128]{1,0:T(1,128)}, bf16[512,1024]{1,0:T(8,128)(2,1)}, f32[512,1024]{1,0:T(8,128)}) custom-call(bf16[512,1024]{1,0:T(8,128)(2,1)} %pick_rows.1.refs_0_.picked_ref.refs_8_, bf16[1,1024]{1,0:T(2,128)(2,1)} %broadcast_in_dim.9.router_ref, bf16[512,1024]{1,0:T(8,128)(2,1)} %pick_only.1.rows_ref, ...), custom_call_target="tpu_custom_call" | custom-call | flops 1024 | bytes 1024 | tf_op jit(solution)/shard_map/act_grads/pallas_call | solution.py:397
  45.4 4.1 %all-to-all-done.refs_2_.heads_ref = bf16[4,512,256]{2,1,0:T(8,128)(2,1)S(1)} async-done(((bf16[4,512,256]{2,1,0:T(8,128)(2,1)}), bf16[4,512,256]{2,1,0:T(8,128)(2,1)S(1)}, u32[]{:S(2)}, u32[]{:S(2)}) %all-to-all-start) | async-done | bytes 1048608 | tf_op jit(solution)/shard_map/all_to_all | solution.py:26
  50.5 9.4 %feed_forward.1 = (f32[128,1024]{1,0:T(8,128)}, bf16[512,1024]{1,0:T(8,128)(2,1)}, bf16[512,1024]{1,0:T(8,128)(2,1)}, bf16[512,1024]{1,0:T(8,128)(2,1)}, bf16[51...) custom-call(s32[1]{0:T(128)} %bitcast.refs_0_.part_ref, ...), custom_call_target="tpu_custom_call" | custom-call | flops 1024 | bytes 1024 | tf_op jit(solution)/shard_map/feed_forward/pallas_call | solution.py:86
  60.0 4.6 %all-to-all-start.1 = ((bf16[4,512,256]{2,1,0:T(8,128)(2,1)}), bf16[4,512,256]{2,1,0:T(8,128)(2,1)}, u32[]{:S(2)}, u32[]{:S(2)}) async-start(bf16[4,512,256]{2,1,0:T(8,128)(2,1)} %get-tuple-element.192), calls=%async_computation.1 | async-start | bytes 2097152 | tf_op jit(solution)/shard_map/all_to_all | solution.py:26
  69.6 3.9 %core_grads.1 = (bf16[2,768,1024]{2,1,0:T(8,128)(2,1)S(1)}, bf16[512,1024]{1,0:T(8,128)(2,1)S(1)}, bf16[512,1024]{1,0:T(8,128)(2,1)S(1)}, bf16[256,1024]{1,0:T(8,128)(2,1)S(1)}, bf16[256,1024]{1,0:T(8,128)(2,1)S(1)}) custom-call(s32[1]{0:T(128)} %bitcast.refs_0_.part_ref, bf16[512,1024]{1,0:T(8,128)(2,1)S(1)} %copy-done.10, bf16[512,1024]{1,0:T(8,128)(2,1)S(1)} %copy-done.6, ...), custom_call_target="tpu_custom_call" | custom-call | flops 1024 | bytes 1024 | tf_op jit(solution)/shard_map/core_grads/pallas_call | solution.py:622
  74.5 2.2 %convolution_convert_fusion = bf16[512,1024]{1,0:T(8,128)(2,1)} fusion(bf16[512,1024]{1,0:T(8,128)(2,1)S(1)} %copy-done.11, bf16[1024,1024]{1,0:T(8,128)(2,1)S(1)} %copy-done.42), kind=kOutput, calls=%fused_computation | convolution fusion | flops 1074266112 | bytes 4194304 | tf_op jit(solution)/shard_map/dot_general | solution.py:17
  76.8 1.6 collective-permute-done.8.refs_1_
  82.9 6.8 %all-to-all-done.1.head_ref = bf16[4,512,256]{2,1,0:T(8,128)(2,1)} async-done(((bf16[4,512,256]{2,1,0:T(8,128)(2,1)}), bf16[4,512,256]{2,1,0:T(8,128)(2,1)}, u32[]{:S(2)}, u32[]{:S(2)}) %all-to-all-start.1) | async-done | bytes 1048608 | tf_op jit(solution)/shard_map/all_to_all | solution.py:26
  89.7 4.2 %all-to-all-start.2 = ((bf16[4,128,1024]{2,1,0:T(8,128)(2,1)}), bf16[4,128,1024]{2,1,0:T(8,128)(2,1)}, u32[]{:S(2)}, u32[]{:S(2)}) async-start(bf16[4,128,1024]{2,1,0:T(8,128)(2,1)} %bitcast.14), calls=%async_computation.2 | async-start | bytes 2097152 | tf_op jit(solution)/shard_map/all_to_all | solution.py:26
  93.9 1.5 collective-permute-start.10
  95.5 1.5 collective-permute-start.11
  100.6 6.7 %attend_back.1 = (bf16[3,512,256]{2,1,0:T(8,128)(2,1)S(1)}, f32[1,1024]{1,0:T(1,128)S(1)}, bf16[512,1024]{1,0:T(8,128)(2,1)}) custom-call(bf16[4,512,256]{2,1,0:T(8,128)(2,1)} %all-to-all-done.1.head_ref, bf16[3,512,256]{2,1,0:T(8,128)(2,1)S(1)} %copy-done.18, bf16[3,1024,256]{2,1,0:T(8,128)(2,1)S(1)} %copy-done.5, bf16[512,1024]{1,0:T(8,128)(2,1)S(1)} %copy-done, ...), custom_call_target="tpu_custom_call" | custom-call | flops 1024 | bytes 1024 | tf_op jit(solution)/shard_map/attend_back/pallas_call | solution.py:473
  109.3 3.4 %collective-permute-done.10.refs_0_ = bf16[384,1024]{1,0:T(8,128)(2,1)S(1)} collective-permute-done((bf16[384,1024]{1,0:T(8,128)(2,1)}, bf16[384,1024]{1,0:T(8,128)(2,1)S(1)}, u32[]{:S(2)}, u32[]{:S(2)}) %collective-permute-start.10) | collective-permute-done | bytes 786464 | tf_op jit(solution)/shard_map/ppermute | solution.py:22
  115.8 3.4 %all-to-all-done.2.terms_ref = bf16[4,128,1024]{2,1,0:T(8,128)(2,1)} async-done(((bf16[4,128,1024]{2,1,0:T(8,128)(2,1)}), bf16[4,128,1024]{2,1,0:T(8,128)(2,1)}, u32[]{:S(2)}, u32[]{:S(2)}) %all-to-all-start.2) | async-done | bytes 1048608 | tf_op jit(solution)/shard_map/all_to_all | solution.py:26
  119.2 3.8 %all-to-all-start.3 = ((bf16[4,128,1024]{2,1,0:T(8,128)(2,1)}), bf16[4,128,1024]{2,1,0:T(8,128)(2,1)S(1)}, u32[]{:S(2)}, u32[]{:S(2)}) async-start(bf16[4,128,1024]{2,1,0:T(8,128)(2,1)} %bitcast.6), calls=%async_computation.3 | async-start | bytes 2097152 | tf_op jit(solution)/shard_map/all_to_all | solution.py:26
  123.1 1.6 collective-permute-start.13
  124.7 1.5 collective-permute-start.14
  126.2 2.6 %finish_rows.1 = (bf16[128,1024]{1,0:T(8,128)(2,1)}, f32[128,1]{1,0:T(8,128)}, f32[4,1024]{1,0:T(4,128)}) custom-call(s32[1]{0:T(128)} %bitcast.1.mine_ref.refs_1_.part_ref, bf16[4,128,1024]{2,1,0:T(8,128)(2,1)} %all-to-all-done.2.terms_ref, bf16[512,1024]{1,0:T(8,128)(2,1)} %pick_rows.1.refs_0_.picked_ref.refs_8_, f32[512,1]{1,0:T(8,128)} %get-tuple-element.238.gating_ref, ...), custom_call_target="tpu_custom_call" | custom-call | flops 1024 | bytes 30000000 | tf_op jit(solution)/shard_map/finish_rows/pallas_call | solution.py:882
  128.8 6.0 %collective-permute-done.13.a_got = bf16[192,1024]{1,0:T(8,128)(2,1)S(1)} collective-permute-done((bf16[192,1024]{1,0:T(8,128)(2,1)}, bf16[192,1024]{1,0:T(8,128)(2,1)S(1)}, u32[]{:S(2)}, u32[]{:S(2)}) %collective-permute-start.13) | collective-permute-done | bytes 393248 | tf_op jit(solution)/shard_map/ppermute | solution.py:22
  134.8 1.3 collective-permute-done.14.b_got
  140.6 1.5 collective-permute-start.16
  144.2 3.6 %collective-permute-done.15.refs_1_ = bf16[128,1024]{1,0:T(8,128)(2,1)} collective-permute-done((bf16[128,1024]{1,0:T(8,128)(2,1)S(1)}, bf16[128,1024]{1,0:T(8,128)(2,1)}, u32[]{:S(2)}, u32[]{:S(2)}) %collective-permute-start.15) | collective-permute-done | bytes 262176 | tf_op jit(solution)/shard_map/ppermute | solution.py:22
  148.1 4.8 %all-to-all-start.4 = ((bf16[4,168,1024]{2,1,0:T(8,128)(2,1)}), bf16[4,168,1024]{2,1,0:T(8,128)(2,1)S(1)}, u32[]{:S(2)}, u32[]{:S(2)}) async-start(bf16[4,168,1024]{2,1,0:T(8,128)(2,1)} %copy-done.9), calls=%async_computation.4 | async-start | bytes 2752512 | tf_op jit(solution)/shard_map/all_to_all | solution.py:26
  152.9 1.5 collective-permute-start.17
  154.4 1.4 collective-permute-start.19
  158.9 1.9 gather_blocks.2
  162.8 3.7 %merge_rows.4.rest_0_ = bf16[4096,1024]{1,0:T(8,128)(2,1)} custom-call(s32[1]{0:T(128)} %bitcast.1.mine_ref.refs_1_.part_ref, bf16[4096,1024]{1,0:T(8,128)(2,1)} %base_ref.10, s32[1,512]{1,0:T(1,128)} %offset_ref.11, bf16[4,128,1024]{2,1,0:T(8,128)(2,1)} %finish_input.1.piece_ref), custom_call_target="tpu_custom_call" | custom-call | flops 1024 | bytes 1024 | tf_op jit(solution)/shard_map/merge_rows/pallas_call | solution.py:232
  168.9 1.4 collective-permute-start.25
  170.3 1.5 collective-permute-start.26
  173.4 8.0 %spread_rows.1 = (f32[1024,1024]{1,0:T(8,128)}, f32[1024,1024]{1,0:T(8,128)}) custom-call(s32[1]{0:T(128)} %bitcast.refs_0_.part_ref, bf16[256,1024]{1,0:T(8,128)(2,1)} %get-tuple-element.265.refs_0_, bf16[256,1024]{1,0:T(8,128)(2,1)} %copy-done.22, bf16[256,1024]{1,0:T(8,128)(2,1)} %collective-permute-done.21.refs_2_, bf16[256,1024]{1,0:T(8,128)(2,1)} %copy-done.45, ...), custom_call_target="tpu_custom_call" | custom-call | flops 1024 | bytes 1024 | tf_op jit(solution)/shard_map/spread_rows/pallas_call | solution.py:517
  181.4 2.7 %all-to-all-done.4.got_ref.piece_ref = bf16[4,168,1024]{2,1,0:T(8,128)(2,1)S(1)} async-done(((bf16[4,168,1024]{2,1,0:T(8,128)(2,1)}), bf16[4,168,1024]{2,1,0:T(8,128)(2,1)S(1)}, u32[]{:S(2)}, u32[]{:S(2)}) %all-to-all-start.4) | async-done | bytes 1376288 | tf_op jit(solution)/shard_map/all_to_all | solution.py:26
  184.1 4.2 %all-to-all-start.5 = ((bf16[4,128,1024]{2,1,0:T(8,128)(2,1)}), bf16[4,128,1024]{2,1,0:T(8,128)(2,1)}, u32[]{:S(2)}, u32[]{:S(2)}) async-start(bf16[4,128,1024]{2,1,0:T(8,128)(2,1)} %finish_input.1.piece_ref), calls=%async_computation.5 | async-start | bytes 2097152 | tf_op jit(solution)/shard_map/all_to_all | solution.py:26
  189.8 1.6 collective-permute-start.29
  191.4 1.3 collective-permute-start.30
  193.2 4.4 %merge_rows.5.rest_0_ = bf16[4096,1024]{1,0:T(8,128)(2,1)} custom-call(s32[1]{0:T(128)} %bitcast.1.mine_ref.refs_1_.part_ref, bf16[4096,1024]{1,0:T(8,128)(2,1)} %base_ref.9, s32[1,512]{1,0:T(1,128)} %offset_ref.11, bf16[4,168,1024]{2,1,0:T(8,128)(2,1)} %copy-done.1), custom_call_target="tpu_custom_call" | custom-call | flops 1024 | bytes 1024 | tf_op jit(solution)/shard_map/merge_rows/pallas_call | solution.py:232
  197.6 4.1 %collective-permute-done.28.refs_1_ = bf16[40,1024]{1,0:T(8,128)(2,1)S(1)} collective-permute-done((bf16[40,1024]{1,0:T(8,128)(2,1)S(1)}, bf16[40,1024]{1,0:T(8,128)(2,1)S(1)}, u32[]{:S(2)}, u32[]{:S(2)}) %collective-permute-start.28) | collective-permute-done | bytes 81952 | tf_op jit(solution)/shard_map/ppermute | solution.py:22
  201.9 1.4 collective-permute-start.27
  204.5 4.4 %merge_rows.6 = bf16[4096,1024]{1,0:T(8,128)(2,1)} custom-call(s32[1]{0:T(128)} %bitcast.1.mine_ref.refs_1_.part_ref, bf16[4096,1024]{1,0:T(8,128)(2,1)} %base_ref.9, s32[1,512]{1,0:T(1,128)} %offset_ref.11, bf16[4,168,1024]{2,1,0:T(8,128)(2,1)} %copy-done.1, bf16[4096,1024]{1,0:T(8,128)(2,1)} %merge_rows.5.rest_0_), custom_call_target="tpu_custom_call", output_to_operand_aliasing={{}: (4, {})} | custom-call | flops 1024 | bytes 1024 | tf_op jit(solution)/shard_map/merge_rows/pallas_call | solution.py:232
  209.5 2.1 spread_qkv.1
  213.6 7.5 %merge_rows.7 = bf16[4096,1024]{1,0:T(8,128)(2,1)} custom-call(s32[1]{0:T(128)} %bitcast.1.mine_ref.refs_1_.part_ref, bf16[4096,1024]{1,0:T(8,128)(2,1)} %base_ref.10, s32[1,512]{1,0:T(1,128)} %offset_ref.11, bf16[4,128,1024]{2,1,0:T(8,128)(2,1)} %all-to-all-done.5.piece_ref, bf16[4096,1024]{1,0:T(8,128)(2,1)} %merge_rows.4.rest_0_), custom_call_target="tpu_custom_call", output_to_operand_aliasing={{}: (4, {})} | custom-call | flops 1024 | bytes 1024 | tf_op jit(solution)/shard_map/merge_rows/pallas_call | solution.py:232
  (175 shorter events, 44.8 us)
Async XLA Ops:
  1.6 18.1 %collective-permute-start.2 = (bf16[64,1024]{1,0:T(8,128)(2,1)S(1)}, bf16[64,1024]{1,0:T(8,128)(2,1)S(1)}, u32[]{:S(2)}, u32[]{:S(2)}) collective-permute-start(bf16[64,1024]{1,0:T(8,128)(2,1)S(1)} %constant_dynamic-slice_fusion), channel_id=1, source_target_pairs={{0,3},{1,2},{2,1},{3,0},{4,7},{5,6},{6,5},{7,4},{8,11},{9,10},{10,... | collective-permute-start | bytes 393224 | tf_op jit(solution)/shard_map/ppermute | solution.py:22
  6.7 12.9 %collective-permute-start.1 = (bf16[64,1024]{1,0:T(8,128)(2,1)S(1)}, bf16[64,1024]{1,0:T(8,128)(2,1)S(1)}, u32[]{:S(2)}, u32[]{:S(2)}) collective-permute-start(bf16[64,1024]{1,0:T(8,128)(2,1)S(1)} %constant_dynamic-slice_fusion), channel_id=1, source_target_pairs={{0,2},{1,3},{2,0},{3,1},{4,6},{5,7},{6,4},{7,5},{8,10},{9,11},{10,... | collective-permute-start | bytes 393224 | tf_op jit(solution)/shard_map/ppermute | solution.py:22
  6.7 13.0 %collective-permute-start = (bf16[64,1024]{1,0:T(8,128)(2,1)S(1)}, bf16[64,1024]{1,0:T(8,128)(2,1)S(1)}, u32[]{:S(2)}, u32[]{:S(2)}) collective-permute-start(bf16[64,1024]{1,0:T(8,128)(2,1)S(1)} %constant_dynamic-slice_fusion), channel_id=1, source_target_pairs={{0,1},{1,0},{2,3},{3,2},{4,5},{5,4},{6,7},{7,6},{8,9},{9,8},{10,11... | collective-permute-start | bytes 393224 | tf_op jit(solution)/shard_map/ppermute | solution.py:22
  19.6 29.9 %all-to-all-start = ((bf16[4,512,256]{2,1,0:T(8,128)(2,1)}), bf16[4,512,256]{2,1,0:T(8,128)(2,1)S(1)}, u32[]{:S(2)}, u32[]{:S(2)}) async-start(bf16[4,512,256]{2,1,0:T(8,128)(2,1)} %get-tuple-element.171), calls=%async_computation | async-start | bytes 2097152 | tf_op jit(solution)/shard_map/all_to_all | solution.py:26
  24.7 7.6 %collective-permute-start.4 = (bf16[3,64,1024]{2,1,0:T(8,128)(2,1)S(1)}, bf16[3,64,1024]{2,1,0:T(8,128)(2,1)S(1)}, u32[]{:S(2)}, u32[]{:S(2)}) collective-permute-start(bf16[3,64,1024]{2,1,0:T(8,128)(2,1)S(1)} %pad_maximum_fusion.refs_4_), channel_id=1, source_target_pairs={{0,4},{4,0},{8,12},{12,8},{16,20},{20,16},{24,28},{28,24},{1,5},{5... | collective-permute-start | bytes 1179656 | tf_op jit(solution)/shard_map/ppermute | solution.py:22
  24.8 11.5 %collective-permute-start.3 = (bf16[3,64,1024]{2,1,0:T(8,128)(2,1)S(1)}, bf16[3,64,1024]{2,1,0:T(8,128)(2,1)S(1)}, u32[]{:S(2)}, u32[]{:S(2)}) collective-permute-start(bf16[3,64,1024]{2,1,0:T(8,128)(2,1)S(1)} %pad_maximum_fusion.refs_4_), channel_id=1, source_target_pairs={{0,8},{4,12},{8,0},{12,4},{16,24},{20,28},{24,16},{28,20},{1,9},{5... | collective-permute-start | bytes 1179656 | tf_op jit(solution)/shard_map/ppermute | solution.py:22
  36.4 9.1 %collective-permute-start.5 = (bf16[3,64,1024]{2,1,0:T(8,128)(2,1)S(1)}, bf16[3,64,1024]{2,1,0:T(8,128)(2,1)S(1)}, u32[]{:S(2)}, u32[]{:S(2)}) collective-permute-start(bf16[3,64,1024]{2,1,0:T(8,128)(2,1)S(1)} %collective-permute-done.3.refs_6_), channel_id=1, source_target_pairs={{0,4},{4,0},{8,12},{12,8},{16,20},{20,16},{24,28},{28,24},{1,5},{5... | collective-permute-start | bytes 1179656 | tf_op jit(solution)/shard_map/ppermute | solution.py:22
  60.0 29.7 %all-to-all-start.1 = ((bf16[4,512,256]{2,1,0:T(8,128)(2,1)}), bf16[4,512,256]{2,1,0:T(8,128)(2,1)}, u32[]{:S(2)}, u32[]{:S(2)}) async-start(bf16[4,512,256]{2,1,0:T(8,128)(2,1)} %get-tuple-element.192), calls=%async_computation.1 | async-start | bytes 2097152 | tf_op jit(solution)/shard_map/all_to_all | solution.py:26
  73.4 5.7 %collective-permute-start.6 = (bf16[512,1024]{1,0:T(8,128)(2,1)S(1)}, bf16[512,1024]{1,0:T(8,128)(2,1)S(1)}, u32[]{:S(2)}, u32[]{:S(2)}) collective-permute-start(bf16[512,1024]{1,0:T(8,128)(2,1)S(1)} %get-tuple-element.197), channel_id=1, source_target_pairs={{0,4},{4,0},{8,12},{12,8},{16,20},{20,16},{24,28},{28,24},{1,5},{5... | collective-permute-start | bytes 3145736 | tf_op jit(solution)/shard_map/ppermute | solution.py:22
  73.5 5.7 %collective-permute-start.7 = (bf16[512,1024]{1,0:T(8,128)(2,1)S(1)}, bf16[512,1024]{1,0:T(8,128)(2,1)S(1)}, u32[]{:S(2)}, u32[]{:S(2)}) collective-permute-start(bf16[512,1024]{1,0:T(8,128)(2,1)S(1)} %get-tuple-element.198), channel_id=1, source_target_pairs={{0,4},{4,0},{8,12},{12,8},{16,20},{20,16},{24,28},{28,24},{1,5},{5... | collective-permute-start | bytes 3145736 | tf_op jit(solution)/shard_map/ppermute | solution.py:22
  74.0 4.4 %collective-permute-start.8 = (bf16[256,1024]{1,0:T(8,128)(2,1)S(1)}, bf16[256,1024]{1,0:T(8,128)(2,1)S(1)}, u32[]{:S(2)}, u32[]{:S(2)}) collective-permute-start(bf16[256,1024]{1,0:T(8,128)(2,1)S(1)} %get-tuple-element.199), channel_id=1, source_target_pairs={{0,4},{4,0},{8,12},{12,8},{16,20},{20,16},{24,28},{28,24},{1,5},{5... | collective-permute-start | bytes 1572872 | tf_op jit(solution)/shard_map/ppermute | solution.py:22
  74.1 5.1 %collective-permute-start.9 = (bf16[256,1024]{1,0:T(8,128)(2,1)S(1)}, bf16[256,1024]{1,0:T(8,128)(2,1)S(1)}, u32[]{:S(2)}, u32[]{:S(2)}) collective-permute-start(bf16[256,1024]{1,0:T(8,128)(2,1)S(1)} %get-tuple-element.200), channel_id=1, source_target_pairs={{0,4},{4,0},{8,12},{12,8},{16,20},{20,16},{24,28},{28,24},{1,5},{5... | collective-permute-start | bytes 1572872 | tf_op jit(solution)/shard_map/ppermute | solution.py:22
  79.2 17.9 %copy-start.5 = (bf16[3,1024,256]{2,1,0:T(8,128)(2,1)S(1)}, bf16[3,1024,256]{2,1,0:T(8,128)(2,1)}, u32[]{:S(2)}) copy-start(bf16[3,1024,256]{2,1,0:T(8,128)(2,1)} %weight_ref.1) | copy-start | bytes 4718596
  82.9 14.1 %copy-start.18 = (bf16[3,512,256]{2,1,0:T(8,128)(2,1)S(1)}, bf16[3,512,256]{2,1,0:T(8,128)(2,1)}, u32[]{:S(2)}) copy-start(bf16[3,512,256]{2,1,0:T(8,128)(2,1)} %get-tuple-element.215.qkv_ref) | copy-start | bytes 2359300
  89.7 29.5 %all-to-all-start.2 = ((bf16[4,128,1024]{2,1,0:T(8,128)(2,1)}), bf16[4,128,1024]{2,1,0:T(8,128)(2,1)}, u32[]{:S(2)}, u32[]{:S(2)}) async-start(bf16[4,128,1024]{2,1,0:T(8,128)(2,1)} %bitcast.14), calls=%async_computation.2 | async-start | bytes 2097152 | tf_op jit(solution)/shard_map/all_to_all | solution.py:26
  93.9 18.8 %collective-permute-start.10 = (bf16[384,1024]{1,0:T(8,128)(2,1)}, bf16[384,1024]{1,0:T(8,128)(2,1)S(1)}, u32[]{:S(2)}, u32[]{:S(2)}) collective-permute-start(bf16[384,1024]{1,0:T(8,128)(2,1)} %copy-done.39), channel_id=1, source_target_pairs={{0,8},{4,12},{8,0},{12,4},{16,24},{20,28},{24,16},{28,20},{1,9},{5... | collective-permute-start | bytes 2359304 | tf_op jit(solution)/shard_map/ppermute | solution.py:22
  95.5 18.4 %collective-permute-start.11 = (bf16[384,1024]{1,0:T(8,128)(2,1)}, bf16[384,1024]{1,0:T(8,128)(2,1)S(1)}, u32[]{:S(2)}, u32[]{:S(2)}) collective-permute-start(bf16[384,1024]{1,0:T(8,128)(2,1)} %copy-done.38), channel_id=1, source_target_pairs={{0,16},{4,20},{8,24},{12,28},{16,0},{20,4},{24,8},{28,12},{1,17},{... | collective-permute-start | bytes 2359304 | tf_op jit(solution)/shard_map/ppermute | solution.py:22
  119.2 28.9 %all-to-all-start.3 = ((bf16[4,128,1024]{2,1,0:T(8,128)(2,1)}), bf16[4,128,1024]{2,1,0:T(8,128)(2,1)S(1)}, u32[]{:S(2)}, u32[]{:S(2)}) async-start(bf16[4,128,1024]{2,1,0:T(8,128)(2,1)} %bitcast.6), calls=%async_computation.3 | async-start | bytes 2097152 | tf_op jit(solution)/shard_map/all_to_all | solution.py:26
  123.0 19.1 %collective-permute-start.12 = (bf16[384,1024]{1,0:T(8,128)(2,1)}, bf16[384,1024]{1,0:T(8,128)(2,1)}, u32[]{:S(2)}, u32[]{:S(2)}) collective-permute-start(bf16[384,1024]{1,0:T(8,128)(2,1)} %copy-done.37), channel_id=1, source_target_pairs={{0,4},{4,0},{8,12},{12,8},{16,20},{20,16},{24,28},{28,24},{1,5},{5... | collective-permute-start | bytes 2359304 | tf_op jit(solution)/shard_map/ppermute | solution.py:22
  123.1 11.7 %collective-permute-start.13 = (bf16[192,1024]{1,0:T(8,128)(2,1)}, bf16[192,1024]{1,0:T(8,128)(2,1)S(1)}, u32[]{:S(2)}, u32[]{:S(2)}) collective-permute-start(bf16[192,1024]{1,0:T(8,128)(2,1)} %copy-done.41), channel_id=1, source_target_pairs={{0,16},{4,20},{8,24},{12,28},{16,0},{20,4},{24,8},{28,12},{1,17},{... | collective-permute-start | bytes 1179656 | tf_op jit(solution)/shard_map/ppermute | solution.py:22
  124.7 11.5 %collective-permute-start.14 = (bf16[192,1024]{1,0:T(8,128)(2,1)}, bf16[192,1024]{1,0:T(8,128)(2,1)}, u32[]{:S(2)}, u32[]{:S(2)}) collective-permute-start(bf16[192,1024]{1,0:T(8,128)(2,1)} %copy-done.40), channel_id=1, source_target_pairs={{0,8},{4,12},{8,0},{12,4},{16,24},{20,28},{24,16},{28,20},{1,9},{5... | collective-permute-start | bytes 1179656 | tf_op jit(solution)/shard_map/ppermute | solution.py:22
  140.1 7.7 %collective-permute-start.15 = (bf16[128,1024]{1,0:T(8,128)(2,1)S(1)}, bf16[128,1024]{1,0:T(8,128)(2,1)}, u32[]{:S(2)}, u32[]{:S(2)}) collective-permute-start(bf16[128,1024]{1,0:T(8,128)(2,1)S(1)} %get-tuple-element.261.refs_0_), channel_id=1, source_target_pairs={{0,16},{4,20},{8,24},{12,28},{16,0},{20,4},{24,8},{28,12},{1,17},{... | collective-permute-start | bytes 786440 | tf_op jit(solution)/shard_map/ppermute | solution.py:22
  140.6 7.5 %collective-permute-start.16 = (bf16[128,1024]{1,0:T(8,128)(2,1)S(1)}, bf16[128,1024]{1,0:T(8,128)(2,1)}, u32[]{:S(2)}, u32[]{:S(2)}) collective-permute-start(bf16[128,1024]{1,0:T(8,128)(2,1)S(1)} %get-tuple-element.263.refs_2_), channel_id=1, source_target_pairs={{0,8},{4,12},{8,0},{12,4},{16,24},{20,28},{24,16},{28,20},{1,9},{5... | collective-permute-start | bytes 786440 | tf_op jit(solution)/shard_map/ppermute | solution.py:22
  144.2 17.3 %copy-start.2 = (bf16[512,1024]{1,0:T(8,128)(2,1)S(1)}, bf16[512,1024]{1,0:T(8,128)(2,1)}, u32[]{:S(2)}) copy-start(bf16[512,1024]{1,0:T(8,128)(2,1)} %pick_only.1.rows_ref) | copy-start | bytes 3145732
  144.2 17.3 %copy-start.33 = (bf16[1,1024]{1,0:T(2,128)(2,1)S(1)}, bf16[1,1024]{1,0:T(2,128)(2,1)}, u32[]{:S(2)}) copy-start(bf16[1,1024]{1,0:T(2,128)(2,1)} %broadcast_in_dim.9.router_ref) | copy-start | bytes 6148
  144.2 17.3 %copy-start.34 = (f32[128,1]{1,0:T(8,128)S(1)}, f32[128,1]{1,0:T(8,128)}, u32[]{:S(2)}) copy-start(f32[128,1]{1,0:T(8,128)} %get-tuple-element.259.score_ref) | copy-start | bytes 1540
  148.1 36.0 %all-to-all-start.4 = ((bf16[4,168,1024]{2,1,0:T(8,128)(2,1)}), bf16[4,168,1024]{2,1,0:T(8,128)(2,1)S(1)}, u32[]{:S(2)}, u32[]{:S(2)}) async-start(bf16[4,168,1024]{2,1,0:T(8,128)(2,1)} %copy-done.9), calls=%async_computation.4 | async-start | bytes 2752512 | tf_op jit(solution)/shard_map/all_to_all | solution.py:26
  152.9 13.6 %collective-permute-start.17 = (bf16[128,1024]{1,0:T(8,128)(2,1)}, bf16[128,1024]{1,0:T(8,128)(2,1)}, u32[]{:S(2)}, u32[]{:S(2)}) collective-permute-start(bf16[128,1024]{1,0:T(8,128)(2,1)} %copy-done.31), channel_id=1, source_target_pairs={{0,8},{4,12},{8,0},{12,4},{16,24},{20,28},{24,16},{28,20},{1,9},{5... | collective-permute-start | bytes 786440 | tf_op jit(solution)/shard_map/ppermute | solution.py:22
  154.4 12.6 %collective-permute-start.19 = (bf16[128,1024]{1,0:T(8,128)(2,1)}, bf16[128,1024]{1,0:T(8,128)(2,1)}, u32[]{:S(2)}, u32[]{:S(2)}) collective-permute-start(bf16[128,1024]{1,0:T(8,128)(2,1)} %copy-done.29), channel_id=1, source_target_pairs={{0,16},{4,20},{8,24},{12,28},{16,0},{20,4},{24,8},{28,12},{1,17},{... | collective-permute-start | bytes 786440 | tf_op jit(solution)/shard_map/ppermute | solution.py:22
  155.8 11.2 %collective-permute-start.18 = (bf16[128,1024]{1,0:T(8,128)(2,1)}, bf16[128,1024]{1,0:T(8,128)(2,1)}, u32[]{:S(2)}, u32[]{:S(2)}) collective-permute-start(bf16[128,1024]{1,0:T(8,128)(2,1)} %collective-permute-done.15.refs_1_), channel_id=1, source_target_pairs={{0,8},{4,12},{8,0},{12,4},{16,24},{20,28},{24,16},{28,20},{1,9},{5... | collective-permute-start | bytes 786440 | tf_op jit(solution)/shard_map/ppermute | solution.py:22
  156.4 10.6 %collective-permute-start.20 = (bf16[128,1024]{1,0:T(8,128)(2,1)}, bf16[128,1024]{1,0:T(8,128)(2,1)}, u32[]{:S(2)}, u32[]{:S(2)}) collective-permute-start(bf16[128,1024]{1,0:T(8,128)(2,1)} %collective-permute-done.16.refs_3_), channel_id=1, source_target_pairs={{0,16},{4,20},{8,24},{12,28},{16,0},{20,4},{24,8},{28,12},{1,17},{... | collective-permute-start | bytes 786440 | tf_op jit(solution)/shard_map/ppermute | solution.py:22
  161.5 8.8 %collective-permute-start.21 = (bf16[256,1024]{1,0:T(8,128)(2,1)}, bf16[256,1024]{1,0:T(8,128)(2,1)}, u32[]{:S(2)}, u32[]{:S(2)}) collective-permute-start(bf16[256,1024]{1,0:T(8,128)(2,1)} %get-tuple-element.265.refs_0_), channel_id=1, source_target_pairs={{0,4},{4,0},{8,12},{12,8},{16,20},{20,16},{24,28},{28,24},{1,5},{5... | collective-permute-start | bytes 1572872 | tf_op jit(solution)/shard_map/ppermute | solution.py:22
  166.5 5.3 %collective-permute-start.23 = (bf16[256,1024]{1,0:T(8,128)(2,1)S(1)}, bf16[256,1024]{1,0:T(8,128)(2,1)S(1)}, u32[]{:S(2)}, u32[]{:S(2)}) collective-permute-start(bf16[256,1024]{1,0:T(8,128)(2,1)S(1)} %copy-done.21), channel_id=1, source_target_pairs={{0,4},{4,0},{8,12},{12,8},{16,20},{20,16},{24,28},{28,24},{1,5},{5... | collective-permute-start | bytes 1572872 | tf_op jit(solution)/shard_map/ppermute | solution.py:22
  168.3 3.5 %collective-permute-start.22 = (bf16[256,1024]{1,0:T(8,128)(2,1)S(1)}, bf16[256,1024]{1,0:T(8,128)(2,1)S(1)}, u32[]{:S(2)}, u32[]{:S(2)}) collective-permute-start(bf16[256,1024]{1,0:T(8,128)(2,1)S(1)} %get-tuple-element.273.refs_1_), channel_id=1, source_target_pairs={{0,4},{4,0},{8,12},{12,8},{16,20},{20,16},{24,28},{28,24},{1,5},{5... | collective-permute-start | bytes 1572872 | tf_op jit(solution)/shard_map/ppermute | solution.py:22
  168.4 5.0 %collective-permute-start.24 = (bf16[256,1024]{1,0:T(8,128)(2,1)S(1)}, bf16[256,1024]{1,0:T(8,128)(2,1)}, u32[]{:S(2)}, u32[]{:S(2)}) collective-permute-start(bf16[256,1024]{1,0:T(8,128)(2,1)S(1)} %get-tuple-element.275.refs_5_), channel_id=1, source_target_pairs={{0,4},{4,0},{8,12},{12,8},{16,20},{20,16},{24,28},{28,24},{1,5},{5... | collective-permute-start | bytes 1572872 | tf_op jit(solution)/shard_map/ppermute | solution.py:22
  168.9 19.6 %collective-permute-start.25 = (bf16[192,1024]{1,0:T(8,128)(2,1)S(1)}, bf16[192,1024]{1,0:T(8,128)(2,1)}, u32[]{:S(2)}, u32[]{:S(2)}) collective-permute-start(bf16[192,1024]{1,0:T(8,128)(2,1)S(1)} %copy-done.25), channel_id=1, source_target_pairs={{0,16},{4,20},{8,24},{12,28},{16,0},{20,4},{24,8},{28,12},{1,17},{... | collective-permute-start | bytes 1179656 | tf_op jit(solution)/shard_map/ppermute | solution.py:22
  170.3 18.2 %collective-permute-start.26 = (bf16[192,1024]{1,0:T(8,128)(2,1)}, bf16[192,1024]{1,0:T(8,128)(2,1)}, u32[]{:S(2)}, u32[]{:S(2)}) collective-permute-start(bf16[192,1024]{1,0:T(8,128)(2,1)} %copy-done.26), channel_id=1, source_target_pairs={{0,8},{4,12},{8,0},{12,4},{16,24},{20,28},{24,16},{28,20},{1,9},{5... | collective-permute-start | bytes 1179656 | tf_op jit(solution)/shard_map/ppermute | solution.py:22
  184.1 29.5 %all-to-all-start.5 = ((bf16[4,128,1024]{2,1,0:T(8,128)(2,1)}), bf16[4,128,1024]{2,1,0:T(8,128)(2,1)}, u32[]{:S(2)}, u32[]{:S(2)}) async-start(bf16[4,128,1024]{2,1,0:T(8,128)(2,1)} %finish_input.1.piece_ref), calls=%async_computation.5 | async-start | bytes 2097152 | tf_op jit(solution)/shard_map/all_to_all | solution.py:26
  189.8 11.9 %collective-permute-start.29 = (bf16[192,1024]{1,0:T(8,128)(2,1)S(1)}, bf16[192,1024]{1,0:T(8,128)(2,1)S(1)}, u32[]{:S(2)}, u32[]{:S(2)}) collective-permute-start(bf16[192,1024]{1,0:T(8,128)(2,1)S(1)} %get-tuple-element.291.a_ref), channel_id=1, source_target_pairs={{0,8},{4,12},{8,0},{12,4},{16,24},{20,28},{24,16},{28,20},{1,9},{5... | collective-permute-start | bytes 1179656 | tf_op jit(solution)/shard_map/ppermute | solution.py:22
  191.4 10.3 %collective-permute-start.30 = (bf16[192,1024]{1,0:T(8,128)(2,1)S(1)}, bf16[192,1024]{1,0:T(8,128)(2,1)S(1)}, u32[]{:S(2)}, u32[]{:S(2)}) collective-permute-start(bf16[192,1024]{1,0:T(8,128)(2,1)S(1)} %get-tuple-element.293.b_ref), channel_id=1, source_target_pairs={{0,16},{4,20},{8,24},{12,28},{16,0},{20,4},{24,8},{28,12},{1,17},{... | collective-permute-start | bytes 1179656 | tf_op jit(solution)/shard_map/ppermute | solution.py:22
  192.7 9.0 %collective-permute-start.28 = (bf16[40,1024]{1,0:T(8,128)(2,1)S(1)}, bf16[40,1024]{1,0:T(8,128)(2,1)S(1)}, u32[]{:S(2)}, u32[]{:S(2)}) collective-permute-start(bf16[40,1024]{1,0:T(8,128)(2,1)S(1)} %first_small.1.refs_0_), channel_id=1, source_target_pairs={{0,8},{4,12},{8,0},{12,4},{16,24},{20,28},{24,16},{28,20},{1,9},{5... | collective-permute-start | bytes 245768 | tf_op jit(solution)/shard_map/ppermute | solution.py:22
  201.8 7.1 %collective-permute-start.32 = (bf16[384,1024]{1,0:T(8,128)(2,1)S(1)}, bf16[384,1024]{1,0:T(8,128)(2,1)S(1)}, u32[]{:S(2)}, u32[]{:S(2)}) collective-permute-start(bf16[384,1024]{1,0:T(8,128)(2,1)S(1)} %joined_lanes.1.near_ref), channel_id=1, source_target_pairs={{0,4},{4,0},{8,12},{12,8},{16,20},{20,16},{24,28},{28,24},{1,5},{5... | collective-permute-start | bytes 2359304 | tf_op jit(solution)/shard_map/ppermute | solution.py:22
  201.9 7.0 %collective-permute-start.27 = (bf16[40,1024]{1,0:T(8,128)(2,1)S(1)}, bf16[40,1024]{1,0:T(8,128)(2,1)S(1)}, u32[]{:S(2)}, u32[]{:S(2)}) collective-permute-start(bf16[40,1024]{1,0:T(8,128)(2,1)S(1)} %first_small.1.refs_0_), channel_id=1, source_target_pairs={{0,16},{4,20},{8,24},{12,28},{16,0},{20,4},{24,8},{28,12},{1,17},{... | collective-permute-start | bytes 245768 | tf_op jit(solution)/shard_map/ppermute | solution.py:22
  203.3 5.6 %collective-permute-start.31 = (bf16[40,1024]{1,0:T(8,128)(2,1)S(1)}, bf16[40,1024]{1,0:T(8,128)(2,1)S(1)}, u32[]{:S(2)}, u32[]{:S(2)}) collective-permute-start(bf16[40,1024]{1,0:T(8,128)(2,1)S(1)} %collective-permute-done.28.refs_1_), channel_id=1, source_target_pairs={{0,16},{4,20},{8,24},{12,28},{16,0},{20,4},{24,8},{28,12},{1,17},{... | collective-permute-start | bytes 245768 | tf_op jit(solution)/shard_map/ppermute | solution.py:22
  204.0 7.6 %collective-permute-start.33 = (bf16[40,1024]{1,0:T(8,128)(2,1)S(1)}, bf16[40,1024]{1,0:T(8,128)(2,1)S(1)}, u32[]{:S(2)}, u32[]{:S(2)}) collective-permute-start(bf16[40,1024]{1,0:T(8,128)(2,1)S(1)} %first_small.1.refs_0_), channel_id=1, source_target_pairs={{0,4},{4,0},{8,12},{12,8},{16,20},{20,16},{24,28},{28,24},{1,5},{5... | collective-permute-start | bytes 245768 | tf_op jit(solution)/shard_map/ppermute | solution.py:22
  204.0 7.6 %collective-permute-start.34 = (bf16[40,1024]{1,0:T(8,128)(2,1)S(1)}, bf16[40,1024]{1,0:T(8,128)(2,1)S(1)}, u32[]{:S(2)}, u32[]{:S(2)}) collective-permute-start(bf16[40,1024]{1,0:T(8,128)(2,1)S(1)} %collective-permute-done.28.refs_1_), channel_id=1, source_target_pairs={{0,4},{4,0},{8,12},{12,8},{16,20},{20,16},{24,28},{28,24},{1,5},{5... | collective-permute-start | bytes 245768 | tf_op jit(solution)/shard_map/ppermute | solution.py:22
  208.9 2.7 %collective-permute-start.35 = (bf16[40,1024]{1,0:T(8,128)(2,1)S(1)}, bf16[40,1024]{1,0:T(8,128)(2,1)S(1)}, u32[]{:S(2)}, u32[]{:S(2)}) collective-permute-start(bf16[40,1024]{1,0:T(8,128)(2,1)S(1)} %collective-permute-done.27.refs_2_), channel_id=1, source_target_pairs={{0,4},{4,0},{8,12},{12,8},{16,20},{20,16},{24,28},{28,24},{1,5},{5... | collective-permute-start | bytes 245768 | tf_op jit(solution)/shard_map/ppermute | solution.py:22
  209.0 2.7 %collective-permute-start.36 = (bf16[40,1024]{1,0:T(8,128)(2,1)S(1)}, bf16[40,1024]{1,0:T(8,128)(2,1)S(1)}, u32[]{:S(2)}, u32[]{:S(2)}) collective-permute-start(bf16[40,1024]{1,0:T(8,128)(2,1)S(1)} %collective-permute-done.31.refs_3_), channel_id=1, source_target_pairs={{0,4},{4,0},{8,12},{12,8},{16,20},{20,16},{24,28},{28,24},{1,5},{5... | collective-permute-start | bytes 245768 | tf_op jit(solution)/shard_map/ppermute | solution.py:22
  (47 other events, 178.5 us)
